TPU v7x, 512 devices: a whole 4x4x16 slice. The times are simulated.
512 devices in a mesh: fsdp: 32 (over y, z_lo, core), head: 4 (over z_hi), seq: 4 (over x).
Axes of the slice: x: 4, y: 4, z: 16 (z_hi: 4, z_lo: 4; z = z_hi * 4 + z_lo), core: 2. Of those that a mesh axis runs over, the one named last changes fastest.
Arguments:
- latents: bfloat16 [6144, 6144], P('fsdp', ('head', 'seq')), may hold values from -100 to 100
- train_qkv: bfloat16 [3, 6144, 4096], P(None, 'fsdp', ('head', 'seq')), may hold values from -0.078125 to 0.078125
- ema_qkv: bfloat16 [3, 6144, 4096], P(None, 'fsdp', ('head', 'seq')), may hold values from -0.078125 to 0.078125
- q_gain: float32 [128], replicated, may hold values from 0.8 to 2.5
- k_gain: float32 [128], replicated, may hold values from 0.8 to 2.5
- out_weight: bfloat16 [4096, 6144], P(('head', 'seq')), may hold values from -0.125 to 0.125
- modulation: float32 [8, 3, 6144], replicated, may hold values from -4 to 4
- timestep: int32 [1], replicated, may hold values from 0 to 7
- step: int32 [1], replicated, may hold values from 0 to 7
Outputs:
- block_output: bfloat16 [6144, 6144], P('fsdp', ('head', 'seq'))
All inputs are finite; a program needn't handle non-finite values.
Results may differ from a plain program's by a relative error of at most 0.025.
Values may be sent and summed in bfloat16 or wider, within the bound.
No kernel may reach another device: no remote copies, remote signals or barrier semaphores. Data moves between devices by JAX's collectives and lax.ppermute only.
A program may use at most 64 MiB of HBM per device.

v0:
```python
import math

import jax
import jax.numpy as jnp
from jax import lax
from jax.sharding import PartitionSpec as P

D = 6144
HD = 128


def head_norm(projected_part, gain, heads):
    shaped = projected_part.reshape(projected_part.shape[0], heads, HD)
    squares = jnp.mean(shaped * shaped, axis=2, keepdims=True)
    return (shaped * lax.rsqrt(squares + 1e-06) * gain).astype(jnp.bfloat16)


def per_device(latents, train_qkv, ema_qkv, q_gain, k_gain, out_weight, modulation, timestep, step):
    rows_here = latents.shape[0]
    local_width = latents.shape[1]
    channels = ema_qkv.shape[2]
    heads = channels // HD
    stepped = step[0].astype(jnp.float32)
    decay = (1.0 + stepped) / (10.0 + stepped)
    ema_weights = (
        decay * ema_qkv.astype(jnp.float32) + (1.0 - decay) * train_qkv.astype(jnp.float32)
    ).astype(jnp.bfloat16)
    chosen = (jnp.arange(modulation.shape[0], dtype=jnp.int32) == timestep[0]).astype(jnp.float32)
    mod_row = jnp.einsum("n,ncd->cd", chosen, modulation, precision=lax.Precision.HIGHEST)
    position = lax.axis_index(("head", "seq")) * local_width
    own_mod = lax.dynamic_slice_in_dim(mod_row, position, local_width, 1)
    widened = latents.astype(jnp.float32)
    average = lax.psum(jnp.sum(widened, axis=1), ("head", "seq")) / D
    centred = widened - average[:, None]
    variance = lax.psum(jnp.sum(centred * centred, axis=1), ("head", "seq")) / D
    shares = (
        centred * lax.rsqrt(variance + 1e-06)[:, None] * (1.0 + own_mod[1]) + own_mod[0]
    ).astype(jnp.bfloat16)
    hidden = lax.all_gather(shares, ("head", "seq"), axis=1, tiled=True)
    full_weights = lax.all_gather(ema_weights, "fsdp", axis=1, tiled=True)
    projected = jnp.einsum("td,jdh->jth", hidden, full_weights, preferred_element_type=jnp.float32)
    queries = head_norm(projected[0], q_gain, heads)
    keys = head_norm(projected[1], k_gain, heads).reshape(rows_here, channels)
    values = projected[2].astype(jnp.bfloat16)
    scaling = 1.0 / math.sqrt(HD)

    def one_block(carry, operands):
        numer, totals = carry
        key_block, value_block = operands
        scores = (
            jnp.einsum("qhd,khd->hqk", queries, key_block, preferred_element_type=jnp.float32)
            * scaling
        )
        expo = jnp.exp(scores)
        weights = expo.astype(jnp.bfloat16)
        numer = numer + jnp.einsum(
            "hqk,khd->qhd", weights, value_block, preferred_element_type=jnp.float32
        )
        totals = totals + jnp.transpose(jnp.sum(expo, axis=2))
        return ((numer, totals), None)

    starting_numer = jnp.zeros((rows_here, heads, HD), jnp.float32)
    starting_totals = jnp.zeros((rows_here, heads), jnp.float32)
    carry = (starting_numer, starting_totals)
    pieces = (
        lax.all_gather(keys, "fsdp", axis=0, tiled=True),
        lax.all_gather(values, "fsdp", axis=0, tiled=True),
    )
    piece_rows = pieces[0].shape[0]
    block_rows = math.gcd(piece_rows, 512)
    count = piece_rows // block_rows
    key_blocks = pieces[0].reshape(count, block_rows, heads, HD)
    value_blocks = pieces[1].reshape(count, block_rows, heads, HD)
    carry, _ = lax.scan(one_block, carry, (key_blocks, value_blocks))
    numer, totals = carry
    attended = (numer / totals[:, :, None]).astype(jnp.bfloat16).reshape(rows_here, channels)
    partial_terms = jnp.dot(attended, out_weight, preferred_element_type=jnp.float32).astype(
        jnp.bfloat16
    )
    summed = lax.psum(partial_terms, ("head", "seq")).astype(jnp.float32)
    branch = lax.dynamic_slice_in_dim(summed, position, local_width, 1)
    return (widened + own_mod[2][None, :] * branch).astype(jnp.bfloat16)


def solution(mesh):
    in_specs = (
        P("fsdp", ("head", "seq")),
        P(None, "fsdp", ("head", "seq")),
        P(None, "fsdp", ("head", "seq")),
        P(),
        P(),
        P(("head", "seq"), None),
        P(),
        P(),
        P(),
    )
    out_specs = P("fsdp", ("head", "seq"))
    return jax.shard_map(
        per_device, mesh=mesh, in_specs=in_specs, out_specs=out_specs, check_vma=False
    )
```

profile of v0, /device:TPU:1, one launch (start us, length us, event | category | flops | bytes accessed | tf_op | source)
XLA Modules:
  0.0 773.7 jit_solution(2207394032525884099)
XLA Ops:
  7.3 1.6 fusion.23
  9.0 1.0 convert_reduce_fusion
  10.0 52.9 %psum.21 = f32[192]{0:T(256)S(1)} all-reduce(f32[192]{0:T(256)S(1)} %convert_reduce_fusion), channel_id=1, replica_groups=mesh['fsdp'=32,'head'=4,'seq'=4] {'head','seq'}, use_global_device_ids=true, to_apply=%region_1.0 | all-reduce | flops 192 | bytes 1536 | tf_op jit(solution)/shard_map/psum | solution.py:33
  62.9 1.1 fusion.11
  64.0 39.3 %psum.22 = f32[192]{0:T(256)S(1)} all-reduce(f32[192]{0:T(256)S(1)} %fusion.11), channel_id=1, replica_groups=mesh['fsdp'=32,'head'=4,'seq'=4] {'head','seq'}, use_global_device_ids=true, to_apply=%region_3.0 | all-reduce | flops 192 | bytes 1536 | tf_op jit(solution)/shard_map/psum | solution.py:35
  103.4 1.7 fusion.14
  105.9 1.9 add_convert_fusion
  107.8 0.7 broadcast_bitcast_fusion
  108.5 107.1 %all-gather.8.cloned.1.call-done = bf16[192,6144]{1,0:T(8,128)(2,1)} async-done(((bf16[192,384]{1,0:T(8,128)(2,1)}), bf16[192,6144]{1,0:T(8,128)(2,1)}) %all-gather.8.cloned.1.call-update) | async-done | bytes 2359312 | tf_op jit(solution)/shard_map/all_gather | solution.py:39
  215.6 75.0 %all-gather.6.cloned.1.call-done = bf16[3,6144,256]{2,1,0:T(8,128)(2,1)} async-done(((bf16[3,192,256]{2,1,0:T(8,128)(2,1)}), bf16[3,6144,256]{2,1,0:T(8,128)(2,1)}) %all-gather.6.cloned.1.call-update) | async-done | bytes 9437200 | tf_op jit(solution)/shard_map/all_gather | solution.py:40
  290.6 6.4 fusion.6
  297.0 0.8 copy-done.2
  297.8 0.7 fusion.30
  298.5 1.0 mul.125
  299.5 0.9 reduce_sum.47
  300.5 0.9 add_rsqrt_fusion
  301.4 0.3 mul.126
  301.6 1.6 fusion.17
  303.3 1.6 slice.31
  305.1 0.3 multiply_reduce_fusion
  305.6 63.6 %all-gather.10.cloned.1.call-done = bf16[6144,256]{1,0:T(8,128)(2,1)} async-done(((bf16[192,256]{1,0:T(8,128)(2,1)}), bf16[6144,256]{1,0:T(8,128)(2,1)}) %all-gather.10.cloned.1.call-update) | async-done | bytes 3145744 | tf_op jit(solution)/shard_map/all_gather | solution.py:66
  369.2 5.5 reshape.43
  374.8 62.2 %all-gather.12.cloned.1.call-done = bf16[1,6144,256]{2,1,0:T(8,128)(2,1)} async-done(((bf16[1,192,256]{2,1,0:T(8,128)(2,1)}), bf16[1,6144,256]{2,1,0:T(8,128)(2,1)}) %all-gather.12.cloned.1.call-update) | async-done | bytes 3145744 | tf_op jit(solution)/shard_map/all_gather | solution.py:67
  437.0 5.5 reshape.42
  442.5 53.4 %while.13 = (s32[]{:T(128)}, f32[192,2,128]{2,0,1:T(8,128)}, f32[192,2]{0,1:T(2,128)S(1)}, bf16[12,512,2,128]{3,2,1,0:T(2,128)(2,1)}, bf16[12,512,2,128]{3,2,1,0...) while((s32[]{:T(128)}, f32[192,2,128]{2,0,1:T(8,128)}, ...), condition=%wide.region_8.9_spmd.clone, body=%wide.region_6.8_spmd.clone.sunk | while | flops 101351808 | bytes 2857060 | solution.py:74
  442.5 1.4 constant_dynamic-slice_fusion.3
  443.9 1.1 fusion.44
  445.0 1.9 fusion.45
  446.9 1.4 constant_dynamic-slice_fusion.3
  448.3 1.1 fusion.44
  449.4 2.0 fusion.45
  451.4 1.4 constant_dynamic-slice_fusion.3
  452.8 1.1 fusion.44
  453.8 2.0 fusion.45
  455.8 1.4 constant_dynamic-slice_fusion.3
  457.2 1.1 fusion.44
  458.3 2.0 fusion.45
  460.3 1.4 constant_dynamic-slice_fusion.3
  461.7 1.1 fusion.44
  462.7 2.0 fusion.45
  464.7 1.4 constant_dynamic-slice_fusion.3
  466.1 1.1 fusion.44
  467.2 2.0 fusion.45
  469.2 1.4 constant_dynamic-slice_fusion.3
  470.6 1.1 fusion.44
  471.6 2.0 fusion.45
  473.6 1.4 constant_dynamic-slice_fusion.3
  475.0 1.1 fusion.44
  476.1 2.0 fusion.45
  478.1 1.4 constant_dynamic-slice_fusion.3
  479.5 1.1 fusion.44
  480.6 2.0 fusion.45
  482.6 1.4 constant_dynamic-slice_fusion.3
  483.9 1.1 fusion.44
  485.0 2.0 fusion.45
  487.0 1.4 constant_dynamic-slice_fusion.3
  488.4 1.1 fusion.44
  489.5 2.0 fusion.45
  491.5 1.4 constant_dynamic-slice_fusion.3
  492.9 1.1 fusion.44
  493.9 2.0 fusion.45
  495.9 3.2 convolution_convert_fusion
  499.2 266.4 %all-reduce.2.cloned.1.call-done = bf16[192,6144]{1,0:T(8,128)(2,1)} async-done(((bf16[192,6144]{1,0:T(8,128)(2,1)}), bf16[192,6144]{1,0:T(8,128)(2,1)}) %all-reduce.2.cloned.1.call-update) | async-done | bytes 2359312 | tf_op jit(solution)/shard_map/psum | solution.py:80
  765.6 1.6 fusion.15
  (39 shorter events, 0.9 us)
Async XLA Ops:
  6.5 489.4 %copy-start = (bf16[256,6144]{1,0:T(8,128)(2,1)S(1)}, bf16[256,6144]{1,0:T(8,128)(2,1)}, u32[]{:S(2)}) copy-start(bf16[256,6144]{1,0:T(8,128)(2,1)} %param.16) | copy-start | bytes 9437188
  6.5 209.0 %all-gather.8.cloned.1.call-start = ((), (), s32[]{:S(2)}) async-start(), calls=%async_computation.1 | async-start | bytes 2506752 | tf_op jit(solution)/shard_map/all_gather | solution.py:39
  105.2 185.4 %all-gather.6.cloned.1.call-start = ((), (), s32[]{:S(2)}) async-start(), calls=%async_computation | async-start | bytes 9732096 | tf_op jit(solution)/shard_map/all_gather | solution.py:40
  107.8 261.4 %all-gather.10.cloned.1.call-start = ((), (), s32[]{:S(2)}) async-start(), calls=%async_computation.2 | async-start | bytes 3244032 | tf_op jit(solution)/shard_map/all_gather | solution.py:66
  297.0 0.8 copy-start.2
  297.8 7.7 copy-start.3
  303.3 133.7 %all-gather.12.cloned.1.call-start = ((), (), s32[]{:S(2)}) async-start(), calls=%async_computation.4 | async-start | bytes 3244032 | tf_op jit(solution)/shard_map/all_gather | solution.py:67
  304.9 460.7 %all-reduce.2.cloned.1.call-start = ((), (), s32[]{:S(2)}) async-start(), calls=%async_computation.3 | async-start | bytes 4718592 | tf_op jit(solution)/shard_map/psum | solution.py:80
  495.9 269.7 %copy-start.1 = (bf16[192,384]{1,0:T(8,128)(2,1)S(1)}, bf16[192,384]{1,0:T(8,128)(2,1)}, u32[]{:S(2)}) copy-start(bf16[192,384]{1,0:T(8,128)(2,1)} %param.11) | copy-start | bytes 442372
Sparse Core Ops, SparseCore 0:
  105.3 110.2 all-gather.7
  217.7 72.8 all-gather.5
  303.4 65.8 all-gather.9
  371.2 65.7 all-gather.11
  499.3 266.2 all-reduce.1
where the time goes:
time: 783 us; the launch traced here: 774 us
  waiting for transfers between devices  574 us (73%)
  blocking collectives  92.2 us (12%)
  matrix products  47.8 us (6%)
  local copies, waits for them, and re-layouts  32.3 us (4%)
  between operations  14.7 us (2%)
  other arithmetic  12.1 us (2%)
    psum x1, waiting for transfers between devices, per_device(): summed = lax.psum(partial_terms, ('head', 'seq')).astype(jnp.float32)  266 us
    all_gather x1, waiting for transfers between devices, per_device(): hidden = lax.all_gather(shares, ('head', 'seq'), axis=1, tiled=True)  107 us
    all_gather x1, waiting for transfers between devices, per_device(): full_weights = lax.all_gather(ema_weights, 'fsdp', axis=1, tiled=True)  75 us
    all_gather x1, waiting for transfers between devices, per_device(): lax.all_gather(keys, 'fsdp', axis=0, tiled=True)  63.6 us
    all_gather x1, waiting for transfers between devices, per_device(): lax.all_gather(values, 'fsdp', axis=0, tiled=True)  62.2 us
    psum x1, blocking collectives, per_device(): average = lax.psum(jnp.sum(widened, axis=1), ('head', 'seq')) / D  52.9 us
    psum x1, blocking collectives, per_device(): variance = lax.psum(jnp.sum(centred * centred, axis=1), ('head', 'seq')) / D  39.3 us
    dot_general x12, matrix products, one_block(): jnp.einsum('hqk,khd->qhd', weights, value_block, preferred_element_type=j...  23.8 us
  transfers between devices with their start and end apart: 5, of which 5 were waited for; matrix products, arithmetic and copies ran while one was open for 1% of the time, Pallas kernels for 0%

commit v1 on v0

v1 whole, which is shorter than its diff:
```python
import math

import jax
import jax.numpy as jnp
from jax import lax
from jax.experimental import pallas as pl
from jax.experimental.pallas import tpu as pltpu
from jax.sharding import Mesh
from jax.sharding import PartitionSpec as P

D = 6144
HD = 128
GRID = 4
BF = jnp.bfloat16
F32 = jnp.float32
LOG2E = 1.4426950408889634
TOKENS = ("y", "zl", "core")


def shift(amount):
    return [(i, (i + amount) % GRID) for i in range(GRID)]


def gather_small(shard, axis_name):
    spread = jnp.broadcast_to(shard[None], (GRID,) + shard.shape)
    return lax.all_to_all(spread, axis_name, 0, 0, tiled=True)


def norm_kernel(raw_ref, mod_ref, out_ref):
    blocks = [(s, h) for s in range(GRID) for h in range(GRID)]
    rows, width = raw_ref.shape[2], raw_ref.shape[3]
    total = jnp.zeros((rows, width), F32)
    for s, h in blocks:
        total = total + raw_ref[s, h].astype(F32)
    average = jnp.sum(total, axis=1, keepdims=True) * (1.0 / D)
    squares = jnp.zeros((rows, width), F32)
    for s, h in blocks:
        centred = raw_ref[s, h].astype(F32) - average
        squares = squares + centred * centred
    variance = jnp.sum(squares, axis=1, keepdims=True) * (1.0 / D)
    inverse = lax.rsqrt(variance + 1e-06)
    for s, h in blocks:
        block = h * GRID + s
        centred = raw_ref[s, h].astype(F32) - average
        scale = mod_ref[1, block : block + 1, :]
        move = mod_ref[0, block : block + 1, :]
        out_ref[block] = (centred * inverse * (1.0 + scale) + move).astype(BF)


def project_kernel(hidden_ref, weight_ref, q_gain_ref, k_gain_ref, q_ref, kv_ref, acc_ref):
    step = pl.program_id(0)

    @pl.when(step == 0)
    def _():
        acc_ref[...] = jnp.zeros_like(acc_ref)

    for b in range(hidden_ref.shape[0]):
        width = hidden_ref.shape[2]
        for j in range(3):
            acc_ref[j] += jnp.dot(
                hidden_ref[b],
                weight_ref[j, b * width : (b + 1) * width, :],
                preferred_element_type=F32,
            )

    @pl.when(step == pl.num_programs(0) - 1)
    def _():
        for h in range(2):
            part = slice(h * HD, (h + 1) * HD)
            for j, gain_ref in ((0, q_gain_ref), (1, k_gain_ref)):
                values = acc_ref[j, :, part]
                squares = jnp.mean(values * values, axis=1, keepdims=True)
                normed = (values * lax.rsqrt(squares + 1e-06) * gain_ref[...]).astype(BF)
                if j == 0:
                    q_ref[h] = normed
                else:
                    kv_ref[h, 0] = normed
            kv_ref[h, 1] = acc_ref[2, :, part].astype(BF)


def attend_kernel(q_ref, kv_ref, out_ref, k_all, v_all):
    rows = q_ref.shape[1]
    blocks = kv_ref.shape[0]

    @pl.when(pl.program_id(0) == 0)
    def _():
        for b in range(blocks):
            k_all[b * rows : (b + 1) * rows, :] = kv_ref[b, 0]
            v_all[b * rows : (b + 1) * rows, :HD] = kv_ref[b, 1]
        v_all[:, HD:] = jnp.ones((blocks * rows, HD), BF)

    chunk = 512
    both = jnp.zeros((rows, 2 * HD), F32)
    for c in range(blocks * rows // chunk):
        part = slice(c * chunk, (c + 1) * chunk)
        scores = lax.dot_general(
            q_ref[0], k_all[part, :], (((1,), (1,)), ((), ())), preferred_element_type=F32
        )
        weights = jnp.exp2(scores * (LOG2E / math.sqrt(HD))).astype(BF)
        both = both + jnp.dot(weights, v_all[part, :], preferred_element_type=F32)
    out_ref[0, :rows, :] = both[:, :HD].astype(BF)
    totals = both[:, HD:]
    lane = lax.broadcasted_iota(jnp.int32, (HD, HD), 1)
    line = lax.broadcasted_iota(jnp.int32, (HD, HD), 0)
    first = jnp.sum(jnp.where(lane == line, totals[:HD], 0.0), axis=0, keepdims=True)
    rest = rows - HD
    second = jnp.sum(
        jnp.where(lane[:rest] == line[:rest], totals[HD:], 0.0), axis=0, keepdims=True
    )
    sub = lax.broadcasted_iota(jnp.int32, (16, HD), 0)
    first_high = first.astype(BF).astype(F32)
    second_high = second.astype(BF).astype(F32)
    packed = jnp.where(sub == 0, first_high, 0.0)
    packed = jnp.where(sub == 1, second_high, packed)
    packed = jnp.where(sub == 2, first - first_high, packed)
    packed = jnp.where(sub == 3, second - second_high, packed)
    out_ref[0, rows:, :] = packed.astype(BF)


def combine_kernel(parts_ref, out_ref):
    rows = out_ref.shape[0]
    lane = lax.broadcasted_iota(jnp.int32, (HD, HD), 1)
    line = lax.broadcasted_iota(jnp.int32, (HD, HD), 0)
    rest = rows - HD
    for h in range(2):
        numer = jnp.zeros((rows, HD), F32)
        packed = jnp.zeros((16, HD), F32)
        for g in range(GRID):
            numer = numer + parts_ref[2 * g + h, :rows, :].astype(F32)
            packed = packed + parts_ref[2 * g + h, rows:, :].astype(F32)
        first = packed[0:1] + packed[2:3]
        second = packed[1:2] + packed[3:4]
        first = jnp.sum(jnp.where(lane == line, first, 0.0), axis=1, keepdims=True)
        second = jnp.sum(
            jnp.where(lane[:rest] == line[:rest], second, 0.0), axis=1, keepdims=True
        )
        part = slice(h * HD, (h + 1) * HD)
        out_ref[:HD, part] = (numer[:HD] / first).astype(BF)
        out_ref[HD:, part] = (numer[HD:] / second).astype(BF)


def branch_kernel(a0, a1, a2, a3, w0, w1, w2, w3, out_ref):
    total = jnp.dot(a0[...], w0[0], preferred_element_type=F32)
    for a, w in ((a1, w1), (a2, w2), (a3, w3)):
        total = total + jnp.dot(a[...], w[0], preferred_element_type=F32)
    out_ref[0] = total.astype(BF)


def per_device(latents, train_qkv, ema_qkv, q_gain, k_gain, out_weight, modulation, timestep, step):
    rows, width = latents.shape
    channels = ema_qkv.shape[2]
    blocks = GRID * GRID
    stepped = step[0].astype(F32)
    decay = (1.0 + stepped) / (10.0 + stepped)
    ema_weights = (decay * ema_qkv.astype(F32) + (1.0 - decay) * train_qkv.astype(F32)).astype(BF)
    full_weights = lax.all_gather(ema_weights, TOKENS, axis=1, tiled=True)

    seq_here = lax.axis_index("seq")
    by_seq = jnp.transpose(out_weight.reshape(channels, GRID, GRID, width), (2, 1, 0, 3))
    out_parts = [
        lax.ppermute(
            lax.dynamic_index_in_dim(by_seq, (seq_here + k) % GRID, 0, keepdims=False), "seq", shift(k)
        )
        if k
        else lax.dynamic_index_in_dim(by_seq, seq_here, 0, keepdims=False)
        for k in range(GRID)
    ]

    mod_row = lax.dynamic_index_in_dim(modulation, timestep[0], 0, keepdims=False)
    raw = gather_small(latents, "head")
    raw = gather_small(raw, "seq").reshape(GRID, GRID, rows, width)
    hidden = pl.pallas_call(
        norm_kernel,
        out_shape=jax.ShapeDtypeStruct((blocks, rows, width), BF),
        name="norm",
    )(raw, mod_row.reshape(3, blocks, width))

    per_step = 2
    queries, pairs = pl.pallas_call(
        project_kernel,
        grid=(blocks // per_step,),
        in_specs=[
            pl.BlockSpec((per_step, rows, width), lambda i: (i, 0, 0)),
            pl.BlockSpec((3, per_step * width, channels), lambda i: (0, i, 0)),
            pl.BlockSpec((1, HD), lambda i: (0, 0)),
            pl.BlockSpec((1, HD), lambda i: (0, 0)),
        ],
        out_specs=[
            pl.BlockSpec((2, rows, HD), lambda i: (0, 0, 0)),
            pl.BlockSpec((2, 2, rows, HD), lambda i: (0, 0, 0, 0)),
        ],
        out_shape=[
            jax.ShapeDtypeStruct((2, rows, HD), BF),
            jax.ShapeDtypeStruct((2, 2, rows, HD), BF),
        ],
        scratch_shapes=[pltpu.VMEM((3, rows, channels), F32)],
        name="project",
    )(hidden, full_weights, q_gain.reshape(1, HD), k_gain.reshape(1, HD))

    pairs = jnp.broadcast_to(pairs[None], (GRID,) + pairs.shape).reshape(2 * GRID, 2, rows, HD)
    pairs = lax.all_to_all(pairs, ("y", "core"), 0, 0, tiled=True)
    queries = jnp.broadcast_to(queries[None], (GRID,) + queries.shape).reshape(2 * GRID, rows, HD)
    queries = lax.all_to_all(queries, ("zl", "core"), 0, 0, tiled=True)

    sent = rows + 16
    parts = pl.pallas_call(
        attend_kernel,
        grid=(2 * GRID,),
        in_specs=[
            pl.BlockSpec((1, rows, HD), lambda i: (i, 0, 0)),
            pl.BlockSpec((2 * GRID, 2, rows, HD), lambda i: (0, 0, 0, 0)),
        ],
        out_specs=pl.BlockSpec((1, sent, HD), lambda i: (i, 0, 0)),
        out_shape=jax.ShapeDtypeStruct((2 * GRID, sent, HD), BF),
        scratch_shapes=[
            pltpu.VMEM((2 * GRID * rows, HD), BF),
            pltpu.VMEM((2 * GRID * rows, 2 * HD), BF),
        ],
        name="attend",
    )(queries, pairs)
    parts = lax.all_to_all(parts, ("zl", "core"), 0, 0, tiled=True)
    attended = pl.pallas_call(
        combine_kernel,
        out_shape=jax.ShapeDtypeStruct((rows, channels), BF),
        name="combine",
    )(parts)

    around = [attended] + [lax.ppermute(attended, "seq", shift(k)) for k in (1, 2, 3)]
    branch = pl.pallas_call(
        branch_kernel,
        grid=(GRID,),
        in_specs=[pl.BlockSpec((rows, channels), lambda i: (0, 0))] * GRID
        + [pl.BlockSpec((1, channels, width), lambda i: (i, 0, 0))] * GRID,
        out_specs=pl.BlockSpec((1, rows, width), lambda i: (i, 0, 0)),
        out_shape=jax.ShapeDtypeStruct((GRID, rows, width), BF),
        name="branch",
    )(*around, *out_parts)
    branch = lax.all_to_all(branch, "head", 0, 0, tiled=True)
    summed = jnp.sum(branch.astype(F32), axis=0)
    position = lax.axis_index(("head", "seq")) * width
    gate = lax.dynamic_slice_in_dim(mod_row[2], position, width, 0)
    return (latents.astype(F32) + gate[None, :] * summed).astype(BF)


def solution(mesh):
    fine = Mesh(
        mesh.devices.reshape(GRID, GRID, 2, GRID, GRID), ("y", "zl", "core", "head", "seq")
    )
    in_specs = (
        P(TOKENS, ("head", "seq")),
        P(None, TOKENS, ("head", "seq")),
        P(None, TOKENS, ("head", "seq")),
        P(),
        P(),
        P(("head", "seq"), None),
        P(),
        P(),
        P(),
    )
    out_specs = P(TOKENS, ("head", "seq"))
    return jax.shard_map(
        per_device, mesh=fine, in_specs=in_specs, out_specs=out_specs, check_vma=False
    )
```

time: 783 us -> 280 us (0.36)
  the two profiles are of different devices: /device:TPU:1 before, /device:TPU:34 now
where the time goes in v1:
time: 280 us; the launch traced here: 278 us
  blocking collectives  87.4 us (31%)
  waiting for transfers between devices  77.9 us (28%)
  starting transfers between devices  45.1 us (16%)
  Pallas kernels  28.9 us (10%)
  local copies, waits for them, and re-layouts  21.2 us (8%)
  between operations  14.9 us (5%)
    all_to_all x1, blocking collectives, gather_small(): return lax.all_to_all(spread, axis_name, 0, 0, tiled=True)  55.9 us
    all_to_all x1, waiting for transfers between devices, per_device(): branch = lax.all_to_all(branch, 'head', 0, 0, tiled=True)  33.1 us
    all_to_all x1, waiting for transfers between devices, gather_small(): return lax.all_to_all(spread, axis_name, 0, 0, tiled=True)  24.3 us
    all_to_all x1, blocking collectives, per_device(): pairs = lax.all_to_all(pairs, ('y', 'core'), 0, 0, tiled=True)  17 us
    ppermute x3, waiting for transfers between devices, per_device(): lax.ppermute(lax.dynamic_index_in_dim(by_seq, (seq_here + k) % GRID, 0, k...  16.6 us
    all_to_all x1, blocking collectives, per_device(): queries = lax.all_to_all(queries, ('zl', 'core'), 0, 0, tiled=True)  14.5 us
    ppermute x3, starting transfers between devices, per_device(): lax.ppermute(attended, 'seq', shift(k))  13.6 us
    unnamed x22, local copies, waits for them, and re-layouts  13.2 us
  transfers between devices with their start and end apart: 10, of which 7 were waited for; matrix products, arithmetic and copies ran while one was open for 6% of the time, Pallas kernels for 3%

profile of v1, /device:TPU:34, one launch (start us, length us, event | category | flops | bytes accessed | tf_op | source)
XLA Modules:
  0.0 278.1 jit_solution(13607166973170600655)
XLA Ops:
  6.5 0.0 copy-start
  6.5 0.0 all-gather.2.cloned.1.call-start
  7.3 1.9 add_convert_fusion
  9.2 0.0 all-gather.2.cloned.1.call-update
  9.2 1.0 broadcast_in_dim.8
  10.2 55.9 %all_to_all.30 = bf16[4,192,384]{2,1,0:T(8,128)(2,1)S(1)} all-to-all(bf16[4,192,384]{2,1,0:T(8,128)(2,1)S(1)} %broadcast_in_dim.8), channel_id=1, replica_groups=mesh['y'=4,'zl'=4,'core'=2,'head'=4,'seq'=4] {'head'}, dimensions={0} | all-to-all | bytes 1179648 | tf_op jit(solution)/shard_map/all_to_all | solution.py:26
  66.1 1.7 broadcast_in_dim.9
  67.8 4.8 %all-to-all-start.1 = ((bf16[4,4,192,384]{3,2,1,0:T(8,128)(2,1)}), bf16[4,4,192,384]{3,2,1,0:T(8,128)(2,1)S(1)}, u32[]{:S(2)}, u32[]{:S(2)}) async-start(bf16[4,4,192,384]{3,2,1,0:T(8,128)(2,1)} %broadcast_in_dim.9), calls=%async_computation.1 | async-start | bytes 4718592 | tf_op jit(solution)/shard_map/all_to_all | solution.py:26
  73.3 0.0 copy-done
  73.3 0.2 dynamic-slice_reduce_fusion
  73.5 0.6 copy.21
  74.1 24.3 %all-to-all-done.1.raw_ref = bf16[4,4,192,384]{3,2,1,0:T(8,128)(2,1)S(1)} async-done(((bf16[4,4,192,384]{3,2,1,0:T(8,128)(2,1)}), bf16[4,4,192,384]{3,2,1,0:T(8,128)(2,1)S(1)}, u32[]{:S(2)}, u32[]{:S(2)}) %all-to-all-start.1) | async-done | bytes 2359328 | tf_op jit(solution)/shard_map/all_to_all | solution.py:26
  98.5 0.0 copy-start.1
  98.5 1.5 copy-done.1
  99.9 5.4 %norm.1.hidden_ref = bf16[16,192,384]{2,1,0:T(8,128)(2,1)} custom-call(bf16[4,4,192,384]{3,2,1,0:T(8,128)(2,1)} %copy-done.1, f32[3,16,384]{2,1,0:T(8,128)} %bitcast.34), custom_call_target="tpu_custom_call" | custom-call | tf_op jit(solution)/shard_map/norm/pallas_call | solution.py:172
  105.3 0.8 all-gather.2.cloned.1.call-done.weight_ref
  106.1 9.1 %project.1 = (bf16[2,192,128]{2,1,0:T(8,128)(2,1)}, bf16[2,2,192,128]{3,2,1,0:T(8,128)(2,1)}) custom-call(bf16[16,192,384]{2,1,0:T(8,128)(2,1)} %norm.1.hidden_ref, bf16[3,6144,256]{2,1,0:T(8,128)(2,1)} %all-gather.2.cloned.1.call-done.weight_ref, f32[1,128]{1,0:T(1,128)} %bitcast.35, f32[1,128]{1,0:T(1,128)} %bitcast.36), custom_call_target="tpu_custom_call" | custom-call | tf_op jit(solution)/shard_map/project/pallas_call | solution.py:179
  115.2 1.1 broadcast_in_dim.11
  116.3 17.0 %all_to_all.31.kv_ref = bf16[8,2,192,128]{3,2,1,0:T(8,128)(2,1)} all-to-all(bf16[8,2,192,128]{3,2,1,0:T(8,128)(2,1)S(1)} %bitcast.27), channel_id=1, replica_groups=mesh['y'=4,'zl'=4,'core'=2,'head'=4,'seq'=4] {'y','core'}, dimensions={0} | all-to-all | bytes 1572864 | tf_op jit(solution)/shard_map/all_to_all | solution.py:201
  133.3 0.9 broadcast_in_dim.10
  134.2 14.5 %all_to_all.32.q_ref = bf16[8,192,128]{2,1,0:T(8,128)(2,1)} all-to-all(bf16[8,192,128]{2,1,0:T(8,128)(2,1)S(1)} %bitcast.29), channel_id=1, replica_groups=mesh['y'=4,'zl'=4,'core'=2,'head'=4,'seq'=4] {'zl','core'}, dimensions={0} | all-to-all | bytes 786432 | tf_op jit(solution)/shard_map/all_to_all | solution.py:203
  148.7 8.0 %attend.1 = bf16[8,208,128]{2,1,0:T(8,128)(2,1)} custom-call(bf16[8,192,128]{2,1,0:T(8,128)(2,1)} %all_to_all.32.q_ref, bf16[8,2,192,128]{3,2,1,0:T(8,128)(2,1)} %all_to_all.31.kv_ref), custom_call_target="tpu_custom_call" | custom-call | tf_op jit(solution)/shard_map/attend/pallas_call | solution.py:206
  156.7 5.2 %all-to-all-start.4 = ((bf16[8,208,128]{2,1,0:T(8,128)(2,1)}), bf16[8,208,128]{2,1,0:T(8,128)(2,1)S(1)}, u32[]{:S(2)}, u32[]{:S(2)}) async-start(bf16[8,208,128]{2,1,0:T(8,128)(2,1)} %attend.1), calls=%async_computation.4 | async-start | bytes 851968 | tf_op jit(solution)/shard_map/all_to_all | solution.py:221
  161.9 4.7 %copy.10 = bf16[256,6144]{0,1:T(8,128)(2,1)} copy(bf16[256,6144]{1,0:T(8,128)(2,1)} %param.14) | data formatting | bytes 6291456 | tf_op args[5]
  166.6 3.0 %constant_dynamic-slice_fusion = (bf16[256,4,1,384]{0,3,2,1:T(8,128)(2,1)S(1)}, bf16[256,4,1,384]{0,3,2,1:T(8,128)(2,1)S(1)}, bf16[256,4,1,384]{0,3,2,1:T(8,128)(2,1)}, bf16[256,4,1,384]{0,3,2,1:T(8,128)(2,1)S(1)}) fusion(bf16[256,4,4,384]{0,3,2,1:T(8,128)(2,1)} %bitcast.26, s32[]{:T(128)S(6)} %select_n.43, s32[]{:T(128)S(6)} %select_n.41, s32[]{:T(128)S(6)} %select_n.39, ...), kind=kLoop, calls=%fused_computation.6 | loop fusion | bytes 6291472 | tf_op jit(solution)/shard_map/dynamic-slice.4
  169.6 2.3 copy.16
  171.9 3.5 %collective-permute-start.3 = (bf16[4,256,384]{2,1,0:T(8,128)(2,1)}, bf16[4,256,384]{2,1,0:T(8,128)(2,1)}, u32[]{:S(2)}, u32[]{:S(2)}) collective-permute-start(bf16[4,256,384]{2,1,0:T(8,128)(2,1)} %bitcast.32), channel_id=1, source_target_pairs={{0,1},{1,2},{2,3},{3,0},{4,5},{5,6},{6,7},{7,4},{8,9},{9,10},{10,1... | collective-permute-start | bytes 2359304 | tf_op jit(solution)/shard_map/ppermute | solution.py:161
  175.4 1.2 copy.17
  176.6 3.8 %collective-permute-start.4 = (bf16[4,256,384]{2,1,0:T(8,128)(2,1)}, bf16[4,256,384]{2,1,0:T(8,128)(2,1)}, u32[]{:S(2)}, u32[]{:S(2)}) collective-permute-start(bf16[4,256,384]{2,1,0:T(8,128)(2,1)} %bitcast.30), channel_id=1, source_target_pairs={{0,2},{1,3},{2,0},{3,1},{4,6},{5,7},{6,4},{7,5},{8,10},{9,11},{10,... | collective-permute-start | bytes 2359304 | tf_op jit(solution)/shard_map/ppermute | solution.py:161
  180.3 0.4 copy.18
  180.7 2.8 %collective-permute-start.5 = (bf16[4,256,384]{2,1,0:T(8,128)(2,1)S(1)}, bf16[4,256,384]{2,1,0:T(8,128)(2,1)S(1)}, u32[]{:S(2)}, u32[]{:S(2)}) collective-permute-start(bf16[4,256,384]{2,1,0:T(8,128)(2,1)S(1)} %bitcast.31), channel_id=1, source_target_pairs={{0,3},{1,0},{2,1},{3,2},{4,7},{5,4},{6,5},{7,6},{8,11},{9,8},{10,9... | collective-permute-start | bytes 2359304 | tf_op jit(solution)/shard_map/ppermute | solution.py:161
  183.6 0.0 all-to-all-done.4.parts_ref
  183.6 0.0 copy-start.2
  183.6 0.8 copy-done.2
  184.3 1.8 combine.1.a0
  186.1 3.0 %collective-permute-start = (bf16[192,256]{1,0:T(8,128)(2,1)}, bf16[192,256]{1,0:T(8,128)(2,1)S(1)}, u32[]{:S(2)}, u32[]{:S(2)}) collective-permute-start(bf16[192,256]{1,0:T(8,128)(2,1)} %combine.1.a0), channel_id=1, source_target_pairs={{0,1},{1,2},{2,3},{3,0},{4,5},{5,6},{6,7},{7,4},{8,9},{9,10},{10,1... | collective-permute-start | bytes 294920 | tf_op jit(solution)/shard_map/ppermute | solution.py:228
  189.1 4.8 %collective-permute-start.1 = (bf16[192,256]{1,0:T(8,128)(2,1)}, bf16[192,256]{1,0:T(8,128)(2,1)S(1)}, u32[]{:S(2)}, u32[]{:S(2)}) collective-permute-start(bf16[192,256]{1,0:T(8,128)(2,1)} %combine.1.a0), channel_id=1, source_target_pairs={{0,2},{1,3},{2,0},{3,1},{4,6},{5,7},{6,4},{7,5},{8,10},{9,11},{10,... | collective-permute-start | bytes 294920 | tf_op jit(solution)/shard_map/ppermute | solution.py:228
  193.9 16.1 %collective-permute-done.3.w1 = bf16[4,256,384]{2,1,0:T(8,128)(2,1)} collective-permute-done((bf16[4,256,384]{2,1,0:T(8,128)(2,1)}, bf16[4,256,384]{2,1,0:T(8,128)(2,1)}, u32[]{:S(2)}, u32[]{:S(2)}) %collective-permute-start.3) | collective-permute-done | bytes 786464 | tf_op jit(solution)/shard_map/ppermute | solution.py:161
  210.0 5.8 %collective-permute-start.2 = (bf16[192,256]{1,0:T(8,128)(2,1)}, bf16[192,256]{1,0:T(8,128)(2,1)S(1)}, u32[]{:S(2)}, u32[]{:S(2)}) collective-permute-start(bf16[192,256]{1,0:T(8,128)(2,1)} %combine.1.a0), channel_id=1, source_target_pairs={{0,3},{1,0},{2,1},{3,2},{4,7},{5,4},{6,5},{7,6},{8,11},{9,8},{10,9... | collective-permute-start | bytes 294920 | tf_op jit(solution)/shard_map/ppermute | solution.py:228
  215.9 1.2 copy.15
  217.0 0.0 copy-start.4
  217.0 0.0 collective-permute-done.4.w2
  217.0 0.4 collective-permute-done.5.w3
  217.5 0.0 copy-start.3
  217.5 0.0 collective-permute-done.a1
  217.5 0.0 copy-start.5
  217.5 2.2 collective-permute-done.1.a2
  219.6 0.0 copy-start.6
  219.6 0.9 collective-permute-done.2.a3
  220.5 0.0 copy-start.7
  220.5 0.0 copy-done.3
  220.5 0.0 copy-done.5
  220.5 0.0 copy-done.6
  220.5 0.6 copy-done.7
  221.2 4.6 %branch.1 = bf16[4,192,384]{2,1,0:T(8,128)(2,1)} custom-call(bf16[192,256]{1,0:T(8,128)(2,1)} %combine.1.a0, bf16[192,256]{1,0:T(8,128)(2,1)} %copy-done.5, bf16[192,256]{1,0:T(8,128)(2,1)} %copy-done.6, bf16[192,256]{1,0:T(8,128)(2,1)} %copy-done.7, bf16[4,256,384]{2,1,0:T(8,128)(2,1)} %bitcast.28, bf16[4,256,384]{2,1,0:T(8,128)(2,1)} %collective-permute-done.3.w1, ...), custom_call_target="tpu_custom_call" | custom-call | tf_op jit(solution)/shard_map/branch/pallas_call | solution.py:229
  225.8 11.4 %all-to-all-start.5 = ((bf16[4,192,384]{2,1,0:T(8,128)(2,1)}), bf16[4,192,384]{2,1,0:T(8,128)(2,1)S(1)}, u32[]{:S(2)}, u32[]{:S(2)}) async-start(bf16[4,192,384]{2,1,0:T(8,128)(2,1)} %branch.1), calls=%async_computation.5 | async-start | bytes 1179648 | tf_op jit(solution)/shard_map/all_to_all | solution.py:238
  237.2 0.1 dynamic-slice_reduce_fusion.1
  237.3 33.1 %all-to-all-done.5 = bf16[4,192,384]{2,1,0:T(8,128)(2,1)S(1)} async-done(((bf16[4,192,384]{2,1,0:T(8,128)(2,1)}), bf16[4,192,384]{2,1,0:T(8,128)(2,1)S(1)}, u32[]{:S(2)}, u32[]{:S(2)}) %all-to-all-start.5) | async-done | bytes 589856 | tf_op jit(solution)/shard_map/all_to_all | solution.py:238
  270.4 0.1 convert_reduce_fusion
  270.5 0.0 copy-done.4
  270.5 0.7 add_convert_fusion.1
Async XLA Ops:
  6.5 66.7 %copy-start = (f32[8,3,6144]{2,0,1:T(8,128)S(1)}, f32[8,3,6144]{2,0,1:T(8,128)}, u32[]{:S(2)}) copy-start(f32[8,3,6144]{2,0,1:T(8,128)} %param.15) | copy-start | bytes 1769476
  6.5 99.5 %all-gather.2.cloned.1.call-start = ((), (), s32[]{:S(2)}) async-start(), calls=%async_computation.6 | async-start | bytes 9732096 | tf_op jit(solution)/shard_map/all_gather | solution.py:156
  67.8 30.7 %all-to-all-start.1 = ((bf16[4,4,192,384]{3,2,1,0:T(8,128)(2,1)}), bf16[4,4,192,384]{3,2,1,0:T(8,128)(2,1)S(1)}, u32[]{:S(2)}, u32[]{:S(2)}) async-start(bf16[4,4,192,384]{3,2,1,0:T(8,128)(2,1)} %broadcast_in_dim.9), calls=%async_computation.1 | async-start | bytes 4718592 | tf_op jit(solution)/shard_map/all_to_all | solution.py:26
  98.5 1.5 copy-start.1
  156.7 26.8 %all-to-all-start.4 = ((bf16[8,208,128]{2,1,0:T(8,128)(2,1)}), bf16[8,208,128]{2,1,0:T(8,128)(2,1)S(1)}, u32[]{:S(2)}, u32[]{:S(2)}) async-start(bf16[8,208,128]{2,1,0:T(8,128)(2,1)} %attend.1), calls=%async_computation.4 | async-start | bytes 851968 | tf_op jit(solution)/shard_map/all_to_all | solution.py:221
  171.9 38.2 %collective-permute-start.3 = (bf16[4,256,384]{2,1,0:T(8,128)(2,1)}, bf16[4,256,384]{2,1,0:T(8,128)(2,1)}, u32[]{:S(2)}, u32[]{:S(2)}) collective-permute-start(bf16[4,256,384]{2,1,0:T(8,128)(2,1)} %bitcast.32), channel_id=1, source_target_pairs={{0,1},{1,2},{2,3},{3,0},{4,5},{5,6},{6,7},{7,4},{8,9},{9,10},{10,1... | collective-permute-start | bytes 2359304 | tf_op jit(solution)/shard_map/ppermute | solution.py:161
  176.6 40.5 %collective-permute-start.4 = (bf16[4,256,384]{2,1,0:T(8,128)(2,1)}, bf16[4,256,384]{2,1,0:T(8,128)(2,1)}, u32[]{:S(2)}, u32[]{:S(2)}) collective-permute-start(bf16[4,256,384]{2,1,0:T(8,128)(2,1)} %bitcast.30), channel_id=1, source_target_pairs={{0,2},{1,3},{2,0},{3,1},{4,6},{5,7},{6,4},{7,5},{8,10},{9,11},{10,... | collective-permute-start | bytes 2359304 | tf_op jit(solution)/shard_map/ppermute | solution.py:161
  180.7 36.8 %collective-permute-start.5 = (bf16[4,256,384]{2,1,0:T(8,128)(2,1)S(1)}, bf16[4,256,384]{2,1,0:T(8,128)(2,1)S(1)}, u32[]{:S(2)}, u32[]{:S(2)}) collective-permute-start(bf16[4,256,384]{2,1,0:T(8,128)(2,1)S(1)} %bitcast.31), channel_id=1, source_target_pairs={{0,3},{1,0},{2,1},{3,2},{4,7},{5,4},{6,5},{7,6},{8,11},{9,8},{10,9... | collective-permute-start | bytes 2359304 | tf_op jit(solution)/shard_map/ppermute | solution.py:161
  183.6 0.8 copy-start.2
  186.1 31.3 %collective-permute-start = (bf16[192,256]{1,0:T(8,128)(2,1)}, bf16[192,256]{1,0:T(8,128)(2,1)S(1)}, u32[]{:S(2)}, u32[]{:S(2)}) collective-permute-start(bf16[192,256]{1,0:T(8,128)(2,1)} %combine.1.a0), channel_id=1, source_target_pairs={{0,1},{1,2},{2,3},{3,0},{4,5},{5,6},{6,7},{7,4},{8,9},{9,10},{10,1... | collective-permute-start | bytes 294920 | tf_op jit(solution)/shard_map/ppermute | solution.py:228
  189.1 30.5 %collective-permute-start.1 = (bf16[192,256]{1,0:T(8,128)(2,1)}, bf16[192,256]{1,0:T(8,128)(2,1)S(1)}, u32[]{:S(2)}, u32[]{:S(2)}) collective-permute-start(bf16[192,256]{1,0:T(8,128)(2,1)} %combine.1.a0), channel_id=1, source_target_pairs={{0,2},{1,3},{2,0},{3,1},{4,6},{5,7},{6,4},{7,5},{8,10},{9,11},{10,... | collective-permute-start | bytes 294920 | tf_op jit(solution)/shard_map/ppermute | solution.py:228
  210.0 10.5 %collective-permute-start.2 = (bf16[192,256]{1,0:T(8,128)(2,1)}, bf16[192,256]{1,0:T(8,128)(2,1)S(1)}, u32[]{:S(2)}, u32[]{:S(2)}) collective-permute-start(bf16[192,256]{1,0:T(8,128)(2,1)} %combine.1.a0), channel_id=1, source_target_pairs={{0,3},{1,0},{2,1},{3,2},{4,7},{5,4},{6,5},{7,6},{8,11},{9,8},{10,9... | collective-permute-start | bytes 294920 | tf_op jit(solution)/shard_map/ppermute | solution.py:228
  217.0 53.5 %copy-start.4 = (bf16[192,384]{1,0:T(8,128)(2,1)S(1)}, bf16[192,384]{1,0:T(8,128)(2,1)}, u32[]{:S(2)}) copy-start(bf16[192,384]{1,0:T(8,128)(2,1)} %param.9) | copy-start | bytes 442372
  217.5 3.1 %copy-start.3 = (bf16[4,256,384]{2,1,0:T(8,128)(2,1)}, bf16[4,256,384]{2,1,0:T(8,128)(2,1)S(1)}, u32[]{:S(2)}) copy-start(bf16[4,256,384]{2,1,0:T(8,128)(2,1)S(1)} %collective-permute-done.5.w3) | copy-start | bytes 2359300
  217.5 3.1 %copy-start.5 = (bf16[192,256]{1,0:T(8,128)(2,1)}, bf16[192,256]{1,0:T(8,128)(2,1)S(1)}, u32[]{:S(2)}) copy-start(bf16[192,256]{1,0:T(8,128)(2,1)S(1)} %collective-permute-done.a1) | copy-start | bytes 294916
  219.6 0.9 copy-start.6
  220.5 0.6 copy-start.7
  225.8 44.6 %all-to-all-start.5 = ((bf16[4,192,384]{2,1,0:T(8,128)(2,1)}), bf16[4,192,384]{2,1,0:T(8,128)(2,1)S(1)}, u32[]{:S(2)}, u32[]{:S(2)}) async-start(bf16[4,192,384]{2,1,0:T(8,128)(2,1)} %branch.1), calls=%async_computation.5 | async-start | bytes 1179648 | tf_op jit(solution)/shard_map/all_to_all | solution.py:238
Sparse Core Ops, SparseCore 0:
  9.5 96.5 all-gather.1

commit v2 on v1

--- a/solution.py
+++ b/solution.py
@@ -78,7 +78,7 @@
             kv_ref[h, 1] = acc_ref[2, :, part].astype(BF)
 
 
-def attend_kernel(q_ref, kv_ref, out_ref, k_all, v_all):
+def attend_kernel(line_ref, q_ref, kv_ref, out_ref, k_all, v_all):
     rows = q_ref.shape[1]
     blocks = kv_ref.shape[0]
 
@@ -174,6 +174,7 @@
         out_shape=jax.ShapeDtypeStruct((blocks, rows, width), BF),
         name="norm",
     )(raw, mod_row.reshape(3, blocks, width))
+    hidden, *out_parts = lax.optimization_barrier((hidden, *out_parts))
 
     per_step = 2
     queries, pairs = pl.pallas_call(
@@ -199,25 +200,38 @@
 
     pairs = jnp.broadcast_to(pairs[None], (GRID,) + pairs.shape).reshape(2 * GRID, 2, rows, HD)
     pairs = lax.all_to_all(pairs, ("y", "core"), 0, 0, tiled=True)
-    queries = jnp.broadcast_to(queries[None], (GRID,) + queries.shape).reshape(2 * GRID, rows, HD)
-    queries = lax.all_to_all(queries, ("zl", "core"), 0, 0, tiled=True)
+    core = lax.axis_index("core")
+    own = lax.dynamic_index_in_dim(queries, core, 0, keepdims=False)
+    other = lax.dynamic_index_in_dim(queries, 1 - core, 0, keepdims=False)
+    other = lax.ppermute(other, "core", [(0, 1), (1, 0)])
+    own, other = jnp.where(core == 0, own, other), jnp.where(core == 0, other, own)
+    queries = jnp.stack([own, other])
+    queries = [queries] + [lax.ppermute(queries, "zl", shift(k)) for k in (1, 2, 3)]
+    queries = jnp.concatenate(queries)
+    line_here = lax.axis_index("zl").astype(jnp.int32).reshape(1)
 
     sent = rows + 16
     parts = pl.pallas_call(
         attend_kernel,
-        grid=(2 * GRID,),
-        in_specs=[
-            pl.BlockSpec((1, rows, HD), lambda i: (i, 0, 0)),
-            pl.BlockSpec((2 * GRID, 2, rows, HD), lambda i: (0, 0, 0, 0)),
-        ],
-        out_specs=pl.BlockSpec((1, sent, HD), lambda i: (i, 0, 0)),
+        grid_spec=pltpu.PrefetchScalarGridSpec(
+            num_scalar_prefetch=1,
+            grid=(2 * GRID,),
+            in_specs=[
+                pl.BlockSpec(
+                    (1, rows, HD),
+                    lambda i, line: (lax.rem(line[0] + GRID - i // 2, GRID) * 2 + i % 2, 0, 0),
+                ),
+                pl.BlockSpec((2 * GRID, 2, rows, HD), lambda i, line: (0, 0, 0, 0)),
+            ],
+            out_specs=pl.BlockSpec((1, sent, HD), lambda i, line: (i, 0, 0)),
+            scratch_shapes=[
+                pltpu.VMEM((2 * GRID * rows, HD), BF),
+                pltpu.VMEM((2 * GRID * rows, 2 * HD), BF),
+            ],
+        ),
         out_shape=jax.ShapeDtypeStruct((2 * GRID, sent, HD), BF),
-        scratch_shapes=[
-            pltpu.VMEM((2 * GRID * rows, HD), BF),
-            pltpu.VMEM((2 * GRID * rows, 2 * HD), BF),
-        ],
         name="attend",
-    )(queries, pairs)
+    )(line_here, queries, pairs)
     parts = lax.all_to_all(parts, ("zl", "core"), 0, 0, tiled=True)
     attended = pl.pallas_call(
         combine_kernel,

time: 280 us -> 261 us (0.932)
  the two profiles are of different devices: /device:TPU:34 before, /device:TPU:1 now
where the time goes in v2:
time: 261 us; the launch traced here: 257 us
  blocking collectives  63.5 us (24%)
  waiting for transfers between devices  61.5 us (24%)
  starting transfers between devices  56.5 us (22%)
  Pallas kernels  29 us (11%)
  local copies, waits for them, and re-layouts  27.1 us (10%)
  between operations  15 us (6%)
  other arithmetic  4.36 us (2%)
    all_to_all x1, blocking collectives, gather_small(): return lax.all_to_all(spread, axis_name, 0, 0, tiled=True)  45.3 us
    all_to_all x1, waiting for transfers between devices, per_device(): branch = lax.all_to_all(branch, 'head', 0, 0, tiled=True)  31.2 us
    ppermute x3, waiting for transfers between devices, per_device(): lax.ppermute(lax.dynamic_index_in_dim(by_seq, (seq_here + k) % GRID, 0, k...  24.3 us
    ppermute x3, starting transfers between devices, per_device(): lax.ppermute(queries, 'zl', shift(k))  19.5 us
    all_to_all x1, blocking collectives, per_device(): parts = lax.all_to_all(parts, ('zl', 'core'), 0, 0, tiled=True)  18.2 us
    unnamed x24, local copies, waits for them, and re-layouts  17.7 us
    ppermute x3, starting transfers between devices, per_device(): lax.ppermute(lax.dynamic_index_in_dim(by_seq, (seq_here + k) % GRID, 0, k...  10.7 us
    pallas_call x1, Pallas kernels, per_device(): pl.pallas_call(project_kernel, grid=(blocks // per_step,), in_specs=[pl.B...  9.12 us
  transfers between devices with their start and end apart: 14, of which 8 were waited for; matrix products, arithmetic and copies ran while one was open for 10% of the time, Pallas kernels for 2%

profile of v2, /device:TPU:1, one launch (start us, length us, event | category | flops | bytes accessed | tf_op | source)
XLA Modules:
  0.0 257.0 jit_solution(11321263996349328355)
XLA Ops:
  6.5 0.0 copy-start
  6.5 0.0 all-gather.2.cloned.1.call-start
  7.3 1.9 add_convert_fusion
  9.2 0.0 all-gather.2.cloned.1.call-update
  9.2 1.0 broadcast_in_dim.6
  10.2 45.3 %all_to_all.25 = bf16[4,192,384]{2,1,0:T(8,128)(2,1)S(1)} all-to-all(bf16[4,192,384]{2,1,0:T(8,128)(2,1)S(1)} %broadcast_in_dim.6), channel_id=1, replica_groups=mesh['y'=4,'zl'=4,'core'=2,'head'=4,'seq'=4] {'head'}, dimensions={0} | all-to-all | bytes 1179648 | tf_op jit(solution)/shard_map/all_to_all | solution.py:26
  55.5 1.7 broadcast_in_dim.7
  57.2 4.2 %all-to-all-start.1 = ((bf16[4,4,192,384]{3,2,1,0:T(8,128)(2,1)}), bf16[4,4,192,384]{3,2,1,0:T(8,128)(2,1)S(1)}, u32[]{:S(2)}, u32[]{:S(2)}) async-start(bf16[4,4,192,384]{3,2,1,0:T(8,128)(2,1)} %broadcast_in_dim.7), calls=%async_computation.1 | async-start | bytes 4718592 | tf_op jit(solution)/shard_map/all_to_all | solution.py:26
  61.4 4.7 %copy.10 = bf16[256,6144]{0,1:T(8,128)(2,1)} copy(bf16[256,6144]{1,0:T(8,128)(2,1)} %param.14) | data formatting | bytes 6291456 | tf_op args[5]
  66.1 3.7 %constant_dynamic-slice_fusion = (bf16[256,4,1,384]{0,3,2,1:T(8,128)(2,1)}, bf16[256,4,1,384]{0,3,2,1:T(8,128)(2,1)}, bf16[256,4,1,384]{0,3,2,1:T(8,128)(2,1)}, bf16[256,4,1,384]{0,3,2,1:T(8,128)(2,1)}) fusion(bf16[256,4,4,384]{0,3,2,1:T(8,128)(2,1)} %bitcast.43, s32[]{:T(128)S(6)} %select_n.63, s32[]{:T(128)S(6)} %select_n.61, s32[]{:T(128)S(6)} %select_n.59, ...), kind=kLoop, calls=%fused_computation.16 | loop fusion | bytes 6291472 | tf_op jit(solution)/shard_map/dynamic-slice.4
  69.8 2.3 copy.16
  72.1 3.3 %collective-permute-start = (bf16[4,256,384]{2,1,0:T(8,128)(2,1)}, bf16[4,256,384]{2,1,0:T(8,128)(2,1)}, u32[]{:S(2)}, u32[]{:S(2)}) collective-permute-start(bf16[4,256,384]{2,1,0:T(8,128)(2,1)} %bitcast.45), channel_id=1, source_target_pairs={{0,1},{1,2},{2,3},{3,0},{4,5},{5,6},{6,7},{7,4},{8,9},{9,10},{10,1... | collective-permute-start | bytes 2359304 | tf_op jit(solution)/shard_map/ppermute | solution.py:161
  75.4 2.3 copy.17
  77.7 4.3 %collective-permute-start.1 = (bf16[4,256,384]{2,1,0:T(8,128)(2,1)}, bf16[4,256,384]{2,1,0:T(8,128)(2,1)}, u32[]{:S(2)}, u32[]{:S(2)}) collective-permute-start(bf16[4,256,384]{2,1,0:T(8,128)(2,1)} %bitcast.46), channel_id=1, source_target_pairs={{0,2},{1,3},{2,0},{3,1},{4,6},{5,7},{6,4},{7,5},{8,10},{9,11},{10,... | collective-permute-start | bytes 2359304 | tf_op jit(solution)/shard_map/ppermute | solution.py:161
  82.0 2.3 copy.18
  84.4 3.0 %collective-permute-start.2 = (bf16[4,256,384]{2,1,0:T(8,128)(2,1)}, bf16[4,256,384]{2,1,0:T(8,128)(2,1)}, u32[]{:S(2)}, u32[]{:S(2)}) collective-permute-start(bf16[4,256,384]{2,1,0:T(8,128)(2,1)} %bitcast.47), channel_id=1, source_target_pairs={{0,3},{1,0},{2,1},{3,2},{4,7},{5,4},{6,5},{7,6},{8,11},{9,8},{10,9... | collective-permute-start | bytes 2359304 | tf_op jit(solution)/shard_map/ppermute | solution.py:161
  87.4 2.3 copy.15
  90.4 0.0 copy-done
  90.4 0.2 dynamic-slice_reduce_fusion
  90.6 0.6 copy.21
  91.3 0.0 all-to-all-done.1.raw_ref
  91.3 1.4 copy-done.1
  92.7 5.4 %norm.1.hidden_ref = bf16[16,192,384]{2,1,0:T(8,128)(2,1)} custom-call(bf16[4,4,192,384]{3,2,1,0:T(8,128)(2,1)} %copy-done.1, f32[3,16,384]{2,1,0:T(8,128)} %bitcast.49), custom_call_target="tpu_custom_call" | custom-call | tf_op jit(solution)/shard_map/norm/pallas_call | solution.py:172
  98.0 9.8 %collective-permute-done.w1 = bf16[4,256,384]{2,1,0:T(8,128)(2,1)} collective-permute-done((bf16[4,256,384]{2,1,0:T(8,128)(2,1)}, bf16[4,256,384]{2,1,0:T(8,128)(2,1)}, u32[]{:S(2)}, u32[]{:S(2)}) %collective-permute-start) | collective-permute-done | bytes 786464 | tf_op jit(solution)/shard_map/ppermute | solution.py:161
  107.8 9.1 %collective-permute-done.1.w2 = bf16[4,256,384]{2,1,0:T(8,128)(2,1)} collective-permute-done((bf16[4,256,384]{2,1,0:T(8,128)(2,1)}, bf16[4,256,384]{2,1,0:T(8,128)(2,1)}, u32[]{:S(2)}, u32[]{:S(2)}) %collective-permute-start.1) | collective-permute-done | bytes 786464 | tf_op jit(solution)/shard_map/ppermute | solution.py:161
  116.9 5.4 %collective-permute-done.2.w3 = bf16[4,256,384]{2,1,0:T(8,128)(2,1)} collective-permute-done((bf16[4,256,384]{2,1,0:T(8,128)(2,1)}, bf16[4,256,384]{2,1,0:T(8,128)(2,1)}, u32[]{:S(2)}, u32[]{:S(2)}) %collective-permute-start.2) | collective-permute-done | bytes 786464 | tf_op jit(solution)/shard_map/ppermute | solution.py:161
  122.3 9.1 %project.1 = (bf16[2,192,128]{2,1,0:T(8,128)(2,1)}, bf16[2,2,192,128]{3,2,1,0:T(8,128)(2,1)}) custom-call(bf16[16,192,384]{2,1,0:T(8,128)(2,1)} %norm.1.hidden_ref, bf16[3,6144,256]{2,1,0:T(8,128)(2,1)} %all-gather.2.cloned.1.call-done.weight_ref, f32[1,128]{1,0:T(1,128)} %bitcast.50, f32[1,128]{1,0:T(1,128)} %bitcast.51), custom_call_target="tpu_custom_call" | custom-call | tf_op jit(solution)/shard_map/project/pallas_call | solution.py:180
  131.4 0.8 dynamic-slice_bitcast_fusion
  132.2 4.9 %collective-permute-start.3 = (bf16[192,128]{1,0:T(8,128)(2,1)S(1)}, bf16[192,128]{1,0:T(8,128)(2,1)S(1)}, u32[]{:S(2)}, u32[]{:S(2)}) collective-permute-start(bf16[192,128]{1,0:T(8,128)(2,1)S(1)} %dynamic-slice_bitcast_fusion), channel_id=1, source_target_pairs={{0,16},{16,0},{1,17},{17,1},{2,18},{18,2},{3,19},{19,3},{4,20},{20... | collective-permute-start | bytes 147464 | tf_op jit(solution)/shard_map/ppermute | solution.py:206
  137.1 2.0 broadcast_in_dim.8
  139.1 5.0 %all-to-all-start.2 = ((bf16[8,2,192,128]{3,2,1,0:T(8,128)(2,1)}), bf16[8,2,192,128]{3,2,1,0:T(8,128)(2,1)S(1)}, u32[]{:S(2)}, u32[]{:S(2)}) async-start(bf16[8,2,192,128]{3,2,1,0:T(8,128)(2,1)} %bitcast.18), calls=%async_computation.2 | async-start | bytes 1572864 | tf_op jit(solution)/shard_map/all_to_all | solution.py:202
  144.1 0.0 collective-permute-done.3
  144.1 0.8 constant_dynamic-update-slice_fusion.4
  144.9 0.8 constant_dynamic-update-slice_fusion.3
  145.8 12.8 %collective-permute-start.4 = (bf16[2,192,128]{2,1,0:T(8,128)(2,1)S(1)}, bf16[2,192,128]{2,1,0:T(8,128)(2,1)S(1)}, u32[]{:S(2)}, u32[]{:S(2)}) collective-permute-start(bf16[2,192,128]{2,1,0:T(8,128)(2,1)S(1)} %pad_maximum_fusion), channel_id=1, source_target_pairs={{0,32},{32,64},{64,96},{96,0},{1,33},{33,65},{65,97},{97,1},{2,34}... | collective-permute-start | bytes 294920 | tf_op jit(solution)/shard_map/ppermute | solution.py:209
  158.6 2.5 collective-permute-start.5
  161.0 4.3 %collective-permute-start.6 = (bf16[2,192,128]{2,1,0:T(8,128)(2,1)S(1)}, bf16[2,192,128]{2,1,0:T(8,128)(2,1)S(1)}, u32[]{:S(2)}, u32[]{:S(2)}) collective-permute-start(bf16[2,192,128]{2,1,0:T(8,128)(2,1)S(1)} %pad_maximum_fusion), channel_id=1, source_target_pairs={{0,96},{32,0},{64,32},{96,64},{1,97},{33,1},{65,33},{97,65},{2,98}... | collective-permute-start | bytes 294920 | tf_op jit(solution)/shard_map/ppermute | solution.py:209
  165.3 0.0 collective-permute-done.4
  165.3 2.4 collective-permute-done.5
  167.7 0.4 collective-permute-done.6
  168.1 0.0 copy-start.4
  168.1 0.0 all-to-all-done.2.kv_ref
  168.1 0.0 copy-start.2
  168.2 0.7 copy-done.4
  168.9 0.3 copy-done.2
  169.2 8.1 %attend.1 = bf16[8,208,128]{2,1,0:T(8,128)(2,1)} custom-call(s32[1]{0:T(128)} %bitcast.1.line_ref, bf16[8,192,128]{2,1,0:T(8,128)(2,1)} %copy-done.4, bf16[8,2,192,128]{3,2,1,0:T(8,128)(2,1)} %copy-done.2), custom_call_target="tpu_custom_call" | custom-call | tf_op jit(solution)/shard_map/attend/pallas_call | solution.py:214
  177.2 18.2 %all_to_all.26.parts_ref = bf16[8,208,128]{2,1,0:T(8,128)(2,1)} all-to-all(bf16[8,208,128]{2,1,0:T(8,128)(2,1)} %attend.1), channel_id=1, replica_groups=mesh['y'=4,'zl'=4,'core'=2,'head'=4,'seq'=4] {'zl','core'}, dimensions={0} | all-to-all | bytes 851968 | tf_op jit(solution)/shard_map/all_to_all | solution.py:235
  195.4 1.8 combine.1.a0
  197.2 2.3 collective-permute-start.7
  199.5 3.7 %collective-permute-start.8 = (bf16[192,256]{1,0:T(8,128)(2,1)}, bf16[192,256]{1,0:T(8,128)(2,1)S(1)}, u32[]{:S(2)}, u32[]{:S(2)}) collective-permute-start(bf16[192,256]{1,0:T(8,128)(2,1)} %combine.1.a0), channel_id=1, source_target_pairs={{0,2},{1,3},{2,0},{3,1},{4,6},{5,7},{6,4},{7,5},{8,10},{9,11},{10,... | collective-permute-start | bytes 294920 | tf_op jit(solution)/shard_map/ppermute | solution.py:242
  203.2 2.8 %collective-permute-start.9 = (bf16[192,256]{1,0:T(8,128)(2,1)}, bf16[192,256]{1,0:T(8,128)(2,1)S(1)}, u32[]{:S(2)}, u32[]{:S(2)}) collective-permute-start(bf16[192,256]{1,0:T(8,128)(2,1)} %combine.1.a0), channel_id=1, source_target_pairs={{0,3},{1,0},{2,1},{3,2},{4,7},{5,4},{6,5},{7,6},{8,11},{9,8},{10,9... | collective-permute-start | bytes 294920 | tf_op jit(solution)/shard_map/ppermute | solution.py:242
  206.0 0.0 collective-permute-done.7.a1
  206.0 0.0 copy-start.5
  206.0 0.5 collective-permute-done.8.a2
  206.5 2.8 %collective-permute-done.9.a3 = bf16[192,256]{1,0:T(8,128)(2,1)S(1)} collective-permute-done((bf16[192,256]{1,0:T(8,128)(2,1)}, bf16[192,256]{1,0:T(8,128)(2,1)S(1)}, u32[]{:S(2)}, u32[]{:S(2)}) %collective-permute-start.9) | collective-permute-done | bytes 98336 | tf_op jit(solution)/shard_map/ppermute | solution.py:242
  209.3 0.0 copy-done.5
  209.3 0.0 copy-done.6
  209.3 0.6 copy-done.7
  209.9 4.6 %branch.1 = bf16[4,192,384]{2,1,0:T(8,128)(2,1)} custom-call(bf16[192,256]{1,0:T(8,128)(2,1)} %combine.1.a0, bf16[192,256]{1,0:T(8,128)(2,1)} %copy-done.5, bf16[192,256]{1,0:T(8,128)(2,1)} %copy-done.6, bf16[192,256]{1,0:T(8,128)(2,1)} %copy-done.7, bf16[4,256,384]{2,1,0:T(8,128)(2,1)} %bitcast.44, bf16[4,256,384]{2,1,0:T(8,128)(2,1)} %collective-permute-done.w1, ...), custom_call_target="tpu_custom_call" | custom-call | tf_op jit(solution)/shard_map/branch/pallas_call | solution.py:243
  214.6 3.5 %all-to-all-start.4 = ((bf16[4,192,384]{2,1,0:T(8,128)(2,1)}), bf16[4,192,384]{2,1,0:T(8,128)(2,1)S(1)}, u32[]{:S(2)}, u32[]{:S(2)}) async-start(bf16[4,192,384]{2,1,0:T(8,128)(2,1)} %branch.1), calls=%async_computation.4 | async-start | bytes 1179648 | tf_op jit(solution)/shard_map/all_to_all | solution.py:252
  218.1 0.1 dynamic-slice_reduce_fusion.1
  218.1 31.2 %all-to-all-done.4 = bf16[4,192,384]{2,1,0:T(8,128)(2,1)S(1)} async-done(((bf16[4,192,384]{2,1,0:T(8,128)(2,1)}), bf16[4,192,384]{2,1,0:T(8,128)(2,1)S(1)}, u32[]{:S(2)}, u32[]{:S(2)}) %all-to-all-start.4) | async-done | bytes 589856 | tf_op jit(solution)/shard_map/all_to_all | solution.py:252
  249.3 0.1 convert_reduce_fusion
  249.4 0.7 add_convert_fusion.1
  (10 shorter events, 0.1 us)
Async XLA Ops:
  6.5 83.9 %copy-start = (f32[8,3,6144]{2,0,1:T(8,128)S(1)}, f32[8,3,6144]{2,0,1:T(8,128)}, u32[]{:S(2)}) copy-start(f32[8,3,6144]{2,0,1:T(8,128)} %param.15) | copy-start | bytes 1769476
  6.5 115.8 %all-gather.2.cloned.1.call-start = ((), (), s32[]{:S(2)}) async-start(), calls=%async_computation.5 | async-start | bytes 9732096 | tf_op jit(solution)/shard_map/all_gather | solution.py:156
  57.2 34.1 %all-to-all-start.1 = ((bf16[4,4,192,384]{3,2,1,0:T(8,128)(2,1)}), bf16[4,4,192,384]{3,2,1,0:T(8,128)(2,1)S(1)}, u32[]{:S(2)}, u32[]{:S(2)}) async-start(bf16[4,4,192,384]{3,2,1,0:T(8,128)(2,1)} %broadcast_in_dim.7), calls=%async_computation.1 | async-start | bytes 4718592 | tf_op jit(solution)/shard_map/all_to_all | solution.py:26
  72.1 35.7 %collective-permute-start = (bf16[4,256,384]{2,1,0:T(8,128)(2,1)}, bf16[4,256,384]{2,1,0:T(8,128)(2,1)}, u32[]{:S(2)}, u32[]{:S(2)}) collective-permute-start(bf16[4,256,384]{2,1,0:T(8,128)(2,1)} %bitcast.45), channel_id=1, source_target_pairs={{0,1},{1,2},{2,3},{3,0},{4,5},{5,6},{6,7},{7,4},{8,9},{9,10},{10,1... | collective-permute-start | bytes 2359304 | tf_op jit(solution)/shard_map/ppermute | solution.py:161
  77.7 39.2 %collective-permute-start.1 = (bf16[4,256,384]{2,1,0:T(8,128)(2,1)}, bf16[4,256,384]{2,1,0:T(8,128)(2,1)}, u32[]{:S(2)}, u32[]{:S(2)}) collective-permute-start(bf16[4,256,384]{2,1,0:T(8,128)(2,1)} %bitcast.46), channel_id=1, source_target_pairs={{0,2},{1,3},{2,0},{3,1},{4,6},{5,7},{6,4},{7,5},{8,10},{9,11},{10,... | collective-permute-start | bytes 2359304 | tf_op jit(solution)/shard_map/ppermute | solution.py:161
  84.4 37.9 %collective-permute-start.2 = (bf16[4,256,384]{2,1,0:T(8,128)(2,1)}, bf16[4,256,384]{2,1,0:T(8,128)(2,1)}, u32[]{:S(2)}, u32[]{:S(2)}) collective-permute-start(bf16[4,256,384]{2,1,0:T(8,128)(2,1)} %bitcast.47), channel_id=1, source_target_pairs={{0,3},{1,0},{2,1},{3,2},{4,7},{5,4},{6,5},{7,6},{8,11},{9,8},{10,9... | collective-permute-start | bytes 2359304 | tf_op jit(solution)/shard_map/ppermute | solution.py:161
  91.3 1.4 copy-start.1
  132.2 11.9 %collective-permute-start.3 = (bf16[192,128]{1,0:T(8,128)(2,1)S(1)}, bf16[192,128]{1,0:T(8,128)(2,1)S(1)}, u32[]{:S(2)}, u32[]{:S(2)}) collective-permute-start(bf16[192,128]{1,0:T(8,128)(2,1)S(1)} %dynamic-slice_bitcast_fusion), channel_id=1, source_target_pairs={{0,16},{16,0},{1,17},{17,1},{2,18},{18,2},{3,19},{19,3},{4,20},{20... | collective-permute-start | bytes 147464 | tf_op jit(solution)/shard_map/ppermute | solution.py:206
  139.1 29.0 %all-to-all-start.2 = ((bf16[8,2,192,128]{3,2,1,0:T(8,128)(2,1)}), bf16[8,2,192,128]{3,2,1,0:T(8,128)(2,1)S(1)}, u32[]{:S(2)}, u32[]{:S(2)}) async-start(bf16[8,2,192,128]{3,2,1,0:T(8,128)(2,1)} %bitcast.18), calls=%async_computation.2 | async-start | bytes 1572864 | tf_op jit(solution)/shard_map/all_to_all | solution.py:202
  145.8 19.5 %collective-permute-start.4 = (bf16[2,192,128]{2,1,0:T(8,128)(2,1)S(1)}, bf16[2,192,128]{2,1,0:T(8,128)(2,1)S(1)}, u32[]{:S(2)}, u32[]{:S(2)}) collective-permute-start(bf16[2,192,128]{2,1,0:T(8,128)(2,1)S(1)} %pad_maximum_fusion), channel_id=1, source_target_pairs={{0,32},{32,64},{64,96},{96,0},{1,33},{33,65},{65,97},{97,1},{2,34}... | collective-permute-start | bytes 294920 | tf_op jit(solution)/shard_map/ppermute | solution.py:209
  158.6 9.1 %collective-permute-start.5 = (bf16[2,192,128]{2,1,0:T(8,128)(2,1)S(1)}, bf16[2,192,128]{2,1,0:T(8,128)(2,1)S(1)}, u32[]{:S(2)}, u32[]{:S(2)}) collective-permute-start(bf16[2,192,128]{2,1,0:T(8,128)(2,1)S(1)} %pad_maximum_fusion), channel_id=1, source_target_pairs={{0,64},{32,96},{64,0},{96,32},{1,65},{33,97},{65,1},{97,33},{2,66}... | collective-permute-start | bytes 294920 | tf_op jit(solution)/shard_map/ppermute | solution.py:209
  161.0 7.1 %collective-permute-start.6 = (bf16[2,192,128]{2,1,0:T(8,128)(2,1)S(1)}, bf16[2,192,128]{2,1,0:T(8,128)(2,1)S(1)}, u32[]{:S(2)}, u32[]{:S(2)}) collective-permute-start(bf16[2,192,128]{2,1,0:T(8,128)(2,1)S(1)} %pad_maximum_fusion), channel_id=1, source_target_pairs={{0,96},{32,0},{64,32},{96,64},{1,97},{33,1},{65,33},{97,65},{2,98}... | collective-permute-start | bytes 294920 | tf_op jit(solution)/shard_map/ppermute | solution.py:209
  168.1 0.7 copy-start.4
  168.1 1.0 copy-start.2
  197.2 52.2 %copy-start.3 = (bf16[192,384]{1,0:T(8,128)(2,1)S(1)}, bf16[192,384]{1,0:T(8,128)(2,1)}, u32[]{:S(2)}) copy-start(bf16[192,384]{1,0:T(8,128)(2,1)} %param.9) | copy-start | bytes 442372
  197.2 8.8 %collective-permute-start.7 = (bf16[192,256]{1,0:T(8,128)(2,1)}, bf16[192,256]{1,0:T(8,128)(2,1)S(1)}, u32[]{:S(2)}, u32[]{:S(2)}) collective-permute-start(bf16[192,256]{1,0:T(8,128)(2,1)} %combine.1.a0), channel_id=1, source_target_pairs={{0,1},{1,2},{2,3},{3,0},{4,5},{5,6},{6,7},{7,4},{8,9},{9,10},{10,1... | collective-permute-start | bytes 294920 | tf_op jit(solution)/shard_map/ppermute | solution.py:242
  199.5 7.1 %collective-permute-start.8 = (bf16[192,256]{1,0:T(8,128)(2,1)}, bf16[192,256]{1,0:T(8,128)(2,1)S(1)}, u32[]{:S(2)}, u32[]{:S(2)}) collective-permute-start(bf16[192,256]{1,0:T(8,128)(2,1)} %combine.1.a0), channel_id=1, source_target_pairs={{0,2},{1,3},{2,0},{3,1},{4,6},{5,7},{6,4},{7,5},{8,10},{9,11},{10,... | collective-permute-start | bytes 294920 | tf_op jit(solution)/shard_map/ppermute | solution.py:242
  203.2 6.1 %collective-permute-start.9 = (bf16[192,256]{1,0:T(8,128)(2,1)}, bf16[192,256]{1,0:T(8,128)(2,1)S(1)}, u32[]{:S(2)}, u32[]{:S(2)}) collective-permute-start(bf16[192,256]{1,0:T(8,128)(2,1)} %combine.1.a0), channel_id=1, source_target_pairs={{0,3},{1,0},{2,1},{3,2},{4,7},{5,4},{6,5},{7,6},{8,11},{9,8},{10,9... | collective-permute-start | bytes 294920 | tf_op jit(solution)/shard_map/ppermute | solution.py:242
  206.0 3.3 %copy-start.5 = (bf16[192,256]{1,0:T(8,128)(2,1)}, bf16[192,256]{1,0:T(8,128)(2,1)S(1)}, u32[]{:S(2)}) copy-start(bf16[192,256]{1,0:T(8,128)(2,1)S(1)} %collective-permute-done.7.a1) | copy-start | bytes 294916
  206.5 2.8 %copy-start.6 = (bf16[192,256]{1,0:T(8,128)(2,1)}, bf16[192,256]{1,0:T(8,128)(2,1)S(1)}, u32[]{:S(2)}) copy-start(bf16[192,256]{1,0:T(8,128)(2,1)S(1)} %collective-permute-done.8.a2) | copy-start | bytes 294916
  209.3 0.6 copy-start.7
  214.6 34.8 %all-to-all-start.4 = ((bf16[4,192,384]{2,1,0:T(8,128)(2,1)}), bf16[4,192,384]{2,1,0:T(8,128)(2,1)S(1)}, u32[]{:S(2)}, u32[]{:S(2)}) async-start(bf16[4,192,384]{2,1,0:T(8,128)(2,1)} %branch.1), calls=%async_computation.4 | async-start | bytes 1179648 | tf_op jit(solution)/shard_map/all_to_all | solution.py:252
Sparse Core Ops, SparseCore 0:
  9.5 98.9 all-gather.1

commit v3 on v2

--- a/solution.py
+++ b/solution.py
@@ -44,49 +44,57 @@
         centred = raw_ref[s, h].astype(F32) - average
         scale = mod_ref[1, block : block + 1, :]
         move = mod_ref[0, block : block + 1, :]
-        out_ref[block] = (centred * inverse * (1.0 + scale) + move).astype(BF)
-
-
-def project_kernel(hidden_ref, weight_ref, q_gain_ref, k_gain_ref, q_ref, kv_ref, acc_ref):
+        out_ref[:, block * width : (block + 1) * width] = (
+            centred * inverse * (1.0 + scale) + move
+        ).astype(BF)
+
+
+def pick_kernel(seq_ref, *refs):
+    for source, target in zip(refs[:GRID], refs[GRID:]):
+        target[0] = source[...]
+
+
+def project_kernel(core_ref, hidden_ref, weight_ref, q_gain_ref, k_gain_ref, own_ref, other_ref, acc_ref):
     step = pl.program_id(0)
 
     @pl.when(step == 0)
     def _():
         acc_ref[...] = jnp.zeros_like(acc_ref)
 
-    for b in range(hidden_ref.shape[0]):
-        width = hidden_ref.shape[2]
-        for j in range(3):
-            acc_ref[j] += jnp.dot(
-                hidden_ref[b],
-                weight_ref[j, b * width : (b + 1) * width, :],
-                preferred_element_type=F32,
-            )
+    for j in range(3):
+        acc_ref[j] += jnp.dot(hidden_ref[...], weight_ref[j], preferred_element_type=F32)
 
     @pl.when(step == pl.num_programs(0) - 1)
     def _():
         for h in range(2):
             part = slice(h * HD, (h + 1) * HD)
+            results = []
             for j, gain_ref in ((0, q_gain_ref), (1, k_gain_ref)):
                 values = acc_ref[j, :, part]
                 squares = jnp.mean(values * values, axis=1, keepdims=True)
-                normed = (values * lax.rsqrt(squares + 1e-06) * gain_ref[...]).astype(BF)
-                if j == 0:
-                    q_ref[h] = normed
-                else:
-                    kv_ref[h, 0] = normed
-            kv_ref[h, 1] = acc_ref[2, :, part].astype(BF)
-
-
-def attend_kernel(line_ref, q_ref, kv_ref, out_ref, k_all, v_all):
-    rows = q_ref.shape[1]
-    blocks = kv_ref.shape[0]
+                results.append((values * lax.rsqrt(squares + 1e-06) * gain_ref[...]).astype(BF))
+            results.append(acc_ref[2, :, part].astype(BF))
+
+            @pl.when(core_ref[0] == h)
+            def _():
+                for j in range(3):
+                    own_ref[j] = results[j]
+
+            @pl.when(core_ref[0] != h)
+            def _():
+                for j in range(3):
+                    other_ref[j] = results[j]
+
+
+def attend_kernel(core_ref, q_ref, kv_ref, out_ref, k_all, v_all):
+    rows = q_ref.shape[2]
+    blocks = kv_ref.shape[0] * 2
 
     @pl.when(pl.program_id(0) == 0)
     def _():
         for b in range(blocks):
-            k_all[b * rows : (b + 1) * rows, :] = kv_ref[b, 0]
-            v_all[b * rows : (b + 1) * rows, :HD] = kv_ref[b, 1]
+            k_all[b * rows : (b + 1) * rows, :] = kv_ref[b // 2, b % 2, 0]
+            v_all[b * rows : (b + 1) * rows, :HD] = kv_ref[b // 2, b % 2, 1]
         v_all[:, HD:] = jnp.ones((blocks * rows, HD), BF)
 
     chunk = 512
@@ -94,7 +102,7 @@
     for c in range(blocks * rows // chunk):
         part = slice(c * chunk, (c + 1) * chunk)
         scores = lax.dot_general(
-            q_ref[0], k_all[part, :], (((1,), (1,)), ((), ())), preferred_element_type=F32
+            q_ref[0, 0], k_all[part, :], (((1,), (1,)), ((), ())), preferred_element_type=F32
         )
         weights = jnp.exp2(scores * (LOG2E / math.sqrt(HD))).astype(BF)
         both = both + jnp.dot(weights, v_all[part, :], preferred_element_type=F32)
@@ -155,60 +163,57 @@
     ema_weights = (decay * ema_qkv.astype(F32) + (1.0 - decay) * train_qkv.astype(F32)).astype(BF)
     full_weights = lax.all_gather(ema_weights, TOKENS, axis=1, tiled=True)
 
-    seq_here = lax.axis_index("seq")
-    by_seq = jnp.transpose(out_weight.reshape(channels, GRID, GRID, width), (2, 1, 0, 3))
-    out_parts = [
-        lax.ppermute(
-            lax.dynamic_index_in_dim(by_seq, (seq_here + k) % GRID, 0, keepdims=False), "seq", shift(k)
-        )
-        if k
-        else lax.dynamic_index_in_dim(by_seq, seq_here, 0, keepdims=False)
-        for k in range(GRID)
-    ]
+    seq_here = lax.axis_index("seq").astype(jnp.int32).reshape(1)
+    core_here = lax.axis_index("core").astype(jnp.int32).reshape(1)
+
+    def column(k):
+        return lambda i, seq: (0, i * GRID + lax.rem(seq[0] + k, GRID))
+
+    out_parts = pl.pallas_call(
+        pick_kernel,
+        grid_spec=pltpu.PrefetchScalarGridSpec(
+            num_scalar_prefetch=1,
+            grid=(GRID,),
+            in_specs=[pl.BlockSpec((channels, width), column(k)) for k in range(GRID)],
+            out_specs=[pl.BlockSpec((1, channels, width), lambda i, seq: (i, 0, 0))] * GRID,
+        ),
+        out_shape=[jax.ShapeDtypeStruct((GRID, channels, width), BF)] * GRID,
+        name="pick",
+    )(seq_here, *([out_weight] * GRID))
+    out_parts = [out_parts[0]] + [lax.ppermute(out_parts[k], "seq", shift(k)) for k in (1, 2, 3)]
 
     mod_row = lax.dynamic_index_in_dim(modulation, timestep[0], 0, keepdims=False)
     raw = gather_small(latents, "head")
+    raw, *out_parts = lax.optimization_barrier((raw, *out_parts))
     raw = gather_small(raw, "seq").reshape(GRID, GRID, rows, width)
     hidden = pl.pallas_call(
         norm_kernel,
-        out_shape=jax.ShapeDtypeStruct((blocks, rows, width), BF),
+        out_shape=jax.ShapeDtypeStruct((rows, blocks * width), BF),
         name="norm",
     )(raw, mod_row.reshape(3, blocks, width))
-    hidden, *out_parts = lax.optimization_barrier((hidden, *out_parts))
-
-    per_step = 2
-    queries, pairs = pl.pallas_call(
+
+    depth = D // GRID
+    own, other = pl.pallas_call(
         project_kernel,
-        grid=(blocks // per_step,),
-        in_specs=[
-            pl.BlockSpec((per_step, rows, width), lambda i: (i, 0, 0)),
-            pl.BlockSpec((3, per_step * width, channels), lambda i: (0, i, 0)),
-            pl.BlockSpec((1, HD), lambda i: (0, 0)),
-            pl.BlockSpec((1, HD), lambda i: (0, 0)),
-        ],
-        out_specs=[
-            pl.BlockSpec((2, rows, HD), lambda i: (0, 0, 0)),
-            pl.BlockSpec((2, 2, rows, HD), lambda i: (0, 0, 0, 0)),
-        ],
-        out_shape=[
-            jax.ShapeDtypeStruct((2, rows, HD), BF),
-            jax.ShapeDtypeStruct((2, 2, rows, HD), BF),
-        ],
-        scratch_shapes=[pltpu.VMEM((3, rows, channels), F32)],
+        grid_spec=pltpu.PrefetchScalarGridSpec(
+            num_scalar_prefetch=1,
+            grid=(GRID,),
+            in_specs=[
+                pl.BlockSpec((rows, depth), lambda i, core: (0, i)),
+                pl.BlockSpec((3, depth, channels), lambda i, core: (0, i, 0)),
+                pl.BlockSpec((1, HD), lambda i, core: (0, 0)),
+                pl.BlockSpec((1, HD), lambda i, core: (0, 0)),
+            ],
+            out_specs=[pl.BlockSpec((3, rows, HD), lambda i, core: (0, 0, 0))] * 2,
+            scratch_shapes=[pltpu.VMEM((3, rows, channels), F32)],
+        ),
+        out_shape=[jax.ShapeDtypeStruct((3, rows, HD), BF)] * 2,
         name="project",
-    )(hidden, full_weights, q_gain.reshape(1, HD), k_gain.reshape(1, HD))
-
-    pairs = jnp.broadcast_to(pairs[None], (GRID,) + pairs.shape).reshape(2 * GRID, 2, rows, HD)
-    pairs = lax.all_to_all(pairs, ("y", "core"), 0, 0, tiled=True)
-    core = lax.axis_index("core")
-    own = lax.dynamic_index_in_dim(queries, core, 0, keepdims=False)
-    other = lax.dynamic_index_in_dim(queries, 1 - core, 0, keepdims=False)
-    other = lax.ppermute(other, "core", [(0, 1), (1, 0)])
-    own, other = jnp.where(core == 0, own, other), jnp.where(core == 0, other, own)
-    queries = jnp.stack([own, other])
-    queries = [queries] + [lax.ppermute(queries, "zl", shift(k)) for k in (1, 2, 3)]
-    queries = jnp.concatenate(queries)
-    line_here = lax.axis_index("zl").astype(jnp.int32).reshape(1)
+    )(core_here, hidden, full_weights, q_gain.reshape(1, HD), k_gain.reshape(1, HD))
+
+    both = jnp.stack([own, lax.ppermute(other, "core", [(0, 1), (1, 0)])])
+    queries = gather_small(both[:, 0], "zl").reshape(GRID, 2, rows, HD)
+    pairs = gather_small(both[:, 1:], "y").reshape(GRID, 2, 2, rows, HD)
 
     sent = rows + 16
     parts = pl.pallas_call(
@@ -218,12 +223,11 @@
             grid=(2 * GRID,),
             in_specs=[
                 pl.BlockSpec(
-                    (1, rows, HD),
-                    lambda i, line: (lax.rem(line[0] + GRID - i // 2, GRID) * 2 + i % 2, 0, 0),
+                    (1, 1, rows, HD), lambda i, core: (i // 2, lax.rem(i + core[0], 2), 0, 0)
                 ),
-                pl.BlockSpec((2 * GRID, 2, rows, HD), lambda i, line: (0, 0, 0, 0)),
+                pl.BlockSpec((GRID, 2, 2, rows, HD), lambda i, core: (0, 0, 0, 0, 0)),
             ],
-            out_specs=pl.BlockSpec((1, sent, HD), lambda i, line: (i, 0, 0)),
+            out_specs=pl.BlockSpec((1, sent, HD), lambda i, core: (i, 0, 0)),
             scratch_shapes=[
                 pltpu.VMEM((2 * GRID * rows, HD), BF),
                 pltpu.VMEM((2 * GRID * rows, 2 * HD), BF),
@@ -231,7 +235,7 @@
         ),
         out_shape=jax.ShapeDtypeStruct((2 * GRID, sent, HD), BF),
         name="attend",
-    )(line_here, queries, pairs)
+    )(core_here, queries, pairs)
     parts = lax.all_to_all(parts, ("zl", "core"), 0, 0, tiled=True)
     attended = pl.pallas_call(
         combine_kernel,

time: 261 us -> 257 us (0.985)
  waiting for transfers between devices: 61.5 us -> 104 us
  blocking collectives: 63.5 us -> 32.1 us
  local copies, waits for them, and re-layouts: 27.1 us -> 8.56 us
  starting transfers between devices: 56.5 us -> 59.4 us
    all_to_all x1 -> x3, waiting for transfers between devices: 0.01 us -> 38.2 us  [gather_small(): return lax.all_to_all(spread, axis_name, 0, 0, tiled=True)]
    all_to_all x1, blocking collectives: 45.3 us -> 13.5 us  [gather_small(): return lax.all_to_all(spread, axis_name, 0, 0, tiled=True)]
    ppermute x7 -> x4, starting transfers between devices: 35.1 us -> 14.6 us  [the longest x3 10.5 us: per_device(): lax.ppermute(out_parts[k], 'seq', shift(k))]
    all_to_all x1 -> x3, starting transfers between devices: 4.19 us -> 24.5 us  [gather_small(): return lax.all_to_all(spread, axis_name, 0, 0, tiled=True)]
    unnamed x24 -> x21, local copies, waits for them, and re-layouts: 17.7 us -> 3.68 us
    all_to_all x1, starting transfers between devices: 3.48 us -> 11.4 us  [per_device(): branch = lax.all_to_all(branch, 'head', 0, 0, tiled=True)]
    all_to_all x1 -> x0, starting transfers between devices: 4.98 us -> none  [per_device(): pairs = lax.all_to_all(pairs, ('y', 'core'), 0, 0, tiled=True)]
    ppermute x7 -> x4, waiting for transfers between devices: 27 us -> 30.9 us  [the longest x3 29.7 us: per_device(): lax.ppermute(out_parts[k], 'seq', shift(k))]
  transfers between devices with their start and end apart: 14 -> 12, of which waited for: 8 -> 9; matrix products, arithmetic and copies ran while one was open for 10% -> 2% of each run, Pallas kernels for 2% -> 4%
where the time goes in v3:
time: 257 us; the launch traced here: 254 us
  waiting for transfers between devices  104 us (40%)
  starting transfers between devices  59.4 us (23%)
  blocking collectives  32.1 us (12%)
  Pallas kernels  31.4 us (12%)
  between operations  14.9 us (6%)
  local copies, waits for them, and re-layouts  8.56 us (3%)
  other arithmetic  3.57 us (1%)
    all_to_all x3, waiting for transfers between devices, gather_small(): return lax.all_to_all(spread, axis_name, 0, 0, tiled=True)  38.2 us
    all_to_all x1, waiting for transfers between devices, per_device(): branch = lax.all_to_all(branch, 'head', 0, 0, tiled=True)  31.3 us
    ppermute x3, waiting for transfers between devices, per_device(): lax.ppermute(out_parts[k], 'seq', shift(k))  29.7 us
    all_to_all x3, starting transfers between devices, gather_small(): return lax.all_to_all(spread, axis_name, 0, 0, tiled=True)  24.5 us
    all_to_all x1, blocking collectives, per_device(): parts = lax.all_to_all(parts, ('zl', 'core'), 0, 0, tiled=True)  18.7 us
    all_to_all x1, blocking collectives, gather_small(): return lax.all_to_all(spread, axis_name, 0, 0, tiled=True)  13.5 us
    all_to_all x1, starting transfers between devices, per_device(): branch = lax.all_to_all(branch, 'head', 0, 0, tiled=True)  11.4 us
    ppermute x3, starting transfers between devices, per_device(): lax.ppermute(out_parts[k], 'seq', shift(k))  10.5 us
  transfers between devices with their start and end apart: 12, of which 9 were waited for; matrix products, arithmetic and copies ran while one was open for 2% of the time, Pallas kernels for 4%

profile of v3, /device:TPU:1, one launch (start us, length us, event | category | flops | bytes accessed | tf_op | source)
XLA Modules:
  0.0 253.7 jit_solution(16912309736871066675)
XLA Ops:
  6.5 0.0 copy-start
  6.5 0.0 all-gather.2.cloned.1.call-start
  7.3 1.9 add_convert_fusion
  9.2 0.0 all-gather.2.cloned.1.call-update
  9.2 1.8 broadcast_in_dim.10
  11.0 15.6 %all-to-all-start = ((bf16[4,192,384]{2,1,0:T(8,128)(2,1)}), bf16[4,192,384]{2,1,0:T(8,128)(2,1)S(1)}, u32[]{:S(2)}, u32[]{:S(2)}) async-start(bf16[4,192,384]{2,1,0:T(8,128)(2,1)} %broadcast_in_dim.10), calls=%async_computation | async-start | bytes 1179648 | tf_op jit(solution)/shard_map/all_to_all | solution.py:26
  26.6 4.4 %pick.1 = (bf16[4,256,384]{2,1,0:T(8,128)(2,1)}, bf16[4,256,384]{2,1,0:T(8,128)(2,1)}, bf16[4,256,384]{2,1,0:T(8,128)(2,1)}, bf16[4,256,384]{2,1,0:T(8,128)(2,1)}) custom-call(s32[1]{0:T(128)} %bitcast.2.seq_ref, bf16[256,6144]{1,0:T(8,128)(2,1)} %refs_3_.1, bf16[256,6144]{1,0:T(8,128)(2,1)} %refs_3_.1, bf16[256,6144]{1,0:T(8,128)(2,1)} %refs_3_.1, ...), custom_call_target="tpu_custom_call" | custom-call | tf_op jit(solution)/shard_map/pick/pallas_call | solution.py:172
  31.0 3.1 %collective-permute-start = (bf16[4,256,384]{2,1,0:T(8,128)(2,1)}, bf16[4,256,384]{2,1,0:T(8,128)(2,1)S(1)}, u32[]{:S(2)}, u32[]{:S(2)}) collective-permute-start(bf16[4,256,384]{2,1,0:T(8,128)(2,1)} %get-tuple-element.17), channel_id=1, source_target_pairs={{0,1},{1,2},{2,3},{3,0},{4,5},{5,6},{6,7},{7,4},{8,9},{9,10},{10,1... | collective-permute-start | bytes 2359304 | tf_op jit(solution)/shard_map/ppermute | solution.py:183
  34.1 4.4 %collective-permute-start.1 = (bf16[4,256,384]{2,1,0:T(8,128)(2,1)}, bf16[4,256,384]{2,1,0:T(8,128)(2,1)S(1)}, u32[]{:S(2)}, u32[]{:S(2)}) collective-permute-start(bf16[4,256,384]{2,1,0:T(8,128)(2,1)} %get-tuple-element.18), channel_id=1, source_target_pairs={{0,2},{1,3},{2,0},{3,1},{4,6},{5,7},{6,4},{7,5},{8,10},{9,11},{10,... | collective-permute-start | bytes 2359304 | tf_op jit(solution)/shard_map/ppermute | solution.py:183
  38.5 3.1 %collective-permute-start.2 = (bf16[4,256,384]{2,1,0:T(8,128)(2,1)}, bf16[4,256,384]{2,1,0:T(8,128)(2,1)}, u32[]{:S(2)}, u32[]{:S(2)}) collective-permute-start(bf16[4,256,384]{2,1,0:T(8,128)(2,1)} %get-tuple-element.19), channel_id=1, source_target_pairs={{0,3},{1,0},{2,1},{3,2},{4,7},{5,4},{6,5},{7,6},{8,11},{9,8},{10,9... | collective-permute-start | bytes 2359304 | tf_op jit(solution)/shard_map/ppermute | solution.py:183
  41.5 10.8 %collective-permute-done.w1 = bf16[4,256,384]{2,1,0:T(8,128)(2,1)S(1)} collective-permute-done((bf16[4,256,384]{2,1,0:T(8,128)(2,1)}, bf16[4,256,384]{2,1,0:T(8,128)(2,1)S(1)}, u32[]{:S(2)}, u32[]{:S(2)}) %collective-permute-start) | collective-permute-done | bytes 786464 | tf_op jit(solution)/shard_map/ppermute | solution.py:183
  52.4 0.0 copy-start.3
  52.4 17.8 %collective-permute-done.1.w2 = bf16[4,256,384]{2,1,0:T(8,128)(2,1)S(1)} collective-permute-done((bf16[4,256,384]{2,1,0:T(8,128)(2,1)}, bf16[4,256,384]{2,1,0:T(8,128)(2,1)S(1)}, u32[]{:S(2)}, u32[]{:S(2)}) %collective-permute-start.1) | collective-permute-done | bytes 786464 | tf_op jit(solution)/shard_map/ppermute | solution.py:183
  70.2 0.0 copy-done.3
  70.2 0.0 copy-start.4
  70.2 0.9 copy-done.4
  71.1 1.1 collective-permute-done.2.w3
  72.2 0.0 all-to-all-done
  72.2 1.7 broadcast_in_dim.11
  73.9 4.7 %all-to-all-start.1 = ((bf16[4,4,192,384]{3,2,1,0:T(8,128)(2,1)}), bf16[4,4,192,384]{3,2,1,0:T(8,128)(2,1)S(1)}, u32[]{:S(2)}, u32[]{:S(2)}) async-start(bf16[4,4,192,384]{3,2,1,0:T(8,128)(2,1)} %broadcast_in_dim.11), calls=%async_computation.1 | async-start | bytes 4718592 | tf_op jit(solution)/shard_map/all_to_all | solution.py:26
  79.2 0.0 copy-done
  79.2 0.2 dynamic-slice_reduce_fusion
  79.5 0.6 copy.12
  80.1 26.5 %all-to-all-done.1.raw_ref = bf16[4,4,192,384]{3,2,1,0:T(8,128)(2,1)S(1)} async-done(((bf16[4,4,192,384]{3,2,1,0:T(8,128)(2,1)}), bf16[4,4,192,384]{3,2,1,0:T(8,128)(2,1)S(1)}, u32[]{:S(2)}, u32[]{:S(2)}) %all-to-all-start.1) | async-done | bytes 2359328 | tf_op jit(solution)/shard_map/all_to_all | solution.py:26
  106.6 0.0 copy-start.1
  106.6 1.5 copy-done.1
  108.0 5.4 %norm.1.hidden_ref = bf16[192,6144]{1,0:T(8,128)(2,1)} custom-call(bf16[4,4,192,384]{3,2,1,0:T(8,128)(2,1)} %copy-done.1, f32[3,16,384]{2,1,0:T(8,128)} %bitcast.22), custom_call_target="tpu_custom_call" | custom-call | tf_op jit(solution)/shard_map/norm/pallas_call | solution.py:189
  113.4 0.0 all-gather.2.cloned.1.call-done.weight_ref
  113.4 7.1 %project.1 = (bf16[3,192,128]{2,1,0:T(8,128)(2,1)}, bf16[3,192,128]{2,1,0:T(8,128)(2,1)}) custom-call(s32[1]{0:T(128)} %bitcast.1.core_ref, bf16[192,6144]{1,0:T(8,128)(2,1)} %norm.1.hidden_ref, bf16[3,6144,256]{2,1,0:T(8,128)(2,1)} %all-gather.2.cloned.1.call-done.weight_ref, f32[1,128]{1,0:T(1,128)} %bitcast.23, f32[1,128]{1,0:T(1,128)} %bitcast.24), custom_call_target="tpu_custom_call" | custom-call | tf_op jit(solution)/shard_map/project/pallas_call | solution.py:196
  120.5 0.0 copy-start.5
  120.5 4.1 %collective-permute-start.3 = (bf16[3,192,128]{2,1,0:T(8,128)(2,1)}, bf16[3,192,128]{2,1,0:T(8,128)(2,1)S(1)}, u32[]{:S(2)}, u32[]{:S(2)}) collective-permute-start(bf16[3,192,128]{2,1,0:T(8,128)(2,1)} %get-tuple-element.22), channel_id=1, source_target_pairs={{0,16},{16,0},{1,17},{17,1},{2,18},{18,2},{3,19},{19,3},{4,20},{20... | collective-permute-start | bytes 442376 | tf_op jit(solution)/shard_map/ppermute | solution.py:214
  124.7 1.2 collective-permute-done.3
  125.9 0.9 pad_maximum_fusion
  126.8 1.0 broadcast_in_dim.14
  127.8 4.2 %all-to-all-start.3 = ((bf16[4,2,2,192,128]{4,3,2,1,0:T(8,128)(2,1)}), bf16[4,2,2,192,128]{4,3,2,1,0:T(8,128)(2,1)S(1)}, u32[]{:S(2)}, u32[]{:S(2)}) async-start(bf16[4,2,2,192,128]{4,3,2,1,0:T(8,128)(2,1)} %broadcast_in_dim.14), calls=%async_computation.3 | async-start | bytes 1572864 | tf_op jit(solution)/shard_map/all_to_all | solution.py:26
  132.0 0.0 copy-done.5
  132.0 11.7 %all-to-all-done.3.kv_ref = bf16[4,2,2,192,128]{4,3,2,1,0:T(8,128)(2,1)S(1)} async-done(((bf16[4,2,2,192,128]{4,3,2,1,0:T(8,128)(2,1)}), bf16[4,2,2,192,128]{4,3,2,1,0:T(8,128)(2,1)S(1)}, u32[]{:S(2)}, u32[]{:S(2)}) %all-to-all-start.3) | async-done | bytes 786464 | tf_op jit(solution)/shard_map/all_to_all | solution.py:26
  143.7 0.0 copy-start.2
  143.7 0.1 broadcast_in_dim.13
  143.8 13.5 %all_to_all.30.q_ref = bf16[4,2,192,128]{3,2,1,0:T(8,128)(2,1)} all-to-all(bf16[4,2,192,128]{3,2,1,0:T(8,128)(2,1)S(1)} %broadcast_in_dim.13), channel_id=1, replica_groups=mesh['y'=4,'zl'=4,'core'=2,'head'=4,'seq'=4] {'zl'}, dimensions={0} | all-to-all | bytes 786432 | tf_op jit(solution)/shard_map/all_to_all | solution.py:26
  157.2 0.0 copy-done.2
  157.2 8.1 %attend.1 = bf16[8,208,128]{2,1,0:T(8,128)(2,1)} custom-call(s32[1]{0:T(128)} %bitcast.1.core_ref, bf16[4,2,192,128]{3,2,1,0:T(8,128)(2,1)} %all_to_all.30.q_ref, bf16[4,2,2,192,128]{4,3,2,1,0:T(8,128)(2,1)} %copy-done.2), custom_call_target="tpu_custom_call" | custom-call | tf_op jit(solution)/shard_map/attend/pallas_call | solution.py:219
  165.3 18.7 %all_to_all.31.parts_ref = bf16[8,208,128]{2,1,0:T(8,128)(2,1)} all-to-all(bf16[8,208,128]{2,1,0:T(8,128)(2,1)} %attend.1), channel_id=1, replica_groups=mesh['y'=4,'zl'=4,'core'=2,'head'=4,'seq'=4] {'zl','core'}, dimensions={0} | all-to-all | bytes 851968 | tf_op jit(solution)/shard_map/all_to_all | solution.py:239
  184.0 1.8 combine.1.a0
  185.7 0.0 copy-start.6
  185.7 2.3 collective-permute-start.4
  188.1 4.3 %collective-permute-start.5 = (bf16[192,256]{1,0:T(8,128)(2,1)}, bf16[192,256]{1,0:T(8,128)(2,1)S(1)}, u32[]{:S(2)}, u32[]{:S(2)}) collective-permute-start(bf16[192,256]{1,0:T(8,128)(2,1)} %combine.1.a0), channel_id=1, source_target_pairs={{0,2},{1,3},{2,0},{3,1},{4,6},{5,7},{6,4},{7,5},{8,10},{9,11},{10,... | collective-permute-start | bytes 294920 | tf_op jit(solution)/shard_map/ppermute | solution.py:246
  192.4 2.2 collective-permute-start.6
  194.6 0.0 collective-permute-done.4.a1
  194.6 0.0 copy-start.7
  194.6 0.5 collective-permute-done.5.a2
  195.1 0.0 copy-start.8
  195.1 2.8 %collective-permute-done.6.a3 = bf16[192,256]{1,0:T(8,128)(2,1)S(1)} collective-permute-done((bf16[192,256]{1,0:T(8,128)(2,1)}, bf16[192,256]{1,0:T(8,128)(2,1)S(1)}, u32[]{:S(2)}, u32[]{:S(2)}) %collective-permute-start.6) | collective-permute-done | bytes 98336 | tf_op jit(solution)/shard_map/ppermute | solution.py:246
  198.0 0.0 copy-done.7
  198.0 0.0 copy-done.8
  198.0 0.0 copy-start.9
  198.0 0.6 copy-done.9
  198.6 4.7 %branch.1 = bf16[4,192,384]{2,1,0:T(8,128)(2,1)} custom-call(bf16[192,256]{1,0:T(8,128)(2,1)} %combine.1.a0, bf16[192,256]{1,0:T(8,128)(2,1)} %copy-done.7, bf16[192,256]{1,0:T(8,128)(2,1)} %copy-done.8, bf16[192,256]{1,0:T(8,128)(2,1)} %copy-done.9, bf16[4,256,384]{2,1,0:T(8,128)(2,1)} %get-tuple-element.23.w0, bf16[4,256,384]{2,1,0:T(8,128)(2,1)} %copy-done.3, ...), custom_call_target="tpu_custom_call" | custom-call | tf_op jit(solution)/shard_map/branch/pallas_call | solution.py:247
  203.3 11.4 %all-to-all-start.5 = ((bf16[4,192,384]{2,1,0:T(8,128)(2,1)}), bf16[4,192,384]{2,1,0:T(8,128)(2,1)S(1)}, u32[]{:S(2)}, u32[]{:S(2)}) async-start(bf16[4,192,384]{2,1,0:T(8,128)(2,1)} %branch.1), calls=%async_computation.5 | async-start | bytes 1179648 | tf_op jit(solution)/shard_map/all_to_all | solution.py:256
  214.7 0.1 dynamic-slice_reduce_fusion.1
  214.8 31.3 %all-to-all-done.5 = bf16[4,192,384]{2,1,0:T(8,128)(2,1)S(1)} async-done(((bf16[4,192,384]{2,1,0:T(8,128)(2,1)}), bf16[4,192,384]{2,1,0:T(8,128)(2,1)S(1)}, u32[]{:S(2)}, u32[]{:S(2)}) %all-to-all-start.5) | async-done | bytes 589856 | tf_op jit(solution)/shard_map/all_to_all | solution.py:256
  246.1 0.1 convert_reduce_fusion
  246.2 0.0 copy-done.6
  246.2 0.7 add_convert_fusion.1
  (1 shorter events, 0.0 us)
Async XLA Ops:
  6.5 72.7 %copy-start = (f32[8,3,6144]{2,0,1:T(8,128)S(1)}, f32[8,3,6144]{2,0,1:T(8,128)}, u32[]{:S(2)}) copy-start(f32[8,3,6144]{2,0,1:T(8,128)} %param.15) | copy-start | bytes 1769476
  6.5 106.9 %all-gather.2.cloned.1.call-start = ((), (), s32[]{:S(2)}) async-start(), calls=%async_computation.6 | async-start | bytes 9732096 | tf_op jit(solution)/shard_map/all_gather | solution.py:164
  11.0 61.2 %all-to-all-start = ((bf16[4,192,384]{2,1,0:T(8,128)(2,1)}), bf16[4,192,384]{2,1,0:T(8,128)(2,1)S(1)}, u32[]{:S(2)}, u32[]{:S(2)}) async-start(bf16[4,192,384]{2,1,0:T(8,128)(2,1)} %broadcast_in_dim.10), calls=%async_computation | async-start | bytes 1179648 | tf_op jit(solution)/shard_map/all_to_all | solution.py:26
  31.0 21.4 %collective-permute-start = (bf16[4,256,384]{2,1,0:T(8,128)(2,1)}, bf16[4,256,384]{2,1,0:T(8,128)(2,1)S(1)}, u32[]{:S(2)}, u32[]{:S(2)}) collective-permute-start(bf16[4,256,384]{2,1,0:T(8,128)(2,1)} %get-tuple-element.17), channel_id=1, source_target_pairs={{0,1},{1,2},{2,3},{3,0},{4,5},{5,6},{6,7},{7,4},{8,9},{9,10},{10,1... | collective-permute-start | bytes 2359304 | tf_op jit(solution)/shard_map/ppermute | solution.py:183
  34.1 36.1 %collective-permute-start.1 = (bf16[4,256,384]{2,1,0:T(8,128)(2,1)}, bf16[4,256,384]{2,1,0:T(8,128)(2,1)S(1)}, u32[]{:S(2)}, u32[]{:S(2)}) collective-permute-start(bf16[4,256,384]{2,1,0:T(8,128)(2,1)} %get-tuple-element.18), channel_id=1, source_target_pairs={{0,2},{1,3},{2,0},{3,1},{4,6},{5,7},{6,4},{7,5},{8,10},{9,11},{10,... | collective-permute-start | bytes 2359304 | tf_op jit(solution)/shard_map/ppermute | solution.py:183
  38.5 33.7 %collective-permute-start.2 = (bf16[4,256,384]{2,1,0:T(8,128)(2,1)}, bf16[4,256,384]{2,1,0:T(8,128)(2,1)}, u32[]{:S(2)}, u32[]{:S(2)}) collective-permute-start(bf16[4,256,384]{2,1,0:T(8,128)(2,1)} %get-tuple-element.19), channel_id=1, source_target_pairs={{0,3},{1,0},{2,1},{3,2},{4,7},{5,4},{6,5},{7,6},{8,11},{9,8},{10,9... | collective-permute-start | bytes 2359304 | tf_op jit(solution)/shard_map/ppermute | solution.py:183
  52.4 17.8 %copy-start.3 = (bf16[4,256,384]{2,1,0:T(8,128)(2,1)}, bf16[4,256,384]{2,1,0:T(8,128)(2,1)S(1)}, u32[]{:S(2)}) copy-start(bf16[4,256,384]{2,1,0:T(8,128)(2,1)S(1)} %collective-permute-done.w1) | copy-start | bytes 2359300
  70.2 0.9 copy-start.4
  73.9 32.7 %all-to-all-start.1 = ((bf16[4,4,192,384]{3,2,1,0:T(8,128)(2,1)}), bf16[4,4,192,384]{3,2,1,0:T(8,128)(2,1)S(1)}, u32[]{:S(2)}, u32[]{:S(2)}) async-start(bf16[4,4,192,384]{3,2,1,0:T(8,128)(2,1)} %broadcast_in_dim.11), calls=%async_computation.1 | async-start | bytes 4718592 | tf_op jit(solution)/shard_map/all_to_all | solution.py:26
  106.6 1.5 copy-start.1
  120.5 11.5 %copy-start.5 = (bf16[3,192,128]{2,1,0:T(8,128)(2,1)S(1)}, bf16[3,192,128]{2,1,0:T(8,128)(2,1)}, u32[]{:S(2)}) copy-start(bf16[3,192,128]{2,1,0:T(8,128)(2,1)} %get-tuple-element.21) | copy-start | bytes 442372
  120.5 5.3 %collective-permute-start.3 = (bf16[3,192,128]{2,1,0:T(8,128)(2,1)}, bf16[3,192,128]{2,1,0:T(8,128)(2,1)S(1)}, u32[]{:S(2)}, u32[]{:S(2)}) collective-permute-start(bf16[3,192,128]{2,1,0:T(8,128)(2,1)} %get-tuple-element.22), channel_id=1, source_target_pairs={{0,16},{16,0},{1,17},{17,1},{2,18},{18,2},{3,19},{19,3},{4,20},{20... | collective-permute-start | bytes 442376 | tf_op jit(solution)/shard_map/ppermute | solution.py:214
  127.8 15.9 %all-to-all-start.3 = ((bf16[4,2,2,192,128]{4,3,2,1,0:T(8,128)(2,1)}), bf16[4,2,2,192,128]{4,3,2,1,0:T(8,128)(2,1)S(1)}, u32[]{:S(2)}, u32[]{:S(2)}) async-start(bf16[4,2,2,192,128]{4,3,2,1,0:T(8,128)(2,1)} %broadcast_in_dim.14), calls=%async_computation.3 | async-start | bytes 1572864 | tf_op jit(solution)/shard_map/all_to_all | solution.py:26
  143.7 13.5 %copy-start.2 = (bf16[4,2,2,192,128]{4,3,2,1,0:T(8,128)(2,1)}, bf16[4,2,2,192,128]{4,3,2,1,0:T(8,128)(2,1)S(1)}, u32[]{:S(2)}) copy-start(bf16[4,2,2,192,128]{4,3,2,1,0:T(8,128)(2,1)S(1)} %all-to-all-done.3.kv_ref) | copy-start | bytes 2359300
  185.7 60.4 %copy-start.6 = (bf16[192,384]{1,0:T(8,128)(2,1)S(1)}, bf16[192,384]{1,0:T(8,128)(2,1)}, u32[]{:S(2)}) copy-start(bf16[192,384]{1,0:T(8,128)(2,1)} %param.9) | copy-start | bytes 442372
  185.7 8.9 %collective-permute-start.4 = (bf16[192,256]{1,0:T(8,128)(2,1)}, bf16[192,256]{1,0:T(8,128)(2,1)S(1)}, u32[]{:S(2)}, u32[]{:S(2)}) collective-permute-start(bf16[192,256]{1,0:T(8,128)(2,1)} %combine.1.a0), channel_id=1, source_target_pairs={{0,1},{1,2},{2,3},{3,0},{4,5},{5,6},{6,7},{7,4},{8,9},{9,10},{10,1... | collective-permute-start | bytes 294920 | tf_op jit(solution)/shard_map/ppermute | solution.py:246
  188.1 7.1 %collective-permute-start.5 = (bf16[192,256]{1,0:T(8,128)(2,1)}, bf16[192,256]{1,0:T(8,128)(2,1)S(1)}, u32[]{:S(2)}, u32[]{:S(2)}) collective-permute-start(bf16[192,256]{1,0:T(8,128)(2,1)} %combine.1.a0), channel_id=1, source_target_pairs={{0,2},{1,3},{2,0},{3,1},{4,6},{5,7},{6,4},{7,5},{8,10},{9,11},{10,... | collective-permute-start | bytes 294920 | tf_op jit(solution)/shard_map/ppermute | solution.py:246
  192.4 5.6 %collective-permute-start.6 = (bf16[192,256]{1,0:T(8,128)(2,1)}, bf16[192,256]{1,0:T(8,128)(2,1)S(1)}, u32[]{:S(2)}, u32[]{:S(2)}) collective-permute-start(bf16[192,256]{1,0:T(8,128)(2,1)} %combine.1.a0), channel_id=1, source_target_pairs={{0,3},{1,0},{2,1},{3,2},{4,7},{5,4},{6,5},{7,6},{8,11},{9,8},{10,9... | collective-permute-start | bytes 294920 | tf_op jit(solution)/shard_map/ppermute | solution.py:246
  194.6 3.4 %copy-start.7 = (bf16[192,256]{1,0:T(8,128)(2,1)}, bf16[192,256]{1,0:T(8,128)(2,1)S(1)}, u32[]{:S(2)}) copy-start(bf16[192,256]{1,0:T(8,128)(2,1)S(1)} %collective-permute-done.4.a1) | copy-start | bytes 294916
  195.1 2.8 %copy-start.8 = (bf16[192,256]{1,0:T(8,128)(2,1)}, bf16[192,256]{1,0:T(8,128)(2,1)S(1)}, u32[]{:S(2)}) copy-start(bf16[192,256]{1,0:T(8,128)(2,1)S(1)} %collective-permute-done.5.a2) | copy-start | bytes 294916
  198.0 0.6 copy-start.9
  203.3 42.8 %all-to-all-start.5 = ((bf16[4,192,384]{2,1,0:T(8,128)(2,1)}), bf16[4,192,384]{2,1,0:T(8,128)(2,1)S(1)}, u32[]{:S(2)}, u32[]{:S(2)}) async-start(bf16[4,192,384]{2,1,0:T(8,128)(2,1)} %branch.1), calls=%async_computation.5 | async-start | bytes 1179648 | tf_op jit(solution)/shard_map/all_to_all | solution.py:256
Sparse Core Ops, SparseCore 0:
  9.5 99.6 all-gather.1

commit v4 on v3

v4 whole, which is shorter than its diff:
```python
import math

import jax
import jax.numpy as jnp
from jax import lax
from jax.experimental import pallas as pl
from jax.experimental.pallas import tpu as pltpu
from jax.sharding import Mesh
from jax.sharding import PartitionSpec as P

D = 6144
HD = 128
GRID = 4
BF = jnp.bfloat16
F32 = jnp.float32
LOG2E = 1.4426950408889634
TOKENS = ("y", "zl", "core")


def shift(amount):
    return [(i, (i + amount) % GRID) for i in range(GRID)]


def gather_small(shard, axis_name):
    spread = jnp.broadcast_to(shard[None], (GRID,) + shard.shape)
    return lax.all_to_all(spread, axis_name, 0, 0, tiled=True)


def average_kernel(step_ref, ema_ref, train_ref, out_ref):
    stepped = jnp.full((1, HD), step_ref[0], jnp.int32).astype(F32)
    decay = (1.0 + stepped) / (10.0 + stepped)
    for h in range(2):
        for j in range(3):
            part = slice(h * HD, (h + 1) * HD)
            ema = ema_ref[j, :, part].astype(F32)
            train = train_ref[j, :, part].astype(F32)
            out_ref[h, :, j * HD : (j + 1) * HD] = (decay * ema + (1.0 - decay) * train).astype(BF)


def norm_kernel(order_ref, raw_ref, mod_ref, out_ref):
    blocks = [(s, k) for s in range(GRID) for k in range(GRID)]
    rows, width = raw_ref.shape[2], raw_ref.shape[3]
    total = jnp.zeros((rows, width), F32)
    for s, k in blocks:
        total = total + raw_ref[s, k].astype(F32)
    average = jnp.sum(total, axis=1, keepdims=True) * (1.0 / D)
    squares = jnp.zeros((rows, width), F32)
    for s, k in blocks:
        centred = raw_ref[s, k].astype(F32) - average
        squares = squares + centred * centred
    variance = jnp.sum(squares, axis=1, keepdims=True) * (1.0 / D)
    inverse = lax.rsqrt(variance + 1e-06)
    for s, k in blocks:
        h = order_ref[k]
        centred = raw_ref[s, k].astype(F32) - average
        scale = mod_ref[1, h, s : s + 1, :]
        move = mod_ref[0, h, s : s + 1, :]
        start = pl.multiple_of((h * GRID + s) * width, HD)
        out_ref[:, pl.ds(start, width)] = (
            centred * inverse * (1.0 + scale) + move
        ).astype(BF)


def pick_kernel(place_ref, *refs):
    for source, target in zip(refs[:GRID], refs[GRID:]):
        target[0] = source[...]


def project_kernel(core_ref, own_ref, other_ref, weight_ref, q_gain_ref, k_gain_ref, q_ref, kv_ref, acc_ref):
    step = pl.program_id(0)

    @pl.when(step == 0)
    def _():
        acc_ref[...] = jnp.zeros_like(acc_ref)

    for t, hidden_ref in enumerate((own_ref, other_ref)):
        acc_ref[t] += jnp.dot(hidden_ref[...], weight_ref[0], preferred_element_type=F32)

    @pl.when(step == pl.num_programs(0) - 1)
    def _():
        for t in range(2):
            for j, gain_ref in ((0, q_gain_ref), (1, k_gain_ref)):
                values = acc_ref[t, :, j * HD : (j + 1) * HD]
                squares = jnp.mean(values * values, axis=1, keepdims=True)
                normed = (values * lax.rsqrt(squares + 1e-06) * gain_ref[...]).astype(BF)
                if j == 0:
                    q_ref[t] = normed
                else:
                    kv_ref[0, t] = normed
            kv_ref[1, t] = acc_ref[t, :, 2 * HD :].astype(BF)


def attend_kernel(place_ref, q_ref, kv0, kv1, kv2, kv3, out_ref, k_all, v_all):
    rows = q_ref.shape[2]
    blocks = 2 * GRID

    @pl.when(pl.program_id(0) == 0)
    def _():
        for g, kv_ref in enumerate((kv0, kv1, kv2, kv3)):
            for t in range(2):
                part = slice((2 * g + t) * rows, (2 * g + t + 1) * rows)
                k_all[part, :] = kv_ref[0, t]
                v_all[part, :HD] = kv_ref[1, t]
        v_all[:, HD:] = jnp.ones((blocks * rows, HD), BF)

    chunk = 512
    both = jnp.zeros((rows, 2 * HD), F32)
    for c in range(blocks * rows // chunk):
        part = slice(c * chunk, (c + 1) * chunk)
        scores = lax.dot_general(
            q_ref[0, 0], k_all[part, :], (((1,), (1,)), ((), ())), preferred_element_type=F32
        )
        weights = jnp.exp2(scores * (LOG2E / math.sqrt(HD))).astype(BF)
        both = both + jnp.dot(weights, v_all[part, :], preferred_element_type=F32)
    out_ref[0, :rows, :] = both[:, :HD].astype(BF)
    totals = both[:, HD:]
    lane = lax.broadcasted_iota(jnp.int32, (HD, HD), 1)
    line = lax.broadcasted_iota(jnp.int32, (HD, HD), 0)
    first = jnp.sum(jnp.where(lane == line, totals[:HD], 0.0), axis=0, keepdims=True)
    rest = rows - HD
    second = jnp.sum(
        jnp.where(lane[:rest] == line[:rest], totals[HD:], 0.0), axis=0, keepdims=True
    )
    sub = lax.broadcasted_iota(jnp.int32, (16, HD), 0)
    first_high = first.astype(BF).astype(F32)
    second_high = second.astype(BF).astype(F32)
    packed = jnp.where(sub == 0, first_high, 0.0)
    packed = jnp.where(sub == 1, second_high, packed)
    packed = jnp.where(sub == 2, first - first_high, packed)
    packed = jnp.where(sub == 3, second - second_high, packed)
    out_ref[0, rows:, :] = packed.astype(BF)


def combine_kernel(parts_ref, out_ref):
    rows = out_ref.shape[0]
    lane = lax.broadcasted_iota(jnp.int32, (HD, HD), 1)
    line = lax.broadcasted_iota(jnp.int32, (HD, HD), 0)
    rest = rows - HD
    for h in range(2):
        numer = jnp.zeros((rows, HD), F32)
        packed = jnp.zeros((16, HD), F32)
        for g in range(GRID):
            numer = numer + parts_ref[2 * g + h, :rows, :].astype(F32)
            packed = packed + parts_ref[2 * g + h, rows:, :].astype(F32)
        first = packed[0:1] + packed[2:3]
        second = packed[1:2] + packed[3:4]
        first = jnp.sum(jnp.where(lane == line, first, 0.0), axis=1, keepdims=True)
        second = jnp.sum(
            jnp.where(lane[:rest] == line[:rest], second, 0.0), axis=1, keepdims=True
        )
        part = slice(h * HD, (h + 1) * HD)
        out_ref[:HD, part] = (numer[:HD] / first).astype(BF)
        out_ref[HD:, part] = (numer[HD:] / second).astype(BF)


def branch_kernel(place_ref, a0, a1, a2, a3, w0, w1, w2, w3, out_ref):
    total = jnp.dot(a0[...], w0[0], preferred_element_type=F32)
    for a, w in ((a1, w1), (a2, w2), (a3, w3)):
        total = total + jnp.dot(a[...], w[0], preferred_element_type=F32)
    out_ref[...] = total.astype(BF)


def per_device(latents, train_qkv, ema_qkv, q_gain, k_gain, out_weight, modulation, timestep, step):
    rows, width = latents.shape
    channels = ema_qkv.shape[2]
    blocks = GRID * GRID
    by_head = pl.pallas_call(
        average_kernel,
        in_specs=[
            pl.BlockSpec(memory_space=pltpu.SMEM),
            pl.BlockSpec(memory_space=pltpu.VMEM),
            pl.BlockSpec(memory_space=pltpu.VMEM),
        ],
        out_specs=pl.BlockSpec(memory_space=pltpu.VMEM),
        out_shape=jax.ShapeDtypeStruct((2, rows, 3 * HD), BF),
        name="average",
    )(step, ema_qkv, train_qkv)
    full_weights = lax.all_gather(by_head, TOKENS, axis=1, tiled=True)

    place = jnp.stack(
        [lax.axis_index(name).astype(jnp.int32) for name in ("core", "zl", "head", "seq")]
    )

    def column(k):
        return lambda i, place: (0, i * GRID + lax.rem(place[3] + k, GRID))

    out_parts = pl.pallas_call(
        pick_kernel,
        grid_spec=pltpu.PrefetchScalarGridSpec(
            num_scalar_prefetch=1,
            grid=(GRID,),
            in_specs=[pl.BlockSpec((channels, width), column(k)) for k in range(GRID)],
            out_specs=[pl.BlockSpec((1, channels, width), lambda i, place: (i, 0, 0))] * GRID,
        ),
        out_shape=[jax.ShapeDtypeStruct((GRID, channels, width), BF)] * GRID,
        name="pick",
    )(place, *([out_weight] * GRID))

    mod_row = lax.dynamic_index_in_dim(modulation, timestep[0], 0, keepdims=False)
    half = rows // 2
    before = lax.ppermute(latents, "head", shift(1))
    after = lax.ppermute(latents, "head", shift(3))
    far = jnp.concatenate(
        [
            lax.ppermute(before[:half], "head", shift(1)),
            lax.ppermute(after[half:], "head", shift(3)),
        ]
    )
    raw = jnp.stack([latents, before, far, after])
    raw = gather_small(raw, "seq").reshape(GRID, GRID, rows, width)
    raw, *out_parts = lax.optimization_barrier((raw, *out_parts))
    out_parts = [out_parts[0]] + [lax.ppermute(out_parts[k], "seq", shift(k)) for k in (1, 2, 3)]
    head_order = lax.rem(place[2] + GRID - jnp.arange(GRID, dtype=jnp.int32), GRID)
    by_place = mod_row.reshape(3, GRID, GRID, width)
    hidden = pl.pallas_call(
        norm_kernel,
        grid_spec=pltpu.PrefetchScalarGridSpec(
            num_scalar_prefetch=1,
            grid=(1,),
            in_specs=[
                pl.BlockSpec((GRID, GRID, rows, width), lambda i, order: (0, 0, 0, 0)),
                pl.BlockSpec((3, GRID, GRID, width), lambda i, order: (0, 0, 0, 0)),
            ],
            out_specs=pl.BlockSpec((rows, blocks * width), lambda i, order: (0, 0)),
        ),
        out_shape=jax.ShapeDtypeStruct((rows, blocks * width), BF),
        name="norm",
    )(head_order, raw, by_place)
    sibling = lax.ppermute(hidden, "core", [(0, 1), (1, 0)])

    depth = D // GRID
    queries, pairs = pl.pallas_call(
        project_kernel,
        grid_spec=pltpu.PrefetchScalarGridSpec(
            num_scalar_prefetch=1,
            grid=(GRID,),
            in_specs=[
                pl.BlockSpec((rows, depth), lambda i, place: (0, i)),
                pl.BlockSpec((rows, depth), lambda i, place: (0, i)),
                pl.BlockSpec((1, depth, 3 * HD), lambda i, place: (place[0], i, 0)),
                pl.BlockSpec((1, HD), lambda i, place: (0, 0)),
                pl.BlockSpec((1, HD), lambda i, place: (0, 0)),
            ],
            out_specs=[
                pl.BlockSpec((2, rows, HD), lambda i, place: (0, 0, 0)),
                pl.BlockSpec((2, 2, rows, HD), lambda i, place: (0, 0, 0, 0)),
            ],
            scratch_shapes=[pltpu.VMEM((2, rows, 3 * HD), F32)],
        ),
        out_shape=[
            jax.ShapeDtypeStruct((2, rows, HD), BF),
            jax.ShapeDtypeStruct((2, 2, rows, HD), BF),
        ],
        name="project",
    )(place, hidden, sibling, full_weights, q_gain.reshape(1, HD), k_gain.reshape(1, HD))

    all_pairs = [pairs] + [lax.ppermute(pairs, "y", shift(k)) for k in (1, 3, 2)]
    queries = jnp.stack([queries] + [lax.ppermute(queries, "zl", shift(k)) for k in (1, 2, 3)])

    sent = rows + 16
    parts = pl.pallas_call(
        attend_kernel,
        grid_spec=pltpu.PrefetchScalarGridSpec(
            num_scalar_prefetch=1,
            grid=(2 * GRID,),
            in_specs=[
                pl.BlockSpec(
                    (1, 1, rows, HD),
                    lambda i, place: (
                        lax.rem(place[1] + GRID - i // 2, GRID),
                        lax.rem(i + place[0], 2),
                        0,
                        0,
                    ),
                ),
            ]
            + [pl.BlockSpec((2, 2, rows, HD), lambda i, place: (0, 0, 0, 0))] * GRID,
            out_specs=pl.BlockSpec((1, sent, HD), lambda i, place: (i, 0, 0)),
            scratch_shapes=[
                pltpu.VMEM((2 * GRID * rows, HD), BF),
                pltpu.VMEM((2 * GRID * rows, 2 * HD), BF),
            ],
        ),
        out_shape=jax.ShapeDtypeStruct((2 * GRID, sent, HD), BF),
        name="attend",
    )(place, queries, *all_pairs)
    parts, *out_parts = lax.optimization_barrier((parts, *out_parts))
    parts = lax.all_to_all(parts, ("zl", "core"), 0, 0, tiled=True)
    attended = pl.pallas_call(
        combine_kernel,
        out_shape=jax.ShapeDtypeStruct((rows, channels), BF),
        name="combine",
    )(parts)

    around = [attended] + [lax.ppermute(attended, "seq", shift(k)) for k in (1, 2, 3)]

    def branch_for(k):
        return pl.pallas_call(
            branch_kernel,
            grid_spec=pltpu.PrefetchScalarGridSpec(
                num_scalar_prefetch=1,
                grid=(1,),
                in_specs=[pl.BlockSpec((rows, channels), lambda i, place: (0, 0))] * GRID
                + [
                    pl.BlockSpec(
                        (1, channels, width), lambda i, place: (lax.rem(place[2] + k, GRID), 0, 0)
                    )
                ]
                * GRID,
                out_specs=pl.BlockSpec((rows, width), lambda i, place: (0, 0)),
            ),
            out_shape=jax.ShapeDtypeStruct((rows, width), BF),
            name="branch",
        )(place, *around, *out_parts)

    shares = [lax.ppermute(branch_for(k), "head", shift(k)) for k in (2, 1, 3)]
    summed = branch_for(0).astype(F32)
    for share in shares:
        summed = summed + share.astype(F32)
    position = lax.axis_index(("head", "seq")) * width
    gate = lax.dynamic_slice_in_dim(mod_row[2], position, width, 0)
    return (latents.astype(F32) + gate[None, :] * summed).astype(BF)


def solution(mesh):
    fine = Mesh(
        mesh.devices.reshape(GRID, GRID, 2, GRID, GRID), ("y", "zl", "core", "head", "seq")
    )
    in_specs = (
        P(TOKENS, ("head", "seq")),
        P(None, TOKENS, ("head", "seq")),
        P(None, TOKENS, ("head", "seq")),
        P(),
        P(),
        P(("head", "seq"), None),
        P(),
        P(),
        P(),
    )
    out_specs = P(TOKENS, ("head", "seq"))
    return jax.shard_map(
        per_device, mesh=fine, in_specs=in_specs, out_specs=out_specs, check_vma=False
    )
```

time: 257 us -> 242 us (0.942)
  waiting for transfers between devices: 104 us -> 45.5 us
  starting transfers between devices: 59.4 us -> 105 us
  blocking collectives: 32.1 us -> 20.2 us
  Pallas kernels: 31.4 us -> 43.3 us
  local copies, waits for them, and re-layouts: 8.56 us -> 5.53 us
    ppermute x1 -> x14, starting transfers between devices: 4.11 us -> 82.4 us  [the longest x3 17.8 us: per_device(): shares = [lax.ppermute(branch_for(k), 'head', shift(k)) for k in (2, 1, 3)]]
    all_to_all x1 -> x0, waiting for transfers between devices: 31.3 us -> none  [per_device(): branch = lax.all_to_all(branch, 'head', 0, 0, tiled=True)]
    ppermute x3, waiting for transfers between devices: 29.7 us -> 0.01 us  [per_device(): lax.ppermute(out_parts[k], 'seq', shift(k))]
    ppermute x1 -> x14, waiting for transfers between devices: 1.2 us -> 26.9 us  [the longest x3 12.6 us: per_device(): shares = [lax.ppermute(branch_for(k), 'head', shift(k)) for k in (2, 1, 3)]]
    all_to_all x3 -> x1, waiting for transfers between devices: 38.2 us -> 16.7 us  [gather_small(): return lax.all_to_all(spread, axis_name, 0, 0, tiled=True)]
    all_to_all x3 -> x1, starting transfers between devices: 24.5 us -> 4.03 us  [gather_small(): return lax.all_to_all(spread, axis_name, 0, 0, tiled=True)]
    all_to_all x1 -> x0, blocking collectives: 13.5 us -> none  [gather_small(): return lax.all_to_all(spread, axis_name, 0, 0, tiled=True)]
    all_to_all x1 -> x0, starting transfers between devices: 11.4 us -> none  [per_device(): branch = lax.all_to_all(branch, 'head', 0, 0, tiled=True)]
  transfers between devices with their start and end apart: 12 -> 22, of which waited for: 9 -> 10; matrix products, arithmetic and copies ran while one was open for 2% -> 3% of each run, Pallas kernels for 4% -> 15%
where the time goes in v4:
time: 242 us; the launch traced here: 240 us
  starting transfers between devices  105 us (43%)
  waiting for transfers between devices  45.5 us (19%)
  Pallas kernels  43.3 us (18%)
  blocking collectives  20.2 us (8%)
  between operations  15.1 us (6%)
  local copies, waits for them, and re-layouts  5.53 us (2%)
  other arithmetic  5.52 us (2%)
    all_to_all x1, blocking collectives, per_device(): parts = lax.all_to_all(parts, ('zl', 'core'), 0, 0, tiled=True)  20.2 us
    ppermute x3, starting transfers between devices, per_device(): shares = [lax.ppermute(branch_for(k), 'head', shift(k)) for k in (2, 1, 3)]  17.8 us
    all_to_all x1, waiting for transfers between devices, gather_small(): return lax.all_to_all(spread, axis_name, 0, 0, tiled=True)  16.7 us
    ppermute x1, starting transfers between devices, per_device(): lax.ppermute(before[:half], 'head', shift(1))  15.1 us
    ppermute x3, waiting for transfers between devices, per_device(): shares = [lax.ppermute(branch_for(k), 'head', shift(k)) for k in (2, 1, 3)]  12.6 us
    ppermute x3, starting transfers between devices, per_device(): lax.ppermute(pairs, 'y', shift(k))  12.3 us
    pallas_call x4, Pallas kernels, branch_for(): pl.pallas_call(branch_kernel, grid_spec=pltpu.PrefetchScalarGridSpec(num_...  12.1 us
    ppermute x3, starting transfers between devices, per_device(): lax.ppermute(queries, 'zl', shift(k))  11.2 us
  transfers between devices with their start and end apart: 22, of which 10 were waited for; matrix products, arithmetic and copies ran while one was open for 3% of the time, Pallas kernels for 15%

profile of v4, /device:TPU:1, one launch (start us, length us, event | category | flops | bytes accessed | tf_op | source)
XLA Modules:
  0.0 240.4 jit_solution(992550030617427385)
XLA Ops:
  7.3 1.9 average.1
  9.1 0.0 all-gather.2.cloned.1.call-update
  9.2 9.6 %collective-permute-start = (bf16[192,384]{1,0:T(8,128)(2,1)}, bf16[192,384]{1,0:T(8,128)(2,1)S(1)}, u32[]{:S(2)}, u32[]{:S(2)}) collective-permute-start(bf16[192,384]{1,0:T(8,128)(2,1)} %param.9), channel_id=1, source_target_pairs={{0,4},{4,8},{8,12},{12,0},{1,5},{5,9},{9,13},{13,1},{2,6},{6,10},{... | collective-permute-start | bytes 442376 | tf_op jit(solution)/shard_map/ppermute | solution.py:201
  18.8 5.6 %collective-permute-start.2 = (bf16[192,384]{1,0:T(8,128)(2,1)}, bf16[192,384]{1,0:T(8,128)(2,1)S(1)}, u32[]{:S(2)}, u32[]{:S(2)}) collective-permute-start(bf16[192,384]{1,0:T(8,128)(2,1)} %param.9), channel_id=1, source_target_pairs={{0,12},{4,0},{8,4},{12,8},{1,13},{5,1},{9,5},{13,9},{2,14},{6,2},{... | collective-permute-start | bytes 442376 | tf_op jit(solution)/shard_map/ppermute | solution.py:202
  24.4 1.5 collective-permute-done
  25.9 15.1 %collective-permute-start.1 = (bf16[96,384]{1,0:T(8,128)(2,1)S(1)}, bf16[96,384]{1,0:T(8,128)(2,1)S(1)}, u32[]{:S(2)}, u32[]{:S(2)}) collective-permute-start(bf16[96,384]{1,0:T(8,128)(2,1)S(1)} %slice.13), channel_id=1, source_target_pairs={{0,4},{4,8},{8,12},{12,0},{1,5},{5,9},{9,13},{13,1},{2,6},{6,10},{... | collective-permute-start | bytes 221192 | tf_op jit(solution)/shard_map/ppermute | solution.py:205
  40.9 0.0 collective-permute-done.2
  41.0 3.3 %collective-permute-start.3 = (bf16[96,384]{1,0:T(8,128)(2,1)S(1)}, bf16[96,384]{1,0:T(8,128)(2,1)S(1)}, u32[]{:S(2)}, u32[]{:S(2)}) collective-permute-start(bf16[96,384]{1,0:T(8,128)(2,1)S(1)} %slice.14), channel_id=1, source_target_pairs={{0,12},{4,0},{8,4},{12,8},{1,13},{5,1},{9,5},{13,9},{2,14},{6,2},{... | collective-permute-start | bytes 221192 | tf_op jit(solution)/shard_map/ppermute | solution.py:206
  44.3 2.2 collective-permute-done.1
  46.5 4.7 %collective-permute-done.3 = bf16[96,384]{1,0:T(8,128)(2,1)S(1)} collective-permute-done((bf16[96,384]{1,0:T(8,128)(2,1)S(1)}, bf16[96,384]{1,0:T(8,128)(2,1)S(1)}, u32[]{:S(2)}, u32[]{:S(2)}) %collective-permute-start.3) | collective-permute-done | bytes 73760 | tf_op jit(solution)/shard_map/ppermute | solution.py:206
  51.3 1.0 pad_maximum_fusion
  52.3 1.7 broadcast_in_dim.2
  54.0 4.0 %all-to-all-start = ((bf16[4,4,192,384]{3,2,1,0:T(8,128)(2,1)}), bf16[4,4,192,384]{3,2,1,0:T(8,128)(2,1)S(1)}, u32[]{:S(2)}, u32[]{:S(2)}) async-start(bf16[4,4,192,384]{3,2,1,0:T(8,128)(2,1)} %broadcast_in_dim.2), calls=%async_computation | async-start | bytes 4718592 | tf_op jit(solution)/shard_map/all_to_all | solution.py:26
  58.7 0.2 dynamic-slice_reduce_fusion
  58.9 0.7 reshape.16.mod_ref
  59.6 0.6 pad_add_fusion.place_ref.core_ref
  60.2 5.1 %pick.1 = (bf16[4,256,384]{2,1,0:T(8,128)(2,1)}, bf16[4,256,384]{2,1,0:T(8,128)(2,1)}, bf16[4,256,384]{2,1,0:T(8,128)(2,1)}, bf16[4,256,384]{2,1,0:T(8,128)(2,1)}) custom-call(s32[4]{0:T(128)} %pad_add_fusion.place_ref.core_ref, bf16[256,6144]{1,0:T(8,128)(2,1)} %refs_3_.1, bf16[256,6144]{1,0:T(8,128)(2,1)} %refs_3_.1, bf16[256,6144]{1,0:T(8,128)(2,1)} %refs_3_.1, ...), custom_call_target="tpu_custom_call" | custom-call | tf_op jit(solution)/shard_map/pick/pallas_call | solution.py:187
  65.3 0.5 compare_select_fusion.order_ref
  65.8 16.7 %all-to-all-done.raw_ref = bf16[4,4,192,384]{3,2,1,0:T(8,128)(2,1)S(1)} async-done(((bf16[4,4,192,384]{3,2,1,0:T(8,128)(2,1)}), bf16[4,4,192,384]{3,2,1,0:T(8,128)(2,1)S(1)}, u32[]{:S(2)}, u32[]{:S(2)}) %all-to-all-start) | async-done | bytes 2359328 | tf_op jit(solution)/shard_map/all_to_all | solution.py:26
  82.5 1.4 copy-done.4
  84.0 6.0 %norm.1.own_ref = bf16[192,6144]{1,0:T(8,128)(2,1)} custom-call(s32[4]{0:T(128)} %compare_select_fusion.order_ref, bf16[4,4,192,384]{3,2,1,0:T(8,128)(2,1)} %copy-done.4, f32[3,4,4,384]{3,2,1,0:T(4,128)} %reshape.16.mod_ref), custom_call_target="tpu_custom_call" | custom-call | tf_op jit(solution)/shard_map/norm/pallas_call | solution.py:215
  90.0 7.5 %collective-permute-start.4 = (bf16[192,6144]{1,0:T(8,128)(2,1)}, bf16[192,6144]{1,0:T(8,128)(2,1)}, u32[]{:S(2)}, u32[]{:S(2)}) collective-permute-start(bf16[192,6144]{1,0:T(8,128)(2,1)} %norm.1.own_ref), channel_id=1, source_target_pairs={{0,16},{16,0},{1,17},{17,1},{2,18},{18,2},{3,19},{19,3},{4,20},{20... | collective-permute-start | bytes 7077896 | tf_op jit(solution)/shard_map/ppermute | solution.py:229
  97.5 2.2 collective-permute-start.11
  99.7 3.7 %collective-permute-start.12 = (bf16[4,256,384]{2,1,0:T(8,128)(2,1)}, bf16[4,256,384]{2,1,0:T(8,128)(2,1)S(1)}, u32[]{:S(2)}, u32[]{:S(2)}) collective-permute-start(bf16[4,256,384]{2,1,0:T(8,128)(2,1)} %get-tuple-element.30), channel_id=1, source_target_pairs={{0,2},{1,3},{2,0},{3,1},{4,6},{5,7},{6,4},{7,5},{8,10},{9,11},{10,... | collective-permute-start | bytes 2359304 | tf_op jit(solution)/shard_map/ppermute | solution.py:212
  103.4 2.5 %collective-permute-start.13 = (bf16[4,256,384]{2,1,0:T(8,128)(2,1)}, bf16[4,256,384]{2,1,0:T(8,128)(2,1)S(1)}, u32[]{:S(2)}, u32[]{:S(2)}) collective-permute-start(bf16[4,256,384]{2,1,0:T(8,128)(2,1)} %get-tuple-element.31), channel_id=1, source_target_pairs={{0,3},{1,0},{2,1},{3,2},{4,7},{5,4},{6,5},{7,6},{8,11},{9,8},{10,9... | collective-permute-start | bytes 2359304 | tf_op jit(solution)/shard_map/ppermute | solution.py:212
  105.9 0.0 collective-permute-done.4.other_ref
  105.9 0.0 all-gather.2.cloned.1.call-done.weight_ref
  106.0 7.5 %project.1 = (bf16[2,192,128]{2,1,0:T(8,128)(2,1)}, bf16[2,2,192,128]{3,2,1,0:T(8,128)(2,1)}) custom-call(s32[4]{0:T(128)} %pad_add_fusion.place_ref.core_ref, bf16[192,6144]{1,0:T(8,128)(2,1)} %norm.1.own_ref, bf16[192,6144]{1,0:T(8,128)(2,1)} %collective-permute-done.4.other_ref, bf16[2,6144,384]{2,1,0:T(8,128)(2,1)} %all-gather.2.cloned.1.call-done.weight_ref, ...), custom_call_target="tpu_custom_call" | custom-call | tf_op jit(solution)/shard_map/project/pallas_call | solution.py:232
  113.4 2.2 collective-permute-start.5
  115.6 7.1 %collective-permute-start.6 = (bf16[2,192,128]{2,1,0:T(8,128)(2,1)}, bf16[2,192,128]{2,1,0:T(8,128)(2,1)S(1)}, u32[]{:S(2)}, u32[]{:S(2)}) collective-permute-start(bf16[2,192,128]{2,1,0:T(8,128)(2,1)} %get-tuple-element.26), channel_id=1, source_target_pairs={{0,64},{32,96},{64,0},{96,32},{1,65},{33,97},{65,1},{97,33},{2,66}... | collective-permute-start | bytes 294920 | tf_op jit(solution)/shard_map/ppermute | solution.py:258
  122.7 0.6 collective-permute-done.5
  123.4 4.9 %collective-permute-start.10 = (bf16[2,2,192,128]{3,2,1,0:T(8,128)(2,1)}, bf16[2,2,192,128]{3,2,1,0:T(8,128)(2,1)S(1)}, u32[]{:S(2)}, u32[]{:S(2)}) collective-permute-start(bf16[2,2,192,128]{3,2,1,0:T(8,128)(2,1)} %get-tuple-element.27.kv0), channel_id=1, source_target_pairs={{0,256},{128,384},{256,0},{384,128},{1,257},{129,385},{257,1},{385... | collective-permute-start | bytes 589832 | tf_op jit(solution)/shard_map/ppermute | solution.py:257
  128.3 0.0 collective-permute-done.6
  128.3 1.9 collective-permute-start.7
  130.2 3.9 %collective-permute-done.7 = bf16[2,192,128]{2,1,0:T(8,128)(2,1)S(1)} collective-permute-done((bf16[2,192,128]{2,1,0:T(8,128)(2,1)}, bf16[2,192,128]{2,1,0:T(8,128)(2,1)S(1)}, u32[]{:S(2)}, u32[]{:S(2)}) %collective-permute-start.7) | collective-permute-done | bytes 98336 | tf_op jit(solution)/shard_map/ppermute | solution.py:258
  134.2 3.0 %collective-permute-start.8 = (bf16[2,2,192,128]{3,2,1,0:T(8,128)(2,1)}, bf16[2,2,192,128]{3,2,1,0:T(8,128)(2,1)S(1)}, u32[]{:S(2)}, u32[]{:S(2)}) collective-permute-start(bf16[2,2,192,128]{3,2,1,0:T(8,128)(2,1)} %get-tuple-element.27.kv0), channel_id=1, source_target_pairs={{0,128},{128,256},{256,384},{384,0},{1,129},{129,257},{257,385},{3... | collective-permute-start | bytes 589832 | tf_op jit(solution)/shard_map/ppermute | solution.py:257
  137.2 0.0 collective-permute-done.10.kv3
  137.2 4.4 %collective-permute-start.9 = (bf16[2,2,192,128]{3,2,1,0:T(8,128)(2,1)}, bf16[2,2,192,128]{3,2,1,0:T(8,128)(2,1)S(1)}, u32[]{:S(2)}, u32[]{:S(2)}) collective-permute-start(bf16[2,2,192,128]{3,2,1,0:T(8,128)(2,1)} %get-tuple-element.27.kv0), channel_id=1, source_target_pairs={{0,384},{128,0},{256,128},{384,256},{1,385},{129,1},{257,129},{385... | collective-permute-start | bytes 589832 | tf_op jit(solution)/shard_map/ppermute | solution.py:257
  141.6 1.7 pad_maximum_fusion.1.q_ref
  143.3 0.0 collective-permute-done.8.kv1
  143.3 1.3 collective-permute-done.9.kv2
  144.6 0.7 copy-done.11
  145.3 8.9 %attend.1 = bf16[8,208,128]{2,1,0:T(8,128)(2,1)} custom-call(s32[4]{0:T(128)} %pad_add_fusion.place_ref.core_ref, bf16[4,2,192,128]{3,2,1,0:T(8,128)(2,1)} %pad_maximum_fusion.1.q_ref, bf16[2,2,192,128]{3,2,1,0:T(8,128)(2,1)} %get-tuple-element.27.kv0, bf16[2,2,192,128]{3,2,1,0:T(8,128)(2,1)} %copy-done.10, bf16[2,2,192,128]{3,2,1,0:T(8,128)(2,1)} %copy-done.11, ...), custom_call_target="tpu_custom_call" | custom-call | tf_op jit(solution)/shard_map/attend/pallas_call | solution.py:261
  154.1 0.0 collective-permute-done.11.w1
  154.1 0.0 collective-permute-done.13.w3
  154.2 20.2 %all_to_all.10.parts_ref = bf16[8,208,128]{2,1,0:T(8,128)(2,1)} all-to-all(bf16[8,208,128]{2,1,0:T(8,128)(2,1)} %attend.1), channel_id=1, replica_groups=mesh['y'=4,'zl'=4,'core'=2,'head'=4,'seq'=4] {'zl','core'}, dimensions={0} | all-to-all | bytes 851968 | tf_op jit(solution)/shard_map/all_to_all | solution.py:288
  174.4 1.8 combine.1.a0
  176.2 3.0 %collective-permute-start.14 = (bf16[192,256]{1,0:T(8,128)(2,1)}, bf16[192,256]{1,0:T(8,128)(2,1)S(1)}, u32[]{:S(2)}, u32[]{:S(2)}) collective-permute-start(bf16[192,256]{1,0:T(8,128)(2,1)} %combine.1.a0), channel_id=1, source_target_pairs={{0,1},{1,2},{2,3},{3,0},{4,5},{5,6},{6,7},{7,4},{8,9},{9,10},{10,1... | collective-permute-start | bytes 294920 | tf_op jit(solution)/shard_map/ppermute | solution.py:295
  179.2 3.4 %collective-permute-start.15 = (bf16[192,256]{1,0:T(8,128)(2,1)}, bf16[192,256]{1,0:T(8,128)(2,1)S(1)}, u32[]{:S(2)}, u32[]{:S(2)}) collective-permute-start(bf16[192,256]{1,0:T(8,128)(2,1)} %combine.1.a0), channel_id=1, source_target_pairs={{0,2},{1,3},{2,0},{3,1},{4,6},{5,7},{6,4},{7,5},{8,10},{9,11},{10,... | collective-permute-start | bytes 294920 | tf_op jit(solution)/shard_map/ppermute | solution.py:295
  182.6 4.0 %collective-permute-start.16 = (bf16[192,256]{1,0:T(8,128)(2,1)}, bf16[192,256]{1,0:T(8,128)(2,1)S(1)}, u32[]{:S(2)}, u32[]{:S(2)}) collective-permute-start(bf16[192,256]{1,0:T(8,128)(2,1)} %combine.1.a0), channel_id=1, source_target_pairs={{0,3},{1,0},{2,1},{3,2},{4,7},{5,4},{6,5},{7,6},{8,11},{9,8},{10,9... | collective-permute-start | bytes 294920 | tf_op jit(solution)/shard_map/ppermute | solution.py:295
  186.6 0.0 collective-permute-done.15.a2
  186.6 1.9 collective-permute-done.16.a3
  188.5 0.6 copy-done.7
  189.2 3.0 %branch.5 = bf16[192,384]{1,0:T(8,128)(2,1)} custom-call(s32[4]{0:T(128)} %pad_add_fusion.place_ref.core_ref, bf16[192,256]{1,0:T(8,128)(2,1)} %combine.1.a0, bf16[192,256]{1,0:T(8,128)(2,1)} %copy-done.5, bf16[192,256]{1,0:T(8,128)(2,1)} %copy-done.6, bf16[192,256]{1,0:T(8,128)(2,1)} %copy-done.7, bf16[4,256,384]{2,1,0:T(8,128)(2,1)} %get-tuple-element.33.w0, ...), custom_call_target="tpu_custom_call" | custom-call | tf_op jit(solution)/shard_map/branch/pallas_call | solution.py:298
  192.2 8.5 %collective-permute-start.17 = (bf16[192,384]{1,0:T(8,128)(2,1)}, bf16[192,384]{1,0:T(8,128)(2,1)S(1)}, u32[]{:S(2)}, u32[]{:S(2)}) collective-permute-start(bf16[192,384]{1,0:T(8,128)(2,1)} %branch.5), channel_id=1, source_target_pairs={{0,8},{4,12},{8,0},{12,4},{1,9},{5,13},{9,1},{13,5},{2,10},{6,14},... | collective-permute-start | bytes 442376 | tf_op jit(solution)/shard_map/ppermute | solution.py:316
  200.8 3.0 %branch.6 = bf16[192,384]{1,0:T(8,128)(2,1)} custom-call(s32[4]{0:T(128)} %pad_add_fusion.place_ref.core_ref, bf16[192,256]{1,0:T(8,128)(2,1)} %combine.1.a0, bf16[192,256]{1,0:T(8,128)(2,1)} %copy-done.5, bf16[192,256]{1,0:T(8,128)(2,1)} %copy-done.6, bf16[192,256]{1,0:T(8,128)(2,1)} %copy-done.7, bf16[4,256,384]{2,1,0:T(8,128)(2,1)} %get-tuple-element.33.w0, ...), custom_call_target="tpu_custom_call" | custom-call | tf_op jit(solution)/shard_map/branch/pallas_call | solution.py:298
  203.8 4.2 %collective-permute-start.18 = (bf16[192,384]{1,0:T(8,128)(2,1)}, bf16[192,384]{1,0:T(8,128)(2,1)S(1)}, u32[]{:S(2)}, u32[]{:S(2)}) collective-permute-start(bf16[192,384]{1,0:T(8,128)(2,1)} %branch.6), channel_id=1, source_target_pairs={{0,4},{4,8},{8,12},{12,0},{1,5},{5,9},{9,13},{13,1},{2,6},{6,10},{... | collective-permute-start | bytes 442376 | tf_op jit(solution)/shard_map/ppermute | solution.py:316
  208.0 3.0 %branch.7 = bf16[192,384]{1,0:T(8,128)(2,1)} custom-call(s32[4]{0:T(128)} %pad_add_fusion.place_ref.core_ref, bf16[192,256]{1,0:T(8,128)(2,1)} %combine.1.a0, bf16[192,256]{1,0:T(8,128)(2,1)} %copy-done.5, bf16[192,256]{1,0:T(8,128)(2,1)} %copy-done.6, bf16[192,256]{1,0:T(8,128)(2,1)} %copy-done.7, bf16[4,256,384]{2,1,0:T(8,128)(2,1)} %get-tuple-element.33.w0, ...), custom_call_target="tpu_custom_call" | custom-call | tf_op jit(solution)/shard_map/branch/pallas_call | solution.py:298
  211.0 5.1 %collective-permute-start.19 = (bf16[192,384]{1,0:T(8,128)(2,1)}, bf16[192,384]{1,0:T(8,128)(2,1)S(1)}, u32[]{:S(2)}, u32[]{:S(2)}) collective-permute-start(bf16[192,384]{1,0:T(8,128)(2,1)} %branch.7), channel_id=1, source_target_pairs={{0,12},{4,0},{8,4},{12,8},{1,13},{5,1},{9,5},{13,9},{2,14},{6,2},{... | collective-permute-start | bytes 442376 | tf_op jit(solution)/shard_map/ppermute | solution.py:316
  216.1 0.1 dynamic-slice_reduce_fusion.1
  216.2 3.0 %branch.4 = bf16[192,384]{1,0:T(8,128)(2,1)} custom-call(s32[4]{0:T(128)} %pad_add_fusion.place_ref.core_ref, bf16[192,256]{1,0:T(8,128)(2,1)} %combine.1.a0, bf16[192,256]{1,0:T(8,128)(2,1)} %copy-done.5, bf16[192,256]{1,0:T(8,128)(2,1)} %copy-done.6, bf16[192,256]{1,0:T(8,128)(2,1)} %copy-done.7, bf16[4,256,384]{2,1,0:T(8,128)(2,1)} %get-tuple-element.33.w0, ...), custom_call_target="tpu_custom_call" | custom-call | tf_op jit(solution)/shard_map/branch/pallas_call | solution.py:298
  219.3 6.4 %collective-permute-done.18 = bf16[192,384]{1,0:T(8,128)(2,1)S(1)} collective-permute-done((bf16[192,384]{1,0:T(8,128)(2,1)}, bf16[192,384]{1,0:T(8,128)(2,1)S(1)}, u32[]{:S(2)}, u32[]{:S(2)}) %collective-permute-start.18) | collective-permute-done | bytes 147488 | tf_op jit(solution)/shard_map/ppermute | solution.py:316
  225.7 6.2 %collective-permute-done.19 = bf16[192,384]{1,0:T(8,128)(2,1)S(1)} collective-permute-done((bf16[192,384]{1,0:T(8,128)(2,1)}, bf16[192,384]{1,0:T(8,128)(2,1)S(1)}, u32[]{:S(2)}, u32[]{:S(2)}) %collective-permute-start.19) | collective-permute-done | bytes 147488 | tf_op jit(solution)/shard_map/ppermute | solution.py:316
  231.8 1.7 add_convert_fusion
  (28 shorter events, 0.1 us)
Async XLA Ops:
  6.5 52.1 %copy-start = (f32[8,3,6144]{2,0,1:T(8,128)S(1)}, f32[8,3,6144]{2,0,1:T(8,128)}, u32[]{:S(2)}) copy-start(f32[8,3,6144]{2,0,1:T(8,128)} %param.15) | copy-start | bytes 1769476
  6.5 99.4 %all-gather.2.cloned.1.call-start = ((), (), s32[]{:S(2)}) async-start(), calls=%async_computation.2 | async-start | bytes 9732096 | tf_op jit(solution)/shard_map/all_gather | solution.py:178
  9.2 16.7 %collective-permute-start = (bf16[192,384]{1,0:T(8,128)(2,1)}, bf16[192,384]{1,0:T(8,128)(2,1)S(1)}, u32[]{:S(2)}, u32[]{:S(2)}) collective-permute-start(bf16[192,384]{1,0:T(8,128)(2,1)} %param.9), channel_id=1, source_target_pairs={{0,4},{4,8},{8,12},{12,0},{1,5},{5,9},{9,13},{13,1},{2,6},{6,10},{... | collective-permute-start | bytes 442376 | tf_op jit(solution)/shard_map/ppermute | solution.py:201
  18.8 22.1 %collective-permute-start.2 = (bf16[192,384]{1,0:T(8,128)(2,1)}, bf16[192,384]{1,0:T(8,128)(2,1)S(1)}, u32[]{:S(2)}, u32[]{:S(2)}) collective-permute-start(bf16[192,384]{1,0:T(8,128)(2,1)} %param.9), channel_id=1, source_target_pairs={{0,12},{4,0},{8,4},{12,8},{1,13},{5,1},{9,5},{13,9},{2,14},{6,2},{... | collective-permute-start | bytes 442376 | tf_op jit(solution)/shard_map/ppermute | solution.py:202
  25.9 20.6 %collective-permute-start.1 = (bf16[96,384]{1,0:T(8,128)(2,1)S(1)}, bf16[96,384]{1,0:T(8,128)(2,1)S(1)}, u32[]{:S(2)}, u32[]{:S(2)}) collective-permute-start(bf16[96,384]{1,0:T(8,128)(2,1)S(1)} %slice.13), channel_id=1, source_target_pairs={{0,4},{4,8},{8,12},{12,0},{1,5},{5,9},{9,13},{13,1},{2,6},{6,10},{... | collective-permute-start | bytes 221192 | tf_op jit(solution)/shard_map/ppermute | solution.py:205
  41.0 10.3 %collective-permute-start.3 = (bf16[96,384]{1,0:T(8,128)(2,1)S(1)}, bf16[96,384]{1,0:T(8,128)(2,1)S(1)}, u32[]{:S(2)}, u32[]{:S(2)}) collective-permute-start(bf16[96,384]{1,0:T(8,128)(2,1)S(1)} %slice.14), channel_id=1, source_target_pairs={{0,12},{4,0},{8,4},{12,8},{1,13},{5,1},{9,5},{13,9},{2,14},{6,2},{... | collective-permute-start | bytes 221192 | tf_op jit(solution)/shard_map/ppermute | solution.py:206
  54.0 28.5 %all-to-all-start = ((bf16[4,4,192,384]{3,2,1,0:T(8,128)(2,1)}), bf16[4,4,192,384]{3,2,1,0:T(8,128)(2,1)S(1)}, u32[]{:S(2)}, u32[]{:S(2)}) async-start(bf16[4,4,192,384]{3,2,1,0:T(8,128)(2,1)} %broadcast_in_dim.2), calls=%async_computation | async-start | bytes 4718592 | tf_op jit(solution)/shard_map/all_to_all | solution.py:26
  82.5 1.4 copy-start.4
  90.0 15.9 %collective-permute-start.4 = (bf16[192,6144]{1,0:T(8,128)(2,1)}, bf16[192,6144]{1,0:T(8,128)(2,1)}, u32[]{:S(2)}, u32[]{:S(2)}) collective-permute-start(bf16[192,6144]{1,0:T(8,128)(2,1)} %norm.1.own_ref), channel_id=1, source_target_pairs={{0,16},{16,0},{1,17},{17,1},{2,18},{18,2},{3,19},{19,3},{4,20},{20... | collective-permute-start | bytes 7077896 | tf_op jit(solution)/shard_map/ppermute | solution.py:229
  97.5 56.6 %collective-permute-start.11 = (bf16[4,256,384]{2,1,0:T(8,128)(2,1)}, bf16[4,256,384]{2,1,0:T(8,128)(2,1)S(1)}, u32[]{:S(2)}, u32[]{:S(2)}) collective-permute-start(bf16[4,256,384]{2,1,0:T(8,128)(2,1)} %get-tuple-element.29), channel_id=1, source_target_pairs={{0,1},{1,2},{2,3},{3,0},{4,5},{5,6},{6,7},{7,4},{8,9},{9,10},{10,1... | collective-permute-start | bytes 2359304 | tf_op jit(solution)/shard_map/ppermute | solution.py:212
  99.7 54.4 %collective-permute-start.12 = (bf16[4,256,384]{2,1,0:T(8,128)(2,1)}, bf16[4,256,384]{2,1,0:T(8,128)(2,1)S(1)}, u32[]{:S(2)}, u32[]{:S(2)}) collective-permute-start(bf16[4,256,384]{2,1,0:T(8,128)(2,1)} %get-tuple-element.30), channel_id=1, source_target_pairs={{0,2},{1,3},{2,0},{3,1},{4,6},{5,7},{6,4},{7,5},{8,10},{9,11},{10,... | collective-permute-start | bytes 2359304 | tf_op jit(solution)/shard_map/ppermute | solution.py:212
  103.4 50.7 %collective-permute-start.13 = (bf16[4,256,384]{2,1,0:T(8,128)(2,1)}, bf16[4,256,384]{2,1,0:T(8,128)(2,1)S(1)}, u32[]{:S(2)}, u32[]{:S(2)}) collective-permute-start(bf16[4,256,384]{2,1,0:T(8,128)(2,1)} %get-tuple-element.31), channel_id=1, source_target_pairs={{0,3},{1,0},{2,1},{3,2},{4,7},{5,4},{6,5},{7,6},{8,11},{9,8},{10,9... | collective-permute-start | bytes 2359304 | tf_op jit(solution)/shard_map/ppermute | solution.py:212
  113.4 9.9 %collective-permute-start.5 = (bf16[2,192,128]{2,1,0:T(8,128)(2,1)}, bf16[2,192,128]{2,1,0:T(8,128)(2,1)S(1)}, u32[]{:S(2)}, u32[]{:S(2)}) collective-permute-start(bf16[2,192,128]{2,1,0:T(8,128)(2,1)} %get-tuple-element.26), channel_id=1, source_target_pairs={{0,32},{32,64},{64,96},{96,0},{1,33},{33,65},{65,97},{97,1},{2,34}... | collective-permute-start | bytes 294920 | tf_op jit(solution)/shard_map/ppermute | solution.py:258
  115.6 12.7 %collective-permute-start.6 = (bf16[2,192,128]{2,1,0:T(8,128)(2,1)}, bf16[2,192,128]{2,1,0:T(8,128)(2,1)S(1)}, u32[]{:S(2)}, u32[]{:S(2)}) collective-permute-start(bf16[2,192,128]{2,1,0:T(8,128)(2,1)} %get-tuple-element.26), channel_id=1, source_target_pairs={{0,64},{32,96},{64,0},{96,32},{1,65},{33,97},{65,1},{97,33},{2,66}... | collective-permute-start | bytes 294920 | tf_op jit(solution)/shard_map/ppermute | solution.py:258
  123.4 13.8 %collective-permute-start.10 = (bf16[2,2,192,128]{3,2,1,0:T(8,128)(2,1)}, bf16[2,2,192,128]{3,2,1,0:T(8,128)(2,1)S(1)}, u32[]{:S(2)}, u32[]{:S(2)}) collective-permute-start(bf16[2,2,192,128]{3,2,1,0:T(8,128)(2,1)} %get-tuple-element.27.kv0), channel_id=1, source_target_pairs={{0,256},{128,384},{256,0},{384,128},{1,257},{129,385},{257,1},{385... | collective-permute-start | bytes 589832 | tf_op jit(solution)/shard_map/ppermute | solution.py:257
  128.3 5.9 %collective-permute-start.7 = (bf16[2,192,128]{2,1,0:T(8,128)(2,1)}, bf16[2,192,128]{2,1,0:T(8,128)(2,1)S(1)}, u32[]{:S(2)}, u32[]{:S(2)}) collective-permute-start(bf16[2,192,128]{2,1,0:T(8,128)(2,1)} %get-tuple-element.26), channel_id=1, source_target_pairs={{0,96},{32,0},{64,32},{96,64},{1,97},{33,1},{65,33},{97,65},{2,98}... | collective-permute-start | bytes 294920 | tf_op jit(solution)/shard_map/ppermute | solution.py:258
  134.2 9.1 %collective-permute-start.8 = (bf16[2,2,192,128]{3,2,1,0:T(8,128)(2,1)}, bf16[2,2,192,128]{3,2,1,0:T(8,128)(2,1)S(1)}, u32[]{:S(2)}, u32[]{:S(2)}) collective-permute-start(bf16[2,2,192,128]{3,2,1,0:T(8,128)(2,1)} %get-tuple-element.27.kv0), channel_id=1, source_target_pairs={{0,128},{128,256},{256,384},{384,0},{1,129},{129,257},{257,385},{3... | collective-permute-start | bytes 589832 | tf_op jit(solution)/shard_map/ppermute | solution.py:257
  137.2 7.4 %copy-start.9 = (bf16[2,2,192,128]{3,2,1,0:T(8,128)(2,1)}, bf16[2,2,192,128]{3,2,1,0:T(8,128)(2,1)S(1)}, u32[]{:S(2)}) copy-start(bf16[2,2,192,128]{3,2,1,0:T(8,128)(2,1)S(1)} %collective-permute-done.10.kv3) | copy-start | bytes 589828
  137.2 7.4 %collective-permute-start.9 = (bf16[2,2,192,128]{3,2,1,0:T(8,128)(2,1)}, bf16[2,2,192,128]{3,2,1,0:T(8,128)(2,1)S(1)}, u32[]{:S(2)}, u32[]{:S(2)}) collective-permute-start(bf16[2,2,192,128]{3,2,1,0:T(8,128)(2,1)} %get-tuple-element.27.kv0), channel_id=1, source_target_pairs={{0,384},{128,0},{256,128},{384,256},{1,385},{129,1},{257,129},{385... | collective-permute-start | bytes 589832 | tf_op jit(solution)/shard_map/ppermute | solution.py:257
  143.3 1.3 copy-start.10
  144.6 0.7 copy-start.11
  154.1 34.4 %copy-start.1 = (bf16[4,256,384]{2,1,0:T(8,128)(2,1)}, bf16[4,256,384]{2,1,0:T(8,128)(2,1)S(1)}, u32[]{:S(2)}) copy-start(bf16[4,256,384]{2,1,0:T(8,128)(2,1)S(1)} %collective-permute-done.11.w1) | copy-start | bytes 2359300
  154.1 34.4 %copy-start.2 = (bf16[4,256,384]{2,1,0:T(8,128)(2,1)}, bf16[4,256,384]{2,1,0:T(8,128)(2,1)S(1)}, u32[]{:S(2)}) copy-start(bf16[4,256,384]{2,1,0:T(8,128)(2,1)S(1)} %collective-permute-done.12.w2) | copy-start | bytes 2359300
  154.2 34.4 %copy-start.3 = (bf16[4,256,384]{2,1,0:T(8,128)(2,1)}, bf16[4,256,384]{2,1,0:T(8,128)(2,1)S(1)}, u32[]{:S(2)}) copy-start(bf16[4,256,384]{2,1,0:T(8,128)(2,1)S(1)} %collective-permute-done.13.w3) | copy-start | bytes 2359300
  176.2 10.4 %collective-permute-start.14 = (bf16[192,256]{1,0:T(8,128)(2,1)}, bf16[192,256]{1,0:T(8,128)(2,1)S(1)}, u32[]{:S(2)}, u32[]{:S(2)}) collective-permute-start(bf16[192,256]{1,0:T(8,128)(2,1)} %combine.1.a0), channel_id=1, source_target_pairs={{0,1},{1,2},{2,3},{3,0},{4,5},{5,6},{6,7},{7,4},{8,9},{9,10},{10,1... | collective-permute-start | bytes 294920 | tf_op jit(solution)/shard_map/ppermute | solution.py:295
  179.2 7.4 %collective-permute-start.15 = (bf16[192,256]{1,0:T(8,128)(2,1)}, bf16[192,256]{1,0:T(8,128)(2,1)S(1)}, u32[]{:S(2)}, u32[]{:S(2)}) collective-permute-start(bf16[192,256]{1,0:T(8,128)(2,1)} %combine.1.a0), channel_id=1, source_target_pairs={{0,2},{1,3},{2,0},{3,1},{4,6},{5,7},{6,4},{7,5},{8,10},{9,11},{10,... | collective-permute-start | bytes 294920 | tf_op jit(solution)/shard_map/ppermute | solution.py:295
  182.6 5.9 %collective-permute-start.16 = (bf16[192,256]{1,0:T(8,128)(2,1)}, bf16[192,256]{1,0:T(8,128)(2,1)S(1)}, u32[]{:S(2)}, u32[]{:S(2)}) collective-permute-start(bf16[192,256]{1,0:T(8,128)(2,1)} %combine.1.a0), channel_id=1, source_target_pairs={{0,3},{1,0},{2,1},{3,2},{4,7},{5,4},{6,5},{7,6},{8,11},{9,8},{10,9... | collective-permute-start | bytes 294920 | tf_op jit(solution)/shard_map/ppermute | solution.py:295
  186.6 1.9 copy-start.5
  186.6 1.9 copy-start.6
  188.5 0.6 copy-start.7
  192.2 27.1 %collective-permute-start.17 = (bf16[192,384]{1,0:T(8,128)(2,1)}, bf16[192,384]{1,0:T(8,128)(2,1)S(1)}, u32[]{:S(2)}, u32[]{:S(2)}) collective-permute-start(bf16[192,384]{1,0:T(8,128)(2,1)} %branch.5), channel_id=1, source_target_pairs={{0,8},{4,12},{8,0},{12,4},{1,9},{5,13},{9,1},{13,5},{2,10},{6,14},... | collective-permute-start | bytes 442376 | tf_op jit(solution)/shard_map/ppermute | solution.py:316
  203.8 21.9 %collective-permute-start.18 = (bf16[192,384]{1,0:T(8,128)(2,1)}, bf16[192,384]{1,0:T(8,128)(2,1)S(1)}, u32[]{:S(2)}, u32[]{:S(2)}) collective-permute-start(bf16[192,384]{1,0:T(8,128)(2,1)} %branch.6), channel_id=1, source_target_pairs={{0,4},{4,8},{8,12},{12,0},{1,5},{5,9},{9,13},{13,1},{2,6},{6,10},{... | collective-permute-start | bytes 442376 | tf_op jit(solution)/shard_map/ppermute | solution.py:316
  211.0 20.8 %copy-start.8 = (bf16[192,384]{1,0:T(8,128)(2,1)S(1)}, bf16[192,384]{1,0:T(8,128)(2,1)}, u32[]{:S(2)}) copy-start(bf16[192,384]{1,0:T(8,128)(2,1)} %param.9) | copy-start | bytes 442372
  211.0 20.8 %collective-permute-start.19 = (bf16[192,384]{1,0:T(8,128)(2,1)}, bf16[192,384]{1,0:T(8,128)(2,1)S(1)}, u32[]{:S(2)}, u32[]{:S(2)}) collective-permute-start(bf16[192,384]{1,0:T(8,128)(2,1)} %branch.7), channel_id=1, source_target_pairs={{0,12},{4,0},{8,4},{12,8},{1,13},{5,1},{9,5},{13,9},{2,14},{6,2},{... | collective-permute-start | bytes 442376 | tf_op jit(solution)/shard_map/ppermute | solution.py:316
Sparse Core Ops, SparseCore 0:
  9.5 92.6 all-gather.1

commit v5 on v4

v5 whole, which is shorter than its diff:
```python
import math

import jax
import jax.numpy as jnp
from jax import lax
from jax.experimental import pallas as pl
from jax.experimental.pallas import tpu as pltpu
from jax.sharding import Mesh
from jax.sharding import PartitionSpec as P

D = 6144
HD = 128
GRID = 4
BF = jnp.bfloat16
F32 = jnp.float32
LOG2E = 1.4426950408889634
TOKENS = ("y", "zl", "core")


def shift(amount):
    return [(i, (i + amount) % GRID) for i in range(GRID)]


def gather_small(shard, axis_name):
    spread = jnp.broadcast_to(shard[None], (GRID,) + shard.shape)
    return lax.all_to_all(spread, axis_name, 0, 0, tiled=True)


def average_kernel(step_ref, ema_ref, train_ref, out_ref):
    stepped = jnp.full((1, HD), step_ref[0], jnp.int32).astype(F32)
    decay = (1.0 + stepped) / (10.0 + stepped)
    for h in range(2):
        for j in range(3):
            part = slice(h * HD, (h + 1) * HD)
            ema = ema_ref[j, :, part].astype(F32)
            train = train_ref[j, :, part].astype(F32)
            out_ref[h, :, j * HD : (j + 1) * HD] = (decay * ema + (1.0 - decay) * train).astype(BF)


def norm_kernel(place_ref, raw_ref, mod_ref, out_ref):
    blocks = [(s, k) for s in range(GRID) for k in range(GRID)]
    rows, width = raw_ref.shape[2], raw_ref.shape[3]
    some = 32

    def one_piece(i, carry):
        part = pl.ds(pl.multiple_of(i * some, some), some)
        total = jnp.zeros((some, width), F32)
        for s, k in blocks:
            total = total + raw_ref[s, k, part, :].astype(F32)
        average = jnp.sum(total, axis=1, keepdims=True) * (1.0 / D)
        squares = jnp.zeros((some, width), F32)
        for s, k in blocks:
            centred = raw_ref[s, k, part, :].astype(F32) - average
            squares = squares + centred * centred
        variance = jnp.sum(squares, axis=1, keepdims=True) * (1.0 / D)
        inverse = lax.rsqrt(variance + 1e-06)
        for s, k in blocks:
            h = lax.rem(place_ref[2] + GRID - k, GRID)
            centred = raw_ref[s, k, part, :].astype(F32) - average
            scale = mod_ref[1, h, s : s + 1, :]
            move = mod_ref[0, h, s : s + 1, :]
            start = pl.multiple_of((h * GRID + s) * width, HD)
            out_ref[part, pl.ds(start, width)] = (
                centred * inverse * (1.0 + scale) + move
            ).astype(BF)
        return carry

    lax.fori_loop(0, rows // some, one_piece, 0)


def pick_kernel(place_ref, *refs):
    for source, target in zip(refs[:GRID], refs[GRID:]):
        target[0] = source[...]


def project_kernel(core_ref, own_ref, other_ref, weight_ref, q_gain_ref, k_gain_ref, q_ref, kv_ref, acc_ref):
    step = pl.program_id(0)

    @pl.when(step == 0)
    def _():
        acc_ref[...] = jnp.zeros_like(acc_ref)

    rows = own_ref.shape[0]
    hidden = jnp.concatenate([own_ref[...], other_ref[...]], axis=0)
    acc_ref[...] += jnp.dot(hidden, weight_ref[0], preferred_element_type=F32)

    @pl.when(step == pl.num_programs(0) - 1)
    def _():
        for t in range(2):
            for j, gain_ref in ((0, q_gain_ref), (1, k_gain_ref)):
                values = acc_ref[t * rows : (t + 1) * rows, j * HD : (j + 1) * HD]
                squares = jnp.mean(values * values, axis=1, keepdims=True)
                normed = (values * lax.rsqrt(squares + 1e-06) * gain_ref[...]).astype(BF)
                if j == 0:
                    q_ref[t] = normed
                else:
                    kv_ref[0, t] = normed
            kv_ref[1, t] = acc_ref[t * rows : (t + 1) * rows, 2 * HD :].astype(BF)


def attend_kernel(place_ref, q_ref, kv_ref, out_ref, k_all, v_all):
    rows = q_ref.shape[2]
    blocks = 2 * GRID

    @pl.when(pl.program_id(0) == 0)
    def _():
        for g in range(GRID):
            for t in range(2):
                part = slice((2 * g + t) * rows, (2 * g + t + 1) * rows)
                k_all[part, :] = kv_ref[g, 0, t]
                v_all[part, :HD] = kv_ref[g, 1, t]
        v_all[:, HD:] = jnp.ones((blocks * rows, HD), BF)

    chunk = 512
    queries = jnp.concatenate([q_ref[0, 0], q_ref[0, 1]], axis=0)
    both = jnp.zeros((2 * rows, 2 * HD), F32)
    for c in range(blocks * rows // chunk):
        part = slice(c * chunk, (c + 1) * chunk)
        scores = lax.dot_general(
            queries, k_all[part, :], (((1,), (1,)), ((), ())), preferred_element_type=F32
        )
        weights = jnp.exp2(scores * (LOG2E / math.sqrt(HD))).astype(BF)
        both = both + jnp.dot(weights, v_all[part, :], preferred_element_type=F32)
    lane = lax.broadcasted_iota(jnp.int32, (HD, HD), 1)
    line = lax.broadcasted_iota(jnp.int32, (HD, HD), 0)
    sub = lax.broadcasted_iota(jnp.int32, (16, HD), 0)
    rest = rows - HD
    for t in range(2):
        target = lax.rem(place_ref[0] + t, 2)
        out_ref[target, :rows, :] = both[t * rows : (t + 1) * rows, :HD].astype(BF)
        totals = both[t * rows : (t + 1) * rows, HD:]
        first = jnp.sum(jnp.where(lane == line, totals[:HD], 0.0), axis=0, keepdims=True)
        second = jnp.sum(
            jnp.where(lane[:rest] == line[:rest], totals[HD:], 0.0), axis=0, keepdims=True
        )
        first_high = first.astype(BF).astype(F32)
        second_high = second.astype(BF).astype(F32)
        packed = jnp.where(sub == 0, first_high, 0.0)
        packed = jnp.where(sub == 1, second_high, packed)
        packed = jnp.where(sub == 2, first - first_high, packed)
        packed = jnp.where(sub == 3, second - second_high, packed)
        out_ref[target, rows:, :] = packed.astype(BF)


def combine_kernel(parts_ref, out_ref):
    rows = out_ref.shape[0]
    lane = lax.broadcasted_iota(jnp.int32, (HD, HD), 1)
    line = lax.broadcasted_iota(jnp.int32, (HD, HD), 0)
    rest = rows - HD
    for h in range(2):
        numer = jnp.zeros((rows, HD), F32)
        packed = jnp.zeros((16, HD), F32)
        for g in range(GRID):
            numer = numer + parts_ref[2 * g + h, :rows, :].astype(F32)
            packed = packed + parts_ref[2 * g + h, rows:, :].astype(F32)
        first = packed[0:1] + packed[2:3]
        second = packed[1:2] + packed[3:4]
        first = jnp.sum(jnp.where(lane == line, first, 0.0), axis=1, keepdims=True)
        second = jnp.sum(
            jnp.where(lane[:rest] == line[:rest], second, 0.0), axis=1, keepdims=True
        )
        part = slice(h * HD, (h + 1) * HD)
        out_ref[:HD, part] = (numer[:HD] / first).astype(BF)
        out_ref[HD:, part] = (numer[HD:] / second).astype(BF)


def branch_kernel(place_ref, a_ref, w0, w1, w2, w3, *out_refs):
    for k, out_ref in enumerate(out_refs):
        total = jnp.zeros(out_ref.shape, F32)
        for away, w_ref in enumerate((w0, w1, w2, w3)):
            total = total + jnp.dot(
                a_ref[lax.rem(place_ref[3] + GRID - away, GRID)],
                w_ref[lax.rem(place_ref[2] + k, GRID)],
                preferred_element_type=F32,
            )
        out_ref[...] = total.astype(BF)


def per_device(latents, train_qkv, ema_qkv, q_gain, k_gain, out_weight, modulation, timestep, step):
    rows, width = latents.shape
    channels = ema_qkv.shape[2]
    blocks = GRID * GRID
    by_head = pl.pallas_call(
        average_kernel,
        in_specs=[
            pl.BlockSpec(memory_space=pltpu.SMEM),
            pl.BlockSpec(memory_space=pltpu.VMEM),
            pl.BlockSpec(memory_space=pltpu.VMEM),
        ],
        out_specs=pl.BlockSpec(memory_space=pltpu.VMEM),
        out_shape=jax.ShapeDtypeStruct((2, rows, 3 * HD), BF),
        name="average",
    )(step, ema_qkv, train_qkv)
    full_weights = lax.all_gather(by_head, TOKENS, axis=1, tiled=True)

    place = jnp.stack(
        [lax.axis_index(name).astype(jnp.int32) for name in ("core", "y", "head", "seq")]
    )

    def column(k):
        return lambda i, place: (0, i * GRID + lax.rem(place[3] + k, GRID))

    out_parts = pl.pallas_call(
        pick_kernel,
        grid_spec=pltpu.PrefetchScalarGridSpec(
            num_scalar_prefetch=1,
            grid=(GRID,),
            in_specs=[pl.BlockSpec((channels, width), column(k)) for k in range(GRID)],
            out_specs=[pl.BlockSpec((1, channels, width), lambda i, place: (i, 0, 0))] * GRID,
        ),
        out_shape=[jax.ShapeDtypeStruct((GRID, channels, width), BF)] * GRID,
        name="pick",
    )(place, *([out_weight] * GRID))

    mod_row = lax.dynamic_index_in_dim(modulation, timestep[0], 0, keepdims=False)
    half = rows // 2
    before = lax.ppermute(latents, "head", shift(1))
    after = lax.ppermute(latents, "head", shift(3))
    far = jnp.concatenate(
        [
            lax.ppermute(before[:half], "head", shift(1)),
            lax.ppermute(after[half:], "head", shift(3)),
        ]
    )
    raw = jnp.stack([latents, before, far, after])
    raw = gather_small(raw, "seq").reshape(GRID, GRID, rows, width)
    raw, *out_parts = lax.optimization_barrier((raw, *out_parts))
    out_parts = [out_parts[0]] + [lax.ppermute(out_parts[k], "seq", shift(k)) for k in (1, 2, 3)]
    in_smem = pl.BlockSpec(memory_space=pltpu.SMEM)
    in_vmem = pl.BlockSpec(memory_space=pltpu.VMEM)
    hidden = pl.pallas_call(
        norm_kernel,
        in_specs=[in_smem, in_vmem, in_vmem],
        out_specs=in_vmem,
        out_shape=jax.ShapeDtypeStruct((rows, blocks * width), BF),
        name="norm",
    )(place, raw, mod_row.reshape(3, GRID, GRID, width))
    sibling = lax.ppermute(hidden, "core", [(0, 1), (1, 0)])

    depth = D // GRID
    queries, pairs = pl.pallas_call(
        project_kernel,
        grid_spec=pltpu.PrefetchScalarGridSpec(
            num_scalar_prefetch=1,
            grid=(GRID,),
            in_specs=[
                pl.BlockSpec((rows, depth), lambda i, place: (0, i)),
                pl.BlockSpec((rows, depth), lambda i, place: (0, i)),
                pl.BlockSpec((1, depth, 3 * HD), lambda i, place: (place[0], i, 0)),
                pl.BlockSpec((1, HD), lambda i, place: (0, 0)),
                pl.BlockSpec((1, HD), lambda i, place: (0, 0)),
            ],
            out_specs=[
                pl.BlockSpec((2, rows, HD), lambda i, place: (0, 0, 0)),
                pl.BlockSpec((2, 2, rows, HD), lambda i, place: (0, 0, 0, 0)),
            ],
            scratch_shapes=[pltpu.VMEM((2 * rows, 3 * HD), F32)],
        ),
        out_shape=[
            jax.ShapeDtypeStruct((2, rows, HD), BF),
            jax.ShapeDtypeStruct((2, 2, rows, HD), BF),
        ],
        name="project",
    )(place, hidden, sibling, full_weights, q_gain.reshape(1, HD), k_gain.reshape(1, HD))

    pairs = gather_small(pairs, "zl").reshape(GRID, 2, 2, rows, HD)
    queries = jnp.stack([queries] + [lax.ppermute(queries, "y", shift(k)) for k in (1, 2, 3)])

    sent = rows + 16
    parts = pl.pallas_call(
        attend_kernel,
        grid_spec=pltpu.PrefetchScalarGridSpec(
            num_scalar_prefetch=1,
            grid=(GRID,),
            in_specs=[
                pl.BlockSpec(
                    (1, 2, rows, HD), lambda i, place: (lax.rem(place[1] + GRID - i, GRID), 0, 0, 0)
                ),
                pl.BlockSpec((GRID, 2, 2, rows, HD), lambda i, place: (0, 0, 0, 0, 0)),
            ],
            out_specs=pl.BlockSpec((2, sent, HD), lambda i, place: (i, 0, 0)),
            scratch_shapes=[
                pltpu.VMEM((2 * GRID * rows, HD), BF),
                pltpu.VMEM((2 * GRID * rows, 2 * HD), BF),
            ],
        ),
        out_shape=jax.ShapeDtypeStruct((2 * GRID, sent, HD), BF),
        name="attend",
    )(place, queries, pairs)
    parts, *out_parts = lax.optimization_barrier((parts, *out_parts))
    parts = lax.all_to_all(parts, ("y", "core"), 0, 0, tiled=True)
    attended = pl.pallas_call(
        combine_kernel,
        out_shape=jax.ShapeDtypeStruct((rows, channels), BF),
        name="combine",
    )(parts)

    around = gather_small(attended, "seq")
    outs = pl.pallas_call(
        branch_kernel,
        in_specs=[in_smem] + [in_vmem] * (GRID + 1),
        out_specs=[in_vmem] * GRID,
        out_shape=[jax.ShapeDtypeStruct((rows, width), BF)] * GRID,
        name="branch",
    )(place, around, *out_parts)
    shares = [lax.ppermute(outs[k], "head", shift(k)) for k in (2, 1, 3)]
    summed = outs[0].astype(F32)
    for share in shares:
        summed = summed + share.astype(F32)
    position = lax.axis_index(("head", "seq")) * width
    gate = lax.dynamic_slice_in_dim(mod_row[2], position, width, 0)
    return (latents.astype(F32) + gate[None, :] * summed).astype(BF)


def solution(mesh):
    fine = Mesh(
        mesh.devices.reshape(GRID, GRID, 2, GRID, GRID), ("y", "zl", "core", "head", "seq")
    )
    in_specs = (
        P(TOKENS, ("head", "seq")),
        P(None, TOKENS, ("head", "seq")),
        P(None, TOKENS, ("head", "seq")),
        P(),
        P(),
        P(("head", "seq"), None),
        P(),
        P(),
        P(),
    )
    out_specs = P(TOKENS, ("head", "seq"))
    return jax.shard_map(
        per_device, mesh=fine, in_specs=in_specs, out_specs=out_specs, check_vma=False
    )
```

time: 242 us -> 238 us (0.983); the launches traced: 240 us -> 233 us
  starting transfers between devices: 105 us -> 88 us
  waiting for transfers between devices: 45.5 us -> 57.9 us
  Pallas kernels: 43.3 us -> 32.5 us
  blocking collectives: 20.2 us -> 26.7 us
  local copies, waits for them, and re-layouts: 5.53 us -> 9.25 us
    ppermute x12 -> x6, starting transfers between devices: 51.7 us -> 28.7 us  [the longest x3 17.6 us: per_device(): shares = [lax.ppermute(outs[k], 'head', shift(k)) for k in (2, 1, 3)]]
    pallas_call x5 -> x2, Pallas kernels: 18.2 us -> 9.09 us  [the longest x1 5.48 us: per_device(): pl.pallas_call(norm_kernel, in_specs=[in_smem, in_vmem, in_vmem], out_spe...]
    ppermute x3, waiting for transfers between devices: 0.01 us -> 9.04 us  [per_device(): lax.ppermute(out_parts[k], 'seq', shift(k))]
    all_to_all x1 -> x2, blocking collectives: 20.2 us -> 26.7 us  [the longest x1 16.5 us: per_device(): parts = lax.all_to_all(parts, ('y', 'core'), 0, 0, tiled=True)]
    all_to_all x1 -> x2, starting transfers between devices: 4.03 us -> 10.5 us  [gather_small(): return lax.all_to_all(spread, axis_name, 0, 0, tiled=True)]
    ppermute x1, waiting for transfers between devices: 0.01 us -> 4.35 us  [per_device(): sibling = lax.ppermute(hidden, 'core', [(0, 1), (1, 0)])]
    broadcast_in_dim x1 -> x3, local copies, waits for them, and re-layouts: 1.7 us -> 4.72 us  [gather_small(): spread = jnp.broadcast_to(shard[None], (GRID,) + shard.shape)]
    ppermute x12 -> x6, waiting for transfers between devices: 20.3 us -> 18.4 us  [the longest x3 15.2 us: per_device(): shares = [lax.ppermute(outs[k], 'head', shift(k)) for k in (2, 1, 3)]]
  transfers between devices with their start and end apart: 22 -> 17, of which waited for: 10 -> 11; matrix products, arithmetic and copies ran while one was open for 3% -> 2% of each run, Pallas kernels for 15% -> 8%
where the time goes in v5:
time: 238 us; the launch traced here: 233 us
  starting transfers between devices  88 us (37%)
  waiting for transfers between devices  57.9 us (24%)
  Pallas kernels  32.5 us (14%)
  blocking collectives  26.7 us (11%)
  between operations  15 us (6%)
  local copies, waits for them, and re-layouts  9.25 us (4%)
  other arithmetic  4.1 us (2%)
    ppermute x3, starting transfers between devices, per_device(): shares = [lax.ppermute(outs[k], 'head', shift(k)) for k in (2, 1, 3)]  17.6 us
    all_to_all x2, waiting for transfers between devices, gather_small(): return lax.all_to_all(spread, axis_name, 0, 0, tiled=True)  17.3 us
    all_to_all x1, blocking collectives, per_device(): parts = lax.all_to_all(parts, ('y', 'core'), 0, 0, tiled=True)  16.5 us
    ppermute x3, waiting for transfers between devices, per_device(): shares = [lax.ppermute(outs[k], 'head', shift(k)) for k in (2, 1, 3)]  15.2 us
    ppermute x1, starting transfers between devices, per_device(): lax.ppermute(before[:half], 'head', shift(1))  15.1 us
    ppermute x3, starting transfers between devices, per_device(): lax.ppermute(queries, 'y', shift(k))  11.1 us
    all_to_all x2, starting transfers between devices, gather_small(): return lax.all_to_all(spread, axis_name, 0, 0, tiled=True)  10.5 us
    all_to_all x1, blocking collectives, gather_small(): return lax.all_to_all(spread, axis_name, 0, 0, tiled=True)  10.3 us
  transfers between devices with their start and end apart: 17, of which 11 were waited for; matrix products, arithmetic and copies ran while one was open for 2% of the time, Pallas kernels for 8%

profile of v5, /device:TPU:1, one launch (start us, length us, event | category | flops | bytes accessed | tf_op | source)
XLA Modules:
  0.0 233.4 jit_solution(17516046004924563320)
XLA Ops:
  6.5 0.0 copy-start
  6.5 0.0 all-gather.2.cloned.1.call-start
  7.3 1.9 average.1
  9.2 0.0 all-gather.2.cloned.1.call-update
  9.2 9.6 %collective-permute-start = (bf16[192,384]{1,0:T(8,128)(2,1)}, bf16[192,384]{1,0:T(8,128)(2,1)S(1)}, u32[]{:S(2)}, u32[]{:S(2)}) collective-permute-start(bf16[192,384]{1,0:T(8,128)(2,1)} %param.9), channel_id=1, source_target_pairs={{0,4},{4,8},{8,12},{12,0},{1,5},{5,9},{9,13},{13,1},{2,6},{6,10},{... | collective-permute-start | bytes 442376 | tf_op jit(solution)/shard_map/ppermute | solution.py:217
  18.8 5.6 %collective-permute-start.2 = (bf16[192,384]{1,0:T(8,128)(2,1)}, bf16[192,384]{1,0:T(8,128)(2,1)S(1)}, u32[]{:S(2)}, u32[]{:S(2)}) collective-permute-start(bf16[192,384]{1,0:T(8,128)(2,1)} %param.9), channel_id=1, source_target_pairs={{0,12},{4,0},{8,4},{12,8},{1,13},{5,1},{9,5},{13,9},{2,14},{6,2},{... | collective-permute-start | bytes 442376 | tf_op jit(solution)/shard_map/ppermute | solution.py:218
  24.4 1.5 collective-permute-done
  25.9 15.1 %collective-permute-start.1 = (bf16[96,384]{1,0:T(8,128)(2,1)S(1)}, bf16[96,384]{1,0:T(8,128)(2,1)S(1)}, u32[]{:S(2)}, u32[]{:S(2)}) collective-permute-start(bf16[96,384]{1,0:T(8,128)(2,1)S(1)} %slice.13), channel_id=1, source_target_pairs={{0,4},{4,8},{8,12},{12,0},{1,5},{5,9},{9,13},{13,1},{2,6},{6,10},{... | collective-permute-start | bytes 221192 | tf_op jit(solution)/shard_map/ppermute | solution.py:221
  41.0 0.0 collective-permute-done.2
  41.0 3.3 %collective-permute-start.3 = (bf16[96,384]{1,0:T(8,128)(2,1)S(1)}, bf16[96,384]{1,0:T(8,128)(2,1)S(1)}, u32[]{:S(2)}, u32[]{:S(2)}) collective-permute-start(bf16[96,384]{1,0:T(8,128)(2,1)S(1)} %slice.14), channel_id=1, source_target_pairs={{0,12},{4,0},{8,4},{12,8},{1,13},{5,1},{9,5},{13,9},{2,14},{6,2},{... | collective-permute-start | bytes 221192 | tf_op jit(solution)/shard_map/ppermute | solution.py:222
  44.3 2.2 collective-permute-done.1
  46.5 4.7 %collective-permute-done.3 = bf16[96,384]{1,0:T(8,128)(2,1)S(1)} collective-permute-done((bf16[96,384]{1,0:T(8,128)(2,1)S(1)}, bf16[96,384]{1,0:T(8,128)(2,1)S(1)}, u32[]{:S(2)}, u32[]{:S(2)}) %collective-permute-start.3) | collective-permute-done | bytes 73760 | tf_op jit(solution)/shard_map/ppermute | solution.py:222
  51.3 1.0 pad_maximum_fusion
  52.3 1.7 broadcast_in_dim.6
  54.0 4.0 %all-to-all-start = ((bf16[4,4,192,384]{3,2,1,0:T(8,128)(2,1)}), bf16[4,4,192,384]{3,2,1,0:T(8,128)(2,1)S(1)}, u32[]{:S(2)}, u32[]{:S(2)}) async-start(bf16[4,4,192,384]{3,2,1,0:T(8,128)(2,1)} %broadcast_in_dim.6), calls=%async_computation | async-start | bytes 4718592 | tf_op jit(solution)/shard_map/all_to_all | solution.py:26
  58.7 0.0 copy-done
  58.7 0.2 dynamic-slice_reduce_fusion
  58.9 0.7 reshape.18.mod_ref
  59.6 0.6 pad_add_fusion.place_ref.core_ref
  60.2 5.1 %pick.1 = (bf16[4,256,384]{2,1,0:T(8,128)(2,1)}, bf16[4,256,384]{2,1,0:T(8,128)(2,1)}, bf16[4,256,384]{2,1,0:T(8,128)(2,1)}, bf16[4,256,384]{2,1,0:T(8,128)(2,1)}) custom-call(s32[4]{0:T(128)} %pad_add_fusion.place_ref.core_ref, bf16[256,6144]{1,0:T(8,128)(2,1)} %refs_3_.1, bf16[256,6144]{1,0:T(8,128)(2,1)} %refs_3_.1, bf16[256,6144]{1,0:T(8,128)(2,1)} %refs_3_.1, ...), custom_call_target="tpu_custom_call" | custom-call | tf_op jit(solution)/shard_map/pick/pallas_call | solution.py:203
  65.3 17.3 %all-to-all-done.raw_ref = bf16[4,4,192,384]{3,2,1,0:T(8,128)(2,1)S(1)} async-done(((bf16[4,4,192,384]{3,2,1,0:T(8,128)(2,1)}), bf16[4,4,192,384]{3,2,1,0:T(8,128)(2,1)S(1)}, u32[]{:S(2)}, u32[]{:S(2)}) %all-to-all-start) | async-done | bytes 2359328 | tf_op jit(solution)/shard_map/all_to_all | solution.py:26
  82.5 1.5 copy-done.1
  84.0 5.5 %norm.1.own_ref = bf16[192,6144]{1,0:T(8,128)(2,1)} custom-call(s32[4]{0:T(128)} %pad_add_fusion.place_ref.core_ref, bf16[4,4,192,384]{3,2,1,0:T(8,128)(2,1)} %copy-done.1, f32[3,4,4,384]{3,2,1,0:T(4,128)} %reshape.18.mod_ref), custom_call_target="tpu_custom_call" | custom-call | tf_op jit(solution)/shard_map/norm/pallas_call | solution.py:231
  89.5 7.5 %collective-permute-start.4 = (bf16[192,6144]{1,0:T(8,128)(2,1)}, bf16[192,6144]{1,0:T(8,128)(2,1)S(1)}, u32[]{:S(2)}, u32[]{:S(2)}) collective-permute-start(bf16[192,6144]{1,0:T(8,128)(2,1)} %norm.1.own_ref), channel_id=1, source_target_pairs={{0,16},{16,0},{1,17},{17,1},{2,18},{18,2},{3,19},{19,3},{4,20},{20... | collective-permute-start | bytes 7077896 | tf_op jit(solution)/shard_map/ppermute | solution.py:238
  96.9 4.3 %collective-permute-done.4.other_ref = bf16[192,6144]{1,0:T(8,128)(2,1)S(1)} collective-permute-done((bf16[192,6144]{1,0:T(8,128)(2,1)}, bf16[192,6144]{1,0:T(8,128)(2,1)S(1)}, u32[]{:S(2)}, u32[]{:S(2)}) %collective-permute-start.4) | collective-permute-done | bytes 2359328 | tf_op jit(solution)/shard_map/ppermute | solution.py:238
  101.3 0.4 all-gather.2.cloned.1.call-done.weight_ref
  101.7 1.1 copy-done.3
  102.7 7.5 %project.1 = (bf16[2,192,128]{2,1,0:T(8,128)(2,1)}, bf16[2,2,192,128]{3,2,1,0:T(8,128)(2,1)}) custom-call(s32[4]{0:T(128)} %pad_add_fusion.place_ref.core_ref, bf16[192,6144]{1,0:T(8,128)(2,1)} %norm.1.own_ref, bf16[192,6144]{1,0:T(8,128)(2,1)} %copy-done.3, bf16[2,6144,384]{2,1,0:T(8,128)(2,1)} %all-gather.2.cloned.1.call-done.weight_ref, ...), custom_call_target="tpu_custom_call" | custom-call | tf_op jit(solution)/shard_map/project/pallas_call | solution.py:241
  110.2 2.1 broadcast_in_dim.7
  112.3 6.5 %all-to-all-start.1 = ((bf16[4,2,2,192,128]{4,3,2,1,0:T(8,128)(2,1)}), bf16[4,2,2,192,128]{4,3,2,1,0:T(8,128)(2,1)S(1)}, u32[]{:S(2)}, u32[]{:S(2)}) async-start(bf16[4,2,2,192,128]{4,3,2,1,0:T(8,128)(2,1)} %broadcast_in_dim.7), calls=%async_computation.1 | async-start | bytes 1572864 | tf_op jit(solution)/shard_map/all_to_all | solution.py:26
  118.7 2.8 %collective-permute-start.10 = (bf16[4,256,384]{2,1,0:T(8,128)(2,1)}, bf16[4,256,384]{2,1,0:T(8,128)(2,1)S(1)}, u32[]{:S(2)}, u32[]{:S(2)}) collective-permute-start(bf16[4,256,384]{2,1,0:T(8,128)(2,1)} %get-tuple-element.35), channel_id=1, source_target_pairs={{0,3},{1,0},{2,1},{3,2},{4,7},{5,4},{6,5},{7,6},{8,11},{9,8},{10,9... | collective-permute-start | bytes 2359304 | tf_op jit(solution)/shard_map/ppermute | solution.py:228
  121.5 2.5 %collective-permute-start.8 = (bf16[4,256,384]{2,1,0:T(8,128)(2,1)}, bf16[4,256,384]{2,1,0:T(8,128)(2,1)S(1)}, u32[]{:S(2)}, u32[]{:S(2)}) collective-permute-start(bf16[4,256,384]{2,1,0:T(8,128)(2,1)} %get-tuple-element.33), channel_id=1, source_target_pairs={{0,1},{1,2},{2,3},{3,0},{4,5},{5,6},{6,7},{7,4},{8,9},{9,10},{10,1... | collective-permute-start | bytes 2359304 | tf_op jit(solution)/shard_map/ppermute | solution.py:228
  124.0 2.5 %collective-permute-start.9 = (bf16[4,256,384]{2,1,0:T(8,128)(2,1)}, bf16[4,256,384]{2,1,0:T(8,128)(2,1)}, u32[]{:S(2)}, u32[]{:S(2)}) collective-permute-start(bf16[4,256,384]{2,1,0:T(8,128)(2,1)} %get-tuple-element.34), channel_id=1, source_target_pairs={{0,2},{1,3},{2,0},{3,1},{4,6},{5,7},{6,4},{7,5},{8,10},{9,11},{10,... | collective-permute-start | bytes 2359304 | tf_op jit(solution)/shard_map/ppermute | solution.py:228
  126.6 0.0 copy-done.7
  126.6 1.9 collective-permute-start.5
  128.5 6.7 %collective-permute-start.6 = (bf16[2,192,128]{2,1,0:T(8,128)(2,1)S(1)}, bf16[2,192,128]{2,1,0:T(8,128)(2,1)S(1)}, u32[]{:S(2)}, u32[]{:S(2)}) collective-permute-start(bf16[2,192,128]{2,1,0:T(8,128)(2,1)S(1)} %copy-done.7), channel_id=1, source_target_pairs={{0,256},{128,384},{256,0},{384,128},{1,257},{129,385},{257,1},{385... | collective-permute-start | bytes 294920 | tf_op jit(solution)/shard_map/ppermute | solution.py:267
  135.2 0.0 collective-permute-done.5
  135.2 2.5 %collective-permute-start.7 = (bf16[2,192,128]{2,1,0:T(8,128)(2,1)S(1)}, bf16[2,192,128]{2,1,0:T(8,128)(2,1)S(1)}, u32[]{:S(2)}, u32[]{:S(2)}) collective-permute-start(bf16[2,192,128]{2,1,0:T(8,128)(2,1)S(1)} %copy-done.7), channel_id=1, source_target_pairs={{0,384},{128,0},{256,128},{384,256},{1,385},{129,1},{257,129},{385... | collective-permute-start | bytes 294920 | tf_op jit(solution)/shard_map/ppermute | solution.py:267
  137.7 0.6 collective-permute-done.6
  138.4 2.5 %collective-permute-done.7 = bf16[2,192,128]{2,1,0:T(8,128)(2,1)S(1)} collective-permute-done((bf16[2,192,128]{2,1,0:T(8,128)(2,1)S(1)}, bf16[2,192,128]{2,1,0:T(8,128)(2,1)S(1)}, u32[]{:S(2)}, u32[]{:S(2)}) %collective-permute-start.7) | collective-permute-done | bytes 98336 | tf_op jit(solution)/shard_map/ppermute | solution.py:267
  140.8 0.8 pad_maximum_fusion.1.q_ref
  141.7 0.0 all-to-all-done.1.kv_ref
  141.7 0.9 copy-done.2
  142.6 7.1 %attend.1 = bf16[8,208,128]{2,1,0:T(8,128)(2,1)} custom-call(s32[4]{0:T(128)} %pad_add_fusion.place_ref.core_ref, bf16[4,2,192,128]{3,2,1,0:T(8,128)(2,1)} %pad_maximum_fusion.1.q_ref, bf16[4,2,2,192,128]{4,3,2,1,0:T(8,128)(2,1)} %copy-done.2), custom_call_target="tpu_custom_call" | custom-call | tf_op jit(solution)/shard_map/attend/pallas_call | solution.py:270
  149.7 0.0 collective-permute-done.10.w3
  149.8 0.0 collective-permute-done.8.w1
  149.8 0.0 copy-start.5
  149.8 9.0 %collective-permute-done.9.w2 = bf16[4,256,384]{2,1,0:T(8,128)(2,1)} collective-permute-done((bf16[4,256,384]{2,1,0:T(8,128)(2,1)}, bf16[4,256,384]{2,1,0:T(8,128)(2,1)}, u32[]{:S(2)}, u32[]{:S(2)}) %collective-permute-start.9) | collective-permute-done | bytes 786464 | tf_op jit(solution)/shard_map/ppermute | solution.py:228
  158.8 16.5 %all_to_all.20.parts_ref = bf16[8,208,128]{2,1,0:T(8,128)(2,1)} all-to-all(bf16[8,208,128]{2,1,0:T(8,128)(2,1)} %attend.1), channel_id=1, replica_groups=mesh['y'=4,'zl'=4,'core'=2,'head'=4,'seq'=4] {'y','core'}, dimensions={0} | all-to-all | bytes 851968 | tf_op jit(solution)/shard_map/all_to_all | solution.py:291
  175.3 1.8 combine.1
  177.1 1.0 broadcast_in_dim.8
  178.0 10.3 %all_to_all.21.a_ref = bf16[4,192,256]{2,1,0:T(8,128)(2,1)} all-to-all(bf16[4,192,256]{2,1,0:T(8,128)(2,1)S(1)} %broadcast_in_dim.8), channel_id=1, replica_groups=mesh['y'=4,'zl'=4,'core'=2,'head'=4,'seq'=4] {'seq'}, dimensions={0} | all-to-all | bytes 786432 | tf_op jit(solution)/shard_map/all_to_all | solution.py:26
  188.3 0.0 copy-done.4
  188.3 0.0 copy-done.5
  188.3 3.6 %branch.1 = (bf16[192,384]{1,0:T(8,128)(2,1)}, bf16[192,384]{1,0:T(8,128)(2,1)}, bf16[192,384]{1,0:T(8,128)(2,1)}, bf16[192,384]{1,0:T(8,128)(2,1)}) custom-call(s32[4]{0:T(128)} %pad_add_fusion.place_ref.core_ref, bf16[4,192,256]{2,1,0:T(8,128)(2,1)} %all_to_all.21.a_ref, bf16[4,256,384]{2,1,0:T(8,128)(2,1)} %get-tuple-element.37.w0, ...), custom_call_target="tpu_custom_call" | custom-call | tf_op jit(solution)/shard_map/branch/pallas_call | solution.py:299
  191.9 8.4 %collective-permute-start.11 = (bf16[192,384]{1,0:T(8,128)(2,1)}, bf16[192,384]{1,0:T(8,128)(2,1)S(1)}, u32[]{:S(2)}, u32[]{:S(2)}) collective-permute-start(bf16[192,384]{1,0:T(8,128)(2,1)} %get-tuple-element.42), channel_id=1, source_target_pairs={{0,8},{4,12},{8,0},{12,4},{1,9},{5,13},{9,1},{13,5},{2,10},{6,14},... | collective-permute-start | bytes 442376 | tf_op jit(solution)/shard_map/ppermute | solution.py:306
  200.3 4.4 %collective-permute-start.12 = (bf16[192,384]{1,0:T(8,128)(2,1)}, bf16[192,384]{1,0:T(8,128)(2,1)S(1)}, u32[]{:S(2)}, u32[]{:S(2)}) collective-permute-start(bf16[192,384]{1,0:T(8,128)(2,1)} %get-tuple-element.43), channel_id=1, source_target_pairs={{0,4},{4,8},{8,12},{12,0},{1,5},{5,9},{9,13},{13,1},{2,6},{6,10},{... | collective-permute-start | bytes 442376 | tf_op jit(solution)/shard_map/ppermute | solution.py:306
  204.7 4.8 %collective-permute-start.13 = (bf16[192,384]{1,0:T(8,128)(2,1)}, bf16[192,384]{1,0:T(8,128)(2,1)S(1)}, u32[]{:S(2)}, u32[]{:S(2)}) collective-permute-start(bf16[192,384]{1,0:T(8,128)(2,1)} %get-tuple-element.44), channel_id=1, source_target_pairs={{0,12},{4,0},{8,4},{12,8},{1,13},{5,1},{9,5},{13,9},{2,14},{6,2},{... | collective-permute-start | bytes 442376 | tf_op jit(solution)/shard_map/ppermute | solution.py:306
  209.5 0.1 dynamic-slice_reduce_fusion.1
  209.6 0.0 collective-permute-done.11
  209.6 7.3 %collective-permute-done.12 = bf16[192,384]{1,0:T(8,128)(2,1)S(1)} collective-permute-done((bf16[192,384]{1,0:T(8,128)(2,1)}, bf16[192,384]{1,0:T(8,128)(2,1)S(1)}, u32[]{:S(2)}, u32[]{:S(2)}) %collective-permute-start.12) | collective-permute-done | bytes 147488 | tf_op jit(solution)/shard_map/ppermute | solution.py:306
  216.9 8.0 %collective-permute-done.13 = bf16[192,384]{1,0:T(8,128)(2,1)S(1)} collective-permute-done((bf16[192,384]{1,0:T(8,128)(2,1)}, bf16[192,384]{1,0:T(8,128)(2,1)S(1)}, u32[]{:S(2)}, u32[]{:S(2)}) %collective-permute-start.13) | collective-permute-done | bytes 147488 | tf_op jit(solution)/shard_map/ppermute | solution.py:306
  224.9 0.0 copy-done.6
  224.9 1.7 add_convert_fusion
  (9 shorter events, 0.0 us)
Async XLA Ops:
  6.5 52.1 %copy-start = (f32[8,3,6144]{2,0,1:T(8,128)S(1)}, f32[8,3,6144]{2,0,1:T(8,128)}, u32[]{:S(2)}) copy-start(f32[8,3,6144]{2,0,1:T(8,128)} %param.15) | copy-start | bytes 1769476
  6.5 95.1 %all-gather.2.cloned.1.call-start = ((), (), s32[]{:S(2)}) async-start(), calls=%async_computation.4 | async-start | bytes 9732096 | tf_op jit(solution)/shard_map/all_gather | solution.py:194
  9.2 16.7 %collective-permute-start = (bf16[192,384]{1,0:T(8,128)(2,1)}, bf16[192,384]{1,0:T(8,128)(2,1)S(1)}, u32[]{:S(2)}, u32[]{:S(2)}) collective-permute-start(bf16[192,384]{1,0:T(8,128)(2,1)} %param.9), channel_id=1, source_target_pairs={{0,4},{4,8},{8,12},{12,0},{1,5},{5,9},{9,13},{13,1},{2,6},{6,10},{... | collective-permute-start | bytes 442376 | tf_op jit(solution)/shard_map/ppermute | solution.py:217
  18.8 22.1 %collective-permute-start.2 = (bf16[192,384]{1,0:T(8,128)(2,1)}, bf16[192,384]{1,0:T(8,128)(2,1)S(1)}, u32[]{:S(2)}, u32[]{:S(2)}) collective-permute-start(bf16[192,384]{1,0:T(8,128)(2,1)} %param.9), channel_id=1, source_target_pairs={{0,12},{4,0},{8,4},{12,8},{1,13},{5,1},{9,5},{13,9},{2,14},{6,2},{... | collective-permute-start | bytes 442376 | tf_op jit(solution)/shard_map/ppermute | solution.py:218
  25.9 20.6 %collective-permute-start.1 = (bf16[96,384]{1,0:T(8,128)(2,1)S(1)}, bf16[96,384]{1,0:T(8,128)(2,1)S(1)}, u32[]{:S(2)}, u32[]{:S(2)}) collective-permute-start(bf16[96,384]{1,0:T(8,128)(2,1)S(1)} %slice.13), channel_id=1, source_target_pairs={{0,4},{4,8},{8,12},{12,0},{1,5},{5,9},{9,13},{13,1},{2,6},{6,10},{... | collective-permute-start | bytes 221192 | tf_op jit(solution)/shard_map/ppermute | solution.py:221
  41.0 10.3 %collective-permute-start.3 = (bf16[96,384]{1,0:T(8,128)(2,1)S(1)}, bf16[96,384]{1,0:T(8,128)(2,1)S(1)}, u32[]{:S(2)}, u32[]{:S(2)}) collective-permute-start(bf16[96,384]{1,0:T(8,128)(2,1)S(1)} %slice.14), channel_id=1, source_target_pairs={{0,12},{4,0},{8,4},{12,8},{1,13},{5,1},{9,5},{13,9},{2,14},{6,2},{... | collective-permute-start | bytes 221192 | tf_op jit(solution)/shard_map/ppermute | solution.py:222
  54.0 28.5 %all-to-all-start = ((bf16[4,4,192,384]{3,2,1,0:T(8,128)(2,1)}), bf16[4,4,192,384]{3,2,1,0:T(8,128)(2,1)S(1)}, u32[]{:S(2)}, u32[]{:S(2)}) async-start(bf16[4,4,192,384]{3,2,1,0:T(8,128)(2,1)} %broadcast_in_dim.6), calls=%async_computation | async-start | bytes 4718592 | tf_op jit(solution)/shard_map/all_to_all | solution.py:26
  82.5 1.5 copy-start.1
  89.5 11.8 %collective-permute-start.4 = (bf16[192,6144]{1,0:T(8,128)(2,1)}, bf16[192,6144]{1,0:T(8,128)(2,1)S(1)}, u32[]{:S(2)}, u32[]{:S(2)}) collective-permute-start(bf16[192,6144]{1,0:T(8,128)(2,1)} %norm.1.own_ref), channel_id=1, source_target_pairs={{0,16},{16,0},{1,17},{17,1},{2,18},{18,2},{3,19},{19,3},{4,20},{20... | collective-permute-start | bytes 7077896 | tf_op jit(solution)/shard_map/ppermute | solution.py:238
  101.3 1.5 copy-start.3
  110.2 16.4 %copy-start.7 = (bf16[2,192,128]{2,1,0:T(8,128)(2,1)S(1)}, bf16[2,192,128]{2,1,0:T(8,128)(2,1)}, u32[]{:S(2)}) copy-start(bf16[2,192,128]{2,1,0:T(8,128)(2,1)} %get-tuple-element.30) | copy-start | bytes 294916
  112.3 29.4 %all-to-all-start.1 = ((bf16[4,2,2,192,128]{4,3,2,1,0:T(8,128)(2,1)}), bf16[4,2,2,192,128]{4,3,2,1,0:T(8,128)(2,1)S(1)}, u32[]{:S(2)}, u32[]{:S(2)}) async-start(bf16[4,2,2,192,128]{4,3,2,1,0:T(8,128)(2,1)} %broadcast_in_dim.7), calls=%async_computation.1 | async-start | bytes 1572864 | tf_op jit(solution)/shard_map/all_to_all | solution.py:26
  118.7 31.0 %collective-permute-start.10 = (bf16[4,256,384]{2,1,0:T(8,128)(2,1)}, bf16[4,256,384]{2,1,0:T(8,128)(2,1)S(1)}, u32[]{:S(2)}, u32[]{:S(2)}) collective-permute-start(bf16[4,256,384]{2,1,0:T(8,128)(2,1)} %get-tuple-element.35), channel_id=1, source_target_pairs={{0,3},{1,0},{2,1},{3,2},{4,7},{5,4},{6,5},{7,6},{8,11},{9,8},{10,9... | collective-permute-start | bytes 2359304 | tf_op jit(solution)/shard_map/ppermute | solution.py:228
  121.5 28.2 %collective-permute-start.8 = (bf16[4,256,384]{2,1,0:T(8,128)(2,1)}, bf16[4,256,384]{2,1,0:T(8,128)(2,1)S(1)}, u32[]{:S(2)}, u32[]{:S(2)}) collective-permute-start(bf16[4,256,384]{2,1,0:T(8,128)(2,1)} %get-tuple-element.33), channel_id=1, source_target_pairs={{0,1},{1,2},{2,3},{3,0},{4,5},{5,6},{6,7},{7,4},{8,9},{9,10},{10,1... | collective-permute-start | bytes 2359304 | tf_op jit(solution)/shard_map/ppermute | solution.py:228
  124.0 34.8 %collective-permute-start.9 = (bf16[4,256,384]{2,1,0:T(8,128)(2,1)}, bf16[4,256,384]{2,1,0:T(8,128)(2,1)}, u32[]{:S(2)}, u32[]{:S(2)}) collective-permute-start(bf16[4,256,384]{2,1,0:T(8,128)(2,1)} %get-tuple-element.34), channel_id=1, source_target_pairs={{0,2},{1,3},{2,0},{3,1},{4,6},{5,7},{6,4},{7,5},{8,10},{9,11},{10,... | collective-permute-start | bytes 2359304 | tf_op jit(solution)/shard_map/ppermute | solution.py:228
  126.6 8.6 %collective-permute-start.5 = (bf16[2,192,128]{2,1,0:T(8,128)(2,1)S(1)}, bf16[2,192,128]{2,1,0:T(8,128)(2,1)S(1)}, u32[]{:S(2)}, u32[]{:S(2)}) collective-permute-start(bf16[2,192,128]{2,1,0:T(8,128)(2,1)S(1)} %copy-done.7), channel_id=1, source_target_pairs={{0,128},{128,256},{256,384},{384,0},{1,129},{129,257},{257,385},{3... | collective-permute-start | bytes 294920 | tf_op jit(solution)/shard_map/ppermute | solution.py:267
  128.5 9.9 %collective-permute-start.6 = (bf16[2,192,128]{2,1,0:T(8,128)(2,1)S(1)}, bf16[2,192,128]{2,1,0:T(8,128)(2,1)S(1)}, u32[]{:S(2)}, u32[]{:S(2)}) collective-permute-start(bf16[2,192,128]{2,1,0:T(8,128)(2,1)S(1)} %copy-done.7), channel_id=1, source_target_pairs={{0,256},{128,384},{256,0},{384,128},{1,257},{129,385},{257,1},{385... | collective-permute-start | bytes 294920 | tf_op jit(solution)/shard_map/ppermute | solution.py:267
  135.2 5.7 %collective-permute-start.7 = (bf16[2,192,128]{2,1,0:T(8,128)(2,1)S(1)}, bf16[2,192,128]{2,1,0:T(8,128)(2,1)S(1)}, u32[]{:S(2)}, u32[]{:S(2)}) collective-permute-start(bf16[2,192,128]{2,1,0:T(8,128)(2,1)S(1)} %copy-done.7), channel_id=1, source_target_pairs={{0,384},{128,0},{256,128},{384,256},{1,385},{129,1},{257,129},{385... | collective-permute-start | bytes 294920 | tf_op jit(solution)/shard_map/ppermute | solution.py:267
  141.7 0.9 copy-start.2
  149.8 38.5 %copy-start.4 = (bf16[4,256,384]{2,1,0:T(8,128)(2,1)}, bf16[4,256,384]{2,1,0:T(8,128)(2,1)S(1)}, u32[]{:S(2)}) copy-start(bf16[4,256,384]{2,1,0:T(8,128)(2,1)S(1)} %collective-permute-done.10.w3) | copy-start | bytes 2359300
  149.8 38.5 %copy-start.5 = (bf16[4,256,384]{2,1,0:T(8,128)(2,1)}, bf16[4,256,384]{2,1,0:T(8,128)(2,1)S(1)}, u32[]{:S(2)}) copy-start(bf16[4,256,384]{2,1,0:T(8,128)(2,1)S(1)} %collective-permute-done.8.w1) | copy-start | bytes 2359300
  177.1 47.8 %copy-start.6 = (bf16[192,384]{1,0:T(8,128)(2,1)S(1)}, bf16[192,384]{1,0:T(8,128)(2,1)}, u32[]{:S(2)}) copy-start(bf16[192,384]{1,0:T(8,128)(2,1)} %param.9) | copy-start | bytes 442372
  191.9 17.7 %collective-permute-start.11 = (bf16[192,384]{1,0:T(8,128)(2,1)}, bf16[192,384]{1,0:T(8,128)(2,1)S(1)}, u32[]{:S(2)}, u32[]{:S(2)}) collective-permute-start(bf16[192,384]{1,0:T(8,128)(2,1)} %get-tuple-element.42), channel_id=1, source_target_pairs={{0,8},{4,12},{8,0},{12,4},{1,9},{5,13},{9,1},{13,5},{2,10},{6,14},... | collective-permute-start | bytes 442376 | tf_op jit(solution)/shard_map/ppermute | solution.py:306
  200.3 16.6 %collective-permute-start.12 = (bf16[192,384]{1,0:T(8,128)(2,1)}, bf16[192,384]{1,0:T(8,128)(2,1)S(1)}, u32[]{:S(2)}, u32[]{:S(2)}) collective-permute-start(bf16[192,384]{1,0:T(8,128)(2,1)} %get-tuple-element.43), channel_id=1, source_target_pairs={{0,4},{4,8},{8,12},{12,0},{1,5},{5,9},{9,13},{13,1},{2,6},{6,10},{... | collective-permute-start | bytes 442376 | tf_op jit(solution)/shard_map/ppermute | solution.py:306
  204.7 20.2 %collective-permute-start.13 = (bf16[192,384]{1,0:T(8,128)(2,1)}, bf16[192,384]{1,0:T(8,128)(2,1)S(1)}, u32[]{:S(2)}, u32[]{:S(2)}) collective-permute-start(bf16[192,384]{1,0:T(8,128)(2,1)} %get-tuple-element.44), channel_id=1, source_target_pairs={{0,12},{4,0},{8,4},{12,8},{1,13},{5,1},{9,5},{13,9},{2,14},{6,2},{... | collective-permute-start | bytes 442376 | tf_op jit(solution)/shard_map/ppermute | solution.py:306
Sparse Core Ops, SparseCore 0:
  9.5 92.1 all-gather.1

commit v6 on v5

v6 whole, which is shorter than its diff:
```python
import math

import jax
import jax.numpy as jnp
from jax import lax
from jax.experimental import pallas as pl
from jax.experimental.pallas import tpu as pltpu
from jax.sharding import Mesh
from jax.sharding import PartitionSpec as P

D = 6144
HD = 128
GRID = 4
BF = jnp.bfloat16
F32 = jnp.float32
LOG2E = 1.4426950408889634
TOKENS = ("y", "zl", "core")
PARAMS = pltpu.CompilerParams(vmem_limit_bytes=24 << 20)


def shift(amount):
    return [(i, (i + amount) % GRID) for i in range(GRID)]


def average_kernel(step_ref, ema_ref, train_ref, out_ref):
    stepped = jnp.full((1, HD), step_ref[0], jnp.int32).astype(F32)
    decay = (1.0 + stepped) / (10.0 + stepped)
    for h in range(2):
        for j in range(3):
            part = slice(h * HD, (h + 1) * HD)
            ema = ema_ref[j, :, part].astype(F32)
            train = train_ref[j, :, part].astype(F32)
            out_ref[h, :, j * HD : (j + 1) * HD] = (decay * ema + (1.0 - decay) * train).astype(BF)


def spread_kernel(own_ref, before_ref, low_ref, high_ref, after_ref, out_ref):
    half = low_ref.shape[0]
    for copy in range(GRID):
        out_ref[copy, 0] = own_ref[...]
        out_ref[copy, 1] = before_ref[...]
        out_ref[copy, 2, :half] = low_ref[...]
        out_ref[copy, 2, half:] = high_ref[...]
        out_ref[copy, 3] = after_ref[...]


def norm_kernel(place_ref, raw_ref, mod_ref, sent_ref, out_ref, sems):
    blocks = [(s, k) for s in range(GRID) for k in range(GRID)]
    rows, width = raw_ref.shape[2], raw_ref.shape[3]
    some = 32

    def one_piece(i, carry):
        part = pl.ds(pl.multiple_of(i * some, some), some)
        total = jnp.zeros((some, width), F32)
        for s, k in blocks:
            total = total + raw_ref[s, k, part, :].astype(F32)
        average = jnp.sum(total, axis=1, keepdims=True) * (1.0 / D)
        squares = jnp.zeros((some, width), F32)
        for s, k in blocks:
            centred = raw_ref[s, k, part, :].astype(F32) - average
            squares = squares + centred * centred
        variance = jnp.sum(squares, axis=1, keepdims=True) * (1.0 / D)
        inverse = lax.rsqrt(variance + 1e-06)
        for s, k in blocks:
            h = lax.rem(place_ref[2] + GRID - k, GRID)
            centred = raw_ref[s, k, part, :].astype(F32) - average
            scale = mod_ref[1, h, s : s + 1, :]
            move = mod_ref[0, h, s : s + 1, :]
            start = pl.multiple_of((h * GRID + s) * width, HD)
            out_ref[part, pl.ds(start, width)] = (
                centred * inverse * (1.0 + scale) + move
            ).astype(BF)
        pltpu.make_async_copy(out_ref.at[part], sent_ref.at[part], sems.at[i]).start()
        return carry

    lax.fori_loop(0, rows // some, one_piece, 0)
    for i in range(rows // some):
        part = pl.ds(i * some, some)
        pltpu.make_async_copy(out_ref.at[part], sent_ref.at[part], sems.at[i]).wait()


def pick_kernel(place_ref, *refs):
    for source, target in zip(refs[:GRID], refs[GRID:]):
        target[0] = source[...]


def project_kernel(place_ref, own_ref, other_ref, weight_ref, q_gain_ref, k_gain_ref, q_ref, kv_ref, held, sems):
    rows = own_ref.shape[0]
    depth = held.shape[1]
    copies = [
        pltpu.make_async_copy(
            weight_ref.at[place_ref[0], pl.ds(i * depth, depth), :], held.at[i], sems.at[i]
        )
        for i in range(held.shape[0])
    ]
    for copy in copies:
        copy.start()
    total = None
    for i, copy in enumerate(copies):
        part = slice(i * depth, (i + 1) * depth)
        hidden = jnp.concatenate([own_ref[:, part], other_ref[:, part]], axis=0)
        copy.wait()
        product = jnp.dot(hidden, held[i], preferred_element_type=F32)
        total = product if total is None else total + product
    for t in range(2):
        here = slice(t * rows, (t + 1) * rows)
        for j, gain_ref in ((0, q_gain_ref), (1, k_gain_ref)):
            values = total[here, j * HD : (j + 1) * HD]
            squares = jnp.mean(values * values, axis=1, keepdims=True)
            normed = (values * lax.rsqrt(squares + 1e-06) * gain_ref[...]).astype(BF)
            if j == 0:
                q_ref[t] = normed
            else:
                for copy in range(GRID):
                    kv_ref[copy, 0, t] = normed
        values = total[here, 2 * HD :].astype(BF)
        for copy in range(GRID):
            kv_ref[copy, 1, t] = values


def attend_kernel(place_ref, q0, q1, q2, q3, kv_ref, out_ref, k_all, v_all):
    rows = q0.shape[1]
    blocks = 2 * GRID
    for g in range(GRID):
        for t in range(2):
            part = slice((2 * g + t) * rows, (2 * g + t + 1) * rows)
            k_all[part, :] = kv_ref[g, 0, t]
            v_all[part, :HD] = kv_ref[g, 1, t]
    v_all[:, HD:] = jnp.ones((blocks * rows, HD), BF)

    chunk = 512
    lane = lax.broadcasted_iota(jnp.int32, (HD, HD), 1)
    line = lax.broadcasted_iota(jnp.int32, (HD, HD), 0)
    sub = lax.broadcasted_iota(jnp.int32, (16, HD), 0)
    rest = rows - HD
    for k, q_ref in enumerate((q0, q1, q2, q3)):
        queries = jnp.concatenate([q_ref[0], q_ref[1]], axis=0)
        both = jnp.zeros((2 * rows, 2 * HD), F32)
        for c in range(blocks * rows // chunk):
            part = slice(c * chunk, (c + 1) * chunk)
            scores = lax.dot_general(
                queries, k_all[part, :], (((1,), (1,)), ((), ())), preferred_element_type=F32
            )
            weights = jnp.exp2(scores * (LOG2E / math.sqrt(HD))).astype(BF)
            both = both + jnp.dot(weights, v_all[part, :], preferred_element_type=F32)
        for t in range(2):
            target = 2 * lax.rem(place_ref[1] + GRID - k, GRID) + lax.rem(place_ref[0] + t, 2)
            out_ref[target, :rows, :] = both[t * rows : (t + 1) * rows, :HD].astype(BF)
            totals = both[t * rows : (t + 1) * rows, HD:]
            first = jnp.sum(jnp.where(lane == line, totals[:HD], 0.0), axis=0, keepdims=True)
            second = jnp.sum(
                jnp.where(lane[:rest] == line[:rest], totals[HD:], 0.0), axis=0, keepdims=True
            )
            first_high = first.astype(BF).astype(F32)
            second_high = second.astype(BF).astype(F32)
            packed = jnp.where(sub == 0, first_high, 0.0)
            packed = jnp.where(sub == 1, second_high, packed)
            packed = jnp.where(sub == 2, first - first_high, packed)
            packed = jnp.where(sub == 3, second - second_high, packed)
            out_ref[target, rows:, :] = packed.astype(BF)


def combine_kernel(parts_ref, out_ref):
    rows = out_ref.shape[1]
    lane = lax.broadcasted_iota(jnp.int32, (HD, HD), 1)
    line = lax.broadcasted_iota(jnp.int32, (HD, HD), 0)
    rest = rows - HD
    for h in range(2):
        numer = jnp.zeros((rows, HD), F32)
        packed = jnp.zeros((16, HD), F32)
        for g in range(GRID):
            numer = numer + parts_ref[2 * g + h, :rows, :].astype(F32)
            packed = packed + parts_ref[2 * g + h, rows:, :].astype(F32)
        first = packed[0:1] + packed[2:3]
        second = packed[1:2] + packed[3:4]
        first = jnp.sum(jnp.where(lane == line, first, 0.0), axis=1, keepdims=True)
        second = jnp.sum(
            jnp.where(lane[:rest] == line[:rest], second, 0.0), axis=1, keepdims=True
        )
        part = slice(h * HD, (h + 1) * HD)
        upper = (numer[:HD] / first).astype(BF)
        lower = (numer[HD:] / second).astype(BF)
        for copy in range(GRID):
            out_ref[copy, :HD, part] = upper
            out_ref[copy, HD:, part] = lower


def branch_kernel(place_ref, a_ref, w0, w1, w2, w3, *out_refs):
    for k, out_ref in enumerate(out_refs):
        total = jnp.zeros(out_ref.shape, F32)
        for away, w_ref in enumerate((w0, w1, w2, w3)):
            total = total + jnp.dot(
                a_ref[lax.rem(place_ref[3] + GRID - away, GRID)],
                w_ref[lax.rem(place_ref[2] + k, GRID)],
                preferred_element_type=F32,
            )
        out_ref[...] = total.astype(BF)


def per_device(latents, train_qkv, ema_qkv, q_gain, k_gain, out_weight, modulation, timestep, step):
    rows, width = latents.shape
    channels = ema_qkv.shape[2]
    blocks = GRID * GRID
    by_head = pl.pallas_call(
        average_kernel,
        in_specs=[
            pl.BlockSpec(memory_space=pltpu.SMEM),
            pl.BlockSpec(memory_space=pltpu.VMEM),
            pl.BlockSpec(memory_space=pltpu.VMEM),
        ],
        out_specs=pl.BlockSpec(memory_space=pltpu.VMEM),
        out_shape=jax.ShapeDtypeStruct((2, rows, 3 * HD), BF),
        name="average",
    )(step, ema_qkv, train_qkv)
    full_weights = lax.all_gather(by_head, TOKENS, axis=1, tiled=True)

    place = jnp.stack(
        [lax.axis_index(name).astype(jnp.int32) for name in ("core", "y", "head", "seq")]
    )

    def column(k):
        return lambda i, place: (0, i * GRID + lax.rem(place[3] + k, GRID))

    out_parts = pl.pallas_call(
        pick_kernel,
        grid_spec=pltpu.PrefetchScalarGridSpec(
            num_scalar_prefetch=1,
            grid=(GRID,),
            in_specs=[pl.BlockSpec((channels, width), column(k)) for k in range(GRID)],
            out_specs=[pl.BlockSpec((1, channels, width), lambda i, place: (i, 0, 0))] * GRID,
        ),
        out_shape=[jax.ShapeDtypeStruct((GRID, channels, width), BF)] * GRID,
        name="pick",
    )(place, *([out_weight] * GRID))

    mod_row = lax.dynamic_index_in_dim(modulation, timestep[0], 0, keepdims=False)
    half = rows // 2
    before = lax.ppermute(latents, "head", shift(1))
    after = lax.ppermute(latents, "head", shift(3))
    far_low = lax.ppermute(before[:half], "head", shift(1))
    far_high = lax.ppermute(after[half:], "head", shift(3))
    in_smem = pl.BlockSpec(memory_space=pltpu.SMEM)
    in_vmem = pl.BlockSpec(memory_space=pltpu.VMEM)
    raw = pl.pallas_call(
        spread_kernel,
        in_specs=[in_vmem] * (GRID + 1),
        out_specs=in_vmem,
        out_shape=jax.ShapeDtypeStruct((GRID, GRID, rows, width), BF),
        name="spread",
    )(latents, before, far_low, far_high, after)
    raw = lax.all_to_all(raw, "seq", 0, 0, tiled=True)
    out0, out1, out2, out3 = out_parts
    raw, out2 = lax.optimization_barrier((raw, out2))
    out2 = lax.ppermute(out2, "seq", shift(2))
    hidden = pl.pallas_call(
        norm_kernel,
        in_specs=[in_smem, in_vmem, in_vmem],
        out_specs=pl.BlockSpec(memory_space=pltpu.HBM),
        out_shape=jax.ShapeDtypeStruct((rows, blocks * width), BF),
        scratch_shapes=[
            pltpu.VMEM((rows, blocks * width), BF),
            pltpu.SemaphoreType.DMA((rows // 32,)),
        ],
        compiler_params=PARAMS,
        name="norm",
    )(place, raw, mod_row.reshape(3, GRID, GRID, width))
    sibling = lax.ppermute(hidden, "core", [(0, 1), (1, 0)])

    depth = D // GRID
    queries, pairs = pl.pallas_call(
        project_kernel,
        in_specs=[in_smem, in_vmem, in_vmem, pl.BlockSpec(memory_space=pltpu.HBM), in_vmem, in_vmem],
        out_specs=[in_vmem, in_vmem],
        out_shape=[
            jax.ShapeDtypeStruct((2, rows, HD), BF),
            jax.ShapeDtypeStruct((GRID, 2, 2, rows, HD), BF),
        ],
        scratch_shapes=[
            pltpu.VMEM((GRID, depth, 3 * HD), BF),
            pltpu.SemaphoreType.DMA((GRID,)),
        ],
        compiler_params=PARAMS,
        name="project",
    )(place, hidden, sibling, pltpu.with_memory_space_constraint(full_weights, pltpu.HBM), q_gain.reshape(1, HD), k_gain.reshape(1, HD))

    pairs = lax.all_to_all(pairs, "zl", 0, 0, tiled=True)
    queries = [queries] + [lax.ppermute(queries, "y", shift(k)) for k in (1, 2, 3)]

    sent = rows + 16
    parts = pl.pallas_call(
        attend_kernel,
        in_specs=[in_smem] + [in_vmem] * (GRID + 1),
        out_specs=in_vmem,
        out_shape=jax.ShapeDtypeStruct((2 * GRID, sent, HD), BF),
        scratch_shapes=[
            pltpu.VMEM((2 * GRID * rows, HD), BF),
            pltpu.VMEM((2 * GRID * rows, 2 * HD), BF),
        ],
        compiler_params=PARAMS,
        name="attend",
    )(place, *queries, pairs)
    parts, out1, out2, out3 = lax.optimization_barrier((parts, out1, out2, out3))
    parts = lax.all_to_all(parts, ("y", "core"), 0, 0, tiled=True)
    out1 = lax.ppermute(out1, "seq", shift(1))
    out3 = lax.ppermute(out3, "seq", shift(3))
    around = pl.pallas_call(
        combine_kernel,
        in_specs=[in_vmem],
        out_specs=in_vmem,
        out_shape=jax.ShapeDtypeStruct((GRID, rows, channels), BF),
        name="combine",
    )(parts)
    around, out1, out3 = lax.optimization_barrier((around, out1, out3))
    around = lax.all_to_all(around, "seq", 0, 0, tiled=True)
    outs = pl.pallas_call(
        branch_kernel,
        in_specs=[in_smem] + [in_vmem] * (GRID + 1),
        out_specs=[in_vmem] * GRID,
        out_shape=[jax.ShapeDtypeStruct((rows, width), BF)] * GRID,
        compiler_params=PARAMS,
        name="branch",
    )(place, around, out0, out1, out2, out3)
    shares = [lax.ppermute(outs[k], "head", shift(k)) for k in (2, 1, 3)]
    summed = outs[0].astype(F32)
    for share in shares:
        summed = summed + share.astype(F32)
    position = lax.axis_index(("head", "seq")) * width
    gate = lax.dynamic_slice_in_dim(mod_row[2], position, width, 0)
    return (latents.astype(F32) + gate[None, :] * summed).astype(BF)


def solution(mesh):
    fine = Mesh(
        mesh.devices.reshape(GRID, GRID, 2, GRID, GRID), ("y", "zl", "core", "head", "seq")
    )
    in_specs = (
        P(TOKENS, ("head", "seq")),
        P(None, TOKENS, ("head", "seq")),
        P(None, TOKENS, ("head", "seq")),
        P(),
        P(),
        P(("head", "seq"), None),
        P(),
        P(),
        P(),
    )
    out_specs = P(TOKENS, ("head", "seq"))
    return jax.shard_map(
        per_device, mesh=fine, in_specs=in_specs, out_specs=out_specs, check_vma=False
    )
```

time: 238 us -> 220 us (0.924)
  Pallas kernels: 32.5 us -> 27.3 us
  local copies, waits for them, and re-layouts: 9.25 us -> 5 us
  waiting for transfers between devices: 57.9 us -> 55.5 us
    ppermute x5, waiting for transfers between devices: 16 us -> 9.48 us  [the longest x1 4.77 us: per_device(): far_high = lax.ppermute(after[half:], 'head', shift(3))]
    broadcast_in_dim x3 -> x0, local copies, waits for them, and re-layouts: 4.72 us -> none  [gather_small(): spread = jnp.broadcast_to(shard[None], (GRID,) + shard.shape)]
    all_to_all x2, waiting for transfers between devices: 17.3 us -> 20.7 us  [the longest x1 17.8 us: per_device(): raw = lax.all_to_all(raw, 'seq', 0, 0, tiled=True)]
    pallas_call x3 -> x4, Pallas kernels: 16.4 us -> 13.3 us  [the longest x1 5.14 us: per_device(): pl.pallas_call(project_kernel, in_specs=[in_smem, in_vmem, in_vmem, pl.Bl...]
  transfers between devices with their start and end apart: 17 -> 17, of which waited for: 11 -> 11; matrix products, arithmetic and copies ran while one was open for 2% -> 0% of each run, Pallas kernels for 8% -> 8%
where the time goes in v6:
time: 220 us; the launch traced here: 216 us
  starting transfers between devices  86.9 us (40%)
  waiting for transfers between devices  55.5 us (25%)
  Pallas kernels  27.3 us (12%)
  blocking collectives  24.4 us (11%)
  between operations  15 us (7%)
  local copies, waits for them, and re-layouts  5 us (2%)
  other arithmetic  2.28 us (1%)
    ppermute x3, starting transfers between devices, per_device(): shares = [lax.ppermute(outs[k], 'head', shift(k)) for k in (2, 1, 3)]  18.4 us
    all_to_all x1, waiting for transfers between devices, per_device(): raw = lax.all_to_all(raw, 'seq', 0, 0, tiled=True)  17.8 us
    ppermute x3, waiting for transfers between devices, per_device(): shares = [lax.ppermute(outs[k], 'head', shift(k)) for k in (2, 1, 3)]  15.5 us
    ppermute x1, starting transfers between devices, per_device(): far_low = lax.ppermute(before[:half], 'head', shift(1))  15.1 us
    all_to_all x1, blocking collectives, per_device(): parts = lax.all_to_all(parts, ('y', 'core'), 0, 0, tiled=True)  14.7 us
    all_to_all x1, blocking collectives, per_device(): around = lax.all_to_all(around, 'seq', 0, 0, tiled=True)  9.66 us
    ppermute x1, starting transfers between devices, per_device(): before = lax.ppermute(latents, 'head', shift(1))  9.65 us
    ppermute x3, starting transfers between devices, per_device(): lax.ppermute(queries, 'y', shift(k))  9.53 us
  transfers between devices with their start and end apart: 17, of which 11 were waited for; matrix products, arithmetic and copies ran while one was open for 0% of the time, Pallas kernels for 8%

profile of v6, /device:TPU:1, one launch (start us, length us, event | category | flops | bytes accessed | tf_op | source)
XLA Modules:
  0.0 216.4 jit_solution(12092762290954100396)
XLA Ops:
  6.5 0.0 copy-start
  6.5 0.0 all-gather.2.cloned.1.call-start
  7.3 1.9 average.1
  9.2 0.0 all-gather.2.cloned.1.call-update
  9.2 9.6 %collective-permute-start = (bf16[192,384]{1,0:T(8,128)(2,1)}, bf16[192,384]{1,0:T(8,128)(2,1)S(1)}, u32[]{:S(2)}, u32[]{:S(2)}) collective-permute-start(bf16[192,384]{1,0:T(8,128)(2,1)} %own_ref.1), channel_id=1, source_target_pairs={{0,4},{4,8},{8,12},{12,0},{1,5},{5,9},{9,13},{13,1},{2,6},{6,10},{... | collective-permute-start | bytes 442376 | tf_op jit(solution)/shard_map/ppermute | solution.py:237
  18.8 5.6 %collective-permute-start.2 = (bf16[192,384]{1,0:T(8,128)(2,1)}, bf16[192,384]{1,0:T(8,128)(2,1)S(1)}, u32[]{:S(2)}, u32[]{:S(2)}) collective-permute-start(bf16[192,384]{1,0:T(8,128)(2,1)} %own_ref.1), channel_id=1, source_target_pairs={{0,12},{4,0},{8,4},{12,8},{1,13},{5,1},{9,5},{13,9},{2,14},{6,2},{... | collective-permute-start | bytes 442376 | tf_op jit(solution)/shard_map/ppermute | solution.py:238
  24.4 1.5 collective-permute-done.before_ref
  25.9 15.1 %collective-permute-start.1 = (bf16[96,384]{1,0:T(8,128)(2,1)S(1)}, bf16[96,384]{1,0:T(8,128)(2,1)S(1)}, u32[]{:S(2)}, u32[]{:S(2)}) collective-permute-start(bf16[96,384]{1,0:T(8,128)(2,1)S(1)} %slice.13), channel_id=1, source_target_pairs={{0,4},{4,8},{8,12},{12,0},{1,5},{5,9},{9,13},{13,1},{2,6},{6,10},{... | collective-permute-start | bytes 221192 | tf_op jit(solution)/shard_map/ppermute | solution.py:239
  41.0 0.0 collective-permute-done.2.after_ref
  41.0 0.0 copy-start.9
  41.0 3.3 %collective-permute-start.3 = (bf16[96,384]{1,0:T(8,128)(2,1)S(1)}, bf16[96,384]{1,0:T(8,128)(2,1)S(1)}, u32[]{:S(2)}, u32[]{:S(2)}) collective-permute-start(bf16[96,384]{1,0:T(8,128)(2,1)S(1)} %slice.14), channel_id=1, source_target_pairs={{0,12},{4,0},{8,4},{12,8},{1,13},{5,1},{9,5},{13,9},{2,14},{6,2},{... | collective-permute-start | bytes 221192 | tf_op jit(solution)/shard_map/ppermute | solution.py:240
  44.3 2.2 %collective-permute-done.1.low_ref = bf16[96,384]{1,0:T(8,128)(2,1)S(1)} collective-permute-done((bf16[96,384]{1,0:T(8,128)(2,1)S(1)}, bf16[96,384]{1,0:T(8,128)(2,1)S(1)}, u32[]{:S(2)}, u32[]{:S(2)}) %collective-permute-start.1) | collective-permute-done | bytes 73760 | tf_op jit(solution)/shard_map/ppermute | solution.py:239
  46.5 4.8 %collective-permute-done.3.high_ref = bf16[96,384]{1,0:T(8,128)(2,1)S(1)} collective-permute-done((bf16[96,384]{1,0:T(8,128)(2,1)S(1)}, bf16[96,384]{1,0:T(8,128)(2,1)S(1)}, u32[]{:S(2)}, u32[]{:S(2)}) %collective-permute-start.3) | collective-permute-done | bytes 73760 | tf_op jit(solution)/shard_map/ppermute | solution.py:240
  51.3 0.0 copy-done.8
  51.3 0.0 copy-done.9
  51.3 0.0 copy-done.10
  51.3 0.0 copy-start.11
  51.3 0.6 copy-done.11
  51.9 2.7 %spread.1 = bf16[4,4,192,384]{3,2,1,0:T(8,128)(2,1)} custom-call(bf16[192,384]{1,0:T(8,128)(2,1)} %own_ref.1, bf16[192,384]{1,0:T(8,128)(2,1)} %copy-done.8, bf16[96,384]{1,0:T(8,128)(2,1)} %copy-done.10, bf16[96,384]{1,0:T(8,128)(2,1)} %copy-done.11, bf16[192,384]{1,0:T(8,128)(2,1)} %copy-done.9), custom_call_target="tpu_custom_call" | custom-call | tf_op jit(solution)/shard_map/spread/pallas_call | solution.py:243
  54.6 4.0 %all-to-all-start = ((bf16[4,4,192,384]{3,2,1,0:T(8,128)(2,1)}), bf16[4,4,192,384]{3,2,1,0:T(8,128)(2,1)S(1)}, u32[]{:S(2)}, u32[]{:S(2)}) async-start(bf16[4,4,192,384]{3,2,1,0:T(8,128)(2,1)} %spread.1), calls=%async_computation | async-start | bytes 4718592 | tf_op jit(solution)/shard_map/all_to_all | solution.py:250
  59.3 0.0 copy-done
  59.3 0.2 dynamic-slice_reduce_fusion
  59.5 0.1 reshape.15.mod_ref
  59.6 0.6 pad_add_fusion.place_ref
  60.2 5.2 %pick.1 = (bf16[4,256,384]{2,1,0:T(8,128)(2,1)}, bf16[4,256,384]{2,1,0:T(8,128)(2,1)}, bf16[4,256,384]{2,1,0:T(8,128)(2,1)}, bf16[4,256,384]{2,1,0:T(8,128)(2,1)}) custom-call(s32[4]{0:T(128)} %pad_add_fusion.place_ref, bf16[256,6144]{1,0:T(8,128)(2,1)} %refs_3_.1, bf16[256,6144]{1,0:T(8,128)(2,1)} %refs_3_.1, bf16[256,6144]{1,0:T(8,128)(2,1)} %refs_3_.1, ...), custom_call_target="tpu_custom_call" | custom-call | tf_op jit(solution)/shard_map/pick/pallas_call | solution.py:223
  65.4 17.8 %all-to-all-done.raw_ref = bf16[4,4,192,384]{3,2,1,0:T(8,128)(2,1)S(1)} async-done(((bf16[4,4,192,384]{3,2,1,0:T(8,128)(2,1)}), bf16[4,4,192,384]{3,2,1,0:T(8,128)(2,1)S(1)}, u32[]{:S(2)}, u32[]{:S(2)}) %all-to-all-start) | async-done | bytes 2359328 | tf_op jit(solution)/shard_map/all_to_all | solution.py:250
  83.2 0.0 copy-done.5
  83.2 4.3 %norm.1.own_ref = bf16[192,6144]{1,0:T(8,128)(2,1)S(1)} custom-call(s32[4]{0:T(128)S(1)} %copy-done.5, bf16[4,4,192,384]{3,2,1,0:T(8,128)(2,1)S(1)} %all-to-all-done.raw_ref, f32[3,4,4,384]{3,2,1,0:T(4,128)S(1)} %reshape.15.mod_ref), custom_call_target="tpu_custom_call" | custom-call | tf_op jit(solution)/shard_map/norm/pallas_call | solution.py:254
  87.4 7.5 %collective-permute-start.4 = (bf16[192,6144]{1,0:T(8,128)(2,1)S(1)}, bf16[192,6144]{1,0:T(8,128)(2,1)S(1)}, u32[]{:S(2)}, u32[]{:S(2)}) collective-permute-start(bf16[192,6144]{1,0:T(8,128)(2,1)S(1)} %norm.1.own_ref), channel_id=1, source_target_pairs={{0,16},{16,0},{1,17},{17,1},{2,18},{18,2},{3,19},{19,3},{4,20},{20... | collective-permute-start | bytes 7077896 | tf_op jit(solution)/shard_map/ppermute | solution.py:266
  94.9 0.0 copy-start.1
  94.9 1.4 copy-done.1
  96.3 2.8 %collective-permute-done.4.other_ref = bf16[192,6144]{1,0:T(8,128)(2,1)S(1)} collective-permute-done((bf16[192,6144]{1,0:T(8,128)(2,1)S(1)}, bf16[192,6144]{1,0:T(8,128)(2,1)S(1)}, u32[]{:S(2)}, u32[]{:S(2)}) %collective-permute-start.4) | collective-permute-done | bytes 2359328 | tf_op jit(solution)/shard_map/ppermute | solution.py:266
  99.1 2.0 all-gather.2.cloned.1.call-done.weight_ref
  101.1 0.0 copy-done.7
  101.1 1.7 copy-done.2
  102.8 5.1 %project.1 = (bf16[2,192,128]{2,1,0:T(8,128)(2,1)S(1)}, bf16[4,2,2,192,128]{4,3,2,1,0:T(8,128)(2,1)S(1)}) custom-call(s32[4]{0:T(128)S(1)} %copy-done.5, bf16[192,6144]{1,0:T(8,128)(2,1)S(1)} %copy-done.2, bf16[192,6144]{1,0:T(8,128)(2,1)S(1)} %collective-permute-done.4.other_ref, bf16[2,6144,384]{2,1,0:T(8,128)(2,1)} %all-gather.2.cloned.1.call-done.weight_ref, ...), custom_call_target="tpu_custom_call" | custom-call | tf_op jit(solution)/shard_map/project/pallas_call | solution.py:269
  107.9 0.9 copy-done.3
  108.8 4.7 %all-to-all-start.1 = ((bf16[4,2,2,192,128]{4,3,2,1,0:T(8,128)(2,1)}), bf16[4,2,2,192,128]{4,3,2,1,0:T(8,128)(2,1)S(1)}, u32[]{:S(2)}, u32[]{:S(2)}) async-start(bf16[4,2,2,192,128]{4,3,2,1,0:T(8,128)(2,1)} %copy-done.3), calls=%async_computation.1 | async-start | bytes 1572864 | tf_op jit(solution)/shard_map/all_to_all | solution.py:285
  113.6 3.7 %collective-permute-start.8 = (bf16[4,256,384]{2,1,0:T(8,128)(2,1)}, bf16[4,256,384]{2,1,0:T(8,128)(2,1)S(1)}, u32[]{:S(2)}, u32[]{:S(2)}) collective-permute-start(bf16[4,256,384]{2,1,0:T(8,128)(2,1)} %get-tuple-element.29), channel_id=1, source_target_pairs={{0,2},{1,3},{2,0},{3,1},{4,6},{5,7},{6,4},{7,5},{8,10},{9,11},{10,... | collective-permute-start | bytes 2359304 | tf_op jit(solution)/shard_map/ppermute | solution.py:253
  117.2 2.7 %collective-permute-start.5 = (bf16[2,192,128]{2,1,0:T(8,128)(2,1)S(1)}, bf16[2,192,128]{2,1,0:T(8,128)(2,1)S(1)}, u32[]{:S(2)}, u32[]{:S(2)}) collective-permute-start(bf16[2,192,128]{2,1,0:T(8,128)(2,1)S(1)} %get-tuple-element.26.q0), channel_id=1, source_target_pairs={{0,128},{128,256},{256,384},{384,0},{1,129},{129,257},{257,385},{3... | collective-permute-start | bytes 294920 | tf_op jit(solution)/shard_map/ppermute | solution.py:286
  119.9 4.7 %collective-permute-start.6 = (bf16[2,192,128]{2,1,0:T(8,128)(2,1)S(1)}, bf16[2,192,128]{2,1,0:T(8,128)(2,1)S(1)}, u32[]{:S(2)}, u32[]{:S(2)}) collective-permute-start(bf16[2,192,128]{2,1,0:T(8,128)(2,1)S(1)} %get-tuple-element.26.q0), channel_id=1, source_target_pairs={{0,256},{128,384},{256,0},{384,128},{1,257},{129,385},{257,1},{385... | collective-permute-start | bytes 294920 | tf_op jit(solution)/shard_map/ppermute | solution.py:286
  124.6 2.2 collective-permute-start.7
  126.8 0.0 collective-permute-done.5.q1
  126.8 0.5 collective-permute-done.6.q2
  127.3 3.0 %collective-permute-done.7.q3 = bf16[2,192,128]{2,1,0:T(8,128)(2,1)S(1)} collective-permute-done((bf16[2,192,128]{2,1,0:T(8,128)(2,1)S(1)}, bf16[2,192,128]{2,1,0:T(8,128)(2,1)S(1)}, u32[]{:S(2)}, u32[]{:S(2)}) %collective-permute-start.7) | collective-permute-done | bytes 98336 | tf_op jit(solution)/shard_map/ppermute | solution.py:286
  130.3 3.0 %all-to-all-done.1.kv_ref = bf16[4,2,2,192,128]{4,3,2,1,0:T(8,128)(2,1)S(1)} async-done(((bf16[4,2,2,192,128]{4,3,2,1,0:T(8,128)(2,1)}), bf16[4,2,2,192,128]{4,3,2,1,0:T(8,128)(2,1)S(1)}, u32[]{:S(2)}, u32[]{:S(2)}) %all-to-all-start.1) | async-done | bytes 786464 | tf_op jit(solution)/shard_map/all_to_all | solution.py:285
  133.3 3.6 %attend.1 = bf16[8,208,128]{2,1,0:T(8,128)(2,1)S(1)} custom-call(s32[4]{0:T(128)S(1)} %copy-done.5, bf16[2,192,128]{2,1,0:T(8,128)(2,1)S(1)} %get-tuple-element.26.q0, bf16[2,192,128]{2,1,0:T(8,128)(2,1)S(1)} %collective-permute-done.5.q1, bf16[2,192,128]{2,1,0:T(8,128)(2,1)S(1)} %collective-permute-done.6.q2, ...), custom_call_target="tpu_custom_call" | custom-call | tf_op jit(solution)/shard_map/attend/pallas_call | solution.py:289
  136.8 0.0 collective-permute-done.8.w2
  136.8 3.6 %collective-permute-start.10 = (bf16[4,256,384]{2,1,0:T(8,128)(2,1)}, bf16[4,256,384]{2,1,0:T(8,128)(2,1)S(1)}, u32[]{:S(2)}, u32[]{:S(2)}) collective-permute-start(bf16[4,256,384]{2,1,0:T(8,128)(2,1)} %get-tuple-element.33), channel_id=1, source_target_pairs={{0,3},{1,0},{2,1},{3,2},{4,7},{5,4},{6,5},{7,6},{8,11},{9,8},{10,9... | collective-permute-start | bytes 2359304 | tf_op jit(solution)/shard_map/ppermute | solution.py:304
  140.5 1.9 collective-permute-start.9
  142.4 14.7 %all_to_all.20.parts_ref = bf16[8,208,128]{2,1,0:T(8,128)(2,1)} all-to-all(bf16[8,208,128]{2,1,0:T(8,128)(2,1)S(1)} %attend.1), channel_id=1, replica_groups=mesh['y'=4,'zl'=4,'core'=2,'head'=4,'seq'=4] {'y','core'}, dimensions={0} | all-to-all | bytes 851968 | tf_op jit(solution)/shard_map/all_to_all | solution.py:302
  157.2 1.9 combine.1
  159.1 0.0 collective-permute-done.10.w3
  159.1 2.5 %collective-permute-done.9.w1 = bf16[4,256,384]{2,1,0:T(8,128)(2,1)} collective-permute-done((bf16[4,256,384]{2,1,0:T(8,128)(2,1)}, bf16[4,256,384]{2,1,0:T(8,128)(2,1)}, u32[]{:S(2)}, u32[]{:S(2)}) %collective-permute-start.9) | collective-permute-done | bytes 786464 | tf_op jit(solution)/shard_map/ppermute | solution.py:303
  161.6 9.7 %all_to_all.21.a_ref = bf16[4,192,256]{2,1,0:T(8,128)(2,1)S(1)} all-to-all(bf16[4,192,256]{2,1,0:T(8,128)(2,1)} %combine.1), channel_id=1, replica_groups=mesh['y'=4,'zl'=4,'core'=2,'head'=4,'seq'=4] {'seq'}, dimensions={0} | all-to-all | bytes 786432 | tf_op jit(solution)/shard_map/all_to_all | solution.py:313
  171.2 2.6 %branch.1 = (bf16[192,384]{1,0:T(8,128)(2,1)S(1)}, bf16[192,384]{1,0:T(8,128)(2,1)S(1)}, bf16[192,384]{1,0:T(8,128)(2,1)}, bf16[192,384]{1,0:T(8,128)(2,1)S(1)}) custom-call(s32[4]{0:T(128)S(1)} %copy-done.5, bf16[4,192,256]{2,1,0:T(8,128)(2,1)S(1)} %all_to_all.21.a_ref, bf16[4,256,384]{2,1,0:T(8,128)(2,1)S(1)} %copy-done.4, ...), custom_call_target="tpu_custom_call" | custom-call | tf_op jit(solution)/shard_map/branch/pallas_call | solution.py:314
  173.8 9.2 %collective-permute-start.11 = (bf16[192,384]{1,0:T(8,128)(2,1)}, bf16[192,384]{1,0:T(8,128)(2,1)S(1)}, u32[]{:S(2)}, u32[]{:S(2)}) collective-permute-start(bf16[192,384]{1,0:T(8,128)(2,1)} %get-tuple-element.40), channel_id=1, source_target_pairs={{0,8},{4,12},{8,0},{12,4},{1,9},{5,13},{9,1},{13,5},{2,10},{6,14},... | collective-permute-start | bytes 442376 | tf_op jit(solution)/shard_map/ppermute | solution.py:322
  183.0 3.7 %collective-permute-start.12 = (bf16[192,384]{1,0:T(8,128)(2,1)S(1)}, bf16[192,384]{1,0:T(8,128)(2,1)S(1)}, u32[]{:S(2)}, u32[]{:S(2)}) collective-permute-start(bf16[192,384]{1,0:T(8,128)(2,1)S(1)} %get-tuple-element.41), channel_id=1, source_target_pairs={{0,4},{4,8},{8,12},{12,0},{1,5},{5,9},{9,13},{13,1},{2,6},{6,10},{... | collective-permute-start | bytes 442376 | tf_op jit(solution)/shard_map/ppermute | solution.py:322
  186.7 5.5 %collective-permute-start.13 = (bf16[192,384]{1,0:T(8,128)(2,1)S(1)}, bf16[192,384]{1,0:T(8,128)(2,1)S(1)}, u32[]{:S(2)}, u32[]{:S(2)}) collective-permute-start(bf16[192,384]{1,0:T(8,128)(2,1)S(1)} %get-tuple-element.42), channel_id=1, source_target_pairs={{0,12},{4,0},{8,4},{12,8},{1,13},{5,1},{9,5},{13,9},{2,14},{6,2},{... | collective-permute-start | bytes 442376 | tf_op jit(solution)/shard_map/ppermute | solution.py:322
  192.2 0.1 dynamic-slice_reduce_fusion.1
  192.3 0.0 collective-permute-done.11
  192.3 15.5 %collective-permute-done.12 = bf16[192,384]{1,0:T(8,128)(2,1)S(1)} collective-permute-done((bf16[192,384]{1,0:T(8,128)(2,1)S(1)}, bf16[192,384]{1,0:T(8,128)(2,1)S(1)}, u32[]{:S(2)}, u32[]{:S(2)}) %collective-permute-start.12) | collective-permute-done | bytes 147488 | tf_op jit(solution)/shard_map/ppermute | solution.py:322
  207.8 0.0 collective-permute-done.13
  207.8 1.7 add_convert_fusion
  (12 shorter events, 0.0 us)
Async XLA Ops:
  6.5 52.8 %copy-start = (f32[8,3,6144]{2,0,1:T(8,128)S(1)}, f32[8,3,6144]{2,0,1:T(8,128)}, u32[]{:S(2)}) copy-start(f32[8,3,6144]{2,0,1:T(8,128)} %param.15) | copy-start | bytes 1769476
  6.5 94.6 %all-gather.2.cloned.1.call-start = ((), (), s32[]{:S(2)}) async-start(), calls=%async_computation.4 | async-start | bytes 9732096 | tf_op jit(solution)/shard_map/all_gather | solution.py:214
  9.2 16.7 %collective-permute-start = (bf16[192,384]{1,0:T(8,128)(2,1)}, bf16[192,384]{1,0:T(8,128)(2,1)S(1)}, u32[]{:S(2)}, u32[]{:S(2)}) collective-permute-start(bf16[192,384]{1,0:T(8,128)(2,1)} %own_ref.1), channel_id=1, source_target_pairs={{0,4},{4,8},{8,12},{12,0},{1,5},{5,9},{9,13},{13,1},{2,6},{6,10},{... | collective-permute-start | bytes 442376 | tf_op jit(solution)/shard_map/ppermute | solution.py:237
  18.8 22.1 %collective-permute-start.2 = (bf16[192,384]{1,0:T(8,128)(2,1)}, bf16[192,384]{1,0:T(8,128)(2,1)S(1)}, u32[]{:S(2)}, u32[]{:S(2)}) collective-permute-start(bf16[192,384]{1,0:T(8,128)(2,1)} %own_ref.1), channel_id=1, source_target_pairs={{0,12},{4,0},{8,4},{12,8},{1,13},{5,1},{9,5},{13,9},{2,14},{6,2},{... | collective-permute-start | bytes 442376 | tf_op jit(solution)/shard_map/ppermute | solution.py:238
  25.9 25.4 %copy-start.8 = (bf16[192,384]{1,0:T(8,128)(2,1)}, bf16[192,384]{1,0:T(8,128)(2,1)S(1)}, u32[]{:S(2)}) copy-start(bf16[192,384]{1,0:T(8,128)(2,1)S(1)} %collective-permute-done.before_ref) | copy-start | bytes 442372
  25.9 20.6 %collective-permute-start.1 = (bf16[96,384]{1,0:T(8,128)(2,1)S(1)}, bf16[96,384]{1,0:T(8,128)(2,1)S(1)}, u32[]{:S(2)}, u32[]{:S(2)}) collective-permute-start(bf16[96,384]{1,0:T(8,128)(2,1)S(1)} %slice.13), channel_id=1, source_target_pairs={{0,4},{4,8},{8,12},{12,0},{1,5},{5,9},{9,13},{13,1},{2,6},{6,10},{... | collective-permute-start | bytes 221192 | tf_op jit(solution)/shard_map/ppermute | solution.py:239
  41.0 10.3 %copy-start.9 = (bf16[192,384]{1,0:T(8,128)(2,1)}, bf16[192,384]{1,0:T(8,128)(2,1)S(1)}, u32[]{:S(2)}) copy-start(bf16[192,384]{1,0:T(8,128)(2,1)S(1)} %collective-permute-done.2.after_ref) | copy-start | bytes 442372
  41.0 10.3 %collective-permute-start.3 = (bf16[96,384]{1,0:T(8,128)(2,1)S(1)}, bf16[96,384]{1,0:T(8,128)(2,1)S(1)}, u32[]{:S(2)}, u32[]{:S(2)}) collective-permute-start(bf16[96,384]{1,0:T(8,128)(2,1)S(1)} %slice.14), channel_id=1, source_target_pairs={{0,12},{4,0},{8,4},{12,8},{1,13},{5,1},{9,5},{13,9},{2,14},{6,2},{... | collective-permute-start | bytes 221192 | tf_op jit(solution)/shard_map/ppermute | solution.py:240
  46.5 4.8 %copy-start.10 = (bf16[96,384]{1,0:T(8,128)(2,1)}, bf16[96,384]{1,0:T(8,128)(2,1)S(1)}, u32[]{:S(2)}) copy-start(bf16[96,384]{1,0:T(8,128)(2,1)S(1)} %collective-permute-done.1.low_ref) | copy-start | bytes 221188
  51.3 0.6 copy-start.11
  54.6 28.5 %all-to-all-start = ((bf16[4,4,192,384]{3,2,1,0:T(8,128)(2,1)}), bf16[4,4,192,384]{3,2,1,0:T(8,128)(2,1)S(1)}, u32[]{:S(2)}, u32[]{:S(2)}) async-start(bf16[4,4,192,384]{3,2,1,0:T(8,128)(2,1)} %spread.1), calls=%async_computation | async-start | bytes 4718592 | tf_op jit(solution)/shard_map/all_to_all | solution.py:250
  60.2 23.0 %copy-start.5 = (s32[4]{0:T(128)S(1)}, s32[4]{0:T(128)}, u32[]{:S(2)}) copy-start(s32[4]{0:T(128)} %pad_add_fusion.place_ref) | copy-start | bytes 52
  83.2 17.9 %copy-start.6 = (f32[128]{0:T(128)S(1)}, f32[128]{0:T(128)}, u32[]{:S(2)}) copy-start(f32[128]{0:T(128)} %param.12) | copy-start | bytes 1540
  83.2 17.9 %copy-start.7 = (f32[128]{0:T(128)S(1)}, f32[128]{0:T(128)}, u32[]{:S(2)}) copy-start(f32[128]{0:T(128)} %param.13) | copy-start | bytes 1540
  87.4 11.6 %collective-permute-start.4 = (bf16[192,6144]{1,0:T(8,128)(2,1)S(1)}, bf16[192,6144]{1,0:T(8,128)(2,1)S(1)}, u32[]{:S(2)}, u32[]{:S(2)}) collective-permute-start(bf16[192,6144]{1,0:T(8,128)(2,1)S(1)} %norm.1.own_ref), channel_id=1, source_target_pairs={{0,16},{16,0},{1,17},{17,1},{2,18},{18,2},{3,19},{19,3},{4,20},{20... | collective-permute-start | bytes 7077896 | tf_op jit(solution)/shard_map/ppermute | solution.py:266
  94.9 1.4 copy-start.1
  101.1 1.7 copy-start.2
  107.9 0.9 copy-start.3
  108.8 24.4 %all-to-all-start.1 = ((bf16[4,2,2,192,128]{4,3,2,1,0:T(8,128)(2,1)}), bf16[4,2,2,192,128]{4,3,2,1,0:T(8,128)(2,1)S(1)}, u32[]{:S(2)}, u32[]{:S(2)}) async-start(bf16[4,2,2,192,128]{4,3,2,1,0:T(8,128)(2,1)} %copy-done.3), calls=%async_computation.1 | async-start | bytes 1572864 | tf_op jit(solution)/shard_map/all_to_all | solution.py:285
  113.6 57.7 %copy-start.4 = (bf16[4,256,384]{2,1,0:T(8,128)(2,1)S(1)}, bf16[4,256,384]{2,1,0:T(8,128)(2,1)}, u32[]{:S(2)}) copy-start(bf16[4,256,384]{2,1,0:T(8,128)(2,1)} %get-tuple-element.35.w0) | copy-start | bytes 2359300
  113.6 23.3 %collective-permute-start.8 = (bf16[4,256,384]{2,1,0:T(8,128)(2,1)}, bf16[4,256,384]{2,1,0:T(8,128)(2,1)S(1)}, u32[]{:S(2)}, u32[]{:S(2)}) collective-permute-start(bf16[4,256,384]{2,1,0:T(8,128)(2,1)} %get-tuple-element.29), channel_id=1, source_target_pairs={{0,2},{1,3},{2,0},{3,1},{4,6},{5,7},{6,4},{7,5},{8,10},{9,11},{10,... | collective-permute-start | bytes 2359304 | tf_op jit(solution)/shard_map/ppermute | solution.py:253
  117.2 9.6 %collective-permute-start.5 = (bf16[2,192,128]{2,1,0:T(8,128)(2,1)S(1)}, bf16[2,192,128]{2,1,0:T(8,128)(2,1)S(1)}, u32[]{:S(2)}, u32[]{:S(2)}) collective-permute-start(bf16[2,192,128]{2,1,0:T(8,128)(2,1)S(1)} %get-tuple-element.26.q0), channel_id=1, source_target_pairs={{0,128},{128,256},{256,384},{384,0},{1,129},{129,257},{257,385},{3... | collective-permute-start | bytes 294920 | tf_op jit(solution)/shard_map/ppermute | solution.py:286
  119.9 7.4 %collective-permute-start.6 = (bf16[2,192,128]{2,1,0:T(8,128)(2,1)S(1)}, bf16[2,192,128]{2,1,0:T(8,128)(2,1)S(1)}, u32[]{:S(2)}, u32[]{:S(2)}) collective-permute-start(bf16[2,192,128]{2,1,0:T(8,128)(2,1)S(1)} %get-tuple-element.26.q0), channel_id=1, source_target_pairs={{0,256},{128,384},{256,0},{384,128},{1,257},{129,385},{257,1},{385... | collective-permute-start | bytes 294920 | tf_op jit(solution)/shard_map/ppermute | solution.py:286
  124.6 5.7 %collective-permute-start.7 = (bf16[2,192,128]{2,1,0:T(8,128)(2,1)S(1)}, bf16[2,192,128]{2,1,0:T(8,128)(2,1)S(1)}, u32[]{:S(2)}, u32[]{:S(2)}) collective-permute-start(bf16[2,192,128]{2,1,0:T(8,128)(2,1)S(1)} %get-tuple-element.26.q0), channel_id=1, source_target_pairs={{0,384},{128,0},{256,128},{384,256},{1,385},{129,1},{257,129},{385... | collective-permute-start | bytes 294920 | tf_op jit(solution)/shard_map/ppermute | solution.py:286
  136.8 22.2 %collective-permute-start.10 = (bf16[4,256,384]{2,1,0:T(8,128)(2,1)}, bf16[4,256,384]{2,1,0:T(8,128)(2,1)S(1)}, u32[]{:S(2)}, u32[]{:S(2)}) collective-permute-start(bf16[4,256,384]{2,1,0:T(8,128)(2,1)} %get-tuple-element.33), channel_id=1, source_target_pairs={{0,3},{1,0},{2,1},{3,2},{4,7},{5,4},{6,5},{7,6},{8,11},{9,8},{10,9... | collective-permute-start | bytes 2359304 | tf_op jit(solution)/shard_map/ppermute | solution.py:304
  140.5 21.1 %collective-permute-start.9 = (bf16[4,256,384]{2,1,0:T(8,128)(2,1)}, bf16[4,256,384]{2,1,0:T(8,128)(2,1)}, u32[]{:S(2)}, u32[]{:S(2)}) collective-permute-start(bf16[4,256,384]{2,1,0:T(8,128)(2,1)} %get-tuple-element.32), channel_id=1, source_target_pairs={{0,1},{1,2},{2,3},{3,0},{4,5},{5,6},{6,7},{7,4},{8,9},{9,10},{10,1... | collective-permute-start | bytes 2359304 | tf_op jit(solution)/shard_map/ppermute | solution.py:303
  173.8 18.5 %collective-permute-start.11 = (bf16[192,384]{1,0:T(8,128)(2,1)}, bf16[192,384]{1,0:T(8,128)(2,1)S(1)}, u32[]{:S(2)}, u32[]{:S(2)}) collective-permute-start(bf16[192,384]{1,0:T(8,128)(2,1)} %get-tuple-element.40), channel_id=1, source_target_pairs={{0,8},{4,12},{8,0},{12,4},{1,9},{5,13},{9,1},{13,5},{2,10},{6,14},... | collective-permute-start | bytes 442376 | tf_op jit(solution)/shard_map/ppermute | solution.py:322
  183.0 24.8 %collective-permute-start.12 = (bf16[192,384]{1,0:T(8,128)(2,1)S(1)}, bf16[192,384]{1,0:T(8,128)(2,1)S(1)}, u32[]{:S(2)}, u32[]{:S(2)}) collective-permute-start(bf16[192,384]{1,0:T(8,128)(2,1)S(1)} %get-tuple-element.41), channel_id=1, source_target_pairs={{0,4},{4,8},{8,12},{12,0},{1,5},{5,9},{9,13},{13,1},{2,6},{6,10},{... | collective-permute-start | bytes 442376 | tf_op jit(solution)/shard_map/ppermute | solution.py:322
  186.7 21.2 %collective-permute-start.13 = (bf16[192,384]{1,0:T(8,128)(2,1)S(1)}, bf16[192,384]{1,0:T(8,128)(2,1)S(1)}, u32[]{:S(2)}, u32[]{:S(2)}) collective-permute-start(bf16[192,384]{1,0:T(8,128)(2,1)S(1)} %get-tuple-element.42), channel_id=1, source_target_pairs={{0,12},{4,0},{8,4},{12,8},{1,13},{5,1},{9,5},{13,9},{2,14},{6,2},{... | collective-permute-start | bytes 442376 | tf_op jit(solution)/shard_map/ppermute | solution.py:322
Sparse Core Ops, SparseCore 0:
  9.5 91.6 all-gather.1

commit v7 on v6

--- a/solution.py
+++ b/solution.py
@@ -33,14 +33,16 @@
             out_ref[h, :, j * HD : (j + 1) * HD] = (decay * ema + (1.0 - decay) * train).astype(BF)
 
 
-def spread_kernel(own_ref, before_ref, low_ref, high_ref, after_ref, out_ref):
-    half = low_ref.shape[0]
-    for copy in range(GRID):
-        out_ref[copy, 0] = own_ref[...]
-        out_ref[copy, 1] = before_ref[...]
-        out_ref[copy, 2, :half] = low_ref[...]
-        out_ref[copy, 2, half:] = high_ref[...]
-        out_ref[copy, 3] = after_ref[...]
+def spread_kernel(r0, r1, r2, r3, out_ref, sems):
+    copies = [
+        pltpu.make_async_copy(ref, out_ref.at[i, k], sems.at[GRID * i + k])
+        for i in range(GRID)
+        for k, ref in enumerate((r0, r1, r2, r3))
+    ]
+    for copy in copies:
+        copy.start()
+    for copy in copies:
+        copy.wait()
 
 
 def norm_kernel(place_ref, raw_ref, mod_ref, sent_ref, out_ref, sems):
@@ -233,20 +235,20 @@
     )(place, *([out_weight] * GRID))
 
     mod_row = lax.dynamic_index_in_dim(modulation, timestep[0], 0, keepdims=False)
-    half = rows // 2
+    far = lax.ppermute(latents, "head", shift(2))
     before = lax.ppermute(latents, "head", shift(1))
     after = lax.ppermute(latents, "head", shift(3))
-    far_low = lax.ppermute(before[:half], "head", shift(1))
-    far_high = lax.ppermute(after[half:], "head", shift(3))
     in_smem = pl.BlockSpec(memory_space=pltpu.SMEM)
     in_vmem = pl.BlockSpec(memory_space=pltpu.VMEM)
+    in_place = pl.BlockSpec(memory_space=pl.ANY)
     raw = pl.pallas_call(
         spread_kernel,
-        in_specs=[in_vmem] * (GRID + 1),
-        out_specs=in_vmem,
+        in_specs=[in_place] * GRID,
+        out_specs=in_place,
         out_shape=jax.ShapeDtypeStruct((GRID, GRID, rows, width), BF),
+        scratch_shapes=[pltpu.SemaphoreType.DMA((blocks,))],
         name="spread",
-    )(latents, before, far_low, far_high, after)
+    )(latents, before, far, after)
     raw = lax.all_to_all(raw, "seq", 0, 0, tiled=True)
     out0, out1, out2, out3 = out_parts
     raw, out2 = lax.optimization_barrier((raw, out2))

time: 220 us -> 296 us (1.35)
  Pallas kernels: 27.3 us -> 97.2 us
  waiting for transfers between devices: 55.5 us -> 64.4 us
    pallas_call x1, Pallas kernels: 2.71 us -> 72.7 us  [per_device(): pl.pallas_call(spread_kernel, in_specs=[in_place] * GRID, out_specs=in_pl...]
    ppermute x2 -> x1, waiting for transfers between devices: 6.97 us -> 15.9 us  [per_device(): far = lax.ppermute(latents, 'head', shift(2))]
    ppermute x2 -> x1, starting transfers between devices: 18.3 us -> 10.6 us  [per_device(): far = lax.ppermute(latents, 'head', shift(2))]
    ppermute x3, waiting for transfers between devices: 15.5 us -> 22.1 us  [per_device(): shares = [lax.ppermute(outs[k], 'head', shift(k)) for k in (2, 1, 3)]]
    all_to_all x1, starting transfers between devices: 4.73 us -> 11.2 us  [per_device(): pairs = lax.all_to_all(pairs, 'zl', 0, 0, tiled=True)]
  transfers between devices with their start and end apart: 17 -> 16, of which waited for: 11 -> 9; matrix products, arithmetic and copies ran while one was open for 0% -> 0% of each run, Pallas kernels for 8% -> 30%
where the time goes in v7:
time: 296 us; the launch traced here: 295 us
  Pallas kernels  97.2 us (33%)
  starting transfers between devices  86.1 us (29%)
  waiting for transfers between devices  64.4 us (22%)
  blocking collectives  24.4 us (8%)
  between operations  15 us (5%)
  local copies, waits for them, and re-layouts  5.68 us (2%)
    pallas_call x1, Pallas kernels, per_device(): pl.pallas_call(spread_kernel, in_specs=[in_place] * GRID, out_specs=in_pl...  72.7 us
    ppermute x3, waiting for transfers between devices, per_device(): shares = [lax.ppermute(outs[k], 'head', shift(k)) for k in (2, 1, 3)]  22.1 us
    ppermute x3, starting transfers between devices, per_device(): shares = [lax.ppermute(outs[k], 'head', shift(k)) for k in (2, 1, 3)]  17.6 us
    all_to_all x1, waiting for transfers between devices, per_device(): raw = lax.all_to_all(raw, 'seq', 0, 0, tiled=True)  16 us
    ppermute x1, waiting for transfers between devices, per_device(): far = lax.ppermute(latents, 'head', shift(2))  15.9 us
    all_to_all x1, blocking collectives, per_device(): parts = lax.all_to_all(parts, ('y', 'core'), 0, 0, tiled=True)  14.6 us
    all_to_all x1, starting transfers between devices, per_device(): pairs = lax.all_to_all(pairs, 'zl', 0, 0, tiled=True)  11.2 us
    ppermute x1, starting transfers between devices, per_device(): far = lax.ppermute(latents, 'head', shift(2))  10.6 us
  transfers between devices with their start and end apart: 16, of which 9 were waited for; matrix products, arithmetic and copies ran while one was open for 0% of the time, Pallas kernels for 30%

profile of v7, /device:TPU:1, one launch (start us, length us, event | category | flops | bytes accessed | tf_op | source)
XLA Modules:
  0.0 295.1 jit_solution(15070625411114497099)
XLA Ops:
  6.5 0.0 copy-start
  6.5 0.0 all-gather.2.cloned.1.call-start
  7.3 1.9 average.1
  9.1 0.0 all-gather.2.cloned.1.call-update
  9.2 9.6 %collective-permute-start = (bf16[192,384]{1,0:T(8,128)(2,1)}, bf16[192,384]{1,0:T(8,128)(2,1)S(1)}, u32[]{:S(2)}, u32[]{:S(2)}) collective-permute-start(bf16[192,384]{1,0:T(8,128)(2,1)} %r0.1), channel_id=1, source_target_pairs={{0,4},{4,8},{8,12},{12,0},{1,5},{5,9},{9,13},{13,1},{2,6},{6,10},{... | collective-permute-start | bytes 442376 | tf_op jit(solution)/shard_map/ppermute | solution.py:239
  18.8 10.6 %collective-permute-start.1 = (bf16[192,384]{1,0:T(8,128)(2,1)}, bf16[192,384]{1,0:T(8,128)(2,1)S(1)}, u32[]{:S(2)}, u32[]{:S(2)}) collective-permute-start(bf16[192,384]{1,0:T(8,128)(2,1)} %r0.1), channel_id=1, source_target_pairs={{0,8},{4,12},{8,0},{12,4},{1,9},{5,13},{9,1},{13,5},{2,10},{6,14},... | collective-permute-start | bytes 442376 | tf_op jit(solution)/shard_map/ppermute | solution.py:238
  29.5 5.2 %collective-permute-start.2 = (bf16[192,384]{1,0:T(8,128)(2,1)}, bf16[192,384]{1,0:T(8,128)(2,1)S(1)}, u32[]{:S(2)}, u32[]{:S(2)}) collective-permute-start(bf16[192,384]{1,0:T(8,128)(2,1)} %r0.1), channel_id=1, source_target_pairs={{0,12},{4,0},{8,4},{12,8},{1,13},{5,1},{9,5},{13,9},{2,14},{6,2},{... | collective-permute-start | bytes 442376 | tf_op jit(solution)/shard_map/ppermute | solution.py:240
  34.7 0.0 collective-permute-done.r1
  34.7 0.0 copy-start.8
  34.7 15.9 %collective-permute-done.1.r2 = bf16[192,384]{1,0:T(8,128)(2,1)S(1)} collective-permute-done((bf16[192,384]{1,0:T(8,128)(2,1)}, bf16[192,384]{1,0:T(8,128)(2,1)S(1)}, u32[]{:S(2)}, u32[]{:S(2)}) %collective-permute-start.1) | collective-permute-done | bytes 147488 | tf_op jit(solution)/shard_map/ppermute | solution.py:238
  50.6 0.0 copy-start.9
  50.6 0.0 collective-permute-done.2.r3
  50.6 0.0 copy-done.8
  50.6 0.6 copy-done.9
  51.3 0.0 copy-start.10
  51.3 0.7 copy-done.10
  52.0 72.7 %spread.1 = bf16[4,4,192,384]{3,2,1,0:T(8,128)(2,1)} custom-call(bf16[192,384]{1,0:T(8,128)(2,1)} %r0.1, bf16[192,384]{1,0:T(8,128)(2,1)} %copy-done.8, bf16[192,384]{1,0:T(8,128)(2,1)} %copy-done.9, bf16[192,384]{1,0:T(8,128)(2,1)} %copy-done.10), custom_call_target="tpu_custom_call" | custom-call | tf_op jit(solution)/shard_map/spread/pallas_call | solution.py:244
  124.7 4.0 %all-to-all-start = ((bf16[4,4,192,384]{3,2,1,0:T(8,128)(2,1)}), bf16[4,4,192,384]{3,2,1,0:T(8,128)(2,1)S(1)}, u32[]{:S(2)}, u32[]{:S(2)}) async-start(bf16[4,4,192,384]{3,2,1,0:T(8,128)(2,1)} %spread.1), calls=%async_computation | async-start | bytes 4718592 | tf_op jit(solution)/shard_map/all_to_all | solution.py:252
  129.4 0.0 copy-done
  129.4 0.2 dynamic-slice_reduce_fusion
  129.6 0.1 reshape.15.mod_ref
  129.7 0.7 pad_add_fusion.place_ref
  130.3 5.1 %pick.1 = (bf16[4,256,384]{2,1,0:T(8,128)(2,1)}, bf16[4,256,384]{2,1,0:T(8,128)(2,1)}, bf16[4,256,384]{2,1,0:T(8,128)(2,1)}, bf16[4,256,384]{2,1,0:T(8,128)(2,1)}) custom-call(s32[4]{0:T(128)} %pad_add_fusion.place_ref, bf16[256,6144]{1,0:T(8,128)(2,1)} %refs_3_.1, bf16[256,6144]{1,0:T(8,128)(2,1)} %refs_3_.1, bf16[256,6144]{1,0:T(8,128)(2,1)} %refs_3_.1, ...), custom_call_target="tpu_custom_call" | custom-call | tf_op jit(solution)/shard_map/pick/pallas_call | solution.py:225
  135.5 16.0 %all-to-all-done.raw_ref = bf16[4,4,192,384]{3,2,1,0:T(8,128)(2,1)S(1)} async-done(((bf16[4,4,192,384]{3,2,1,0:T(8,128)(2,1)}), bf16[4,4,192,384]{3,2,1,0:T(8,128)(2,1)S(1)}, u32[]{:S(2)}, u32[]{:S(2)}) %all-to-all-start) | async-done | bytes 2359328 | tf_op jit(solution)/shard_map/all_to_all | solution.py:252
  151.5 0.0 copy-done.5
  151.5 4.3 %norm.1.own_ref = bf16[192,6144]{1,0:T(8,128)(2,1)S(1)} custom-call(s32[4]{0:T(128)S(1)} %copy-done.5, bf16[4,4,192,384]{3,2,1,0:T(8,128)(2,1)S(1)} %all-to-all-done.raw_ref, f32[3,4,4,384]{3,2,1,0:T(4,128)S(1)} %reshape.15.mod_ref), custom_call_target="tpu_custom_call" | custom-call | tf_op jit(solution)/shard_map/norm/pallas_call | solution.py:256
  155.8 9.2 %collective-permute-start.3 = (bf16[192,6144]{1,0:T(8,128)(2,1)S(1)}, bf16[192,6144]{1,0:T(8,128)(2,1)S(1)}, u32[]{:S(2)}, u32[]{:S(2)}) collective-permute-start(bf16[192,6144]{1,0:T(8,128)(2,1)S(1)} %norm.1.own_ref), channel_id=1, source_target_pairs={{0,16},{16,0},{1,17},{17,1},{2,18},{18,2},{3,19},{19,3},{4,20},{20... | collective-permute-start | bytes 7077896 | tf_op jit(solution)/shard_map/ppermute | solution.py:268
  165.0 0.0 copy-start.1
  165.0 1.4 copy-done.1
  166.4 2.7 collective-permute-done.3.other_ref
  169.1 0.0 copy-done.6
  169.1 0.0 copy-done.7
  169.1 1.7 copy-done.2
  170.8 5.1 %project.1 = (bf16[2,192,128]{2,1,0:T(8,128)(2,1)S(1)}, bf16[4,2,2,192,128]{4,3,2,1,0:T(8,128)(2,1)S(1)}) custom-call(s32[4]{0:T(128)S(1)} %copy-done.5, bf16[192,6144]{1,0:T(8,128)(2,1)S(1)} %copy-done.2, bf16[192,6144]{1,0:T(8,128)(2,1)S(1)} %collective-permute-done.3.other_ref, bf16[2,6144,384]{2,1,0:T(8,128)(2,1)} %all-gather.2.cloned.1.call-done.weight_ref, ...), custom_call_target="tpu_custom_call" | custom-call | tf_op jit(solution)/shard_map/project/pallas_call | solution.py:271
  176.0 0.0 copy-start.3
  176.0 0.9 copy-done.3
  176.8 11.2 %all-to-all-start.1 = ((bf16[4,2,2,192,128]{4,3,2,1,0:T(8,128)(2,1)}), bf16[4,2,2,192,128]{4,3,2,1,0:T(8,128)(2,1)S(1)}, u32[]{:S(2)}, u32[]{:S(2)}) async-start(bf16[4,2,2,192,128]{4,3,2,1,0:T(8,128)(2,1)} %copy-done.3), calls=%async_computation.1 | async-start | bytes 1572864 | tf_op jit(solution)/shard_map/all_to_all | solution.py:287
  188.1 2.3 collective-permute-start.7
  190.4 2.8 collective-permute-start.4
  193.2 5.0 %collective-permute-start.5 = (bf16[2,192,128]{2,1,0:T(8,128)(2,1)S(1)}, bf16[2,192,128]{2,1,0:T(8,128)(2,1)S(1)}, u32[]{:S(2)}, u32[]{:S(2)}) collective-permute-start(bf16[2,192,128]{2,1,0:T(8,128)(2,1)S(1)} %get-tuple-element.26.q0), channel_id=1, source_target_pairs={{0,256},{128,384},{256,0},{384,128},{1,257},{129,385},{257,1},{385... | collective-permute-start | bytes 294920 | tf_op jit(solution)/shard_map/ppermute | solution.py:288
  198.2 1.9 collective-permute-start.6
  200.1 0.0 collective-permute-done.4.q1
  200.1 0.9 collective-permute-done.5.q2
  201.0 2.9 collective-permute-done.6.q3
  203.9 3.9 %all-to-all-done.1.kv_ref = bf16[4,2,2,192,128]{4,3,2,1,0:T(8,128)(2,1)S(1)} async-done(((bf16[4,2,2,192,128]{4,3,2,1,0:T(8,128)(2,1)}), bf16[4,2,2,192,128]{4,3,2,1,0:T(8,128)(2,1)S(1)}, u32[]{:S(2)}, u32[]{:S(2)}) %all-to-all-start.1) | async-done | bytes 786464 | tf_op jit(solution)/shard_map/all_to_all | solution.py:287
  207.8 3.6 %attend.1 = bf16[8,208,128]{2,1,0:T(8,128)(2,1)S(1)} custom-call(s32[4]{0:T(128)S(1)} %copy-done.5, bf16[2,192,128]{2,1,0:T(8,128)(2,1)S(1)} %get-tuple-element.26.q0, bf16[2,192,128]{2,1,0:T(8,128)(2,1)S(1)} %collective-permute-done.4.q1, bf16[2,192,128]{2,1,0:T(8,128)(2,1)S(1)} %collective-permute-done.5.q2, ...), custom_call_target="tpu_custom_call" | custom-call | tf_op jit(solution)/shard_map/attend/pallas_call | solution.py:291
  211.3 0.0 collective-permute-done.7.w2
  211.3 2.2 collective-permute-start.8
  213.5 4.3 %collective-permute-start.9 = (bf16[4,256,384]{2,1,0:T(8,128)(2,1)}, bf16[4,256,384]{2,1,0:T(8,128)(2,1)}, u32[]{:S(2)}, u32[]{:S(2)}) collective-permute-start(bf16[4,256,384]{2,1,0:T(8,128)(2,1)} %get-tuple-element.33), channel_id=1, source_target_pairs={{0,3},{1,0},{2,1},{3,2},{4,7},{5,4},{6,5},{7,6},{8,11},{9,8},{10,9... | collective-permute-start | bytes 2359304 | tf_op jit(solution)/shard_map/ppermute | solution.py:306
  217.8 14.6 %all_to_all.20.parts_ref = bf16[8,208,128]{2,1,0:T(8,128)(2,1)} all-to-all(bf16[8,208,128]{2,1,0:T(8,128)(2,1)S(1)} %attend.1), channel_id=1, replica_groups=mesh['y'=4,'zl'=4,'core'=2,'head'=4,'seq'=4] {'y','core'}, dimensions={0} | all-to-all | bytes 851968 | tf_op jit(solution)/shard_map/all_to_all | solution.py:304
  232.4 1.9 combine.1
  234.3 0.0 collective-permute-done.8.w1
  234.3 0.0 collective-permute-done.9.w3
  234.4 9.8 %all_to_all.21.a_ref = bf16[4,192,256]{2,1,0:T(8,128)(2,1)S(1)} all-to-all(bf16[4,192,256]{2,1,0:T(8,128)(2,1)} %combine.1), channel_id=1, replica_groups=mesh['y'=4,'zl'=4,'core'=2,'head'=4,'seq'=4] {'seq'}, dimensions={0} | all-to-all | bytes 786432 | tf_op jit(solution)/shard_map/all_to_all | solution.py:315
  244.2 0.0 copy-done.4
  244.2 2.6 branch.1
  246.8 8.2 %collective-permute-start.10 = (bf16[192,384]{1,0:T(8,128)(2,1)}, bf16[192,384]{1,0:T(8,128)(2,1)S(1)}, u32[]{:S(2)}, u32[]{:S(2)}) collective-permute-start(bf16[192,384]{1,0:T(8,128)(2,1)} %get-tuple-element.40), channel_id=1, source_target_pairs={{0,8},{4,12},{8,0},{12,4},{1,9},{5,13},{9,1},{13,5},{2,10},{6,14},... | collective-permute-start | bytes 442376 | tf_op jit(solution)/shard_map/ppermute | solution.py:324
  255.0 7.5 %collective-permute-start.11 = (bf16[192,384]{1,0:T(8,128)(2,1)S(1)}, bf16[192,384]{1,0:T(8,128)(2,1)S(1)}, u32[]{:S(2)}, u32[]{:S(2)}) collective-permute-start(bf16[192,384]{1,0:T(8,128)(2,1)S(1)} %get-tuple-element.41), channel_id=1, source_target_pairs={{0,4},{4,8},{8,12},{12,0},{1,5},{5,9},{9,13},{13,1},{2,6},{6,10},{... | collective-permute-start | bytes 442376 | tf_op jit(solution)/shard_map/ppermute | solution.py:324
  262.5 1.9 collective-permute-start.12
  264.4 0.1 dynamic-slice_reduce_fusion.1
  264.5 0.2 collective-permute-done.10
  264.7 6.9 %collective-permute-done.11 = bf16[192,384]{1,0:T(8,128)(2,1)S(1)} collective-permute-done((bf16[192,384]{1,0:T(8,128)(2,1)S(1)}, bf16[192,384]{1,0:T(8,128)(2,1)S(1)}, u32[]{:S(2)}, u32[]{:S(2)}) %collective-permute-start.11) | collective-permute-done | bytes 147488 | tf_op jit(solution)/shard_map/ppermute | solution.py:324
  271.6 14.9 %collective-permute-done.12 = bf16[192,384]{1,0:T(8,128)(2,1)S(1)} collective-permute-done((bf16[192,384]{1,0:T(8,128)(2,1)S(1)}, bf16[192,384]{1,0:T(8,128)(2,1)S(1)}, u32[]{:S(2)}, u32[]{:S(2)}) %collective-permute-start.12) | collective-permute-done | bytes 147488 | tf_op jit(solution)/shard_map/ppermute | solution.py:324
  286.6 1.7 add_convert_fusion
  (6 shorter events, 0.0 us)
Async XLA Ops:
  6.5 122.8 %copy-start = (f32[8,3,6144]{2,0,1:T(8,128)S(1)}, f32[8,3,6144]{2,0,1:T(8,128)}, u32[]{:S(2)}) copy-start(f32[8,3,6144]{2,0,1:T(8,128)} %param.15) | copy-start | bytes 1769476
  6.5 162.6 %all-gather.2.cloned.1.call-start = ((), (), s32[]{:S(2)}) async-start(), calls=%async_computation.4 | async-start | bytes 9732096 | tf_op jit(solution)/shard_map/all_gather | solution.py:216
  9.2 25.5 %collective-permute-start = (bf16[192,384]{1,0:T(8,128)(2,1)}, bf16[192,384]{1,0:T(8,128)(2,1)S(1)}, u32[]{:S(2)}, u32[]{:S(2)}) collective-permute-start(bf16[192,384]{1,0:T(8,128)(2,1)} %r0.1), channel_id=1, source_target_pairs={{0,4},{4,8},{8,12},{12,0},{1,5},{5,9},{9,13},{13,1},{2,6},{6,10},{... | collective-permute-start | bytes 442376 | tf_op jit(solution)/shard_map/ppermute | solution.py:239
  18.8 31.8 %collective-permute-start.1 = (bf16[192,384]{1,0:T(8,128)(2,1)}, bf16[192,384]{1,0:T(8,128)(2,1)S(1)}, u32[]{:S(2)}, u32[]{:S(2)}) collective-permute-start(bf16[192,384]{1,0:T(8,128)(2,1)} %r0.1), channel_id=1, source_target_pairs={{0,8},{4,12},{8,0},{12,4},{1,9},{5,13},{9,1},{13,5},{2,10},{6,14},... | collective-permute-start | bytes 442376 | tf_op jit(solution)/shard_map/ppermute | solution.py:238
  29.5 21.2 %collective-permute-start.2 = (bf16[192,384]{1,0:T(8,128)(2,1)}, bf16[192,384]{1,0:T(8,128)(2,1)S(1)}, u32[]{:S(2)}, u32[]{:S(2)}) collective-permute-start(bf16[192,384]{1,0:T(8,128)(2,1)} %r0.1), channel_id=1, source_target_pairs={{0,12},{4,0},{8,4},{12,8},{1,13},{5,1},{9,5},{13,9},{2,14},{6,2},{... | collective-permute-start | bytes 442376 | tf_op jit(solution)/shard_map/ppermute | solution.py:240
  34.7 16.0 %copy-start.8 = (bf16[192,384]{1,0:T(8,128)(2,1)}, bf16[192,384]{1,0:T(8,128)(2,1)S(1)}, u32[]{:S(2)}) copy-start(bf16[192,384]{1,0:T(8,128)(2,1)S(1)} %collective-permute-done.r1) | copy-start | bytes 442372
  50.6 0.7 copy-start.9
  51.3 0.7 copy-start.10
  124.7 26.8 %all-to-all-start = ((bf16[4,4,192,384]{3,2,1,0:T(8,128)(2,1)}), bf16[4,4,192,384]{3,2,1,0:T(8,128)(2,1)S(1)}, u32[]{:S(2)}, u32[]{:S(2)}) async-start(bf16[4,4,192,384]{3,2,1,0:T(8,128)(2,1)} %spread.1), calls=%async_computation | async-start | bytes 4718592 | tf_op jit(solution)/shard_map/all_to_all | solution.py:252
  130.3 21.2 %copy-start.5 = (s32[4]{0:T(128)S(1)}, s32[4]{0:T(128)}, u32[]{:S(2)}) copy-start(s32[4]{0:T(128)} %pad_add_fusion.place_ref) | copy-start | bytes 52
  151.5 17.6 %copy-start.6 = (f32[128]{0:T(128)S(1)}, f32[128]{0:T(128)}, u32[]{:S(2)}) copy-start(f32[128]{0:T(128)} %param.12) | copy-start | bytes 1540
  151.5 17.6 %copy-start.7 = (f32[128]{0:T(128)S(1)}, f32[128]{0:T(128)}, u32[]{:S(2)}) copy-start(f32[128]{0:T(128)} %param.13) | copy-start | bytes 1540
  155.8 13.4 %collective-permute-start.3 = (bf16[192,6144]{1,0:T(8,128)(2,1)S(1)}, bf16[192,6144]{1,0:T(8,128)(2,1)S(1)}, u32[]{:S(2)}, u32[]{:S(2)}) collective-permute-start(bf16[192,6144]{1,0:T(8,128)(2,1)S(1)} %norm.1.own_ref), channel_id=1, source_target_pairs={{0,16},{16,0},{1,17},{17,1},{2,18},{18,2},{3,19},{19,3},{4,20},{20... | collective-permute-start | bytes 7077896 | tf_op jit(solution)/shard_map/ppermute | solution.py:268
  165.0 1.4 copy-start.1
  169.1 1.7 copy-start.2
  176.0 0.9 copy-start.3
  176.8 30.9 %all-to-all-start.1 = ((bf16[4,2,2,192,128]{4,3,2,1,0:T(8,128)(2,1)}), bf16[4,2,2,192,128]{4,3,2,1,0:T(8,128)(2,1)S(1)}, u32[]{:S(2)}, u32[]{:S(2)}) async-start(bf16[4,2,2,192,128]{4,3,2,1,0:T(8,128)(2,1)} %copy-done.3), calls=%async_computation.1 | async-start | bytes 1572864 | tf_op jit(solution)/shard_map/all_to_all | solution.py:287
  188.1 56.1 %copy-start.4 = (bf16[4,256,384]{2,1,0:T(8,128)(2,1)S(1)}, bf16[4,256,384]{2,1,0:T(8,128)(2,1)}, u32[]{:S(2)}) copy-start(bf16[4,256,384]{2,1,0:T(8,128)(2,1)} %get-tuple-element.35.w0) | copy-start | bytes 2359300
  188.1 23.2 %collective-permute-start.7 = (bf16[4,256,384]{2,1,0:T(8,128)(2,1)}, bf16[4,256,384]{2,1,0:T(8,128)(2,1)S(1)}, u32[]{:S(2)}, u32[]{:S(2)}) collective-permute-start(bf16[4,256,384]{2,1,0:T(8,128)(2,1)} %get-tuple-element.29), channel_id=1, source_target_pairs={{0,2},{1,3},{2,0},{3,1},{4,6},{5,7},{6,4},{7,5},{8,10},{9,11},{10,... | collective-permute-start | bytes 2359304 | tf_op jit(solution)/shard_map/ppermute | solution.py:255
  190.4 9.7 %collective-permute-start.4 = (bf16[2,192,128]{2,1,0:T(8,128)(2,1)S(1)}, bf16[2,192,128]{2,1,0:T(8,128)(2,1)S(1)}, u32[]{:S(2)}, u32[]{:S(2)}) collective-permute-start(bf16[2,192,128]{2,1,0:T(8,128)(2,1)S(1)} %get-tuple-element.26.q0), channel_id=1, source_target_pairs={{0,128},{128,256},{256,384},{384,0},{1,129},{129,257},{257,385},{3... | collective-permute-start | bytes 294920 | tf_op jit(solution)/shard_map/ppermute | solution.py:288
  193.2 7.8 %collective-permute-start.5 = (bf16[2,192,128]{2,1,0:T(8,128)(2,1)S(1)}, bf16[2,192,128]{2,1,0:T(8,128)(2,1)S(1)}, u32[]{:S(2)}, u32[]{:S(2)}) collective-permute-start(bf16[2,192,128]{2,1,0:T(8,128)(2,1)S(1)} %get-tuple-element.26.q0), channel_id=1, source_target_pairs={{0,256},{128,384},{256,0},{384,128},{1,257},{129,385},{257,1},{385... | collective-permute-start | bytes 294920 | tf_op jit(solution)/shard_map/ppermute | solution.py:288
  198.2 5.7 %collective-permute-start.6 = (bf16[2,192,128]{2,1,0:T(8,128)(2,1)S(1)}, bf16[2,192,128]{2,1,0:T(8,128)(2,1)S(1)}, u32[]{:S(2)}, u32[]{:S(2)}) collective-permute-start(bf16[2,192,128]{2,1,0:T(8,128)(2,1)S(1)} %get-tuple-element.26.q0), channel_id=1, source_target_pairs={{0,384},{128,0},{256,128},{384,256},{1,385},{129,1},{257,129},{385... | collective-permute-start | bytes 294920 | tf_op jit(solution)/shard_map/ppermute | solution.py:288
  211.3 23.0 %collective-permute-start.8 = (bf16[4,256,384]{2,1,0:T(8,128)(2,1)}, bf16[4,256,384]{2,1,0:T(8,128)(2,1)S(1)}, u32[]{:S(2)}, u32[]{:S(2)}) collective-permute-start(bf16[4,256,384]{2,1,0:T(8,128)(2,1)} %get-tuple-element.32), channel_id=1, source_target_pairs={{0,1},{1,2},{2,3},{3,0},{4,5},{5,6},{6,7},{7,4},{8,9},{9,10},{10,1... | collective-permute-start | bytes 2359304 | tf_op jit(solution)/shard_map/ppermute | solution.py:305
  213.5 20.8 %collective-permute-start.9 = (bf16[4,256,384]{2,1,0:T(8,128)(2,1)}, bf16[4,256,384]{2,1,0:T(8,128)(2,1)}, u32[]{:S(2)}, u32[]{:S(2)}) collective-permute-start(bf16[4,256,384]{2,1,0:T(8,128)(2,1)} %get-tuple-element.33), channel_id=1, source_target_pairs={{0,3},{1,0},{2,1},{3,2},{4,7},{5,4},{6,5},{7,6},{8,11},{9,8},{10,9... | collective-permute-start | bytes 2359304 | tf_op jit(solution)/shard_map/ppermute | solution.py:306
  246.8 17.9 %collective-permute-start.10 = (bf16[192,384]{1,0:T(8,128)(2,1)}, bf16[192,384]{1,0:T(8,128)(2,1)S(1)}, u32[]{:S(2)}, u32[]{:S(2)}) collective-permute-start(bf16[192,384]{1,0:T(8,128)(2,1)} %get-tuple-element.40), channel_id=1, source_target_pairs={{0,8},{4,12},{8,0},{12,4},{1,9},{5,13},{9,1},{13,5},{2,10},{6,14},... | collective-permute-start | bytes 442376 | tf_op jit(solution)/shard_map/ppermute | solution.py:324
  255.0 16.6 %collective-permute-start.11 = (bf16[192,384]{1,0:T(8,128)(2,1)S(1)}, bf16[192,384]{1,0:T(8,128)(2,1)S(1)}, u32[]{:S(2)}, u32[]{:S(2)}) collective-permute-start(bf16[192,384]{1,0:T(8,128)(2,1)S(1)} %get-tuple-element.41), channel_id=1, source_target_pairs={{0,4},{4,8},{8,12},{12,0},{1,5},{5,9},{9,13},{13,1},{2,6},{6,10},{... | collective-permute-start | bytes 442376 | tf_op jit(solution)/shard_map/ppermute | solution.py:324
  262.5 24.1 %collective-permute-start.12 = (bf16[192,384]{1,0:T(8,128)(2,1)S(1)}, bf16[192,384]{1,0:T(8,128)(2,1)S(1)}, u32[]{:S(2)}, u32[]{:S(2)}) collective-permute-start(bf16[192,384]{1,0:T(8,128)(2,1)S(1)} %get-tuple-element.42), channel_id=1, source_target_pairs={{0,12},{4,0},{8,4},{12,8},{1,13},{5,1},{9,5},{13,9},{2,14},{6,2},{... | collective-permute-start | bytes 442376 | tf_op jit(solution)/shard_map/ppermute | solution.py:324
Sparse Core Ops, SparseCore 0:
  9.5 101.8 all-gather.1

commit v8 on v6

--- a/solution.py
+++ b/solution.py
@@ -26,21 +26,19 @@
     stepped = jnp.full((1, HD), step_ref[0], jnp.int32).astype(F32)
     decay = (1.0 + stepped) / (10.0 + stepped)
     for h in range(2):
-        for j in range(3):
-            part = slice(h * HD, (h + 1) * HD)
-            ema = ema_ref[j, :, part].astype(F32)
-            train = train_ref[j, :, part].astype(F32)
-            out_ref[h, :, j * HD : (j + 1) * HD] = (decay * ema + (1.0 - decay) * train).astype(BF)
+        part = slice(h * HD, (h + 1) * HD)
+        ema = ema_ref[0, :, part].astype(F32)
+        train = train_ref[0, :, part].astype(F32)
+        out_ref[h] = (decay * ema + (1.0 - decay) * train).astype(BF)
 
 
 def spread_kernel(own_ref, before_ref, low_ref, high_ref, after_ref, out_ref):
     half = low_ref.shape[0]
-    for copy in range(GRID):
-        out_ref[copy, 0] = own_ref[...]
-        out_ref[copy, 1] = before_ref[...]
-        out_ref[copy, 2, :half] = low_ref[...]
-        out_ref[copy, 2, half:] = high_ref[...]
-        out_ref[copy, 3] = after_ref[...]
+    out_ref[0, 0] = own_ref[...]
+    out_ref[0, 1] = before_ref[...]
+    out_ref[0, 2, :half] = low_ref[...]
+    out_ref[0, 2, half:] = high_ref[...]
+    out_ref[0, 3] = after_ref[...]
 
 
 def norm_kernel(place_ref, raw_ref, mod_ref, sent_ref, out_ref, sems):
@@ -202,12 +200,13 @@
     blocks = GRID * GRID
     by_head = pl.pallas_call(
         average_kernel,
+        grid=(3,),
         in_specs=[
             pl.BlockSpec(memory_space=pltpu.SMEM),
-            pl.BlockSpec(memory_space=pltpu.VMEM),
-            pl.BlockSpec(memory_space=pltpu.VMEM),
-        ],
-        out_specs=pl.BlockSpec(memory_space=pltpu.VMEM),
+            pl.BlockSpec((1, rows, channels), lambda j: (j, 0, 0)),
+            pl.BlockSpec((1, rows, channels), lambda j: (j, 0, 0)),
+        ],
+        out_specs=pl.BlockSpec((2, rows, HD), lambda j: (0, 0, j)),
         out_shape=jax.ShapeDtypeStruct((2, rows, 3 * HD), BF),
         name="average",
     )(step, ema_qkv, train_qkv)
@@ -242,8 +241,12 @@
     in_vmem = pl.BlockSpec(memory_space=pltpu.VMEM)
     raw = pl.pallas_call(
         spread_kernel,
-        in_specs=[in_vmem] * (GRID + 1),
-        out_specs=in_vmem,
+        grid=(GRID,),
+        in_specs=[
+            pl.BlockSpec(part.shape, lambda i: (0, 0))
+            for part in (latents, before, far_low, far_high, after)
+        ],
+        out_specs=pl.BlockSpec((1, GRID, rows, width), lambda i: (i, 0, 0, 0)),
         out_shape=jax.ShapeDtypeStruct((GRID, GRID, rows, width), BF),
         name="spread",
     )(latents, before, far_low, far_high, after)
@@ -309,7 +312,6 @@
         out_shape=jax.ShapeDtypeStruct((GRID, rows, channels), BF),
         name="combine",
     )(parts)
-    around, out1, out3 = lax.optimization_barrier((around, out1, out3))
     around = lax.all_to_all(around, "seq", 0, 0, tiled=True)
     outs = pl.pallas_call(
         branch_kernel,

time: 220 us -> 219 us (level)
    ppermute x1, waiting for transfers between devices: 2.5 us -> 0.01 us  [per_device(): out1 = lax.ppermute(out1, 'seq', shift(1))]
where the time goes in v8:
time: 219 us; the launch traced here: 216 us
  starting transfers between devices  86.1 us (39%)
  waiting for transfers between devices  53.5 us (24%)
  Pallas kernels  28.5 us (13%)
  blocking collectives  25.4 us (12%)
  between operations  15 us (7%)
  local copies, waits for them, and re-layouts  5 us (2%)
  other arithmetic  2.28 us (1%)
    ppermute x3, starting transfers between devices, per_device(): shares = [lax.ppermute(outs[k], 'head', shift(k)) for k in (2, 1, 3)]  17.9 us
    all_to_all x1, waiting for transfers between devices, per_device(): raw = lax.all_to_all(raw, 'seq', 0, 0, tiled=True)  17.7 us
    ppermute x3, waiting for transfers between devices, per_device(): shares = [lax.ppermute(outs[k], 'head', shift(k)) for k in (2, 1, 3)]  16 us
    ppermute x1, starting transfers between devices, per_device(): far_low = lax.ppermute(before[:half], 'head', shift(1))  15.1 us
    all_to_all x1, blocking collectives, per_device(): parts = lax.all_to_all(parts, ('y', 'core'), 0, 0, tiled=True)  15 us
    all_to_all x1, blocking collectives, per_device(): around = lax.all_to_all(around, 'seq', 0, 0, tiled=True)  10.4 us
    ppermute x1, starting transfers between devices, per_device(): before = lax.ppermute(latents, 'head', shift(1))  9.65 us
    ppermute x3, starting transfers between devices, per_device(): lax.ppermute(queries, 'y', shift(k))  9.57 us
  transfers between devices with their start and end apart: 17, of which 11 were waited for; matrix products, arithmetic and copies ran while one was open for 0% of the time, Pallas kernels for 8%

profile of v8, /device:TPU:1, one launch (start us, length us, event | category | flops | bytes accessed | tf_op | source)
XLA Modules:
  0.0 215.8 jit_solution(1911879622755257178)
XLA Ops:
  6.5 0.0 copy-start
  6.5 0.0 all-gather.2.cloned.1.call-start
  7.3 2.7 %average.1 = bf16[2,192,384]{2,1,0:T(8,128)(2,1)} custom-call(s32[1]{0:T(128)S(6)} %copy.11.step_ref, bf16[3,192,256]{2,1,0:T(8,128)(2,1)} %ema_ref.1, bf16[3,192,256]{2,1,0:T(8,128)(2,1)} %train_ref.1), custom_call_target="tpu_custom_call" | custom-call | tf_op jit(solution)/shard_map/average/pallas_call | solution.py:201
  10.0 0.0 all-gather.2.cloned.1.call-update
  10.0 9.6 %collective-permute-start = (bf16[192,384]{1,0:T(8,128)(2,1)}, bf16[192,384]{1,0:T(8,128)(2,1)S(1)}, u32[]{:S(2)}, u32[]{:S(2)}) collective-permute-start(bf16[192,384]{1,0:T(8,128)(2,1)} %own_ref.1), channel_id=1, source_target_pairs={{0,4},{4,8},{8,12},{12,0},{1,5},{5,9},{9,13},{13,1},{2,6},{6,10},{... | collective-permute-start | bytes 442376 | tf_op jit(solution)/shard_map/ppermute | solution.py:236
  19.7 5.6 %collective-permute-start.2 = (bf16[192,384]{1,0:T(8,128)(2,1)}, bf16[192,384]{1,0:T(8,128)(2,1)S(1)}, u32[]{:S(2)}, u32[]{:S(2)}) collective-permute-start(bf16[192,384]{1,0:T(8,128)(2,1)} %own_ref.1), channel_id=1, source_target_pairs={{0,12},{4,0},{8,4},{12,8},{1,13},{5,1},{9,5},{13,9},{2,14},{6,2},{... | collective-permute-start | bytes 442376 | tf_op jit(solution)/shard_map/ppermute | solution.py:237
  25.3 1.5 collective-permute-done.before_ref
  26.7 15.1 %collective-permute-start.1 = (bf16[96,384]{1,0:T(8,128)(2,1)S(1)}, bf16[96,384]{1,0:T(8,128)(2,1)S(1)}, u32[]{:S(2)}, u32[]{:S(2)}) collective-permute-start(bf16[96,384]{1,0:T(8,128)(2,1)S(1)} %slice.13), channel_id=1, source_target_pairs={{0,4},{4,8},{8,12},{12,0},{1,5},{5,9},{9,13},{13,1},{2,6},{6,10},{... | collective-permute-start | bytes 221192 | tf_op jit(solution)/shard_map/ppermute | solution.py:238
  41.8 0.0 collective-permute-done.2.after_ref
  41.8 0.0 copy-start.9
  41.8 3.3 %collective-permute-start.3 = (bf16[96,384]{1,0:T(8,128)(2,1)S(1)}, bf16[96,384]{1,0:T(8,128)(2,1)S(1)}, u32[]{:S(2)}, u32[]{:S(2)}) collective-permute-start(bf16[96,384]{1,0:T(8,128)(2,1)S(1)} %slice.14), channel_id=1, source_target_pairs={{0,12},{4,0},{8,4},{12,8},{1,13},{5,1},{9,5},{13,9},{2,14},{6,2},{... | collective-permute-start | bytes 221192 | tf_op jit(solution)/shard_map/ppermute | solution.py:239
  45.1 2.2 %collective-permute-done.1.low_ref = bf16[96,384]{1,0:T(8,128)(2,1)S(1)} collective-permute-done((bf16[96,384]{1,0:T(8,128)(2,1)S(1)}, bf16[96,384]{1,0:T(8,128)(2,1)S(1)}, u32[]{:S(2)}, u32[]{:S(2)}) %collective-permute-start.1) | collective-permute-done | bytes 73760 | tf_op jit(solution)/shard_map/ppermute | solution.py:238
  47.4 4.8 %collective-permute-done.3.high_ref = bf16[96,384]{1,0:T(8,128)(2,1)S(1)} collective-permute-done((bf16[96,384]{1,0:T(8,128)(2,1)S(1)}, bf16[96,384]{1,0:T(8,128)(2,1)S(1)}, u32[]{:S(2)}, u32[]{:S(2)}) %collective-permute-start.3) | collective-permute-done | bytes 73760 | tf_op jit(solution)/shard_map/ppermute | solution.py:239
  52.2 0.0 copy-done.8
  52.2 0.0 copy-done.9
  52.2 0.0 copy-done.10
  52.2 0.0 copy-start.11
  52.2 0.6 copy-done.11
  52.8 3.1 %spread.1 = bf16[4,4,192,384]{3,2,1,0:T(8,128)(2,1)} custom-call(bf16[192,384]{1,0:T(8,128)(2,1)} %own_ref.1, bf16[192,384]{1,0:T(8,128)(2,1)} %copy-done.8, bf16[96,384]{1,0:T(8,128)(2,1)} %copy-done.10, bf16[96,384]{1,0:T(8,128)(2,1)} %copy-done.11, bf16[192,384]{1,0:T(8,128)(2,1)} %copy-done.9), custom_call_target="tpu_custom_call" | custom-call | tf_op jit(solution)/shard_map/spread/pallas_call | solution.py:242
  55.9 4.0 %all-to-all-start = ((bf16[4,4,192,384]{3,2,1,0:T(8,128)(2,1)}), bf16[4,4,192,384]{3,2,1,0:T(8,128)(2,1)S(1)}, u32[]{:S(2)}, u32[]{:S(2)}) async-start(bf16[4,4,192,384]{3,2,1,0:T(8,128)(2,1)} %spread.1), calls=%async_computation | async-start | bytes 4718592 | tf_op jit(solution)/shard_map/all_to_all | solution.py:253
  60.5 0.0 copy-done
  60.5 0.2 dynamic-slice_reduce_fusion
  60.8 0.1 reshape.15.mod_ref
  60.8 0.6 pad_add_fusion.place_ref
  61.4 5.2 %pick.1 = (bf16[4,256,384]{2,1,0:T(8,128)(2,1)}, bf16[4,256,384]{2,1,0:T(8,128)(2,1)}, bf16[4,256,384]{2,1,0:T(8,128)(2,1)}, bf16[4,256,384]{2,1,0:T(8,128)(2,1)}) custom-call(s32[4]{0:T(128)} %pad_add_fusion.place_ref, bf16[256,6144]{1,0:T(8,128)(2,1)} %refs_3_.1, bf16[256,6144]{1,0:T(8,128)(2,1)} %refs_3_.1, bf16[256,6144]{1,0:T(8,128)(2,1)} %refs_3_.1, ...), custom_call_target="tpu_custom_call" | custom-call | tf_op jit(solution)/shard_map/pick/pallas_call | solution.py:222
  66.7 17.7 %all-to-all-done.raw_ref = bf16[4,4,192,384]{3,2,1,0:T(8,128)(2,1)S(1)} async-done(((bf16[4,4,192,384]{3,2,1,0:T(8,128)(2,1)}), bf16[4,4,192,384]{3,2,1,0:T(8,128)(2,1)S(1)}, u32[]{:S(2)}, u32[]{:S(2)}) %all-to-all-start) | async-done | bytes 2359328 | tf_op jit(solution)/shard_map/all_to_all | solution.py:253
  84.4 0.0 copy-done.5
  84.4 4.3 %norm.1.own_ref = bf16[192,6144]{1,0:T(8,128)(2,1)S(1)} custom-call(s32[4]{0:T(128)S(1)} %copy-done.5, bf16[4,4,192,384]{3,2,1,0:T(8,128)(2,1)S(1)} %all-to-all-done.raw_ref, f32[3,4,4,384]{3,2,1,0:T(4,128)S(1)} %reshape.15.mod_ref), custom_call_target="tpu_custom_call" | custom-call | tf_op jit(solution)/shard_map/norm/pallas_call | solution.py:257
  88.7 7.5 %collective-permute-start.4 = (bf16[192,6144]{1,0:T(8,128)(2,1)S(1)}, bf16[192,6144]{1,0:T(8,128)(2,1)S(1)}, u32[]{:S(2)}, u32[]{:S(2)}) collective-permute-start(bf16[192,6144]{1,0:T(8,128)(2,1)S(1)} %norm.1.own_ref), channel_id=1, source_target_pairs={{0,16},{16,0},{1,17},{17,1},{2,18},{18,2},{3,19},{19,3},{4,20},{20... | collective-permute-start | bytes 7077896 | tf_op jit(solution)/shard_map/ppermute | solution.py:269
  96.2 0.0 copy-start.1
  96.2 1.4 copy-done.1
  97.6 2.8 %collective-permute-done.4.other_ref = bf16[192,6144]{1,0:T(8,128)(2,1)S(1)} collective-permute-done((bf16[192,6144]{1,0:T(8,128)(2,1)S(1)}, bf16[192,6144]{1,0:T(8,128)(2,1)S(1)}, u32[]{:S(2)}, u32[]{:S(2)}) %collective-permute-start.4) | collective-permute-done | bytes 2359328 | tf_op jit(solution)/shard_map/ppermute | solution.py:269
  100.3 1.7 all-gather.2.cloned.1.call-done.weight_ref
  102.0 1.7 copy-done.2
  103.7 5.1 %project.1 = (bf16[2,192,128]{2,1,0:T(8,128)(2,1)S(1)}, bf16[4,2,2,192,128]{4,3,2,1,0:T(8,128)(2,1)S(1)}) custom-call(s32[4]{0:T(128)S(1)} %copy-done.5, bf16[192,6144]{1,0:T(8,128)(2,1)S(1)} %copy-done.2, bf16[192,6144]{1,0:T(8,128)(2,1)S(1)} %collective-permute-done.4.other_ref, bf16[2,6144,384]{2,1,0:T(8,128)(2,1)} %all-gather.2.cloned.1.call-done.weight_ref, ...), custom_call_target="tpu_custom_call" | custom-call | tf_op jit(solution)/shard_map/project/pallas_call | solution.py:272
  108.8 0.9 copy-done.3
  109.7 5.0 %all-to-all-start.1 = ((bf16[4,2,2,192,128]{4,3,2,1,0:T(8,128)(2,1)}), bf16[4,2,2,192,128]{4,3,2,1,0:T(8,128)(2,1)S(1)}, u32[]{:S(2)}, u32[]{:S(2)}) async-start(bf16[4,2,2,192,128]{4,3,2,1,0:T(8,128)(2,1)} %copy-done.3), calls=%async_computation.1 | async-start | bytes 1572864 | tf_op jit(solution)/shard_map/all_to_all | solution.py:288
  114.8 3.3 %collective-permute-start.8 = (bf16[4,256,384]{2,1,0:T(8,128)(2,1)}, bf16[4,256,384]{2,1,0:T(8,128)(2,1)S(1)}, u32[]{:S(2)}, u32[]{:S(2)}) collective-permute-start(bf16[4,256,384]{2,1,0:T(8,128)(2,1)} %get-tuple-element.26), channel_id=1, source_target_pairs={{0,2},{1,3},{2,0},{3,1},{4,6},{5,7},{6,4},{7,5},{8,10},{9,11},{10,... | collective-permute-start | bytes 2359304 | tf_op jit(solution)/shard_map/ppermute | solution.py:256
  118.1 2.7 %collective-permute-start.5 = (bf16[2,192,128]{2,1,0:T(8,128)(2,1)S(1)}, bf16[2,192,128]{2,1,0:T(8,128)(2,1)S(1)}, u32[]{:S(2)}, u32[]{:S(2)}) collective-permute-start(bf16[2,192,128]{2,1,0:T(8,128)(2,1)S(1)} %get-tuple-element.23.q0), channel_id=1, source_target_pairs={{0,128},{128,256},{256,384},{384,0},{1,129},{129,257},{257,385},{3... | collective-permute-start | bytes 294920 | tf_op jit(solution)/shard_map/ppermute | solution.py:289
  120.8 5.0 %collective-permute-start.6 = (bf16[2,192,128]{2,1,0:T(8,128)(2,1)S(1)}, bf16[2,192,128]{2,1,0:T(8,128)(2,1)S(1)}, u32[]{:S(2)}, u32[]{:S(2)}) collective-permute-start(bf16[2,192,128]{2,1,0:T(8,128)(2,1)S(1)} %get-tuple-element.23.q0), channel_id=1, source_target_pairs={{0,256},{128,384},{256,0},{384,128},{1,257},{129,385},{257,1},{385... | collective-permute-start | bytes 294920 | tf_op jit(solution)/shard_map/ppermute | solution.py:289
  125.7 1.9 collective-permute-start.7
  127.7 0.0 collective-permute-done.5.q1
  127.7 0.9 collective-permute-done.6.q2
  128.5 2.8 %collective-permute-done.7.q3 = bf16[2,192,128]{2,1,0:T(8,128)(2,1)S(1)} collective-permute-done((bf16[2,192,128]{2,1,0:T(8,128)(2,1)S(1)}, bf16[2,192,128]{2,1,0:T(8,128)(2,1)S(1)}, u32[]{:S(2)}, u32[]{:S(2)}) %collective-permute-start.7) | collective-permute-done | bytes 98336 | tf_op jit(solution)/shard_map/ppermute | solution.py:289
  131.4 3.1 %all-to-all-done.1.kv_ref = bf16[4,2,2,192,128]{4,3,2,1,0:T(8,128)(2,1)S(1)} async-done(((bf16[4,2,2,192,128]{4,3,2,1,0:T(8,128)(2,1)}), bf16[4,2,2,192,128]{4,3,2,1,0:T(8,128)(2,1)S(1)}, u32[]{:S(2)}, u32[]{:S(2)}) %all-to-all-start.1) | async-done | bytes 786464 | tf_op jit(solution)/shard_map/all_to_all | solution.py:288
  134.5 3.6 %attend.1 = bf16[8,208,128]{2,1,0:T(8,128)(2,1)S(1)} custom-call(s32[4]{0:T(128)S(1)} %copy-done.5, bf16[2,192,128]{2,1,0:T(8,128)(2,1)S(1)} %get-tuple-element.23.q0, bf16[2,192,128]{2,1,0:T(8,128)(2,1)S(1)} %collective-permute-done.5.q1, bf16[2,192,128]{2,1,0:T(8,128)(2,1)S(1)} %collective-permute-done.6.q2, ...), custom_call_target="tpu_custom_call" | custom-call | tf_op jit(solution)/shard_map/attend/pallas_call | solution.py:292
  138.0 0.0 collective-permute-done.8.w2
  138.0 3.0 %collective-permute-start.10 = (bf16[4,256,384]{2,1,0:T(8,128)(2,1)}, bf16[4,256,384]{2,1,0:T(8,128)(2,1)S(1)}, u32[]{:S(2)}, u32[]{:S(2)}) collective-permute-start(bf16[4,256,384]{2,1,0:T(8,128)(2,1)} %get-tuple-element.32), channel_id=1, source_target_pairs={{0,3},{1,0},{2,1},{3,2},{4,7},{5,4},{6,5},{7,6},{8,11},{9,8},{10,9... | collective-permute-start | bytes 2359304 | tf_op jit(solution)/shard_map/ppermute | solution.py:307
  141.1 2.3 %collective-permute-start.9 = (bf16[4,256,384]{2,1,0:T(8,128)(2,1)}, bf16[4,256,384]{2,1,0:T(8,128)(2,1)}, u32[]{:S(2)}, u32[]{:S(2)}) collective-permute-start(bf16[4,256,384]{2,1,0:T(8,128)(2,1)} %get-tuple-element.30), channel_id=1, source_target_pairs={{0,1},{1,2},{2,3},{3,0},{4,5},{5,6},{6,7},{7,4},{8,9},{9,10},{10,1... | collective-permute-start | bytes 2359304 | tf_op jit(solution)/shard_map/ppermute | solution.py:306
  143.3 15.0 %all_to_all.20.parts_ref = bf16[8,208,128]{2,1,0:T(8,128)(2,1)} all-to-all(bf16[8,208,128]{2,1,0:T(8,128)(2,1)S(1)} %attend.1), channel_id=1, replica_groups=mesh['y'=4,'zl'=4,'core'=2,'head'=4,'seq'=4] {'y','core'}, dimensions={0} | all-to-all | bytes 851968 | tf_op jit(solution)/shard_map/all_to_all | solution.py:305
  158.4 1.9 combine.1
  160.3 10.4 %all_to_all.21.a_ref = bf16[4,192,256]{2,1,0:T(8,128)(2,1)S(1)} all-to-all(bf16[4,192,256]{2,1,0:T(8,128)(2,1)} %combine.1), channel_id=1, replica_groups=mesh['y'=4,'zl'=4,'core'=2,'head'=4,'seq'=4] {'seq'}, dimensions={0} | all-to-all | bytes 786432 | tf_op jit(solution)/shard_map/all_to_all | solution.py:315
  170.7 0.0 collective-permute-done.10.w3
  170.7 0.0 collective-permute-done.9.w1
  170.7 0.0 copy-done.4
  170.7 2.6 %branch.1 = (bf16[192,384]{1,0:T(8,128)(2,1)S(1)}, bf16[192,384]{1,0:T(8,128)(2,1)S(1)}, bf16[192,384]{1,0:T(8,128)(2,1)}, bf16[192,384]{1,0:T(8,128)(2,1)S(1)}) custom-call(s32[4]{0:T(128)S(1)} %copy-done.5, bf16[4,192,256]{2,1,0:T(8,128)(2,1)S(1)} %all_to_all.21.a_ref, bf16[4,256,384]{2,1,0:T(8,128)(2,1)S(1)} %copy-done.4, ...), custom_call_target="tpu_custom_call" | custom-call | tf_op jit(solution)/shard_map/branch/pallas_call | solution.py:316
  173.3 8.7 %collective-permute-start.11 = (bf16[192,384]{1,0:T(8,128)(2,1)}, bf16[192,384]{1,0:T(8,128)(2,1)S(1)}, u32[]{:S(2)}, u32[]{:S(2)}) collective-permute-start(bf16[192,384]{1,0:T(8,128)(2,1)} %get-tuple-element.34), channel_id=1, source_target_pairs={{0,8},{4,12},{8,0},{12,4},{1,9},{5,13},{9,1},{13,5},{2,10},{6,14},... | collective-permute-start | bytes 442376 | tf_op jit(solution)/shard_map/ppermute | solution.py:324
  182.0 4.2 %collective-permute-start.12 = (bf16[192,384]{1,0:T(8,128)(2,1)S(1)}, bf16[192,384]{1,0:T(8,128)(2,1)S(1)}, u32[]{:S(2)}, u32[]{:S(2)}) collective-permute-start(bf16[192,384]{1,0:T(8,128)(2,1)S(1)} %get-tuple-element.35), channel_id=1, source_target_pairs={{0,4},{4,8},{8,12},{12,0},{1,5},{5,9},{9,13},{13,1},{2,6},{6,10},{... | collective-permute-start | bytes 442376 | tf_op jit(solution)/shard_map/ppermute | solution.py:324
  186.2 5.0 %collective-permute-start.13 = (bf16[192,384]{1,0:T(8,128)(2,1)S(1)}, bf16[192,384]{1,0:T(8,128)(2,1)S(1)}, u32[]{:S(2)}, u32[]{:S(2)}) collective-permute-start(bf16[192,384]{1,0:T(8,128)(2,1)S(1)} %get-tuple-element.36), channel_id=1, source_target_pairs={{0,12},{4,0},{8,4},{12,8},{1,13},{5,1},{9,5},{13,9},{2,14},{6,2},{... | collective-permute-start | bytes 442376 | tf_op jit(solution)/shard_map/ppermute | solution.py:324
  191.2 0.1 dynamic-slice_reduce_fusion.1
  191.3 0.0 collective-permute-done.11
  191.3 13.1 %collective-permute-done.12 = bf16[192,384]{1,0:T(8,128)(2,1)S(1)} collective-permute-done((bf16[192,384]{1,0:T(8,128)(2,1)S(1)}, bf16[192,384]{1,0:T(8,128)(2,1)S(1)}, u32[]{:S(2)}, u32[]{:S(2)}) %collective-permute-start.12) | collective-permute-done | bytes 147488 | tf_op jit(solution)/shard_map/ppermute | solution.py:324
  204.3 3.0 %collective-permute-done.13 = bf16[192,384]{1,0:T(8,128)(2,1)S(1)} collective-permute-done((bf16[192,384]{1,0:T(8,128)(2,1)S(1)}, bf16[192,384]{1,0:T(8,128)(2,1)S(1)}, u32[]{:S(2)}, u32[]{:S(2)}) %collective-permute-start.13) | collective-permute-done | bytes 147488 | tf_op jit(solution)/shard_map/ppermute | solution.py:324
  207.3 1.7 add_convert_fusion
  (12 shorter events, 0.0 us)
Async XLA Ops:
  6.5 54.0 %copy-start = (f32[8,3,6144]{2,0,1:T(8,128)S(1)}, f32[8,3,6144]{2,0,1:T(8,128)}, u32[]{:S(2)}) copy-start(f32[8,3,6144]{2,0,1:T(8,128)} %param.15) | copy-start | bytes 1769476
  6.5 95.5 %all-gather.2.cloned.1.call-start = ((), (), s32[]{:S(2)}) async-start(), calls=%async_computation.4 | async-start | bytes 9732096 | tf_op jit(solution)/shard_map/all_gather | solution.py:213
  10.0 16.7 %collective-permute-start = (bf16[192,384]{1,0:T(8,128)(2,1)}, bf16[192,384]{1,0:T(8,128)(2,1)S(1)}, u32[]{:S(2)}, u32[]{:S(2)}) collective-permute-start(bf16[192,384]{1,0:T(8,128)(2,1)} %own_ref.1), channel_id=1, source_target_pairs={{0,4},{4,8},{8,12},{12,0},{1,5},{5,9},{9,13},{13,1},{2,6},{6,10},{... | collective-permute-start | bytes 442376 | tf_op jit(solution)/shard_map/ppermute | solution.py:236
  19.7 22.1 %collective-permute-start.2 = (bf16[192,384]{1,0:T(8,128)(2,1)}, bf16[192,384]{1,0:T(8,128)(2,1)S(1)}, u32[]{:S(2)}, u32[]{:S(2)}) collective-permute-start(bf16[192,384]{1,0:T(8,128)(2,1)} %own_ref.1), channel_id=1, source_target_pairs={{0,12},{4,0},{8,4},{12,8},{1,13},{5,1},{9,5},{13,9},{2,14},{6,2},{... | collective-permute-start | bytes 442376 | tf_op jit(solution)/shard_map/ppermute | solution.py:237
  26.7 25.4 %copy-start.8 = (bf16[192,384]{1,0:T(8,128)(2,1)}, bf16[192,384]{1,0:T(8,128)(2,1)S(1)}, u32[]{:S(2)}) copy-start(bf16[192,384]{1,0:T(8,128)(2,1)S(1)} %collective-permute-done.before_ref) | copy-start | bytes 442372
  26.7 20.6 %collective-permute-start.1 = (bf16[96,384]{1,0:T(8,128)(2,1)S(1)}, bf16[96,384]{1,0:T(8,128)(2,1)S(1)}, u32[]{:S(2)}, u32[]{:S(2)}) collective-permute-start(bf16[96,384]{1,0:T(8,128)(2,1)S(1)} %slice.13), channel_id=1, source_target_pairs={{0,4},{4,8},{8,12},{12,0},{1,5},{5,9},{9,13},{13,1},{2,6},{6,10},{... | collective-permute-start | bytes 221192 | tf_op jit(solution)/shard_map/ppermute | solution.py:238
  41.8 10.3 %copy-start.9 = (bf16[192,384]{1,0:T(8,128)(2,1)}, bf16[192,384]{1,0:T(8,128)(2,1)S(1)}, u32[]{:S(2)}) copy-start(bf16[192,384]{1,0:T(8,128)(2,1)S(1)} %collective-permute-done.2.after_ref) | copy-start | bytes 442372
  41.8 10.3 %collective-permute-start.3 = (bf16[96,384]{1,0:T(8,128)(2,1)S(1)}, bf16[96,384]{1,0:T(8,128)(2,1)S(1)}, u32[]{:S(2)}, u32[]{:S(2)}) collective-permute-start(bf16[96,384]{1,0:T(8,128)(2,1)S(1)} %slice.14), channel_id=1, source_target_pairs={{0,12},{4,0},{8,4},{12,8},{1,13},{5,1},{9,5},{13,9},{2,14},{6,2},{... | collective-permute-start | bytes 221192 | tf_op jit(solution)/shard_map/ppermute | solution.py:239
  47.4 4.8 %copy-start.10 = (bf16[96,384]{1,0:T(8,128)(2,1)}, bf16[96,384]{1,0:T(8,128)(2,1)S(1)}, u32[]{:S(2)}) copy-start(bf16[96,384]{1,0:T(8,128)(2,1)S(1)} %collective-permute-done.1.low_ref) | copy-start | bytes 221188
  52.2 0.6 copy-start.11
  55.9 28.5 %all-to-all-start = ((bf16[4,4,192,384]{3,2,1,0:T(8,128)(2,1)}), bf16[4,4,192,384]{3,2,1,0:T(8,128)(2,1)S(1)}, u32[]{:S(2)}, u32[]{:S(2)}) async-start(bf16[4,4,192,384]{3,2,1,0:T(8,128)(2,1)} %spread.1), calls=%async_computation | async-start | bytes 4718592 | tf_op jit(solution)/shard_map/all_to_all | solution.py:253
  61.4 22.9 %copy-start.5 = (s32[4]{0:T(128)S(1)}, s32[4]{0:T(128)}, u32[]{:S(2)}) copy-start(s32[4]{0:T(128)} %pad_add_fusion.place_ref) | copy-start | bytes 52
  84.4 17.6 %copy-start.6 = (f32[128]{0:T(128)S(1)}, f32[128]{0:T(128)}, u32[]{:S(2)}) copy-start(f32[128]{0:T(128)} %param.12) | copy-start | bytes 1540
  84.4 17.6 %copy-start.7 = (f32[128]{0:T(128)S(1)}, f32[128]{0:T(128)}, u32[]{:S(2)}) copy-start(f32[128]{0:T(128)} %param.13) | copy-start | bytes 1540
  88.7 11.6 %collective-permute-start.4 = (bf16[192,6144]{1,0:T(8,128)(2,1)S(1)}, bf16[192,6144]{1,0:T(8,128)(2,1)S(1)}, u32[]{:S(2)}, u32[]{:S(2)}) collective-permute-start(bf16[192,6144]{1,0:T(8,128)(2,1)S(1)} %norm.1.own_ref), channel_id=1, source_target_pairs={{0,16},{16,0},{1,17},{17,1},{2,18},{18,2},{3,19},{19,3},{4,20},{20... | collective-permute-start | bytes 7077896 | tf_op jit(solution)/shard_map/ppermute | solution.py:269
  96.2 1.4 copy-start.1
  102.0 1.7 copy-start.2
  108.8 0.9 copy-start.3
  109.7 24.7 %all-to-all-start.1 = ((bf16[4,2,2,192,128]{4,3,2,1,0:T(8,128)(2,1)}), bf16[4,2,2,192,128]{4,3,2,1,0:T(8,128)(2,1)S(1)}, u32[]{:S(2)}, u32[]{:S(2)}) async-start(bf16[4,2,2,192,128]{4,3,2,1,0:T(8,128)(2,1)} %copy-done.3), calls=%async_computation.1 | async-start | bytes 1572864 | tf_op jit(solution)/shard_map/all_to_all | solution.py:288
  114.8 55.9 %copy-start.4 = (bf16[4,256,384]{2,1,0:T(8,128)(2,1)S(1)}, bf16[4,256,384]{2,1,0:T(8,128)(2,1)}, u32[]{:S(2)}) copy-start(bf16[4,256,384]{2,1,0:T(8,128)(2,1)} %get-tuple-element.29.w0) | copy-start | bytes 2359300
  114.8 23.3 %collective-permute-start.8 = (bf16[4,256,384]{2,1,0:T(8,128)(2,1)}, bf16[4,256,384]{2,1,0:T(8,128)(2,1)S(1)}, u32[]{:S(2)}, u32[]{:S(2)}) collective-permute-start(bf16[4,256,384]{2,1,0:T(8,128)(2,1)} %get-tuple-element.26), channel_id=1, source_target_pairs={{0,2},{1,3},{2,0},{3,1},{4,6},{5,7},{6,4},{7,5},{8,10},{9,11},{10,... | collective-permute-start | bytes 2359304 | tf_op jit(solution)/shard_map/ppermute | solution.py:256
  118.1 9.6 %collective-permute-start.5 = (bf16[2,192,128]{2,1,0:T(8,128)(2,1)S(1)}, bf16[2,192,128]{2,1,0:T(8,128)(2,1)S(1)}, u32[]{:S(2)}, u32[]{:S(2)}) collective-permute-start(bf16[2,192,128]{2,1,0:T(8,128)(2,1)S(1)} %get-tuple-element.23.q0), channel_id=1, source_target_pairs={{0,128},{128,256},{256,384},{384,0},{1,129},{129,257},{257,385},{3... | collective-permute-start | bytes 294920 | tf_op jit(solution)/shard_map/ppermute | solution.py:289
  120.8 7.8 %collective-permute-start.6 = (bf16[2,192,128]{2,1,0:T(8,128)(2,1)S(1)}, bf16[2,192,128]{2,1,0:T(8,128)(2,1)S(1)}, u32[]{:S(2)}, u32[]{:S(2)}) collective-permute-start(bf16[2,192,128]{2,1,0:T(8,128)(2,1)S(1)} %get-tuple-element.23.q0), channel_id=1, source_target_pairs={{0,256},{128,384},{256,0},{384,128},{1,257},{129,385},{257,1},{385... | collective-permute-start | bytes 294920 | tf_op jit(solution)/shard_map/ppermute | solution.py:289
  125.7 5.7 %collective-permute-start.7 = (bf16[2,192,128]{2,1,0:T(8,128)(2,1)S(1)}, bf16[2,192,128]{2,1,0:T(8,128)(2,1)S(1)}, u32[]{:S(2)}, u32[]{:S(2)}) collective-permute-start(bf16[2,192,128]{2,1,0:T(8,128)(2,1)S(1)} %get-tuple-element.23.q0), channel_id=1, source_target_pairs={{0,384},{128,0},{256,128},{384,256},{1,385},{129,1},{257,129},{385... | collective-permute-start | bytes 294920 | tf_op jit(solution)/shard_map/ppermute | solution.py:289
  138.0 32.6 %collective-permute-start.10 = (bf16[4,256,384]{2,1,0:T(8,128)(2,1)}, bf16[4,256,384]{2,1,0:T(8,128)(2,1)S(1)}, u32[]{:S(2)}, u32[]{:S(2)}) collective-permute-start(bf16[4,256,384]{2,1,0:T(8,128)(2,1)} %get-tuple-element.32), channel_id=1, source_target_pairs={{0,3},{1,0},{2,1},{3,2},{4,7},{5,4},{6,5},{7,6},{8,11},{9,8},{10,9... | collective-permute-start | bytes 2359304 | tf_op jit(solution)/shard_map/ppermute | solution.py:307
  141.1 29.6 %collective-permute-start.9 = (bf16[4,256,384]{2,1,0:T(8,128)(2,1)}, bf16[4,256,384]{2,1,0:T(8,128)(2,1)}, u32[]{:S(2)}, u32[]{:S(2)}) collective-permute-start(bf16[4,256,384]{2,1,0:T(8,128)(2,1)} %get-tuple-element.30), channel_id=1, source_target_pairs={{0,1},{1,2},{2,3},{3,0},{4,5},{5,6},{6,7},{7,4},{8,9},{9,10},{10,1... | collective-permute-start | bytes 2359304 | tf_op jit(solution)/shard_map/ppermute | solution.py:306
  173.3 18.0 %collective-permute-start.11 = (bf16[192,384]{1,0:T(8,128)(2,1)}, bf16[192,384]{1,0:T(8,128)(2,1)S(1)}, u32[]{:S(2)}, u32[]{:S(2)}) collective-permute-start(bf16[192,384]{1,0:T(8,128)(2,1)} %get-tuple-element.34), channel_id=1, source_target_pairs={{0,8},{4,12},{8,0},{12,4},{1,9},{5,13},{9,1},{13,5},{2,10},{6,14},... | collective-permute-start | bytes 442376 | tf_op jit(solution)/shard_map/ppermute | solution.py:324
  182.0 22.4 %collective-permute-start.12 = (bf16[192,384]{1,0:T(8,128)(2,1)S(1)}, bf16[192,384]{1,0:T(8,128)(2,1)S(1)}, u32[]{:S(2)}, u32[]{:S(2)}) collective-permute-start(bf16[192,384]{1,0:T(8,128)(2,1)S(1)} %get-tuple-element.35), channel_id=1, source_target_pairs={{0,4},{4,8},{8,12},{12,0},{1,5},{5,9},{9,13},{13,1},{2,6},{6,10},{... | collective-permute-start | bytes 442376 | tf_op jit(solution)/shard_map/ppermute | solution.py:324
  186.2 21.1 %collective-permute-start.13 = (bf16[192,384]{1,0:T(8,128)(2,1)S(1)}, bf16[192,384]{1,0:T(8,128)(2,1)S(1)}, u32[]{:S(2)}, u32[]{:S(2)}) collective-permute-start(bf16[192,384]{1,0:T(8,128)(2,1)S(1)} %get-tuple-element.36), channel_id=1, source_target_pairs={{0,12},{4,0},{8,4},{12,8},{1,13},{5,1},{9,5},{13,9},{2,14},{6,2},{... | collective-permute-start | bytes 442376 | tf_op jit(solution)/shard_map/ppermute | solution.py:324
Sparse Core Ops, SparseCore 0:
  10.1 91.7 all-gather.1

commit v9 on v6

--- a/solution.py
+++ b/solution.py
@@ -83,7 +83,7 @@
         target[0] = source[...]
 
 
-def project_kernel(place_ref, own_ref, other_ref, weight_ref, q_gain_ref, k_gain_ref, q_ref, kv_ref, held, sems):
+def project_kernel(place_ref, own_ref, other_ref, weight_ref, q_gain_ref, k_gain_ref, q_ref, kv_ref, held, own, sems):
     rows = own_ref.shape[0]
     depth = held.shape[1]
     copies = [
@@ -92,12 +92,20 @@
         )
         for i in range(held.shape[0])
     ]
-    for copy in copies:
-        copy.start()
+    more = [
+        pltpu.make_async_copy(
+            own_ref.at[:, pl.ds(i * depth, depth)], own.at[i], sems.at[held.shape[0] + i]
+        )
+        for i in range(held.shape[0])
+    ]
+    for first, second in zip(copies, more):
+        first.start()
+        second.start()
     total = None
     for i, copy in enumerate(copies):
         part = slice(i * depth, (i + 1) * depth)
-        hidden = jnp.concatenate([own_ref[:, part], other_ref[:, part]], axis=0)
+        more[i].wait()
+        hidden = jnp.concatenate([own[i], other_ref[:, part]], axis=0)
         copy.wait()
         product = jnp.dot(hidden, held[i], preferred_element_type=F32)
         total = product if total is None else total + product
@@ -266,9 +274,10 @@
     sibling = lax.ppermute(hidden, "core", [(0, 1), (1, 0)])
 
     depth = D // GRID
+    in_hbm = pl.BlockSpec(memory_space=pltpu.HBM)
     queries, pairs = pl.pallas_call(
         project_kernel,
-        in_specs=[in_smem, in_vmem, in_vmem, pl.BlockSpec(memory_space=pltpu.HBM), in_vmem, in_vmem],
+        in_specs=[in_smem, in_hbm, in_vmem, in_hbm, in_vmem, in_vmem],
         out_specs=[in_vmem, in_vmem],
         out_shape=[
             jax.ShapeDtypeStruct((2, rows, HD), BF),
@@ -276,11 +285,19 @@
         ],
         scratch_shapes=[
             pltpu.VMEM((GRID, depth, 3 * HD), BF),
-            pltpu.SemaphoreType.DMA((GRID,)),
+            pltpu.VMEM((GRID, rows, depth), BF),
+            pltpu.SemaphoreType.DMA((2 * GRID,)),
         ],
         compiler_params=PARAMS,
         name="project",
-    )(place, hidden, sibling, pltpu.with_memory_space_constraint(full_weights, pltpu.HBM), q_gain.reshape(1, HD), k_gain.reshape(1, HD))
+    )(
+        place,
+        pltpu.with_memory_space_constraint(hidden, pltpu.HBM),
+        sibling,
+        pltpu.with_memory_space_constraint(full_weights, pltpu.HBM),
+        q_gain.reshape(1, HD),
+        k_gain.reshape(1, HD),
+    )
 
     pairs = lax.all_to_all(pairs, "zl", 0, 0, tiled=True)
     queries = [queries] + [lax.ppermute(queries, "y", shift(k)) for k in (1, 2, 3)]
@@ -307,9 +324,9 @@
         in_specs=[in_vmem],
         out_specs=in_vmem,
         out_shape=jax.ShapeDtypeStruct((GRID, rows, channels), BF),
+        compiler_params=PARAMS,
         name="combine",
     )(parts)
-    around, out1, out3 = lax.optimization_barrier((around, out1, out3))
     around = lax.all_to_all(around, "seq", 0, 0, tiled=True)
     outs = pl.pallas_call(
         branch_kernel,

time: 220 us -> 214 us (0.973)
  Pallas kernels: 27.3 us -> 24.9 us
  waiting for transfers between devices: 55.5 us -> 53.3 us
    ppermute x1, waiting for transfers between devices: 2.5 us -> 0.01 us  [per_device(): out1 = lax.ppermute(out1, 'seq', shift(1))]
where the time goes in v9:
time: 214 us; the launch traced here: 210 us
  starting transfers between devices  87 us (41%)
  waiting for transfers between devices  53.3 us (25%)
  blocking collectives  25.2 us (12%)
  Pallas kernels  24.9 us (12%)
  between operations  15 us (7%)
  local copies, waits for them, and re-layouts  3.34 us (2%)
    ppermute x3, starting transfers between devices, per_device(): shares = [lax.ppermute(outs[k], 'head', shift(k)) for k in (2, 1, 3)]  17.8 us
    all_to_all x1, waiting for transfers between devices, per_device(): raw = lax.all_to_all(raw, 'seq', 0, 0, tiled=True)  17.8 us
    ppermute x3, waiting for transfers between devices, per_device(): shares = [lax.ppermute(outs[k], 'head', shift(k)) for k in (2, 1, 3)]  15.4 us
    ppermute x1, starting transfers between devices, per_device(): far_low = lax.ppermute(before[:half], 'head', shift(1))  15.1 us
    all_to_all x1, blocking collectives, per_device(): parts = lax.all_to_all(parts, ('y', 'core'), 0, 0, tiled=True)  15 us
    ppermute x3, starting transfers between devices, per_device(): lax.ppermute(queries, 'y', shift(k))  10.2 us
    all_to_all x1, blocking collectives, per_device(): around = lax.all_to_all(around, 'seq', 0, 0, tiled=True)  10.2 us
    ppermute x1, starting transfers between devices, per_device(): before = lax.ppermute(latents, 'head', shift(1))  9.65 us
  transfers between devices with their start and end apart: 17, of which 11 were waited for; matrix products, arithmetic and copies ran while one was open for 0% of the time, Pallas kernels for 8%

profile of v9, /device:TPU:1, one launch (start us, length us, event | category | flops | bytes accessed | tf_op | source)
XLA Modules:
  0.0 210.1 jit_solution(728587984740137298)
XLA Ops:
  6.5 0.0 copy-start
  6.5 0.0 all-gather.2.cloned.1.call-start
  7.3 1.9 average.1
  9.2 0.0 all-gather.2.cloned.1.call-update
  9.2 9.6 %collective-permute-start = (bf16[192,384]{1,0:T(8,128)(2,1)}, bf16[192,384]{1,0:T(8,128)(2,1)S(1)}, u32[]{:S(2)}, u32[]{:S(2)}) collective-permute-start(bf16[192,384]{1,0:T(8,128)(2,1)} %own_ref.1), channel_id=1, source_target_pairs={{0,4},{4,8},{8,12},{12,0},{1,5},{5,9},{9,13},{13,1},{2,6},{6,10},{... | collective-permute-start | bytes 442376 | tf_op jit(solution)/shard_map/ppermute | solution.py:245
  18.8 5.6 %collective-permute-start.2 = (bf16[192,384]{1,0:T(8,128)(2,1)}, bf16[192,384]{1,0:T(8,128)(2,1)S(1)}, u32[]{:S(2)}, u32[]{:S(2)}) collective-permute-start(bf16[192,384]{1,0:T(8,128)(2,1)} %own_ref.1), channel_id=1, source_target_pairs={{0,12},{4,0},{8,4},{12,8},{1,13},{5,1},{9,5},{13,9},{2,14},{6,2},{... | collective-permute-start | bytes 442376 | tf_op jit(solution)/shard_map/ppermute | solution.py:246
  24.4 1.5 collective-permute-done.before_ref
  25.9 15.1 %collective-permute-start.1 = (bf16[96,384]{1,0:T(8,128)(2,1)S(1)}, bf16[96,384]{1,0:T(8,128)(2,1)S(1)}, u32[]{:S(2)}, u32[]{:S(2)}) collective-permute-start(bf16[96,384]{1,0:T(8,128)(2,1)S(1)} %slice.13), channel_id=1, source_target_pairs={{0,4},{4,8},{8,12},{12,0},{1,5},{5,9},{9,13},{13,1},{2,6},{6,10},{... | collective-permute-start | bytes 221192 | tf_op jit(solution)/shard_map/ppermute | solution.py:247
  41.0 0.0 collective-permute-done.2.after_ref
  41.0 0.0 copy-start.9
  41.0 3.3 %collective-permute-start.3 = (bf16[96,384]{1,0:T(8,128)(2,1)S(1)}, bf16[96,384]{1,0:T(8,128)(2,1)S(1)}, u32[]{:S(2)}, u32[]{:S(2)}) collective-permute-start(bf16[96,384]{1,0:T(8,128)(2,1)S(1)} %slice.14), channel_id=1, source_target_pairs={{0,12},{4,0},{8,4},{12,8},{1,13},{5,1},{9,5},{13,9},{2,14},{6,2},{... | collective-permute-start | bytes 221192 | tf_op jit(solution)/shard_map/ppermute | solution.py:248
  44.3 2.2 %collective-permute-done.1.low_ref = bf16[96,384]{1,0:T(8,128)(2,1)S(1)} collective-permute-done((bf16[96,384]{1,0:T(8,128)(2,1)S(1)}, bf16[96,384]{1,0:T(8,128)(2,1)S(1)}, u32[]{:S(2)}, u32[]{:S(2)}) %collective-permute-start.1) | collective-permute-done | bytes 73760 | tf_op jit(solution)/shard_map/ppermute | solution.py:247
  46.5 4.8 %collective-permute-done.3.high_ref = bf16[96,384]{1,0:T(8,128)(2,1)S(1)} collective-permute-done((bf16[96,384]{1,0:T(8,128)(2,1)S(1)}, bf16[96,384]{1,0:T(8,128)(2,1)S(1)}, u32[]{:S(2)}, u32[]{:S(2)}) %collective-permute-start.3) | collective-permute-done | bytes 73760 | tf_op jit(solution)/shard_map/ppermute | solution.py:248
  51.3 0.0 copy-done.8
  51.3 0.0 copy-done.9
  51.3 0.0 copy-done.10
  51.3 0.0 copy-start.11
  51.3 0.6 copy-done.11
  51.9 2.7 %spread.1 = bf16[4,4,192,384]{3,2,1,0:T(8,128)(2,1)} custom-call(bf16[192,384]{1,0:T(8,128)(2,1)} %own_ref.1, bf16[192,384]{1,0:T(8,128)(2,1)} %copy-done.8, bf16[96,384]{1,0:T(8,128)(2,1)} %copy-done.10, bf16[96,384]{1,0:T(8,128)(2,1)} %copy-done.11, bf16[192,384]{1,0:T(8,128)(2,1)} %copy-done.9), custom_call_target="tpu_custom_call" | custom-call | tf_op jit(solution)/shard_map/spread/pallas_call | solution.py:251
  54.6 4.0 %all-to-all-start = ((bf16[4,4,192,384]{3,2,1,0:T(8,128)(2,1)}), bf16[4,4,192,384]{3,2,1,0:T(8,128)(2,1)S(1)}, u32[]{:S(2)}, u32[]{:S(2)}) async-start(bf16[4,4,192,384]{3,2,1,0:T(8,128)(2,1)} %spread.1), calls=%async_computation | async-start | bytes 4718592 | tf_op jit(solution)/shard_map/all_to_all | solution.py:258
  59.3 0.0 copy-done
  59.3 0.2 dynamic-slice_reduce_fusion
  59.5 0.1 reshape.15.mod_ref
  59.6 0.6 pad_add_fusion.place_ref
  60.2 5.2 %pick.1 = (bf16[4,256,384]{2,1,0:T(8,128)(2,1)}, bf16[4,256,384]{2,1,0:T(8,128)(2,1)}, bf16[4,256,384]{2,1,0:T(8,128)(2,1)}, bf16[4,256,384]{2,1,0:T(8,128)(2,1)}) custom-call(s32[4]{0:T(128)} %pad_add_fusion.place_ref, bf16[256,6144]{1,0:T(8,128)(2,1)} %refs_3_.1, bf16[256,6144]{1,0:T(8,128)(2,1)} %refs_3_.1, bf16[256,6144]{1,0:T(8,128)(2,1)} %refs_3_.1, ...), custom_call_target="tpu_custom_call" | custom-call | tf_op jit(solution)/shard_map/pick/pallas_call | solution.py:231
  65.4 17.8 %all-to-all-done.raw_ref = bf16[4,4,192,384]{3,2,1,0:T(8,128)(2,1)S(1)} async-done(((bf16[4,4,192,384]{3,2,1,0:T(8,128)(2,1)}), bf16[4,4,192,384]{3,2,1,0:T(8,128)(2,1)S(1)}, u32[]{:S(2)}, u32[]{:S(2)}) %all-to-all-start) | async-done | bytes 2359328 | tf_op jit(solution)/shard_map/all_to_all | solution.py:258
  83.2 4.3 %norm.1.own_ref = bf16[192,6144]{1,0:T(8,128)(2,1)S(1)} custom-call(s32[4]{0:T(128)S(1)} %copy-done.4, bf16[4,4,192,384]{3,2,1,0:T(8,128)(2,1)S(1)} %all-to-all-done.raw_ref, f32[3,4,4,384]{3,2,1,0:T(4,128)S(1)} %reshape.15.mod_ref), custom_call_target="tpu_custom_call" | custom-call | tf_op jit(solution)/shard_map/norm/pallas_call | solution.py:262
  87.4 1.4 copy-done.1
  88.8 7.5 %collective-permute-start.4 = (bf16[192,6144]{1,0:T(8,128)(2,1)S(1)}, bf16[192,6144]{1,0:T(8,128)(2,1)S(1)}, u32[]{:S(2)}, u32[]{:S(2)}) collective-permute-start(bf16[192,6144]{1,0:T(8,128)(2,1)S(1)} %norm.1.own_ref), channel_id=1, source_target_pairs={{0,16},{16,0},{1,17},{17,1},{2,18},{18,2},{3,19},{19,3},{4,20},{20... | collective-permute-start | bytes 7077896 | tf_op jit(solution)/shard_map/ppermute | solution.py:274
  96.3 4.3 %collective-permute-done.4.other_ref = bf16[192,6144]{1,0:T(8,128)(2,1)S(1)} collective-permute-done((bf16[192,6144]{1,0:T(8,128)(2,1)S(1)}, bf16[192,6144]{1,0:T(8,128)(2,1)S(1)}, u32[]{:S(2)}, u32[]{:S(2)}) %collective-permute-start.4) | collective-permute-done | bytes 2359328 | tf_op jit(solution)/shard_map/ppermute | solution.py:274
  100.6 0.5 all-gather.2.cloned.1.call-done.weight_ref
  101.1 0.0 copy-done.5
  101.1 5.6 %project.1 = (bf16[2,192,128]{2,1,0:T(8,128)(2,1)S(1)}, bf16[4,2,2,192,128]{4,3,2,1,0:T(8,128)(2,1)S(1)}) custom-call(s32[4]{0:T(128)S(1)} %copy-done.4, bf16[192,6144]{1,0:T(8,128)(2,1)} %copy-done.1, bf16[192,6144]{1,0:T(8,128)(2,1)S(1)} %collective-permute-done.4.other_ref, bf16[2,6144,384]{2,1,0:T(8,128)(2,1)} %all-gather.2.cloned.1.call-done.weight_ref, ...), custom_call_target="tpu_custom_call" | custom-call | tf_op jit(solution)/shard_map/project/pallas_call | solution.py:278
  106.7 0.0 copy-start.2
  106.7 0.9 copy-done.2
  107.6 6.0 %all-to-all-start.1 = ((bf16[4,2,2,192,128]{4,3,2,1,0:T(8,128)(2,1)}), bf16[4,2,2,192,128]{4,3,2,1,0:T(8,128)(2,1)S(1)}, u32[]{:S(2)}, u32[]{:S(2)}) async-start(bf16[4,2,2,192,128]{4,3,2,1,0:T(8,128)(2,1)} %copy-done.2), calls=%async_computation.1 | async-start | bytes 1572864 | tf_op jit(solution)/shard_map/all_to_all | solution.py:302
  113.6 2.6 %collective-permute-start.8 = (bf16[4,256,384]{2,1,0:T(8,128)(2,1)}, bf16[4,256,384]{2,1,0:T(8,128)(2,1)S(1)}, u32[]{:S(2)}, u32[]{:S(2)}) collective-permute-start(bf16[4,256,384]{2,1,0:T(8,128)(2,1)} %get-tuple-element.26), channel_id=1, source_target_pairs={{0,2},{1,3},{2,0},{3,1},{4,6},{5,7},{6,4},{7,5},{8,10},{9,11},{10,... | collective-permute-start | bytes 2359304 | tf_op jit(solution)/shard_map/ppermute | solution.py:261
  116.2 2.5 %collective-permute-start.5 = (bf16[2,192,128]{2,1,0:T(8,128)(2,1)S(1)}, bf16[2,192,128]{2,1,0:T(8,128)(2,1)S(1)}, u32[]{:S(2)}, u32[]{:S(2)}) collective-permute-start(bf16[2,192,128]{2,1,0:T(8,128)(2,1)S(1)} %get-tuple-element.23.q0), channel_id=1, source_target_pairs={{0,128},{128,256},{256,384},{384,0},{1,129},{129,257},{257,385},{3... | collective-permute-start | bytes 294920 | tf_op jit(solution)/shard_map/ppermute | solution.py:303
  118.7 5.8 %collective-permute-start.6 = (bf16[2,192,128]{2,1,0:T(8,128)(2,1)S(1)}, bf16[2,192,128]{2,1,0:T(8,128)(2,1)S(1)}, u32[]{:S(2)}, u32[]{:S(2)}) collective-permute-start(bf16[2,192,128]{2,1,0:T(8,128)(2,1)S(1)} %get-tuple-element.23.q0), channel_id=1, source_target_pairs={{0,256},{128,384},{256,0},{384,128},{1,257},{129,385},{257,1},{385... | collective-permute-start | bytes 294920 | tf_op jit(solution)/shard_map/ppermute | solution.py:303
  124.6 1.9 collective-permute-start.7
  126.5 0.0 collective-permute-done.5.q1
  126.5 0.9 collective-permute-done.6.q2
  127.4 2.8 %collective-permute-done.7.q3 = bf16[2,192,128]{2,1,0:T(8,128)(2,1)S(1)} collective-permute-done((bf16[2,192,128]{2,1,0:T(8,128)(2,1)S(1)}, bf16[2,192,128]{2,1,0:T(8,128)(2,1)S(1)}, u32[]{:S(2)}, u32[]{:S(2)}) %collective-permute-start.7) | collective-permute-done | bytes 98336 | tf_op jit(solution)/shard_map/ppermute | solution.py:303
  130.2 3.1 %all-to-all-done.1.kv_ref = bf16[4,2,2,192,128]{4,3,2,1,0:T(8,128)(2,1)S(1)} async-done(((bf16[4,2,2,192,128]{4,3,2,1,0:T(8,128)(2,1)}), bf16[4,2,2,192,128]{4,3,2,1,0:T(8,128)(2,1)S(1)}, u32[]{:S(2)}, u32[]{:S(2)}) %all-to-all-start.1) | async-done | bytes 786464 | tf_op jit(solution)/shard_map/all_to_all | solution.py:302
  133.3 3.6 %attend.1 = bf16[8,208,128]{2,1,0:T(8,128)(2,1)S(1)} custom-call(s32[4]{0:T(128)S(1)} %copy-done.4, bf16[2,192,128]{2,1,0:T(8,128)(2,1)S(1)} %get-tuple-element.23.q0, bf16[2,192,128]{2,1,0:T(8,128)(2,1)S(1)} %collective-permute-done.5.q1, bf16[2,192,128]{2,1,0:T(8,128)(2,1)S(1)} %collective-permute-done.6.q2, ...), custom_call_target="tpu_custom_call" | custom-call | tf_op jit(solution)/shard_map/attend/pallas_call | solution.py:306
  136.9 0.0 collective-permute-done.8.w2
  136.9 2.7 %collective-permute-start.10 = (bf16[4,256,384]{2,1,0:T(8,128)(2,1)}, bf16[4,256,384]{2,1,0:T(8,128)(2,1)S(1)}, u32[]{:S(2)}, u32[]{:S(2)}) collective-permute-start(bf16[4,256,384]{2,1,0:T(8,128)(2,1)} %get-tuple-element.32), channel_id=1, source_target_pairs={{0,3},{1,0},{2,1},{3,2},{4,7},{5,4},{6,5},{7,6},{8,11},{9,8},{10,9... | collective-permute-start | bytes 2359304 | tf_op jit(solution)/shard_map/ppermute | solution.py:321
  139.5 2.6 %collective-permute-start.9 = (bf16[4,256,384]{2,1,0:T(8,128)(2,1)}, bf16[4,256,384]{2,1,0:T(8,128)(2,1)S(1)}, u32[]{:S(2)}, u32[]{:S(2)}) collective-permute-start(bf16[4,256,384]{2,1,0:T(8,128)(2,1)} %get-tuple-element.30), channel_id=1, source_target_pairs={{0,1},{1,2},{2,3},{3,0},{4,5},{5,6},{6,7},{7,4},{8,9},{9,10},{10,1... | collective-permute-start | bytes 2359304 | tf_op jit(solution)/shard_map/ppermute | solution.py:320
  142.2 15.0 %all_to_all.20.parts_ref = bf16[8,208,128]{2,1,0:T(8,128)(2,1)S(1)} all-to-all(bf16[8,208,128]{2,1,0:T(8,128)(2,1)S(1)} %attend.1), channel_id=1, replica_groups=mesh['y'=4,'zl'=4,'core'=2,'head'=4,'seq'=4] {'y','core'}, dimensions={0} | all-to-all | bytes 851968 | tf_op jit(solution)/shard_map/all_to_all | solution.py:319
  157.2 0.1 combine.1
  157.4 0.0 copy-start.7
  157.4 10.2 %all_to_all.21.a_ref = bf16[4,192,256]{2,1,0:T(8,128)(2,1)S(1)} all-to-all(bf16[4,192,256]{2,1,0:T(8,128)(2,1)S(1)} %combine.1), channel_id=1, replica_groups=mesh['y'=4,'zl'=4,'core'=2,'head'=4,'seq'=4] {'seq'}, dimensions={0} | all-to-all | bytes 786432 | tf_op jit(solution)/shard_map/all_to_all | solution.py:330
  167.6 0.0 collective-permute-done.10.w3
  167.6 0.0 collective-permute-done.9.w1
  167.6 1.5 branch.1
  169.1 8.6 %collective-permute-start.11 = (bf16[192,384]{1,0:T(8,128)(2,1)S(1)}, bf16[192,384]{1,0:T(8,128)(2,1)S(1)}, u32[]{:S(2)}, u32[]{:S(2)}) collective-permute-start(bf16[192,384]{1,0:T(8,128)(2,1)S(1)} %get-tuple-element.34), channel_id=1, source_target_pairs={{0,8},{4,12},{8,0},{12,4},{1,9},{5,13},{9,1},{13,5},{2,10},{6,14},... | collective-permute-start | bytes 442376 | tf_op jit(solution)/shard_map/ppermute | solution.py:339
  177.8 4.1 %collective-permute-start.12 = (bf16[192,384]{1,0:T(8,128)(2,1)S(1)}, bf16[192,384]{1,0:T(8,128)(2,1)S(1)}, u32[]{:S(2)}, u32[]{:S(2)}) collective-permute-start(bf16[192,384]{1,0:T(8,128)(2,1)S(1)} %get-tuple-element.35), channel_id=1, source_target_pairs={{0,4},{4,8},{8,12},{12,0},{1,5},{5,9},{9,13},{13,1},{2,6},{6,10},{... | collective-permute-start | bytes 442376 | tf_op jit(solution)/shard_map/ppermute | solution.py:339
  181.9 5.1 %collective-permute-start.13 = (bf16[192,384]{1,0:T(8,128)(2,1)S(1)}, bf16[192,384]{1,0:T(8,128)(2,1)S(1)}, u32[]{:S(2)}, u32[]{:S(2)}) collective-permute-start(bf16[192,384]{1,0:T(8,128)(2,1)S(1)} %get-tuple-element.36), channel_id=1, source_target_pairs={{0,12},{4,0},{8,4},{12,8},{1,13},{5,1},{9,5},{13,9},{2,14},{6,2},{... | collective-permute-start | bytes 442376 | tf_op jit(solution)/shard_map/ppermute | solution.py:339
  187.0 0.1 dynamic-slice_reduce_fusion.1
  187.1 0.0 collective-permute-done.11
  187.1 13.2 %collective-permute-done.12 = bf16[192,384]{1,0:T(8,128)(2,1)S(1)} collective-permute-done((bf16[192,384]{1,0:T(8,128)(2,1)S(1)}, bf16[192,384]{1,0:T(8,128)(2,1)S(1)}, u32[]{:S(2)}, u32[]{:S(2)}) %collective-permute-start.12) | collective-permute-done | bytes 147488 | tf_op jit(solution)/shard_map/ppermute | solution.py:339
  200.2 2.2 %collective-permute-done.13 = bf16[192,384]{1,0:T(8,128)(2,1)S(1)} collective-permute-done((bf16[192,384]{1,0:T(8,128)(2,1)S(1)}, bf16[192,384]{1,0:T(8,128)(2,1)S(1)}, u32[]{:S(2)}, u32[]{:S(2)}) %collective-permute-start.13) | collective-permute-done | bytes 147488 | tf_op jit(solution)/shard_map/ppermute | solution.py:339
  202.5 0.0 copy-done.7
  202.5 0.8 add_convert_fusion
  (12 shorter events, 0.0 us)
Async XLA Ops:
  6.5 52.8 %copy-start = (f32[8,3,6144]{2,0,1:T(8,128)S(1)}, f32[8,3,6144]{2,0,1:T(8,128)}, u32[]{:S(2)}) copy-start(f32[8,3,6144]{2,0,1:T(8,128)} %param.15) | copy-start | bytes 1769476
  6.5 94.6 %all-gather.2.cloned.1.call-start = ((), (), s32[]{:S(2)}) async-start(), calls=%async_computation.4 | async-start | bytes 9732096 | tf_op jit(solution)/shard_map/all_gather | solution.py:222
  9.2 16.7 %collective-permute-start = (bf16[192,384]{1,0:T(8,128)(2,1)}, bf16[192,384]{1,0:T(8,128)(2,1)S(1)}, u32[]{:S(2)}, u32[]{:S(2)}) collective-permute-start(bf16[192,384]{1,0:T(8,128)(2,1)} %own_ref.1), channel_id=1, source_target_pairs={{0,4},{4,8},{8,12},{12,0},{1,5},{5,9},{9,13},{13,1},{2,6},{6,10},{... | collective-permute-start | bytes 442376 | tf_op jit(solution)/shard_map/ppermute | solution.py:245
  18.8 22.1 %collective-permute-start.2 = (bf16[192,384]{1,0:T(8,128)(2,1)}, bf16[192,384]{1,0:T(8,128)(2,1)S(1)}, u32[]{:S(2)}, u32[]{:S(2)}) collective-permute-start(bf16[192,384]{1,0:T(8,128)(2,1)} %own_ref.1), channel_id=1, source_target_pairs={{0,12},{4,0},{8,4},{12,8},{1,13},{5,1},{9,5},{13,9},{2,14},{6,2},{... | collective-permute-start | bytes 442376 | tf_op jit(solution)/shard_map/ppermute | solution.py:246
  25.9 25.4 %copy-start.8 = (bf16[192,384]{1,0:T(8,128)(2,1)}, bf16[192,384]{1,0:T(8,128)(2,1)S(1)}, u32[]{:S(2)}) copy-start(bf16[192,384]{1,0:T(8,128)(2,1)S(1)} %collective-permute-done.before_ref) | copy-start | bytes 442372
  25.9 20.6 %collective-permute-start.1 = (bf16[96,384]{1,0:T(8,128)(2,1)S(1)}, bf16[96,384]{1,0:T(8,128)(2,1)S(1)}, u32[]{:S(2)}, u32[]{:S(2)}) collective-permute-start(bf16[96,384]{1,0:T(8,128)(2,1)S(1)} %slice.13), channel_id=1, source_target_pairs={{0,4},{4,8},{8,12},{12,0},{1,5},{5,9},{9,13},{13,1},{2,6},{6,10},{... | collective-permute-start | bytes 221192 | tf_op jit(solution)/shard_map/ppermute | solution.py:247
  41.0 10.3 %copy-start.9 = (bf16[192,384]{1,0:T(8,128)(2,1)}, bf16[192,384]{1,0:T(8,128)(2,1)S(1)}, u32[]{:S(2)}) copy-start(bf16[192,384]{1,0:T(8,128)(2,1)S(1)} %collective-permute-done.2.after_ref) | copy-start | bytes 442372
  41.0 10.3 %collective-permute-start.3 = (bf16[96,384]{1,0:T(8,128)(2,1)S(1)}, bf16[96,384]{1,0:T(8,128)(2,1)S(1)}, u32[]{:S(2)}, u32[]{:S(2)}) collective-permute-start(bf16[96,384]{1,0:T(8,128)(2,1)S(1)} %slice.14), channel_id=1, source_target_pairs={{0,12},{4,0},{8,4},{12,8},{1,13},{5,1},{9,5},{13,9},{2,14},{6,2},{... | collective-permute-start | bytes 221192 | tf_op jit(solution)/shard_map/ppermute | solution.py:248
  46.5 4.8 %copy-start.10 = (bf16[96,384]{1,0:T(8,128)(2,1)}, bf16[96,384]{1,0:T(8,128)(2,1)S(1)}, u32[]{:S(2)}) copy-start(bf16[96,384]{1,0:T(8,128)(2,1)S(1)} %collective-permute-done.1.low_ref) | copy-start | bytes 221188
  51.3 0.6 copy-start.11
  54.6 28.5 %all-to-all-start = ((bf16[4,4,192,384]{3,2,1,0:T(8,128)(2,1)}), bf16[4,4,192,384]{3,2,1,0:T(8,128)(2,1)S(1)}, u32[]{:S(2)}, u32[]{:S(2)}) async-start(bf16[4,4,192,384]{3,2,1,0:T(8,128)(2,1)} %spread.1), calls=%async_computation | async-start | bytes 4718592 | tf_op jit(solution)/shard_map/all_to_all | solution.py:258
  60.2 23.0 %copy-start.4 = (s32[4]{0:T(128)S(1)}, s32[4]{0:T(128)}, u32[]{:S(2)}) copy-start(s32[4]{0:T(128)} %pad_add_fusion.place_ref) | copy-start | bytes 52
  83.2 18.0 %copy-start.5 = (f32[128]{0:T(128)S(1)}, f32[128]{0:T(128)}, u32[]{:S(2)}) copy-start(f32[128]{0:T(128)} %param.12) | copy-start | bytes 1540
  83.2 18.0 %copy-start.6 = (f32[128]{0:T(128)S(1)}, f32[128]{0:T(128)}, u32[]{:S(2)}) copy-start(f32[128]{0:T(128)} %param.13) | copy-start | bytes 1540
  87.4 1.4 copy-start.1
  88.8 11.8 %collective-permute-start.4 = (bf16[192,6144]{1,0:T(8,128)(2,1)S(1)}, bf16[192,6144]{1,0:T(8,128)(2,1)S(1)}, u32[]{:S(2)}, u32[]{:S(2)}) collective-permute-start(bf16[192,6144]{1,0:T(8,128)(2,1)S(1)} %norm.1.own_ref), channel_id=1, source_target_pairs={{0,16},{16,0},{1,17},{17,1},{2,18},{18,2},{3,19},{19,3},{4,20},{20... | collective-permute-start | bytes 7077896 | tf_op jit(solution)/shard_map/ppermute | solution.py:274
  106.7 0.9 copy-start.2
  107.6 25.7 %all-to-all-start.1 = ((bf16[4,2,2,192,128]{4,3,2,1,0:T(8,128)(2,1)}), bf16[4,2,2,192,128]{4,3,2,1,0:T(8,128)(2,1)S(1)}, u32[]{:S(2)}, u32[]{:S(2)}) async-start(bf16[4,2,2,192,128]{4,3,2,1,0:T(8,128)(2,1)} %copy-done.2), calls=%async_computation.1 | async-start | bytes 1572864 | tf_op jit(solution)/shard_map/all_to_all | solution.py:302
  113.6 54.0 %copy-start.3 = (bf16[4,256,384]{2,1,0:T(8,128)(2,1)S(1)}, bf16[4,256,384]{2,1,0:T(8,128)(2,1)}, u32[]{:S(2)}) copy-start(bf16[4,256,384]{2,1,0:T(8,128)(2,1)} %get-tuple-element.29.w0) | copy-start | bytes 2359300
  113.6 23.3 %collective-permute-start.8 = (bf16[4,256,384]{2,1,0:T(8,128)(2,1)}, bf16[4,256,384]{2,1,0:T(8,128)(2,1)S(1)}, u32[]{:S(2)}, u32[]{:S(2)}) collective-permute-start(bf16[4,256,384]{2,1,0:T(8,128)(2,1)} %get-tuple-element.26), channel_id=1, source_target_pairs={{0,2},{1,3},{2,0},{3,1},{4,6},{5,7},{6,4},{7,5},{8,10},{9,11},{10,... | collective-permute-start | bytes 2359304 | tf_op jit(solution)/shard_map/ppermute | solution.py:261
  116.2 10.3 %collective-permute-start.5 = (bf16[2,192,128]{2,1,0:T(8,128)(2,1)S(1)}, bf16[2,192,128]{2,1,0:T(8,128)(2,1)S(1)}, u32[]{:S(2)}, u32[]{:S(2)}) collective-permute-start(bf16[2,192,128]{2,1,0:T(8,128)(2,1)S(1)} %get-tuple-element.23.q0), channel_id=1, source_target_pairs={{0,128},{128,256},{256,384},{384,0},{1,129},{129,257},{257,385},{3... | collective-permute-start | bytes 294920 | tf_op jit(solution)/shard_map/ppermute | solution.py:303
  118.7 8.6 %collective-permute-start.6 = (bf16[2,192,128]{2,1,0:T(8,128)(2,1)S(1)}, bf16[2,192,128]{2,1,0:T(8,128)(2,1)S(1)}, u32[]{:S(2)}, u32[]{:S(2)}) collective-permute-start(bf16[2,192,128]{2,1,0:T(8,128)(2,1)S(1)} %get-tuple-element.23.q0), channel_id=1, source_target_pairs={{0,256},{128,384},{256,0},{384,128},{1,257},{129,385},{257,1},{385... | collective-permute-start | bytes 294920 | tf_op jit(solution)/shard_map/ppermute | solution.py:303
  124.6 5.7 %collective-permute-start.7 = (bf16[2,192,128]{2,1,0:T(8,128)(2,1)S(1)}, bf16[2,192,128]{2,1,0:T(8,128)(2,1)S(1)}, u32[]{:S(2)}, u32[]{:S(2)}) collective-permute-start(bf16[2,192,128]{2,1,0:T(8,128)(2,1)S(1)} %get-tuple-element.23.q0), channel_id=1, source_target_pairs={{0,384},{128,0},{256,128},{384,256},{1,385},{129,1},{257,129},{385... | collective-permute-start | bytes 294920 | tf_op jit(solution)/shard_map/ppermute | solution.py:303
  136.9 30.7 %collective-permute-start.10 = (bf16[4,256,384]{2,1,0:T(8,128)(2,1)}, bf16[4,256,384]{2,1,0:T(8,128)(2,1)S(1)}, u32[]{:S(2)}, u32[]{:S(2)}) collective-permute-start(bf16[4,256,384]{2,1,0:T(8,128)(2,1)} %get-tuple-element.32), channel_id=1, source_target_pairs={{0,3},{1,0},{2,1},{3,2},{4,7},{5,4},{6,5},{7,6},{8,11},{9,8},{10,9... | collective-permute-start | bytes 2359304 | tf_op jit(solution)/shard_map/ppermute | solution.py:321
  139.5 28.0 %collective-permute-start.9 = (bf16[4,256,384]{2,1,0:T(8,128)(2,1)}, bf16[4,256,384]{2,1,0:T(8,128)(2,1)S(1)}, u32[]{:S(2)}, u32[]{:S(2)}) collective-permute-start(bf16[4,256,384]{2,1,0:T(8,128)(2,1)} %get-tuple-element.30), channel_id=1, source_target_pairs={{0,1},{1,2},{2,3},{3,0},{4,5},{5,6},{6,7},{7,4},{8,9},{9,10},{10,1... | collective-permute-start | bytes 2359304 | tf_op jit(solution)/shard_map/ppermute | solution.py:320
  157.4 45.1 %copy-start.7 = (bf16[192,384]{1,0:T(8,128)(2,1)S(1)}, bf16[192,384]{1,0:T(8,128)(2,1)}, u32[]{:S(2)}) copy-start(bf16[192,384]{1,0:T(8,128)(2,1)} %own_ref.1) | copy-start | bytes 442372
  169.1 18.0 %collective-permute-start.11 = (bf16[192,384]{1,0:T(8,128)(2,1)S(1)}, bf16[192,384]{1,0:T(8,128)(2,1)S(1)}, u32[]{:S(2)}, u32[]{:S(2)}) collective-permute-start(bf16[192,384]{1,0:T(8,128)(2,1)S(1)} %get-tuple-element.34), channel_id=1, source_target_pairs={{0,8},{4,12},{8,0},{12,4},{1,9},{5,13},{9,1},{13,5},{2,10},{6,14},... | collective-permute-start | bytes 442376 | tf_op jit(solution)/shard_map/ppermute | solution.py:339
  177.8 22.5 %collective-permute-start.12 = (bf16[192,384]{1,0:T(8,128)(2,1)S(1)}, bf16[192,384]{1,0:T(8,128)(2,1)S(1)}, u32[]{:S(2)}, u32[]{:S(2)}) collective-permute-start(bf16[192,384]{1,0:T(8,128)(2,1)S(1)} %get-tuple-element.35), channel_id=1, source_target_pairs={{0,4},{4,8},{8,12},{12,0},{1,5},{5,9},{9,13},{13,1},{2,6},{6,10},{... | collective-permute-start | bytes 442376 | tf_op jit(solution)/shard_map/ppermute | solution.py:339
  181.9 20.6 %collective-permute-start.13 = (bf16[192,384]{1,0:T(8,128)(2,1)S(1)}, bf16[192,384]{1,0:T(8,128)(2,1)S(1)}, u32[]{:S(2)}, u32[]{:S(2)}) collective-permute-start(bf16[192,384]{1,0:T(8,128)(2,1)S(1)} %get-tuple-element.36), channel_id=1, source_target_pairs={{0,12},{4,0},{8,4},{12,8},{1,13},{5,1},{9,5},{13,9},{2,14},{6,2},{... | collective-permute-start | bytes 442376 | tf_op jit(solution)/shard_map/ppermute | solution.py:339
Sparse Core Ops, SparseCore 0:
  9.5 91.6 all-gather.1

commit v10 on v9

--- a/solution.py
+++ b/solution.py
@@ -253,11 +253,12 @@
         in_specs=[in_vmem] * (GRID + 1),
         out_specs=in_vmem,
         out_shape=jax.ShapeDtypeStruct((GRID, GRID, rows, width), BF),
+        compiler_params=PARAMS,
         name="spread",
     )(latents, before, far_low, far_high, after)
     raw = lax.all_to_all(raw, "seq", 0, 0, tiled=True)
     out0, out1, out2, out3 = out_parts
-    raw, out2 = lax.optimization_barrier((raw, out2))
+    raw, out1, out2, out3 = lax.optimization_barrier((raw, out1, out2, out3))
     out2 = lax.ppermute(out2, "seq", shift(2))
     hidden = pl.pallas_call(
         norm_kernel,
@@ -301,6 +302,9 @@
 
     pairs = lax.all_to_all(pairs, "zl", 0, 0, tiled=True)
     queries = [queries] + [lax.ppermute(queries, "y", shift(k)) for k in (1, 2, 3)]
+    *queries, out1, out3 = lax.optimization_barrier((*queries, out1, out3))
+    out1 = lax.ppermute(out1, "seq", shift(1))
+    out3 = lax.ppermute(out3, "seq", shift(3))
 
     sent = rows + 16
     parts = pl.pallas_call(
@@ -315,10 +319,8 @@
         compiler_params=PARAMS,
         name="attend",
     )(place, *queries, pairs)
-    parts, out1, out2, out3 = lax.optimization_barrier((parts, out1, out2, out3))
+    parts, out2 = lax.optimization_barrier((parts, out2))
     parts = lax.all_to_all(parts, ("y", "core"), 0, 0, tiled=True)
-    out1 = lax.ppermute(out1, "seq", shift(1))
-    out3 = lax.ppermute(out3, "seq", shift(3))
     around = pl.pallas_call(
         combine_kernel,
         in_specs=[in_vmem],
@@ -336,7 +338,7 @@
         compiler_params=PARAMS,
         name="branch",
     )(place, around, out0, out1, out2, out3)
-    shares = [lax.ppermute(outs[k], "head", shift(k)) for k in (2, 1, 3)]
+    shares = [lax.ppermute(outs[k], "head", shift(k)) for k in (1, 3, 2)]
     summed = outs[0].astype(F32)
     for share in shares:
         summed = summed + share.astype(F32)

time: 214 us -> 214 us (level)
  the two profiles are of different devices: /device:TPU:1 before, /device:TPU:32 now
where the time goes in v10:
time: 214 us; the launch traced here: 213 us
  starting transfers between devices  80.7 us (38%)
  waiting for transfers between devices  75.1 us (35%)
  Pallas kernels  24 us (11%)
  between operations  15 us (7%)
  blocking collectives  11.7 us (5%)
  local copies, waits for them, and re-layouts  5.01 us (2%)
    ppermute x3, waiting for transfers between devices, per_device(): shares = [lax.ppermute(outs[k], 'head', shift(k)) for k in (1, 3, 2)]  18.9 us
    ppermute x3, starting transfers between devices, per_device(): shares = [lax.ppermute(outs[k], 'head', shift(k)) for k in (1, 3, 2)]  18.6 us
    all_to_all x1, waiting for transfers between devices, per_device(): raw = lax.all_to_all(raw, 'seq', 0, 0, tiled=True)  16.5 us
    all_to_all x1, blocking collectives, per_device(): parts = lax.all_to_all(parts, ('y', 'core'), 0, 0, tiled=True)  11.7 us
    ppermute x3, starting transfers between devices, per_device(): lax.ppermute(queries, 'y', shift(k))  10.6 us
    ppermute x1, starting transfers between devices, per_device(): before = lax.ppermute(latents, 'head', shift(1))  9.1 us
    ppermute x1, waiting for transfers between devices, per_device(): far_high = lax.ppermute(after[half:], 'head', shift(3))  8.89 us
    all_to_all x1, waiting for transfers between devices, per_device(): around = lax.all_to_all(around, 'seq', 0, 0, tiled=True)  7.83 us
  transfers between devices with their start and end apart: 18, of which 11 were waited for; matrix products, arithmetic and copies ran while one was open for 0% of the time, Pallas kernels for 7%

profile of v10, /device:TPU:32, one launch (start us, length us, event | category | flops | bytes accessed | tf_op | source)
XLA Modules:
  0.0 212.8 jit_solution(17686168155917340408)
XLA Ops:
  6.5 0.0 copy-start
  6.5 0.0 all-gather.2.cloned.1.call-start
  7.3 1.9 average.1
  9.2 0.0 all-gather.2.cloned.1.call-update
  9.2 9.1 %collective-permute-start = (bf16[192,384]{1,0:T(8,128)(2,1)}, bf16[192,384]{1,0:T(8,128)(2,1)S(1)}, u32[]{:S(2)}, u32[]{:S(2)}) collective-permute-start(bf16[192,384]{1,0:T(8,128)(2,1)} %own_ref.1), channel_id=1, source_target_pairs={{0,4},{4,8},{8,12},{12,0},{1,5},{5,9},{9,13},{13,1},{2,6},{6,10},{... | collective-permute-start | bytes 442376 | tf_op jit(solution)/shard_map/ppermute | solution.py:245
  18.3 4.7 %collective-permute-start.2 = (bf16[192,384]{1,0:T(8,128)(2,1)}, bf16[192,384]{1,0:T(8,128)(2,1)S(1)}, u32[]{:S(2)}, u32[]{:S(2)}) collective-permute-start(bf16[192,384]{1,0:T(8,128)(2,1)} %own_ref.1), channel_id=1, source_target_pairs={{0,12},{4,0},{8,4},{12,8},{1,13},{5,1},{9,5},{13,9},{2,14},{6,2},{... | collective-permute-start | bytes 442376 | tf_op jit(solution)/shard_map/ppermute | solution.py:246
  23.0 6.5 %collective-permute-done.before_ref = bf16[192,384]{1,0:T(8,128)(2,1)S(1)} collective-permute-done((bf16[192,384]{1,0:T(8,128)(2,1)}, bf16[192,384]{1,0:T(8,128)(2,1)S(1)}, u32[]{:S(2)}, u32[]{:S(2)}) %collective-permute-start) | collective-permute-done | bytes 147488 | tf_op jit(solution)/shard_map/ppermute | solution.py:245
  29.5 5.3 %collective-permute-start.1 = (bf16[96,384]{1,0:T(8,128)(2,1)S(1)}, bf16[96,384]{1,0:T(8,128)(2,1)S(1)}, u32[]{:S(2)}, u32[]{:S(2)}) collective-permute-start(bf16[96,384]{1,0:T(8,128)(2,1)S(1)} %slice.13), channel_id=1, source_target_pairs={{0,4},{4,8},{8,12},{12,0},{1,5},{5,9},{9,13},{13,1},{2,6},{6,10},{... | collective-permute-start | bytes 221192 | tf_op jit(solution)/shard_map/ppermute | solution.py:247
  34.8 5.2 %collective-permute-done.2.after_ref = bf16[192,384]{1,0:T(8,128)(2,1)S(1)} collective-permute-done((bf16[192,384]{1,0:T(8,128)(2,1)}, bf16[192,384]{1,0:T(8,128)(2,1)S(1)}, u32[]{:S(2)}, u32[]{:S(2)}) %collective-permute-start.2) | collective-permute-done | bytes 147488 | tf_op jit(solution)/shard_map/ppermute | solution.py:246
  40.0 5.9 %collective-permute-start.3 = (bf16[96,384]{1,0:T(8,128)(2,1)S(1)}, bf16[96,384]{1,0:T(8,128)(2,1)S(1)}, u32[]{:S(2)}, u32[]{:S(2)}) collective-permute-start(bf16[96,384]{1,0:T(8,128)(2,1)S(1)} %slice.14), channel_id=1, source_target_pairs={{0,12},{4,0},{8,4},{12,8},{1,13},{5,1},{9,5},{13,9},{2,14},{6,2},{... | collective-permute-start | bytes 221192 | tf_op jit(solution)/shard_map/ppermute | solution.py:248
  45.9 0.0 collective-permute-done.1.low_ref
  45.9 8.9 %collective-permute-done.3.high_ref = bf16[96,384]{1,0:T(8,128)(2,1)S(1)} collective-permute-done((bf16[96,384]{1,0:T(8,128)(2,1)S(1)}, bf16[96,384]{1,0:T(8,128)(2,1)S(1)}, u32[]{:S(2)}, u32[]{:S(2)}) %collective-permute-start.3) | collective-permute-done | bytes 73760 | tf_op jit(solution)/shard_map/ppermute | solution.py:248
  54.8 0.9 copy-done.5
  55.8 0.2 spread.1
  56.0 0.0 copy-start.1
  56.0 1.4 copy-done.1
  57.3 4.4 %all-to-all-start = ((bf16[4,4,192,384]{3,2,1,0:T(8,128)(2,1)}), bf16[4,4,192,384]{3,2,1,0:T(8,128)(2,1)S(1)}, u32[]{:S(2)}, u32[]{:S(2)}) async-start(bf16[4,4,192,384]{3,2,1,0:T(8,128)(2,1)} %copy-done.1), calls=%async_computation | async-start | bytes 4718592 | tf_op jit(solution)/shard_map/all_to_all | solution.py:259
  62.4 0.0 copy-done
  62.4 0.2 dynamic-slice_reduce_fusion
  62.6 0.1 reshape.15.mod_ref
  62.7 0.6 pad_add_fusion.place_ref
  63.3 5.2 %pick.1 = (bf16[4,256,384]{2,1,0:T(8,128)(2,1)}, bf16[4,256,384]{2,1,0:T(8,128)(2,1)}, bf16[4,256,384]{2,1,0:T(8,128)(2,1)}, bf16[4,256,384]{2,1,0:T(8,128)(2,1)}) custom-call(s32[4]{0:T(128)} %pad_add_fusion.place_ref, bf16[256,6144]{1,0:T(8,128)(2,1)} %refs_3_.1, bf16[256,6144]{1,0:T(8,128)(2,1)} %refs_3_.1, bf16[256,6144]{1,0:T(8,128)(2,1)} %refs_3_.1, ...), custom_call_target="tpu_custom_call" | custom-call | tf_op jit(solution)/shard_map/pick/pallas_call | solution.py:231
  68.5 16.5 %all-to-all-done.raw_ref = bf16[4,4,192,384]{3,2,1,0:T(8,128)(2,1)S(1)} async-done(((bf16[4,4,192,384]{3,2,1,0:T(8,128)(2,1)}), bf16[4,4,192,384]{3,2,1,0:T(8,128)(2,1)S(1)}, u32[]{:S(2)}, u32[]{:S(2)}) %all-to-all-start) | async-done | bytes 2359328 | tf_op jit(solution)/shard_map/all_to_all | solution.py:259
  85.0 0.0 copy-done.7
  85.0 4.3 %norm.1.own_ref = bf16[192,6144]{1,0:T(8,128)(2,1)S(1)} custom-call(s32[4]{0:T(128)S(1)} %copy-done.7, bf16[4,4,192,384]{3,2,1,0:T(8,128)(2,1)S(1)} %all-to-all-done.raw_ref, f32[3,4,4,384]{3,2,1,0:T(4,128)S(1)} %reshape.15.mod_ref), custom_call_target="tpu_custom_call" | custom-call | tf_op jit(solution)/shard_map/norm/pallas_call | solution.py:263
  89.3 0.0 copy-start.2
  89.3 1.4 copy-done.2
  90.7 1.9 collective-permute-start.4
  92.6 4.6 %collective-permute-done.4.other_ref = bf16[192,6144]{1,0:T(8,128)(2,1)S(1)} collective-permute-done((bf16[192,6144]{1,0:T(8,128)(2,1)S(1)}, bf16[192,6144]{1,0:T(8,128)(2,1)S(1)}, u32[]{:S(2)}, u32[]{:S(2)}) %collective-permute-start.4) | collective-permute-done | bytes 2359328 | tf_op jit(solution)/shard_map/ppermute | solution.py:275
  97.2 2.2 %all-gather.2.cloned.1.call-done.weight_ref = bf16[2,6144,384]{2,1,0:T(8,128)(2,1)} async-done(((bf16[2,192,384]{2,1,0:T(8,128)(2,1)}), bf16[2,6144,384]{2,1,0:T(8,128)(2,1)}) %all-gather.2.cloned.1.call-update) | async-done | bytes 9437200 | tf_op jit(solution)/shard_map/all_gather | solution.py:222
  99.3 0.0 copy-done.8
  99.3 0.0 copy-done.9
  99.3 5.6 %project.1 = (bf16[2,192,128]{2,1,0:T(8,128)(2,1)S(1)}, bf16[4,2,2,192,128]{4,3,2,1,0:T(8,128)(2,1)S(1)}) custom-call(s32[4]{0:T(128)S(1)} %copy-done.7, bf16[192,6144]{1,0:T(8,128)(2,1)} %copy-done.2, bf16[192,6144]{1,0:T(8,128)(2,1)S(1)} %collective-permute-done.4.other_ref, bf16[2,6144,384]{2,1,0:T(8,128)(2,1)} %all-gather.2.cloned.1.call-done.weight_ref, ...), custom_call_target="tpu_custom_call" | custom-call | tf_op jit(solution)/shard_map/project/pallas_call | solution.py:279
  104.9 0.0 copy-start.3
  104.9 0.9 copy-done.3
  105.8 6.1 %all-to-all-start.1 = ((bf16[4,2,2,192,128]{4,3,2,1,0:T(8,128)(2,1)}), bf16[4,2,2,192,128]{4,3,2,1,0:T(8,128)(2,1)S(1)}, u32[]{:S(2)}, u32[]{:S(2)}) async-start(bf16[4,2,2,192,128]{4,3,2,1,0:T(8,128)(2,1)} %copy-done.3), calls=%async_computation.1 | async-start | bytes 1572864 | tf_op jit(solution)/shard_map/all_to_all | solution.py:303
  111.9 3.0 %collective-permute-start.8 = (bf16[4,256,384]{2,1,0:T(8,128)(2,1)}, bf16[4,256,384]{2,1,0:T(8,128)(2,1)S(1)}, u32[]{:S(2)}, u32[]{:S(2)}) collective-permute-start(bf16[4,256,384]{2,1,0:T(8,128)(2,1)} %get-tuple-element.39), channel_id=1, source_target_pairs={{0,2},{1,3},{2,0},{3,1},{4,6},{5,7},{6,4},{7,5},{8,10},{9,11},{10,... | collective-permute-start | bytes 2359304 | tf_op jit(solution)/shard_map/ppermute | solution.py:262
  114.9 3.2 %collective-permute-start.5 = (bf16[2,192,128]{2,1,0:T(8,128)(2,1)S(1)}, bf16[2,192,128]{2,1,0:T(8,128)(2,1)S(1)}, u32[]{:S(2)}, u32[]{:S(2)}) collective-permute-start(bf16[2,192,128]{2,1,0:T(8,128)(2,1)S(1)} %get-tuple-element.34.q0), channel_id=1, source_target_pairs={{0,128},{128,256},{256,384},{384,0},{1,129},{129,257},{257,385},{3... | collective-permute-start | bytes 294920 | tf_op jit(solution)/shard_map/ppermute | solution.py:304
  118.1 5.4 %collective-permute-start.6 = (bf16[2,192,128]{2,1,0:T(8,128)(2,1)S(1)}, bf16[2,192,128]{2,1,0:T(8,128)(2,1)S(1)}, u32[]{:S(2)}, u32[]{:S(2)}) collective-permute-start(bf16[2,192,128]{2,1,0:T(8,128)(2,1)S(1)} %get-tuple-element.34.q0), channel_id=1, source_target_pairs={{0,256},{128,384},{256,0},{384,128},{1,257},{129,385},{257,1},{385... | collective-permute-start | bytes 294920 | tf_op jit(solution)/shard_map/ppermute | solution.py:304
  123.5 2.0 collective-permute-start.7
  125.6 0.0 collective-permute-done.5.q1
  125.6 0.7 collective-permute-done.6.q2
  126.3 3.8 %collective-permute-done.7.q3 = bf16[2,192,128]{2,1,0:T(8,128)(2,1)S(1)} collective-permute-done((bf16[2,192,128]{2,1,0:T(8,128)(2,1)S(1)}, bf16[2,192,128]{2,1,0:T(8,128)(2,1)S(1)}, u32[]{:S(2)}, u32[]{:S(2)}) %collective-permute-start.7) | collective-permute-done | bytes 98336 | tf_op jit(solution)/shard_map/ppermute | solution.py:304
  130.0 4.6 %collective-permute-start.10 = (bf16[4,256,384]{2,1,0:T(8,128)(2,1)}, bf16[4,256,384]{2,1,0:T(8,128)(2,1)}, u32[]{:S(2)}, u32[]{:S(2)}) collective-permute-start(bf16[4,256,384]{2,1,0:T(8,128)(2,1)} %get-tuple-element.44), channel_id=1, source_target_pairs={{0,3},{1,0},{2,1},{3,2},{4,7},{5,4},{6,5},{7,6},{8,11},{9,8},{10,9... | collective-permute-start | bytes 2359304 | tf_op jit(solution)/shard_map/ppermute | solution.py:307
  134.6 1.9 collective-permute-start.9
  136.5 0.0 all-to-all-done.1.kv_ref
  136.6 3.6 %attend.1 = bf16[8,208,128]{2,1,0:T(8,128)(2,1)S(1)} custom-call(s32[4]{0:T(128)S(1)} %copy-done.7, bf16[2,192,128]{2,1,0:T(8,128)(2,1)S(1)} %get-tuple-element.34.q0, bf16[2,192,128]{2,1,0:T(8,128)(2,1)S(1)} %collective-permute-done.5.q1, bf16[2,192,128]{2,1,0:T(8,128)(2,1)S(1)} %collective-permute-done.6.q2, ...), custom_call_target="tpu_custom_call" | custom-call | tf_op jit(solution)/shard_map/attend/pallas_call | solution.py:310
  140.1 0.0 collective-permute-done.8.w2
  140.1 11.7 %all_to_all.20.parts_ref = bf16[8,208,128]{2,1,0:T(8,128)(2,1)S(1)} all-to-all(bf16[8,208,128]{2,1,0:T(8,128)(2,1)S(1)} %attend.1), channel_id=1, replica_groups=mesh['y'=4,'zl'=4,'core'=2,'head'=4,'seq'=4] {'y','core'}, dimensions={0} | all-to-all | bytes 851968 | tf_op jit(solution)/shard_map/all_to_all | solution.py:323
  151.8 0.9 combine.1
  152.8 4.6 %all-to-all-start.3 = ((bf16[4,192,256]{2,1,0:T(8,128)(2,1)}), bf16[4,192,256]{2,1,0:T(8,128)(2,1)S(1)}, u32[]{:S(2)}, u32[]{:S(2)}) async-start(bf16[4,192,256]{2,1,0:T(8,128)(2,1)} %combine.1), calls=%async_computation.3 | async-start | bytes 786432 | tf_op jit(solution)/shard_map/all_to_all | solution.py:332
  157.4 0.0 collective-permute-done.10.w3
  157.4 0.0 collective-permute-done.9.w1
  157.4 7.8 %all-to-all-done.3.a_ref = bf16[4,192,256]{2,1,0:T(8,128)(2,1)S(1)} async-done(((bf16[4,192,256]{2,1,0:T(8,128)(2,1)}), bf16[4,192,256]{2,1,0:T(8,128)(2,1)S(1)}, u32[]{:S(2)}, u32[]{:S(2)}) %all-to-all-start.3) | async-done | bytes 393248 | tf_op jit(solution)/shard_map/all_to_all | solution.py:332
  165.2 0.0 copy-done.4
  165.2 2.4 %branch.1 = (bf16[192,384]{1,0:T(8,128)(2,1)S(1)}, bf16[192,384]{1,0:T(8,128)(2,1)S(1)}, bf16[192,384]{1,0:T(8,128)(2,1)S(1)}, bf16[192,384]{1,0:T(8,128)(2,1)S(1)}) custom-call(s32[4]{0:T(128)S(1)} %copy-done.7, bf16[4,192,256]{2,1,0:T(8,128)(2,1)S(1)} %all-to-all-done.3.a_ref, bf16[4,256,384]{2,1,0:T(8,128)(2,1)S(1)} %copy-done.4, ...), custom_call_target="tpu_custom_call" | custom-call | tf_op jit(solution)/shard_map/branch/pallas_call | solution.py:333
  167.6 7.3 %collective-permute-start.11 = (bf16[192,384]{1,0:T(8,128)(2,1)S(1)}, bf16[192,384]{1,0:T(8,128)(2,1)S(1)}, u32[]{:S(2)}, u32[]{:S(2)}) collective-permute-start(bf16[192,384]{1,0:T(8,128)(2,1)S(1)} %get-tuple-element.46), channel_id=1, source_target_pairs={{0,4},{4,8},{8,12},{12,0},{1,5},{5,9},{9,13},{13,1},{2,6},{6,10},{... | collective-permute-start | bytes 442376 | tf_op jit(solution)/shard_map/ppermute | solution.py:341
  174.9 2.5 %collective-permute-start.12 = (bf16[192,384]{1,0:T(8,128)(2,1)S(1)}, bf16[192,384]{1,0:T(8,128)(2,1)S(1)}, u32[]{:S(2)}, u32[]{:S(2)}) collective-permute-start(bf16[192,384]{1,0:T(8,128)(2,1)S(1)} %get-tuple-element.47), channel_id=1, source_target_pairs={{0,12},{4,0},{8,4},{12,8},{1,13},{5,1},{9,5},{13,9},{2,14},{6,2},{... | collective-permute-start | bytes 442376 | tf_op jit(solution)/shard_map/ppermute | solution.py:341
  177.4 8.9 %collective-permute-start.13 = (bf16[192,384]{1,0:T(8,128)(2,1)S(1)}, bf16[192,384]{1,0:T(8,128)(2,1)S(1)}, u32[]{:S(2)}, u32[]{:S(2)}) collective-permute-start(bf16[192,384]{1,0:T(8,128)(2,1)S(1)} %get-tuple-element.48), channel_id=1, source_target_pairs={{0,8},{4,12},{8,0},{12,4},{1,9},{5,13},{9,1},{13,5},{2,10},{6,14},... | collective-permute-start | bytes 442376 | tf_op jit(solution)/shard_map/ppermute | solution.py:341
  186.2 0.1 dynamic-slice_reduce_fusion.1
  186.3 0.0 collective-permute-done.11
  186.3 15.5 %collective-permute-done.12 = bf16[192,384]{1,0:T(8,128)(2,1)S(1)} collective-permute-done((bf16[192,384]{1,0:T(8,128)(2,1)S(1)}, bf16[192,384]{1,0:T(8,128)(2,1)S(1)}, u32[]{:S(2)}, u32[]{:S(2)}) %collective-permute-start.12) | collective-permute-done | bytes 147488 | tf_op jit(solution)/shard_map/ppermute | solution.py:341
  201.9 3.3 %collective-permute-done.13 = bf16[192,384]{1,0:T(8,128)(2,1)S(1)} collective-permute-done((bf16[192,384]{1,0:T(8,128)(2,1)S(1)}, bf16[192,384]{1,0:T(8,128)(2,1)S(1)}, u32[]{:S(2)}, u32[]{:S(2)}) %collective-permute-start.13) | collective-permute-done | bytes 147488 | tf_op jit(solution)/shard_map/ppermute | solution.py:341
  205.2 0.8 add_convert_fusion
  (9 shorter events, 0.0 us)
Async XLA Ops:
  6.5 55.9 %copy-start = (f32[8,3,6144]{2,0,1:T(8,128)S(1)}, f32[8,3,6144]{2,0,1:T(8,128)}, u32[]{:S(2)}) copy-start(f32[8,3,6144]{2,0,1:T(8,128)} %param.15) | copy-start | bytes 1769476
  6.5 92.8 %all-gather.2.cloned.1.call-start = ((), (), s32[]{:S(2)}) async-start(), calls=%async_computation.4 | async-start | bytes 9732096 | tf_op jit(solution)/shard_map/all_gather | solution.py:222
  9.2 20.3 %collective-permute-start = (bf16[192,384]{1,0:T(8,128)(2,1)}, bf16[192,384]{1,0:T(8,128)(2,1)S(1)}, u32[]{:S(2)}, u32[]{:S(2)}) collective-permute-start(bf16[192,384]{1,0:T(8,128)(2,1)} %own_ref.1), channel_id=1, source_target_pairs={{0,4},{4,8},{8,12},{12,0},{1,5},{5,9},{9,13},{13,1},{2,6},{6,10},{... | collective-permute-start | bytes 442376 | tf_op jit(solution)/shard_map/ppermute | solution.py:245
  18.3 21.7 %collective-permute-start.2 = (bf16[192,384]{1,0:T(8,128)(2,1)}, bf16[192,384]{1,0:T(8,128)(2,1)S(1)}, u32[]{:S(2)}, u32[]{:S(2)}) collective-permute-start(bf16[192,384]{1,0:T(8,128)(2,1)} %own_ref.1), channel_id=1, source_target_pairs={{0,12},{4,0},{8,4},{12,8},{1,13},{5,1},{9,5},{13,9},{2,14},{6,2},{... | collective-permute-start | bytes 442376 | tf_op jit(solution)/shard_map/ppermute | solution.py:246
  29.5 16.4 %collective-permute-start.1 = (bf16[96,384]{1,0:T(8,128)(2,1)S(1)}, bf16[96,384]{1,0:T(8,128)(2,1)S(1)}, u32[]{:S(2)}, u32[]{:S(2)}) collective-permute-start(bf16[96,384]{1,0:T(8,128)(2,1)S(1)} %slice.13), channel_id=1, source_target_pairs={{0,4},{4,8},{8,12},{12,0},{1,5},{5,9},{9,13},{13,1},{2,6},{6,10},{... | collective-permute-start | bytes 221192 | tf_op jit(solution)/shard_map/ppermute | solution.py:247
  40.0 14.8 %collective-permute-start.3 = (bf16[96,384]{1,0:T(8,128)(2,1)S(1)}, bf16[96,384]{1,0:T(8,128)(2,1)S(1)}, u32[]{:S(2)}, u32[]{:S(2)}) collective-permute-start(bf16[96,384]{1,0:T(8,128)(2,1)S(1)} %slice.14), channel_id=1, source_target_pairs={{0,12},{4,0},{8,4},{12,8},{1,13},{5,1},{9,5},{13,9},{2,14},{6,2},{... | collective-permute-start | bytes 221192 | tf_op jit(solution)/shard_map/ppermute | solution.py:248
  54.8 0.9 copy-start.5
  56.0 1.4 copy-start.1
  57.3 27.7 %all-to-all-start = ((bf16[4,4,192,384]{3,2,1,0:T(8,128)(2,1)}), bf16[4,4,192,384]{3,2,1,0:T(8,128)(2,1)S(1)}, u32[]{:S(2)}, u32[]{:S(2)}) async-start(bf16[4,4,192,384]{3,2,1,0:T(8,128)(2,1)} %copy-done.1), calls=%async_computation | async-start | bytes 4718592 | tf_op jit(solution)/shard_map/all_to_all | solution.py:259
  63.3 21.8 %copy-start.7 = (s32[4]{0:T(128)S(1)}, s32[4]{0:T(128)}, u32[]{:S(2)}) copy-start(s32[4]{0:T(128)} %pad_add_fusion.place_ref) | copy-start | bytes 52
  85.0 14.3 %copy-start.8 = (f32[128]{0:T(128)S(1)}, f32[128]{0:T(128)}, u32[]{:S(2)}) copy-start(f32[128]{0:T(128)} %param.12) | copy-start | bytes 1540
  85.0 14.3 %copy-start.9 = (f32[128]{0:T(128)S(1)}, f32[128]{0:T(128)}, u32[]{:S(2)}) copy-start(f32[128]{0:T(128)} %param.13) | copy-start | bytes 1540
  89.3 1.4 copy-start.2
  90.7 6.5 %collective-permute-start.4 = (bf16[192,6144]{1,0:T(8,128)(2,1)S(1)}, bf16[192,6144]{1,0:T(8,128)(2,1)S(1)}, u32[]{:S(2)}, u32[]{:S(2)}) collective-permute-start(bf16[192,6144]{1,0:T(8,128)(2,1)S(1)} %norm.1.own_ref), channel_id=1, source_target_pairs={{0,16},{16,0},{1,17},{17,1},{2,18},{18,2},{3,19},{19,3},{4,20},{20... | collective-permute-start | bytes 7077896 | tf_op jit(solution)/shard_map/ppermute | solution.py:275
  104.9 0.9 copy-start.3
  105.8 30.7 %all-to-all-start.1 = ((bf16[4,2,2,192,128]{4,3,2,1,0:T(8,128)(2,1)}), bf16[4,2,2,192,128]{4,3,2,1,0:T(8,128)(2,1)S(1)}, u32[]{:S(2)}, u32[]{:S(2)}) async-start(bf16[4,2,2,192,128]{4,3,2,1,0:T(8,128)(2,1)} %copy-done.3), calls=%async_computation.1 | async-start | bytes 1572864 | tf_op jit(solution)/shard_map/all_to_all | solution.py:303
  111.9 53.3 %copy-start.4 = (bf16[4,256,384]{2,1,0:T(8,128)(2,1)S(1)}, bf16[4,256,384]{2,1,0:T(8,128)(2,1)}, u32[]{:S(2)}) copy-start(bf16[4,256,384]{2,1,0:T(8,128)(2,1)} %get-tuple-element.41.w0) | copy-start | bytes 2359300
  111.9 28.2 %collective-permute-start.8 = (bf16[4,256,384]{2,1,0:T(8,128)(2,1)}, bf16[4,256,384]{2,1,0:T(8,128)(2,1)S(1)}, u32[]{:S(2)}, u32[]{:S(2)}) collective-permute-start(bf16[4,256,384]{2,1,0:T(8,128)(2,1)} %get-tuple-element.39), channel_id=1, source_target_pairs={{0,2},{1,3},{2,0},{3,1},{4,6},{5,7},{6,4},{7,5},{8,10},{9,11},{10,... | collective-permute-start | bytes 2359304 | tf_op jit(solution)/shard_map/ppermute | solution.py:262
  114.9 10.7 %collective-permute-start.5 = (bf16[2,192,128]{2,1,0:T(8,128)(2,1)S(1)}, bf16[2,192,128]{2,1,0:T(8,128)(2,1)S(1)}, u32[]{:S(2)}, u32[]{:S(2)}) collective-permute-start(bf16[2,192,128]{2,1,0:T(8,128)(2,1)S(1)} %get-tuple-element.34.q0), channel_id=1, source_target_pairs={{0,128},{128,256},{256,384},{384,0},{1,129},{129,257},{257,385},{3... | collective-permute-start | bytes 294920 | tf_op jit(solution)/shard_map/ppermute | solution.py:304
  118.1 8.2 %collective-permute-start.6 = (bf16[2,192,128]{2,1,0:T(8,128)(2,1)S(1)}, bf16[2,192,128]{2,1,0:T(8,128)(2,1)S(1)}, u32[]{:S(2)}, u32[]{:S(2)}) collective-permute-start(bf16[2,192,128]{2,1,0:T(8,128)(2,1)S(1)} %get-tuple-element.34.q0), channel_id=1, source_target_pairs={{0,256},{128,384},{256,0},{384,128},{1,257},{129,385},{257,1},{385... | collective-permute-start | bytes 294920 | tf_op jit(solution)/shard_map/ppermute | solution.py:304
  123.5 6.5 %collective-permute-start.7 = (bf16[2,192,128]{2,1,0:T(8,128)(2,1)S(1)}, bf16[2,192,128]{2,1,0:T(8,128)(2,1)S(1)}, u32[]{:S(2)}, u32[]{:S(2)}) collective-permute-start(bf16[2,192,128]{2,1,0:T(8,128)(2,1)S(1)} %get-tuple-element.34.q0), channel_id=1, source_target_pairs={{0,384},{128,0},{256,128},{384,256},{1,385},{129,1},{257,129},{385... | collective-permute-start | bytes 294920 | tf_op jit(solution)/shard_map/ppermute | solution.py:304
  130.0 27.3 %collective-permute-start.10 = (bf16[4,256,384]{2,1,0:T(8,128)(2,1)}, bf16[4,256,384]{2,1,0:T(8,128)(2,1)}, u32[]{:S(2)}, u32[]{:S(2)}) collective-permute-start(bf16[4,256,384]{2,1,0:T(8,128)(2,1)} %get-tuple-element.44), channel_id=1, source_target_pairs={{0,3},{1,0},{2,1},{3,2},{4,7},{5,4},{6,5},{7,6},{8,11},{9,8},{10,9... | collective-permute-start | bytes 2359304 | tf_op jit(solution)/shard_map/ppermute | solution.py:307
  134.6 22.8 %collective-permute-start.9 = (bf16[4,256,384]{2,1,0:T(8,128)(2,1)}, bf16[4,256,384]{2,1,0:T(8,128)(2,1)}, u32[]{:S(2)}, u32[]{:S(2)}) collective-permute-start(bf16[4,256,384]{2,1,0:T(8,128)(2,1)} %get-tuple-element.42), channel_id=1, source_target_pairs={{0,1},{1,2},{2,3},{3,0},{4,5},{5,6},{6,7},{7,4},{8,9},{9,10},{10,1... | collective-permute-start | bytes 2359304 | tf_op jit(solution)/shard_map/ppermute | solution.py:306
  152.7 52.5 %copy-start.6 = (bf16[192,384]{1,0:T(8,128)(2,1)S(1)}, bf16[192,384]{1,0:T(8,128)(2,1)}, u32[]{:S(2)}) copy-start(bf16[192,384]{1,0:T(8,128)(2,1)} %own_ref.1) | copy-start | bytes 442372
  152.8 12.5 %all-to-all-start.3 = ((bf16[4,192,256]{2,1,0:T(8,128)(2,1)}), bf16[4,192,256]{2,1,0:T(8,128)(2,1)S(1)}, u32[]{:S(2)}, u32[]{:S(2)}) async-start(bf16[4,192,256]{2,1,0:T(8,128)(2,1)} %combine.1), calls=%async_computation.3 | async-start | bytes 786432 | tf_op jit(solution)/shard_map/all_to_all | solution.py:332
  167.6 18.7 %collective-permute-start.11 = (bf16[192,384]{1,0:T(8,128)(2,1)S(1)}, bf16[192,384]{1,0:T(8,128)(2,1)S(1)}, u32[]{:S(2)}, u32[]{:S(2)}) collective-permute-start(bf16[192,384]{1,0:T(8,128)(2,1)S(1)} %get-tuple-element.46), channel_id=1, source_target_pairs={{0,4},{4,8},{8,12},{12,0},{1,5},{5,9},{9,13},{13,1},{2,6},{6,10},{... | collective-permute-start | bytes 442376 | tf_op jit(solution)/shard_map/ppermute | solution.py:341
  174.9 27.0 %collective-permute-start.12 = (bf16[192,384]{1,0:T(8,128)(2,1)S(1)}, bf16[192,384]{1,0:T(8,128)(2,1)S(1)}, u32[]{:S(2)}, u32[]{:S(2)}) collective-permute-start(bf16[192,384]{1,0:T(8,128)(2,1)S(1)} %get-tuple-element.47), channel_id=1, source_target_pairs={{0,12},{4,0},{8,4},{12,8},{1,13},{5,1},{9,5},{13,9},{2,14},{6,2},{... | collective-permute-start | bytes 442376 | tf_op jit(solution)/shard_map/ppermute | solution.py:341
  177.4 27.8 %collective-permute-start.13 = (bf16[192,384]{1,0:T(8,128)(2,1)S(1)}, bf16[192,384]{1,0:T(8,128)(2,1)S(1)}, u32[]{:S(2)}, u32[]{:S(2)}) collective-permute-start(bf16[192,384]{1,0:T(8,128)(2,1)S(1)} %get-tuple-element.48), channel_id=1, source_target_pairs={{0,8},{4,12},{8,0},{12,4},{1,9},{5,13},{9,1},{13,5},{2,10},{6,14},... | collective-permute-start | bytes 442376 | tf_op jit(solution)/shard_map/ppermute | solution.py:341
Sparse Core Ops, SparseCore 0:
  9.5 89.8 all-gather.1

commit v11 on v10

--- a/solution.py
+++ b/solution.py
@@ -16,6 +16,7 @@
 LOG2E = 1.4426950408889634
 TOKENS = ("y", "zl", "core")
 PARAMS = pltpu.CompilerParams(vmem_limit_bytes=24 << 20)
+SPREAD_PARAMS = pltpu.CompilerParams(vmem_limit_bytes=53 << 20)
 
 
 def shift(amount):
@@ -253,7 +254,7 @@
         in_specs=[in_vmem] * (GRID + 1),
         out_specs=in_vmem,
         out_shape=jax.ShapeDtypeStruct((GRID, GRID, rows, width), BF),
-        compiler_params=PARAMS,
+        compiler_params=SPREAD_PARAMS,
         name="spread",
     )(latents, before, far_low, far_high, after)
     raw = lax.all_to_all(raw, "seq", 0, 0, tiled=True)

time: 214 us -> 214 us (level)
    unnamed x20 -> x18, local copies, waits for them, and re-layouts: 4.61 us -> 3.22 us
where the time goes in v11:
time: 214 us; the launch traced here: 213 us
  starting transfers between devices  81.1 us (38%)
  waiting for transfers between devices  74.8 us (35%)
  Pallas kernels  25.3 us (12%)
  between operations  15 us (7%)
  blocking collectives  11.7 us (5%)
  local copies, waits for them, and re-layouts  3.62 us (2%)
    ppermute x3, waiting for transfers between devices, per_device(): shares = [lax.ppermute(outs[k], 'head', shift(k)) for k in (1, 3, 2)]  19 us
    ppermute x3, starting transfers between devices, per_device(): shares = [lax.ppermute(outs[k], 'head', shift(k)) for k in (1, 3, 2)]  18.6 us
    all_to_all x1, waiting for transfers between devices, per_device(): raw = lax.all_to_all(raw, 'seq', 0, 0, tiled=True)  16.5 us
    all_to_all x1, blocking collectives, per_device(): parts = lax.all_to_all(parts, ('y', 'core'), 0, 0, tiled=True)  11.7 us
    ppermute x3, starting transfers between devices, per_device(): lax.ppermute(queries, 'y', shift(k))  10.7 us
    ppermute x1, starting transfers between devices, per_device(): before = lax.ppermute(latents, 'head', shift(1))  9.1 us
    ppermute x1, waiting for transfers between devices, per_device(): far_high = lax.ppermute(after[half:], 'head', shift(3))  8.87 us
    all_to_all x1, waiting for transfers between devices, per_device(): around = lax.all_to_all(around, 'seq', 0, 0, tiled=True)  7.83 us
  transfers between devices with their start and end apart: 18, of which 11 were waited for; matrix products, arithmetic and copies ran while one was open for 0% of the time, Pallas kernels for 7%

profile of v11, /device:TPU:32, one launch (start us, length us, event | category | flops | bytes accessed | tf_op | source)
XLA Modules:
  0.0 212.9 jit_solution(11765839771585151687)
XLA Ops:
  6.5 0.0 copy-start
  6.5 0.0 all-gather.2.cloned.1.call-start
  7.3 1.9 average.1
  9.1 0.0 all-gather.2.cloned.1.call-update
  9.2 9.1 %collective-permute-start = (bf16[192,384]{1,0:T(8,128)(2,1)}, bf16[192,384]{1,0:T(8,128)(2,1)S(1)}, u32[]{:S(2)}, u32[]{:S(2)}) collective-permute-start(bf16[192,384]{1,0:T(8,128)(2,1)} %own_ref.1), channel_id=1, source_target_pairs={{0,4},{4,8},{8,12},{12,0},{1,5},{5,9},{9,13},{13,1},{2,6},{6,10},{... | collective-permute-start | bytes 442376 | tf_op jit(solution)/shard_map/ppermute | solution.py:246
  18.3 4.7 %collective-permute-start.2 = (bf16[192,384]{1,0:T(8,128)(2,1)}, bf16[192,384]{1,0:T(8,128)(2,1)S(1)}, u32[]{:S(2)}, u32[]{:S(2)}) collective-permute-start(bf16[192,384]{1,0:T(8,128)(2,1)} %own_ref.1), channel_id=1, source_target_pairs={{0,12},{4,0},{8,4},{12,8},{1,13},{5,1},{9,5},{13,9},{2,14},{6,2},{... | collective-permute-start | bytes 442376 | tf_op jit(solution)/shard_map/ppermute | solution.py:247
  22.9 6.5 %collective-permute-done.before_ref = bf16[192,384]{1,0:T(8,128)(2,1)S(1)} collective-permute-done((bf16[192,384]{1,0:T(8,128)(2,1)}, bf16[192,384]{1,0:T(8,128)(2,1)S(1)}, u32[]{:S(2)}, u32[]{:S(2)}) %collective-permute-start) | collective-permute-done | bytes 147488 | tf_op jit(solution)/shard_map/ppermute | solution.py:246
  29.5 5.3 %collective-permute-start.1 = (bf16[96,384]{1,0:T(8,128)(2,1)S(1)}, bf16[96,384]{1,0:T(8,128)(2,1)S(1)}, u32[]{:S(2)}, u32[]{:S(2)}) collective-permute-start(bf16[96,384]{1,0:T(8,128)(2,1)S(1)} %slice.13), channel_id=1, source_target_pairs={{0,4},{4,8},{8,12},{12,0},{1,5},{5,9},{9,13},{13,1},{2,6},{6,10},{... | collective-permute-start | bytes 221192 | tf_op jit(solution)/shard_map/ppermute | solution.py:248
  34.8 5.2 %collective-permute-done.2.after_ref = bf16[192,384]{1,0:T(8,128)(2,1)S(1)} collective-permute-done((bf16[192,384]{1,0:T(8,128)(2,1)}, bf16[192,384]{1,0:T(8,128)(2,1)S(1)}, u32[]{:S(2)}, u32[]{:S(2)}) %collective-permute-start.2) | collective-permute-done | bytes 147488 | tf_op jit(solution)/shard_map/ppermute | solution.py:247
  40.0 5.9 %collective-permute-start.3 = (bf16[96,384]{1,0:T(8,128)(2,1)S(1)}, bf16[96,384]{1,0:T(8,128)(2,1)S(1)}, u32[]{:S(2)}, u32[]{:S(2)}) collective-permute-start(bf16[96,384]{1,0:T(8,128)(2,1)S(1)} %slice.14), channel_id=1, source_target_pairs={{0,12},{4,0},{8,4},{12,8},{1,13},{5,1},{9,5},{13,9},{2,14},{6,2},{... | collective-permute-start | bytes 221192 | tf_op jit(solution)/shard_map/ppermute | solution.py:249
  45.9 0.0 collective-permute-done.1.low_ref
  45.9 8.9 %collective-permute-done.3.high_ref = bf16[96,384]{1,0:T(8,128)(2,1)S(1)} collective-permute-done((bf16[96,384]{1,0:T(8,128)(2,1)S(1)}, bf16[96,384]{1,0:T(8,128)(2,1)S(1)}, u32[]{:S(2)}, u32[]{:S(2)}) %collective-permute-start.3) | collective-permute-done | bytes 73760 | tf_op jit(solution)/shard_map/ppermute | solution.py:249
  54.8 0.0 copy-start.4
  54.8 0.9 copy-done.4
  55.7 1.6 spread.1
  57.3 4.4 %all-to-all-start = ((bf16[4,4,192,384]{3,2,1,0:T(8,128)(2,1)}), bf16[4,4,192,384]{3,2,1,0:T(8,128)(2,1)S(1)}, u32[]{:S(2)}, u32[]{:S(2)}) async-start(bf16[4,4,192,384]{3,2,1,0:T(8,128)(2,1)} %spread.1), calls=%async_computation | async-start | bytes 4718592 | tf_op jit(solution)/shard_map/all_to_all | solution.py:260
  62.4 0.0 copy-done
  62.4 0.2 dynamic-slice_reduce_fusion
  62.6 0.1 reshape.15.mod_ref
  62.7 0.7 pad_add_fusion.place_ref
  63.3 5.2 %pick.1 = (bf16[4,256,384]{2,1,0:T(8,128)(2,1)}, bf16[4,256,384]{2,1,0:T(8,128)(2,1)}, bf16[4,256,384]{2,1,0:T(8,128)(2,1)}, bf16[4,256,384]{2,1,0:T(8,128)(2,1)}) custom-call(s32[4]{0:T(128)} %pad_add_fusion.place_ref, bf16[256,6144]{1,0:T(8,128)(2,1)} %refs_3_.1, bf16[256,6144]{1,0:T(8,128)(2,1)} %refs_3_.1, bf16[256,6144]{1,0:T(8,128)(2,1)} %refs_3_.1, ...), custom_call_target="tpu_custom_call" | custom-call | tf_op jit(solution)/shard_map/pick/pallas_call | solution.py:232
  68.5 16.5 %all-to-all-done.raw_ref = bf16[4,4,192,384]{3,2,1,0:T(8,128)(2,1)S(1)} async-done(((bf16[4,4,192,384]{3,2,1,0:T(8,128)(2,1)}), bf16[4,4,192,384]{3,2,1,0:T(8,128)(2,1)S(1)}, u32[]{:S(2)}, u32[]{:S(2)}) %all-to-all-start) | async-done | bytes 2359328 | tf_op jit(solution)/shard_map/all_to_all | solution.py:260
  85.0 0.0 copy-done.6
  85.0 4.3 %norm.1.own_ref = bf16[192,6144]{1,0:T(8,128)(2,1)S(1)} custom-call(s32[4]{0:T(128)S(1)} %copy-done.6, bf16[4,4,192,384]{3,2,1,0:T(8,128)(2,1)S(1)} %all-to-all-done.raw_ref, f32[3,4,4,384]{3,2,1,0:T(4,128)S(1)} %reshape.15.mod_ref), custom_call_target="tpu_custom_call" | custom-call | tf_op jit(solution)/shard_map/norm/pallas_call | solution.py:264
  89.3 0.0 copy-start.1
  89.3 1.4 copy-done.1
  90.7 1.9 collective-permute-start.4
  92.6 4.5 %collective-permute-done.4.other_ref = bf16[192,6144]{1,0:T(8,128)(2,1)S(1)} collective-permute-done((bf16[192,6144]{1,0:T(8,128)(2,1)S(1)}, bf16[192,6144]{1,0:T(8,128)(2,1)S(1)}, u32[]{:S(2)}, u32[]{:S(2)}) %collective-permute-start.4) | collective-permute-done | bytes 2359328 | tf_op jit(solution)/shard_map/ppermute | solution.py:276
  97.1 1.9 all-gather.2.cloned.1.call-done.weight_ref
  99.0 0.0 copy-done.7
  99.0 0.0 copy-done.8
  99.0 5.6 %project.1 = (bf16[2,192,128]{2,1,0:T(8,128)(2,1)S(1)}, bf16[4,2,2,192,128]{4,3,2,1,0:T(8,128)(2,1)S(1)}) custom-call(s32[4]{0:T(128)S(1)} %copy-done.6, bf16[192,6144]{1,0:T(8,128)(2,1)} %copy-done.1, bf16[192,6144]{1,0:T(8,128)(2,1)S(1)} %collective-permute-done.4.other_ref, bf16[2,6144,384]{2,1,0:T(8,128)(2,1)} %all-gather.2.cloned.1.call-done.weight_ref, ...), custom_call_target="tpu_custom_call" | custom-call | tf_op jit(solution)/shard_map/project/pallas_call | solution.py:280
  104.6 0.0 copy-start.2
  104.6 0.9 copy-done.2
  105.5 6.3 %all-to-all-start.1 = ((bf16[4,2,2,192,128]{4,3,2,1,0:T(8,128)(2,1)}), bf16[4,2,2,192,128]{4,3,2,1,0:T(8,128)(2,1)S(1)}, u32[]{:S(2)}, u32[]{:S(2)}) async-start(bf16[4,2,2,192,128]{4,3,2,1,0:T(8,128)(2,1)} %copy-done.2), calls=%async_computation.1 | async-start | bytes 1572864 | tf_op jit(solution)/shard_map/all_to_all | solution.py:304
  111.8 3.0 %collective-permute-start.8 = (bf16[4,256,384]{2,1,0:T(8,128)(2,1)}, bf16[4,256,384]{2,1,0:T(8,128)(2,1)S(1)}, u32[]{:S(2)}, u32[]{:S(2)}) collective-permute-start(bf16[4,256,384]{2,1,0:T(8,128)(2,1)} %get-tuple-element.39), channel_id=1, source_target_pairs={{0,2},{1,3},{2,0},{3,1},{4,6},{5,7},{6,4},{7,5},{8,10},{9,11},{10,... | collective-permute-start | bytes 2359304 | tf_op jit(solution)/shard_map/ppermute | solution.py:263
  114.8 3.2 %collective-permute-start.5 = (bf16[2,192,128]{2,1,0:T(8,128)(2,1)S(1)}, bf16[2,192,128]{2,1,0:T(8,128)(2,1)S(1)}, u32[]{:S(2)}, u32[]{:S(2)}) collective-permute-start(bf16[2,192,128]{2,1,0:T(8,128)(2,1)S(1)} %get-tuple-element.34.q0), channel_id=1, source_target_pairs={{0,128},{128,256},{256,384},{384,0},{1,129},{129,257},{257,385},{3... | collective-permute-start | bytes 294920 | tf_op jit(solution)/shard_map/ppermute | solution.py:305
  118.1 5.4 %collective-permute-start.6 = (bf16[2,192,128]{2,1,0:T(8,128)(2,1)S(1)}, bf16[2,192,128]{2,1,0:T(8,128)(2,1)S(1)}, u32[]{:S(2)}, u32[]{:S(2)}) collective-permute-start(bf16[2,192,128]{2,1,0:T(8,128)(2,1)S(1)} %get-tuple-element.34.q0), channel_id=1, source_target_pairs={{0,256},{128,384},{256,0},{384,128},{1,257},{129,385},{257,1},{385... | collective-permute-start | bytes 294920 | tf_op jit(solution)/shard_map/ppermute | solution.py:305
  123.5 2.0 collective-permute-start.7
  125.5 0.0 collective-permute-done.5.q1
  125.6 0.7 collective-permute-done.6.q2
  126.3 3.8 %collective-permute-done.7.q3 = bf16[2,192,128]{2,1,0:T(8,128)(2,1)S(1)} collective-permute-done((bf16[2,192,128]{2,1,0:T(8,128)(2,1)S(1)}, bf16[2,192,128]{2,1,0:T(8,128)(2,1)S(1)}, u32[]{:S(2)}, u32[]{:S(2)}) %collective-permute-start.7) | collective-permute-done | bytes 98336 | tf_op jit(solution)/shard_map/ppermute | solution.py:305
  130.0 4.6 %collective-permute-start.10 = (bf16[4,256,384]{2,1,0:T(8,128)(2,1)}, bf16[4,256,384]{2,1,0:T(8,128)(2,1)}, u32[]{:S(2)}, u32[]{:S(2)}) collective-permute-start(bf16[4,256,384]{2,1,0:T(8,128)(2,1)} %get-tuple-element.44), channel_id=1, source_target_pairs={{0,3},{1,0},{2,1},{3,2},{4,7},{5,4},{6,5},{7,6},{8,11},{9,8},{10,9... | collective-permute-start | bytes 2359304 | tf_op jit(solution)/shard_map/ppermute | solution.py:308
  134.6 1.9 collective-permute-start.9
  136.5 0.0 all-to-all-done.1.kv_ref
  136.6 3.6 %attend.1 = bf16[8,208,128]{2,1,0:T(8,128)(2,1)S(1)} custom-call(s32[4]{0:T(128)S(1)} %copy-done.6, bf16[2,192,128]{2,1,0:T(8,128)(2,1)S(1)} %get-tuple-element.34.q0, bf16[2,192,128]{2,1,0:T(8,128)(2,1)S(1)} %collective-permute-done.5.q1, bf16[2,192,128]{2,1,0:T(8,128)(2,1)S(1)} %collective-permute-done.6.q2, ...), custom_call_target="tpu_custom_call" | custom-call | tf_op jit(solution)/shard_map/attend/pallas_call | solution.py:311
  140.1 0.0 collective-permute-done.8.w2
  140.1 11.7 %all_to_all.20.parts_ref = bf16[8,208,128]{2,1,0:T(8,128)(2,1)S(1)} all-to-all(bf16[8,208,128]{2,1,0:T(8,128)(2,1)S(1)} %attend.1), channel_id=1, replica_groups=mesh['y'=4,'zl'=4,'core'=2,'head'=4,'seq'=4] {'y','core'}, dimensions={0} | all-to-all | bytes 851968 | tf_op jit(solution)/shard_map/all_to_all | solution.py:324
  151.8 0.9 combine.1
  152.7 4.6 %all-to-all-start.3 = ((bf16[4,192,256]{2,1,0:T(8,128)(2,1)}), bf16[4,192,256]{2,1,0:T(8,128)(2,1)S(1)}, u32[]{:S(2)}, u32[]{:S(2)}) async-start(bf16[4,192,256]{2,1,0:T(8,128)(2,1)} %combine.1), calls=%async_computation.3 | async-start | bytes 786432 | tf_op jit(solution)/shard_map/all_to_all | solution.py:333
  157.4 0.0 collective-permute-done.10.w3
  157.4 0.0 collective-permute-done.9.w1
  157.4 7.8 %all-to-all-done.3.a_ref = bf16[4,192,256]{2,1,0:T(8,128)(2,1)S(1)} async-done(((bf16[4,192,256]{2,1,0:T(8,128)(2,1)}), bf16[4,192,256]{2,1,0:T(8,128)(2,1)S(1)}, u32[]{:S(2)}, u32[]{:S(2)}) %all-to-all-start.3) | async-done | bytes 393248 | tf_op jit(solution)/shard_map/all_to_all | solution.py:333
  165.2 0.0 copy-done.3
  165.2 2.4 %branch.1 = (bf16[192,384]{1,0:T(8,128)(2,1)S(1)}, bf16[192,384]{1,0:T(8,128)(2,1)S(1)}, bf16[192,384]{1,0:T(8,128)(2,1)S(1)}, bf16[192,384]{1,0:T(8,128)(2,1)S(1)}) custom-call(s32[4]{0:T(128)S(1)} %copy-done.6, bf16[4,192,256]{2,1,0:T(8,128)(2,1)S(1)} %all-to-all-done.3.a_ref, bf16[4,256,384]{2,1,0:T(8,128)(2,1)S(1)} %copy-done.3, ...), custom_call_target="tpu_custom_call" | custom-call | tf_op jit(solution)/shard_map/branch/pallas_call | solution.py:334
  167.6 7.1 %collective-permute-start.11 = (bf16[192,384]{1,0:T(8,128)(2,1)S(1)}, bf16[192,384]{1,0:T(8,128)(2,1)S(1)}, u32[]{:S(2)}, u32[]{:S(2)}) collective-permute-start(bf16[192,384]{1,0:T(8,128)(2,1)S(1)} %get-tuple-element.46), channel_id=1, source_target_pairs={{0,4},{4,8},{8,12},{12,0},{1,5},{5,9},{9,13},{13,1},{2,6},{6,10},{... | collective-permute-start | bytes 442376 | tf_op jit(solution)/shard_map/ppermute | solution.py:342
  174.7 2.6 %collective-permute-start.12 = (bf16[192,384]{1,0:T(8,128)(2,1)S(1)}, bf16[192,384]{1,0:T(8,128)(2,1)S(1)}, u32[]{:S(2)}, u32[]{:S(2)}) collective-permute-start(bf16[192,384]{1,0:T(8,128)(2,1)S(1)} %get-tuple-element.47), channel_id=1, source_target_pairs={{0,12},{4,0},{8,4},{12,8},{1,13},{5,1},{9,5},{13,9},{2,14},{6,2},{... | collective-permute-start | bytes 442376 | tf_op jit(solution)/shard_map/ppermute | solution.py:342
  177.3 8.9 %collective-permute-start.13 = (bf16[192,384]{1,0:T(8,128)(2,1)S(1)}, bf16[192,384]{1,0:T(8,128)(2,1)S(1)}, u32[]{:S(2)}, u32[]{:S(2)}) collective-permute-start(bf16[192,384]{1,0:T(8,128)(2,1)S(1)} %get-tuple-element.48), channel_id=1, source_target_pairs={{0,8},{4,12},{8,0},{12,4},{1,9},{5,13},{9,1},{13,5},{2,10},{6,14},... | collective-permute-start | bytes 442376 | tf_op jit(solution)/shard_map/ppermute | solution.py:342
  186.2 0.1 dynamic-slice_reduce_fusion.1
  186.3 0.0 collective-permute-done.11
  186.3 15.2 %collective-permute-done.12 = bf16[192,384]{1,0:T(8,128)(2,1)S(1)} collective-permute-done((bf16[192,384]{1,0:T(8,128)(2,1)S(1)}, bf16[192,384]{1,0:T(8,128)(2,1)S(1)}, u32[]{:S(2)}, u32[]{:S(2)}) %collective-permute-start.12) | collective-permute-done | bytes 147488 | tf_op jit(solution)/shard_map/ppermute | solution.py:342
  201.5 3.8 %collective-permute-done.13 = bf16[192,384]{1,0:T(8,128)(2,1)S(1)} collective-permute-done((bf16[192,384]{1,0:T(8,128)(2,1)S(1)}, bf16[192,384]{1,0:T(8,128)(2,1)S(1)}, u32[]{:S(2)}, u32[]{:S(2)}) %collective-permute-start.13) | collective-permute-done | bytes 147488 | tf_op jit(solution)/shard_map/ppermute | solution.py:342
  205.3 0.0 copy-done.5
  205.3 0.8 add_convert_fusion
  (7 shorter events, 0.0 us)
Async XLA Ops:
  6.5 55.9 %copy-start = (f32[8,3,6144]{2,0,1:T(8,128)S(1)}, f32[8,3,6144]{2,0,1:T(8,128)}, u32[]{:S(2)}) copy-start(f32[8,3,6144]{2,0,1:T(8,128)} %param.15) | copy-start | bytes 1769476
  6.5 92.5 %all-gather.2.cloned.1.call-start = ((), (), s32[]{:S(2)}) async-start(), calls=%async_computation.4 | async-start | bytes 9732096 | tf_op jit(solution)/shard_map/all_gather | solution.py:223
  9.2 20.3 %collective-permute-start = (bf16[192,384]{1,0:T(8,128)(2,1)}, bf16[192,384]{1,0:T(8,128)(2,1)S(1)}, u32[]{:S(2)}, u32[]{:S(2)}) collective-permute-start(bf16[192,384]{1,0:T(8,128)(2,1)} %own_ref.1), channel_id=1, source_target_pairs={{0,4},{4,8},{8,12},{12,0},{1,5},{5,9},{9,13},{13,1},{2,6},{6,10},{... | collective-permute-start | bytes 442376 | tf_op jit(solution)/shard_map/ppermute | solution.py:246
  18.3 21.7 %collective-permute-start.2 = (bf16[192,384]{1,0:T(8,128)(2,1)}, bf16[192,384]{1,0:T(8,128)(2,1)S(1)}, u32[]{:S(2)}, u32[]{:S(2)}) collective-permute-start(bf16[192,384]{1,0:T(8,128)(2,1)} %own_ref.1), channel_id=1, source_target_pairs={{0,12},{4,0},{8,4},{12,8},{1,13},{5,1},{9,5},{13,9},{2,14},{6,2},{... | collective-permute-start | bytes 442376 | tf_op jit(solution)/shard_map/ppermute | solution.py:247
  29.5 16.4 %collective-permute-start.1 = (bf16[96,384]{1,0:T(8,128)(2,1)S(1)}, bf16[96,384]{1,0:T(8,128)(2,1)S(1)}, u32[]{:S(2)}, u32[]{:S(2)}) collective-permute-start(bf16[96,384]{1,0:T(8,128)(2,1)S(1)} %slice.13), channel_id=1, source_target_pairs={{0,4},{4,8},{8,12},{12,0},{1,5},{5,9},{9,13},{13,1},{2,6},{6,10},{... | collective-permute-start | bytes 221192 | tf_op jit(solution)/shard_map/ppermute | solution.py:248
  40.0 14.8 %collective-permute-start.3 = (bf16[96,384]{1,0:T(8,128)(2,1)S(1)}, bf16[96,384]{1,0:T(8,128)(2,1)S(1)}, u32[]{:S(2)}, u32[]{:S(2)}) collective-permute-start(bf16[96,384]{1,0:T(8,128)(2,1)S(1)} %slice.14), channel_id=1, source_target_pairs={{0,12},{4,0},{8,4},{12,8},{1,13},{5,1},{9,5},{13,9},{2,14},{6,2},{... | collective-permute-start | bytes 221192 | tf_op jit(solution)/shard_map/ppermute | solution.py:249
  54.8 0.9 copy-start.4
  57.3 27.7 %all-to-all-start = ((bf16[4,4,192,384]{3,2,1,0:T(8,128)(2,1)}), bf16[4,4,192,384]{3,2,1,0:T(8,128)(2,1)S(1)}, u32[]{:S(2)}, u32[]{:S(2)}) async-start(bf16[4,4,192,384]{3,2,1,0:T(8,128)(2,1)} %spread.1), calls=%async_computation | async-start | bytes 4718592 | tf_op jit(solution)/shard_map/all_to_all | solution.py:260
  63.3 21.7 %copy-start.6 = (s32[4]{0:T(128)S(1)}, s32[4]{0:T(128)}, u32[]{:S(2)}) copy-start(s32[4]{0:T(128)} %pad_add_fusion.place_ref) | copy-start | bytes 52
  85.0 14.0 %copy-start.7 = (f32[128]{0:T(128)S(1)}, f32[128]{0:T(128)}, u32[]{:S(2)}) copy-start(f32[128]{0:T(128)} %param.12) | copy-start | bytes 1540
  85.0 14.0 %copy-start.8 = (f32[128]{0:T(128)S(1)}, f32[128]{0:T(128)}, u32[]{:S(2)}) copy-start(f32[128]{0:T(128)} %param.13) | copy-start | bytes 1540
  89.3 1.4 copy-start.1
  90.7 6.4 %collective-permute-start.4 = (bf16[192,6144]{1,0:T(8,128)(2,1)S(1)}, bf16[192,6144]{1,0:T(8,128)(2,1)S(1)}, u32[]{:S(2)}, u32[]{:S(2)}) collective-permute-start(bf16[192,6144]{1,0:T(8,128)(2,1)S(1)} %norm.1.own_ref), channel_id=1, source_target_pairs={{0,16},{16,0},{1,17},{17,1},{2,18},{18,2},{3,19},{19,3},{4,20},{20... | collective-permute-start | bytes 7077896 | tf_op jit(solution)/shard_map/ppermute | solution.py:276
  104.6 0.9 copy-start.2
  105.5 31.0 %all-to-all-start.1 = ((bf16[4,2,2,192,128]{4,3,2,1,0:T(8,128)(2,1)}), bf16[4,2,2,192,128]{4,3,2,1,0:T(8,128)(2,1)S(1)}, u32[]{:S(2)}, u32[]{:S(2)}) async-start(bf16[4,2,2,192,128]{4,3,2,1,0:T(8,128)(2,1)} %copy-done.2), calls=%async_computation.1 | async-start | bytes 1572864 | tf_op jit(solution)/shard_map/all_to_all | solution.py:304
  111.8 53.4 %copy-start.3 = (bf16[4,256,384]{2,1,0:T(8,128)(2,1)S(1)}, bf16[4,256,384]{2,1,0:T(8,128)(2,1)}, u32[]{:S(2)}) copy-start(bf16[4,256,384]{2,1,0:T(8,128)(2,1)} %get-tuple-element.41.w0) | copy-start | bytes 2359300
  111.8 28.3 %collective-permute-start.8 = (bf16[4,256,384]{2,1,0:T(8,128)(2,1)}, bf16[4,256,384]{2,1,0:T(8,128)(2,1)S(1)}, u32[]{:S(2)}, u32[]{:S(2)}) collective-permute-start(bf16[4,256,384]{2,1,0:T(8,128)(2,1)} %get-tuple-element.39), channel_id=1, source_target_pairs={{0,2},{1,3},{2,0},{3,1},{4,6},{5,7},{6,4},{7,5},{8,10},{9,11},{10,... | collective-permute-start | bytes 2359304 | tf_op jit(solution)/shard_map/ppermute | solution.py:263
  114.8 10.7 %collective-permute-start.5 = (bf16[2,192,128]{2,1,0:T(8,128)(2,1)S(1)}, bf16[2,192,128]{2,1,0:T(8,128)(2,1)S(1)}, u32[]{:S(2)}, u32[]{:S(2)}) collective-permute-start(bf16[2,192,128]{2,1,0:T(8,128)(2,1)S(1)} %get-tuple-element.34.q0), channel_id=1, source_target_pairs={{0,128},{128,256},{256,384},{384,0},{1,129},{129,257},{257,385},{3... | collective-permute-start | bytes 294920 | tf_op jit(solution)/shard_map/ppermute | solution.py:305
  118.1 8.2 %collective-permute-start.6 = (bf16[2,192,128]{2,1,0:T(8,128)(2,1)S(1)}, bf16[2,192,128]{2,1,0:T(8,128)(2,1)S(1)}, u32[]{:S(2)}, u32[]{:S(2)}) collective-permute-start(bf16[2,192,128]{2,1,0:T(8,128)(2,1)S(1)} %get-tuple-element.34.q0), channel_id=1, source_target_pairs={{0,256},{128,384},{256,0},{384,128},{1,257},{129,385},{257,1},{385... | collective-permute-start | bytes 294920 | tf_op jit(solution)/shard_map/ppermute | solution.py:305
  123.5 6.5 %collective-permute-start.7 = (bf16[2,192,128]{2,1,0:T(8,128)(2,1)S(1)}, bf16[2,192,128]{2,1,0:T(8,128)(2,1)S(1)}, u32[]{:S(2)}, u32[]{:S(2)}) collective-permute-start(bf16[2,192,128]{2,1,0:T(8,128)(2,1)S(1)} %get-tuple-element.34.q0), channel_id=1, source_target_pairs={{0,384},{128,0},{256,128},{384,256},{1,385},{129,1},{257,129},{385... | collective-permute-start | bytes 294920 | tf_op jit(solution)/shard_map/ppermute | solution.py:305
  130.0 27.3 %collective-permute-start.10 = (bf16[4,256,384]{2,1,0:T(8,128)(2,1)}, bf16[4,256,384]{2,1,0:T(8,128)(2,1)}, u32[]{:S(2)}, u32[]{:S(2)}) collective-permute-start(bf16[4,256,384]{2,1,0:T(8,128)(2,1)} %get-tuple-element.44), channel_id=1, source_target_pairs={{0,3},{1,0},{2,1},{3,2},{4,7},{5,4},{6,5},{7,6},{8,11},{9,8},{10,9... | collective-permute-start | bytes 2359304 | tf_op jit(solution)/shard_map/ppermute | solution.py:308
  134.6 22.8 %collective-permute-start.9 = (bf16[4,256,384]{2,1,0:T(8,128)(2,1)}, bf16[4,256,384]{2,1,0:T(8,128)(2,1)}, u32[]{:S(2)}, u32[]{:S(2)}) collective-permute-start(bf16[4,256,384]{2,1,0:T(8,128)(2,1)} %get-tuple-element.42), channel_id=1, source_target_pairs={{0,1},{1,2},{2,3},{3,0},{4,5},{5,6},{6,7},{7,4},{8,9},{9,10},{10,1... | collective-permute-start | bytes 2359304 | tf_op jit(solution)/shard_map/ppermute | solution.py:307
  152.7 52.5 %copy-start.5 = (bf16[192,384]{1,0:T(8,128)(2,1)S(1)}, bf16[192,384]{1,0:T(8,128)(2,1)}, u32[]{:S(2)}) copy-start(bf16[192,384]{1,0:T(8,128)(2,1)} %own_ref.1) | copy-start | bytes 442372
  152.7 12.5 %all-to-all-start.3 = ((bf16[4,192,256]{2,1,0:T(8,128)(2,1)}), bf16[4,192,256]{2,1,0:T(8,128)(2,1)S(1)}, u32[]{:S(2)}, u32[]{:S(2)}) async-start(bf16[4,192,256]{2,1,0:T(8,128)(2,1)} %combine.1), calls=%async_computation.3 | async-start | bytes 786432 | tf_op jit(solution)/shard_map/all_to_all | solution.py:333
  167.6 18.7 %collective-permute-start.11 = (bf16[192,384]{1,0:T(8,128)(2,1)S(1)}, bf16[192,384]{1,0:T(8,128)(2,1)S(1)}, u32[]{:S(2)}, u32[]{:S(2)}) collective-permute-start(bf16[192,384]{1,0:T(8,128)(2,1)S(1)} %get-tuple-element.46), channel_id=1, source_target_pairs={{0,4},{4,8},{8,12},{12,0},{1,5},{5,9},{9,13},{13,1},{2,6},{6,10},{... | collective-permute-start | bytes 442376 | tf_op jit(solution)/shard_map/ppermute | solution.py:342
  174.7 26.7 %collective-permute-start.12 = (bf16[192,384]{1,0:T(8,128)(2,1)S(1)}, bf16[192,384]{1,0:T(8,128)(2,1)S(1)}, u32[]{:S(2)}, u32[]{:S(2)}) collective-permute-start(bf16[192,384]{1,0:T(8,128)(2,1)S(1)} %get-tuple-element.47), channel_id=1, source_target_pairs={{0,12},{4,0},{8,4},{12,8},{1,13},{5,1},{9,5},{13,9},{2,14},{6,2},{... | collective-permute-start | bytes 442376 | tf_op jit(solution)/shard_map/ppermute | solution.py:342
  177.3 27.9 %collective-permute-start.13 = (bf16[192,384]{1,0:T(8,128)(2,1)S(1)}, bf16[192,384]{1,0:T(8,128)(2,1)S(1)}, u32[]{:S(2)}, u32[]{:S(2)}) collective-permute-start(bf16[192,384]{1,0:T(8,128)(2,1)S(1)} %get-tuple-element.48), channel_id=1, source_target_pairs={{0,8},{4,12},{8,0},{12,4},{1,9},{5,13},{9,1},{13,5},{2,10},{6,14},... | collective-permute-start | bytes 442376 | tf_op jit(solution)/shard_map/ppermute | solution.py:342
Sparse Core Ops, SparseCore 0:
  9.5 89.5 all-gather.1

commit v12 on v11

--- a/solution.py
+++ b/solution.py
@@ -339,7 +339,7 @@
         compiler_params=PARAMS,
         name="branch",
     )(place, around, out0, out1, out2, out3)
-    shares = [lax.ppermute(outs[k], "head", shift(k)) for k in (1, 3, 2)]
+    shares = [lax.ppermute(outs[k], "head", shift(k)) for k in (2, 1, 3)]
     summed = outs[0].astype(F32)
     for share in shares:
         summed = summed + share.astype(F32)

time: 214 us -> 212 us (level)
  the two profiles are of different devices: /device:TPU:32 before, /device:TPU:1 now
where the time goes in v12:
time: 212 us; the launch traced here: 208 us
  starting transfers between devices  91.4 us (43%)
  waiting for transfers between devices  57.3 us (27%)
  Pallas kernels  25.4 us (12%)
  between operations  15 us (7%)
  blocking collectives  13.4 us (6%)
  local copies, waits for them, and re-layouts  3.62 us (2%)
    ppermute x3, starting transfers between devices, per_device(): shares = [lax.ppermute(outs[k], 'head', shift(k)) for k in (2, 1, 3)]  17.8 us
    all_to_all x1, waiting for transfers between devices, per_device(): raw = lax.all_to_all(raw, 'seq', 0, 0, tiled=True)  17.7 us
    ppermute x3, waiting for transfers between devices, per_device(): shares = [lax.ppermute(outs[k], 'head', shift(k)) for k in (2, 1, 3)]  15.5 us
    ppermute x1, starting transfers between devices, per_device(): far_low = lax.ppermute(before[:half], 'head', shift(1))  15.1 us
    all_to_all x1, blocking collectives, per_device(): parts = lax.all_to_all(parts, ('y', 'core'), 0, 0, tiled=True)  13.4 us
    ppermute x3, starting transfers between devices, per_device(): lax.ppermute(queries, 'y', shift(k))  9.96 us
    ppermute x1, starting transfers between devices, per_device(): before = lax.ppermute(latents, 'head', shift(1))  9.65 us
    ppermute x1, starting transfers between devices, per_device(): sibling = lax.ppermute(hidden, 'core', [(0, 1), (1, 0)])  7.49 us
  transfers between devices with their start and end apart: 18, of which 11 were waited for; matrix products, arithmetic and copies ran while one was open for 1% of the time, Pallas kernels for 7%

profile of v12, /device:TPU:1, one launch (start us, length us, event | category | flops | bytes accessed | tf_op | source)
XLA Modules:
  0.0 207.6 jit_solution(8236981303274408189)
XLA Ops:
  6.5 0.0 copy-start
  6.5 0.0 all-gather.2.cloned.1.call-start
  7.3 1.9 average.1
  9.1 0.0 all-gather.2.cloned.1.call-update
  9.2 9.6 %collective-permute-start = (bf16[192,384]{1,0:T(8,128)(2,1)}, bf16[192,384]{1,0:T(8,128)(2,1)S(1)}, u32[]{:S(2)}, u32[]{:S(2)}) collective-permute-start(bf16[192,384]{1,0:T(8,128)(2,1)} %own_ref.1), channel_id=1, source_target_pairs={{0,4},{4,8},{8,12},{12,0},{1,5},{5,9},{9,13},{13,1},{2,6},{6,10},{... | collective-permute-start | bytes 442376 | tf_op jit(solution)/shard_map/ppermute | solution.py:246
  18.8 5.6 %collective-permute-start.2 = (bf16[192,384]{1,0:T(8,128)(2,1)}, bf16[192,384]{1,0:T(8,128)(2,1)S(1)}, u32[]{:S(2)}, u32[]{:S(2)}) collective-permute-start(bf16[192,384]{1,0:T(8,128)(2,1)} %own_ref.1), channel_id=1, source_target_pairs={{0,12},{4,0},{8,4},{12,8},{1,13},{5,1},{9,5},{13,9},{2,14},{6,2},{... | collective-permute-start | bytes 442376 | tf_op jit(solution)/shard_map/ppermute | solution.py:247
  24.4 1.5 collective-permute-done.before_ref
  25.9 15.1 %collective-permute-start.1 = (bf16[96,384]{1,0:T(8,128)(2,1)S(1)}, bf16[96,384]{1,0:T(8,128)(2,1)S(1)}, u32[]{:S(2)}, u32[]{:S(2)}) collective-permute-start(bf16[96,384]{1,0:T(8,128)(2,1)S(1)} %slice.13), channel_id=1, source_target_pairs={{0,4},{4,8},{8,12},{12,0},{1,5},{5,9},{9,13},{13,1},{2,6},{6,10},{... | collective-permute-start | bytes 221192 | tf_op jit(solution)/shard_map/ppermute | solution.py:248
  40.9 0.0 collective-permute-done.2.after_ref
  41.0 3.3 %collective-permute-start.3 = (bf16[96,384]{1,0:T(8,128)(2,1)S(1)}, bf16[96,384]{1,0:T(8,128)(2,1)S(1)}, u32[]{:S(2)}, u32[]{:S(2)}) collective-permute-start(bf16[96,384]{1,0:T(8,128)(2,1)S(1)} %slice.14), channel_id=1, source_target_pairs={{0,12},{4,0},{8,4},{12,8},{1,13},{5,1},{9,5},{13,9},{2,14},{6,2},{... | collective-permute-start | bytes 221192 | tf_op jit(solution)/shard_map/ppermute | solution.py:249
  44.3 2.2 %collective-permute-done.1.low_ref = bf16[96,384]{1,0:T(8,128)(2,1)S(1)} collective-permute-done((bf16[96,384]{1,0:T(8,128)(2,1)S(1)}, bf16[96,384]{1,0:T(8,128)(2,1)S(1)}, u32[]{:S(2)}, u32[]{:S(2)}) %collective-permute-start.1) | collective-permute-done | bytes 73760 | tf_op jit(solution)/shard_map/ppermute | solution.py:248
  46.5 4.8 %collective-permute-done.3.high_ref = bf16[96,384]{1,0:T(8,128)(2,1)S(1)} collective-permute-done((bf16[96,384]{1,0:T(8,128)(2,1)S(1)}, bf16[96,384]{1,0:T(8,128)(2,1)S(1)}, u32[]{:S(2)}, u32[]{:S(2)}) %collective-permute-start.3) | collective-permute-done | bytes 73760 | tf_op jit(solution)/shard_map/ppermute | solution.py:249
  51.2 0.0 copy-start.4
  51.2 0.9 copy-done.4
  52.1 1.6 spread.1
  53.7 4.0 %all-to-all-start = ((bf16[4,4,192,384]{3,2,1,0:T(8,128)(2,1)}), bf16[4,4,192,384]{3,2,1,0:T(8,128)(2,1)S(1)}, u32[]{:S(2)}, u32[]{:S(2)}) async-start(bf16[4,4,192,384]{3,2,1,0:T(8,128)(2,1)} %spread.1), calls=%async_computation | async-start | bytes 4718592 | tf_op jit(solution)/shard_map/all_to_all | solution.py:260
  58.4 0.0 copy-done
  58.4 0.2 dynamic-slice_reduce_fusion
  58.7 0.1 reshape.15.mod_ref
  58.7 0.7 pad_add_fusion.place_ref
  59.4 5.2 %pick.1 = (bf16[4,256,384]{2,1,0:T(8,128)(2,1)}, bf16[4,256,384]{2,1,0:T(8,128)(2,1)}, bf16[4,256,384]{2,1,0:T(8,128)(2,1)}, bf16[4,256,384]{2,1,0:T(8,128)(2,1)}) custom-call(s32[4]{0:T(128)} %pad_add_fusion.place_ref, bf16[256,6144]{1,0:T(8,128)(2,1)} %refs_3_.1, bf16[256,6144]{1,0:T(8,128)(2,1)} %refs_3_.1, bf16[256,6144]{1,0:T(8,128)(2,1)} %refs_3_.1, ...), custom_call_target="tpu_custom_call" | custom-call | tf_op jit(solution)/shard_map/pick/pallas_call | solution.py:232
  64.6 17.7 %all-to-all-done.raw_ref = bf16[4,4,192,384]{3,2,1,0:T(8,128)(2,1)S(1)} async-done(((bf16[4,4,192,384]{3,2,1,0:T(8,128)(2,1)}), bf16[4,4,192,384]{3,2,1,0:T(8,128)(2,1)S(1)}, u32[]{:S(2)}, u32[]{:S(2)}) %all-to-all-start) | async-done | bytes 2359328 | tf_op jit(solution)/shard_map/all_to_all | solution.py:260
  82.3 0.0 copy-done.6
  82.3 4.3 %norm.1.own_ref = bf16[192,6144]{1,0:T(8,128)(2,1)S(1)} custom-call(s32[4]{0:T(128)S(1)} %copy-done.6, bf16[4,4,192,384]{3,2,1,0:T(8,128)(2,1)S(1)} %all-to-all-done.raw_ref, f32[3,4,4,384]{3,2,1,0:T(4,128)S(1)} %reshape.15.mod_ref), custom_call_target="tpu_custom_call" | custom-call | tf_op jit(solution)/shard_map/norm/pallas_call | solution.py:264
  86.5 0.0 copy-start.1
  86.5 1.4 copy-done.1
  87.9 7.5 %collective-permute-start.4 = (bf16[192,6144]{1,0:T(8,128)(2,1)S(1)}, bf16[192,6144]{1,0:T(8,128)(2,1)S(1)}, u32[]{:S(2)}, u32[]{:S(2)}) collective-permute-start(bf16[192,6144]{1,0:T(8,128)(2,1)S(1)} %norm.1.own_ref), channel_id=1, source_target_pairs={{0,16},{16,0},{1,17},{17,1},{2,18},{18,2},{3,19},{19,3},{4,20},{20... | collective-permute-start | bytes 7077896 | tf_op jit(solution)/shard_map/ppermute | solution.py:276
  95.4 4.1 %collective-permute-done.4.other_ref = bf16[192,6144]{1,0:T(8,128)(2,1)S(1)} collective-permute-done((bf16[192,6144]{1,0:T(8,128)(2,1)S(1)}, bf16[192,6144]{1,0:T(8,128)(2,1)S(1)}, u32[]{:S(2)}, u32[]{:S(2)}) %collective-permute-start.4) | collective-permute-done | bytes 2359328 | tf_op jit(solution)/shard_map/ppermute | solution.py:276
  99.6 1.4 all-gather.2.cloned.1.call-done.weight_ref
  101.0 0.0 copy-done.7
  101.0 0.0 copy-done.8
  101.0 5.6 %project.1 = (bf16[2,192,128]{2,1,0:T(8,128)(2,1)S(1)}, bf16[4,2,2,192,128]{4,3,2,1,0:T(8,128)(2,1)S(1)}) custom-call(s32[4]{0:T(128)S(1)} %copy-done.6, bf16[192,6144]{1,0:T(8,128)(2,1)} %copy-done.1, bf16[192,6144]{1,0:T(8,128)(2,1)S(1)} %collective-permute-done.4.other_ref, bf16[2,6144,384]{2,1,0:T(8,128)(2,1)} %all-gather.2.cloned.1.call-done.weight_ref, ...), custom_call_target="tpu_custom_call" | custom-call | tf_op jit(solution)/shard_map/project/pallas_call | solution.py:280
  106.6 0.0 copy-start.2
  106.6 0.9 copy-done.2
  107.5 5.1 %all-to-all-start.1 = ((bf16[4,2,2,192,128]{4,3,2,1,0:T(8,128)(2,1)}), bf16[4,2,2,192,128]{4,3,2,1,0:T(8,128)(2,1)S(1)}, u32[]{:S(2)}, u32[]{:S(2)}) async-start(bf16[4,2,2,192,128]{4,3,2,1,0:T(8,128)(2,1)} %copy-done.2), calls=%async_computation.1 | async-start | bytes 1572864 | tf_op jit(solution)/shard_map/all_to_all | solution.py:304
  112.5 3.1 %collective-permute-start.8 = (bf16[4,256,384]{2,1,0:T(8,128)(2,1)}, bf16[4,256,384]{2,1,0:T(8,128)(2,1)S(1)}, u32[]{:S(2)}, u32[]{:S(2)}) collective-permute-start(bf16[4,256,384]{2,1,0:T(8,128)(2,1)} %get-tuple-element.39), channel_id=1, source_target_pairs={{0,2},{1,3},{2,0},{3,1},{4,6},{5,7},{6,4},{7,5},{8,10},{9,11},{10,... | collective-permute-start | bytes 2359304 | tf_op jit(solution)/shard_map/ppermute | solution.py:263
  115.7 3.0 %collective-permute-start.5 = (bf16[2,192,128]{2,1,0:T(8,128)(2,1)S(1)}, bf16[2,192,128]{2,1,0:T(8,128)(2,1)S(1)}, u32[]{:S(2)}, u32[]{:S(2)}) collective-permute-start(bf16[2,192,128]{2,1,0:T(8,128)(2,1)S(1)} %get-tuple-element.34.q0), channel_id=1, source_target_pairs={{0,128},{128,256},{256,384},{384,0},{1,129},{129,257},{257,385},{3... | collective-permute-start | bytes 294920 | tf_op jit(solution)/shard_map/ppermute | solution.py:305
  118.7 4.8 %collective-permute-start.6 = (bf16[2,192,128]{2,1,0:T(8,128)(2,1)S(1)}, bf16[2,192,128]{2,1,0:T(8,128)(2,1)S(1)}, u32[]{:S(2)}, u32[]{:S(2)}) collective-permute-start(bf16[2,192,128]{2,1,0:T(8,128)(2,1)S(1)} %get-tuple-element.34.q0), channel_id=1, source_target_pairs={{0,256},{128,384},{256,0},{384,128},{1,257},{129,385},{257,1},{385... | collective-permute-start | bytes 294920 | tf_op jit(solution)/shard_map/ppermute | solution.py:305
  123.5 2.1 %collective-permute-start.7 = (bf16[2,192,128]{2,1,0:T(8,128)(2,1)S(1)}, bf16[2,192,128]{2,1,0:T(8,128)(2,1)S(1)}, u32[]{:S(2)}, u32[]{:S(2)}) collective-permute-start(bf16[2,192,128]{2,1,0:T(8,128)(2,1)S(1)} %get-tuple-element.34.q0), channel_id=1, source_target_pairs={{0,384},{128,0},{256,128},{384,256},{1,385},{129,1},{257,129},{385... | collective-permute-start | bytes 294920 | tf_op jit(solution)/shard_map/ppermute | solution.py:305
  125.6 0.0 collective-permute-done.5.q1
  125.7 0.6 collective-permute-done.6.q2
  126.3 2.9 %collective-permute-done.7.q3 = bf16[2,192,128]{2,1,0:T(8,128)(2,1)S(1)} collective-permute-done((bf16[2,192,128]{2,1,0:T(8,128)(2,1)S(1)}, bf16[2,192,128]{2,1,0:T(8,128)(2,1)S(1)}, u32[]{:S(2)}, u32[]{:S(2)}) %collective-permute-start.7) | collective-permute-done | bytes 98336 | tf_op jit(solution)/shard_map/ppermute | solution.py:305
  129.2 4.2 %collective-permute-start.10 = (bf16[4,256,384]{2,1,0:T(8,128)(2,1)}, bf16[4,256,384]{2,1,0:T(8,128)(2,1)}, u32[]{:S(2)}, u32[]{:S(2)}) collective-permute-start(bf16[4,256,384]{2,1,0:T(8,128)(2,1)} %get-tuple-element.44), channel_id=1, source_target_pairs={{0,3},{1,0},{2,1},{3,2},{4,7},{5,4},{6,5},{7,6},{8,11},{9,8},{10,9... | collective-permute-start | bytes 2359304 | tf_op jit(solution)/shard_map/ppermute | solution.py:308
  133.4 1.9 collective-permute-start.9
  135.3 0.0 all-to-all-done.1.kv_ref
  135.3 3.6 %attend.1 = bf16[8,208,128]{2,1,0:T(8,128)(2,1)S(1)} custom-call(s32[4]{0:T(128)S(1)} %copy-done.6, bf16[2,192,128]{2,1,0:T(8,128)(2,1)S(1)} %get-tuple-element.34.q0, bf16[2,192,128]{2,1,0:T(8,128)(2,1)S(1)} %collective-permute-done.5.q1, bf16[2,192,128]{2,1,0:T(8,128)(2,1)S(1)} %collective-permute-done.6.q2, ...), custom_call_target="tpu_custom_call" | custom-call | tf_op jit(solution)/shard_map/attend/pallas_call | solution.py:311
  138.9 0.0 collective-permute-done.8.w2
  138.9 13.4 %all_to_all.20.parts_ref = bf16[8,208,128]{2,1,0:T(8,128)(2,1)S(1)} all-to-all(bf16[8,208,128]{2,1,0:T(8,128)(2,1)S(1)} %attend.1), channel_id=1, replica_groups=mesh['y'=4,'zl'=4,'core'=2,'head'=4,'seq'=4] {'y','core'}, dimensions={0} | all-to-all | bytes 851968 | tf_op jit(solution)/shard_map/all_to_all | solution.py:324
  152.3 0.9 combine.1
  153.2 4.3 %all-to-all-start.3 = ((bf16[4,192,256]{2,1,0:T(8,128)(2,1)}), bf16[4,192,256]{2,1,0:T(8,128)(2,1)S(1)}, u32[]{:S(2)}, u32[]{:S(2)}) async-start(bf16[4,192,256]{2,1,0:T(8,128)(2,1)} %combine.1), calls=%async_computation.3 | async-start | bytes 786432 | tf_op jit(solution)/shard_map/all_to_all | solution.py:333
  157.6 0.0 collective-permute-done.10.w3
  157.6 0.0 collective-permute-done.9.w1
  157.6 6.6 %all-to-all-done.3.a_ref = bf16[4,192,256]{2,1,0:T(8,128)(2,1)S(1)} async-done(((bf16[4,192,256]{2,1,0:T(8,128)(2,1)}), bf16[4,192,256]{2,1,0:T(8,128)(2,1)S(1)}, u32[]{:S(2)}, u32[]{:S(2)}) %all-to-all-start.3) | async-done | bytes 393248 | tf_op jit(solution)/shard_map/all_to_all | solution.py:333
  164.2 0.0 copy-done.3
  164.2 2.4 %branch.1 = (bf16[192,384]{1,0:T(8,128)(2,1)S(1)}, bf16[192,384]{1,0:T(8,128)(2,1)S(1)}, bf16[192,384]{1,0:T(8,128)(2,1)S(1)}, bf16[192,384]{1,0:T(8,128)(2,1)S(1)}) custom-call(s32[4]{0:T(128)S(1)} %copy-done.6, bf16[4,192,256]{2,1,0:T(8,128)(2,1)S(1)} %all-to-all-done.3.a_ref, bf16[4,256,384]{2,1,0:T(8,128)(2,1)S(1)} %copy-done.3, ...), custom_call_target="tpu_custom_call" | custom-call | tf_op jit(solution)/shard_map/branch/pallas_call | solution.py:334
  166.6 8.6 %collective-permute-start.11 = (bf16[192,384]{1,0:T(8,128)(2,1)S(1)}, bf16[192,384]{1,0:T(8,128)(2,1)S(1)}, u32[]{:S(2)}, u32[]{:S(2)}) collective-permute-start(bf16[192,384]{1,0:T(8,128)(2,1)S(1)} %get-tuple-element.46), channel_id=1, source_target_pairs={{0,8},{4,12},{8,0},{12,4},{1,9},{5,13},{9,1},{13,5},{2,10},{6,14},... | collective-permute-start | bytes 442376 | tf_op jit(solution)/shard_map/ppermute | solution.py:342
  175.2 4.2 %collective-permute-start.12 = (bf16[192,384]{1,0:T(8,128)(2,1)S(1)}, bf16[192,384]{1,0:T(8,128)(2,1)S(1)}, u32[]{:S(2)}, u32[]{:S(2)}) collective-permute-start(bf16[192,384]{1,0:T(8,128)(2,1)S(1)} %get-tuple-element.47), channel_id=1, source_target_pairs={{0,4},{4,8},{8,12},{12,0},{1,5},{5,9},{9,13},{13,1},{2,6},{6,10},{... | collective-permute-start | bytes 442376 | tf_op jit(solution)/shard_map/ppermute | solution.py:342
  179.4 5.0 %collective-permute-start.13 = (bf16[192,384]{1,0:T(8,128)(2,1)S(1)}, bf16[192,384]{1,0:T(8,128)(2,1)S(1)}, u32[]{:S(2)}, u32[]{:S(2)}) collective-permute-start(bf16[192,384]{1,0:T(8,128)(2,1)S(1)} %get-tuple-element.48), channel_id=1, source_target_pairs={{0,12},{4,0},{8,4},{12,8},{1,13},{5,1},{9,5},{13,9},{2,14},{6,2},{... | collective-permute-start | bytes 442376 | tf_op jit(solution)/shard_map/ppermute | solution.py:342
  184.4 0.1 dynamic-slice_reduce_fusion.1
  184.5 0.0 collective-permute-done.11
  184.5 10.6 %collective-permute-done.12 = bf16[192,384]{1,0:T(8,128)(2,1)S(1)} collective-permute-done((bf16[192,384]{1,0:T(8,128)(2,1)S(1)}, bf16[192,384]{1,0:T(8,128)(2,1)S(1)}, u32[]{:S(2)}, u32[]{:S(2)}) %collective-permute-start.12) | collective-permute-done | bytes 147488 | tf_op jit(solution)/shard_map/ppermute | solution.py:342
  195.1 4.9 %collective-permute-done.13 = bf16[192,384]{1,0:T(8,128)(2,1)S(1)} collective-permute-done((bf16[192,384]{1,0:T(8,128)(2,1)S(1)}, bf16[192,384]{1,0:T(8,128)(2,1)S(1)}, u32[]{:S(2)}, u32[]{:S(2)}) %collective-permute-start.13) | collective-permute-done | bytes 147488 | tf_op jit(solution)/shard_map/ppermute | solution.py:342
  200.0 0.0 copy-done.5
  200.0 0.8 add_convert_fusion
  (7 shorter events, 0.0 us)
Async XLA Ops:
  6.5 51.9 %copy-start = (f32[8,3,6144]{2,0,1:T(8,128)S(1)}, f32[8,3,6144]{2,0,1:T(8,128)}, u32[]{:S(2)}) copy-start(f32[8,3,6144]{2,0,1:T(8,128)} %param.15) | copy-start | bytes 1769476
  6.5 94.4 %all-gather.2.cloned.1.call-start = ((), (), s32[]{:S(2)}) async-start(), calls=%async_computation.4 | async-start | bytes 9732096 | tf_op jit(solution)/shard_map/all_gather | solution.py:223
  9.2 16.7 %collective-permute-start = (bf16[192,384]{1,0:T(8,128)(2,1)}, bf16[192,384]{1,0:T(8,128)(2,1)S(1)}, u32[]{:S(2)}, u32[]{:S(2)}) collective-permute-start(bf16[192,384]{1,0:T(8,128)(2,1)} %own_ref.1), channel_id=1, source_target_pairs={{0,4},{4,8},{8,12},{12,0},{1,5},{5,9},{9,13},{13,1},{2,6},{6,10},{... | collective-permute-start | bytes 442376 | tf_op jit(solution)/shard_map/ppermute | solution.py:246
  18.8 22.1 %collective-permute-start.2 = (bf16[192,384]{1,0:T(8,128)(2,1)}, bf16[192,384]{1,0:T(8,128)(2,1)S(1)}, u32[]{:S(2)}, u32[]{:S(2)}) collective-permute-start(bf16[192,384]{1,0:T(8,128)(2,1)} %own_ref.1), channel_id=1, source_target_pairs={{0,12},{4,0},{8,4},{12,8},{1,13},{5,1},{9,5},{13,9},{2,14},{6,2},{... | collective-permute-start | bytes 442376 | tf_op jit(solution)/shard_map/ppermute | solution.py:247
  25.9 20.6 %collective-permute-start.1 = (bf16[96,384]{1,0:T(8,128)(2,1)S(1)}, bf16[96,384]{1,0:T(8,128)(2,1)S(1)}, u32[]{:S(2)}, u32[]{:S(2)}) collective-permute-start(bf16[96,384]{1,0:T(8,128)(2,1)S(1)} %slice.13), channel_id=1, source_target_pairs={{0,4},{4,8},{8,12},{12,0},{1,5},{5,9},{9,13},{13,1},{2,6},{6,10},{... | collective-permute-start | bytes 221192 | tf_op jit(solution)/shard_map/ppermute | solution.py:248
  41.0 10.3 %collective-permute-start.3 = (bf16[96,384]{1,0:T(8,128)(2,1)S(1)}, bf16[96,384]{1,0:T(8,128)(2,1)S(1)}, u32[]{:S(2)}, u32[]{:S(2)}) collective-permute-start(bf16[96,384]{1,0:T(8,128)(2,1)S(1)} %slice.14), channel_id=1, source_target_pairs={{0,12},{4,0},{8,4},{12,8},{1,13},{5,1},{9,5},{13,9},{2,14},{6,2},{... | collective-permute-start | bytes 221192 | tf_op jit(solution)/shard_map/ppermute | solution.py:249
  51.2 0.9 copy-start.4
  53.7 28.5 %all-to-all-start = ((bf16[4,4,192,384]{3,2,1,0:T(8,128)(2,1)}), bf16[4,4,192,384]{3,2,1,0:T(8,128)(2,1)S(1)}, u32[]{:S(2)}, u32[]{:S(2)}) async-start(bf16[4,4,192,384]{3,2,1,0:T(8,128)(2,1)} %spread.1), calls=%async_computation | async-start | bytes 4718592 | tf_op jit(solution)/shard_map/all_to_all | solution.py:260
  59.4 22.9 %copy-start.6 = (s32[4]{0:T(128)S(1)}, s32[4]{0:T(128)}, u32[]{:S(2)}) copy-start(s32[4]{0:T(128)} %pad_add_fusion.place_ref) | copy-start | bytes 52
  82.3 18.7 %copy-start.7 = (f32[128]{0:T(128)S(1)}, f32[128]{0:T(128)}, u32[]{:S(2)}) copy-start(f32[128]{0:T(128)} %param.12) | copy-start | bytes 1540
  82.3 18.7 %copy-start.8 = (f32[128]{0:T(128)S(1)}, f32[128]{0:T(128)}, u32[]{:S(2)}) copy-start(f32[128]{0:T(128)} %param.13) | copy-start | bytes 1540
  86.5 1.4 copy-start.1
  87.9 11.6 %collective-permute-start.4 = (bf16[192,6144]{1,0:T(8,128)(2,1)S(1)}, bf16[192,6144]{1,0:T(8,128)(2,1)S(1)}, u32[]{:S(2)}, u32[]{:S(2)}) collective-permute-start(bf16[192,6144]{1,0:T(8,128)(2,1)S(1)} %norm.1.own_ref), channel_id=1, source_target_pairs={{0,16},{16,0},{1,17},{17,1},{2,18},{18,2},{3,19},{19,3},{4,20},{20... | collective-permute-start | bytes 7077896 | tf_op jit(solution)/shard_map/ppermute | solution.py:276
  106.6 0.9 copy-start.2
  107.5 27.8 %all-to-all-start.1 = ((bf16[4,2,2,192,128]{4,3,2,1,0:T(8,128)(2,1)}), bf16[4,2,2,192,128]{4,3,2,1,0:T(8,128)(2,1)S(1)}, u32[]{:S(2)}, u32[]{:S(2)}) async-start(bf16[4,2,2,192,128]{4,3,2,1,0:T(8,128)(2,1)} %copy-done.2), calls=%async_computation.1 | async-start | bytes 1572864 | tf_op jit(solution)/shard_map/all_to_all | solution.py:304
  112.5 51.7 %copy-start.3 = (bf16[4,256,384]{2,1,0:T(8,128)(2,1)S(1)}, bf16[4,256,384]{2,1,0:T(8,128)(2,1)}, u32[]{:S(2)}) copy-start(bf16[4,256,384]{2,1,0:T(8,128)(2,1)} %get-tuple-element.41.w0) | copy-start | bytes 2359300
  112.5 26.4 %collective-permute-start.8 = (bf16[4,256,384]{2,1,0:T(8,128)(2,1)}, bf16[4,256,384]{2,1,0:T(8,128)(2,1)S(1)}, u32[]{:S(2)}, u32[]{:S(2)}) collective-permute-start(bf16[4,256,384]{2,1,0:T(8,128)(2,1)} %get-tuple-element.39), channel_id=1, source_target_pairs={{0,2},{1,3},{2,0},{3,1},{4,6},{5,7},{6,4},{7,5},{8,10},{9,11},{10,... | collective-permute-start | bytes 2359304 | tf_op jit(solution)/shard_map/ppermute | solution.py:263
  115.7 10.0 %collective-permute-start.5 = (bf16[2,192,128]{2,1,0:T(8,128)(2,1)S(1)}, bf16[2,192,128]{2,1,0:T(8,128)(2,1)S(1)}, u32[]{:S(2)}, u32[]{:S(2)}) collective-permute-start(bf16[2,192,128]{2,1,0:T(8,128)(2,1)S(1)} %get-tuple-element.34.q0), channel_id=1, source_target_pairs={{0,128},{128,256},{256,384},{384,0},{1,129},{129,257},{257,385},{3... | collective-permute-start | bytes 294920 | tf_op jit(solution)/shard_map/ppermute | solution.py:305
  118.7 7.6 %collective-permute-start.6 = (bf16[2,192,128]{2,1,0:T(8,128)(2,1)S(1)}, bf16[2,192,128]{2,1,0:T(8,128)(2,1)S(1)}, u32[]{:S(2)}, u32[]{:S(2)}) collective-permute-start(bf16[2,192,128]{2,1,0:T(8,128)(2,1)S(1)} %get-tuple-element.34.q0), channel_id=1, source_target_pairs={{0,256},{128,384},{256,0},{384,128},{1,257},{129,385},{257,1},{385... | collective-permute-start | bytes 294920 | tf_op jit(solution)/shard_map/ppermute | solution.py:305
  123.5 5.7 %collective-permute-start.7 = (bf16[2,192,128]{2,1,0:T(8,128)(2,1)S(1)}, bf16[2,192,128]{2,1,0:T(8,128)(2,1)S(1)}, u32[]{:S(2)}, u32[]{:S(2)}) collective-permute-start(bf16[2,192,128]{2,1,0:T(8,128)(2,1)S(1)} %get-tuple-element.34.q0), channel_id=1, source_target_pairs={{0,384},{128,0},{256,128},{384,256},{1,385},{129,1},{257,129},{385... | collective-permute-start | bytes 294920 | tf_op jit(solution)/shard_map/ppermute | solution.py:305
  129.2 28.4 %collective-permute-start.10 = (bf16[4,256,384]{2,1,0:T(8,128)(2,1)}, bf16[4,256,384]{2,1,0:T(8,128)(2,1)}, u32[]{:S(2)}, u32[]{:S(2)}) collective-permute-start(bf16[4,256,384]{2,1,0:T(8,128)(2,1)} %get-tuple-element.44), channel_id=1, source_target_pairs={{0,3},{1,0},{2,1},{3,2},{4,7},{5,4},{6,5},{7,6},{8,11},{9,8},{10,9... | collective-permute-start | bytes 2359304 | tf_op jit(solution)/shard_map/ppermute | solution.py:308
  133.4 24.2 %collective-permute-start.9 = (bf16[4,256,384]{2,1,0:T(8,128)(2,1)}, bf16[4,256,384]{2,1,0:T(8,128)(2,1)}, u32[]{:S(2)}, u32[]{:S(2)}) collective-permute-start(bf16[4,256,384]{2,1,0:T(8,128)(2,1)} %get-tuple-element.42), channel_id=1, source_target_pairs={{0,1},{1,2},{2,3},{3,0},{4,5},{5,6},{6,7},{7,4},{8,9},{9,10},{10,1... | collective-permute-start | bytes 2359304 | tf_op jit(solution)/shard_map/ppermute | solution.py:307
  153.2 46.7 %copy-start.5 = (bf16[192,384]{1,0:T(8,128)(2,1)S(1)}, bf16[192,384]{1,0:T(8,128)(2,1)}, u32[]{:S(2)}) copy-start(bf16[192,384]{1,0:T(8,128)(2,1)} %own_ref.1) | copy-start | bytes 442372
  153.2 11.0 %all-to-all-start.3 = ((bf16[4,192,256]{2,1,0:T(8,128)(2,1)}), bf16[4,192,256]{2,1,0:T(8,128)(2,1)S(1)}, u32[]{:S(2)}, u32[]{:S(2)}) async-start(bf16[4,192,256]{2,1,0:T(8,128)(2,1)} %combine.1), calls=%async_computation.3 | async-start | bytes 786432 | tf_op jit(solution)/shard_map/all_to_all | solution.py:333
  166.6 17.9 %collective-permute-start.11 = (bf16[192,384]{1,0:T(8,128)(2,1)S(1)}, bf16[192,384]{1,0:T(8,128)(2,1)S(1)}, u32[]{:S(2)}, u32[]{:S(2)}) collective-permute-start(bf16[192,384]{1,0:T(8,128)(2,1)S(1)} %get-tuple-element.46), channel_id=1, source_target_pairs={{0,8},{4,12},{8,0},{12,4},{1,9},{5,13},{9,1},{13,5},{2,10},{6,14},... | collective-permute-start | bytes 442376 | tf_op jit(solution)/shard_map/ppermute | solution.py:342
  175.2 19.9 %collective-permute-start.12 = (bf16[192,384]{1,0:T(8,128)(2,1)S(1)}, bf16[192,384]{1,0:T(8,128)(2,1)S(1)}, u32[]{:S(2)}, u32[]{:S(2)}) collective-permute-start(bf16[192,384]{1,0:T(8,128)(2,1)S(1)} %get-tuple-element.47), channel_id=1, source_target_pairs={{0,4},{4,8},{8,12},{12,0},{1,5},{5,9},{9,13},{13,1},{2,6},{6,10},{... | collective-permute-start | bytes 442376 | tf_op jit(solution)/shard_map/ppermute | solution.py:342
  179.4 20.6 %collective-permute-start.13 = (bf16[192,384]{1,0:T(8,128)(2,1)S(1)}, bf16[192,384]{1,0:T(8,128)(2,1)S(1)}, u32[]{:S(2)}, u32[]{:S(2)}) collective-permute-start(bf16[192,384]{1,0:T(8,128)(2,1)S(1)} %get-tuple-element.48), channel_id=1, source_target_pairs={{0,12},{4,0},{8,4},{12,8},{1,13},{5,1},{9,5},{13,9},{2,14},{6,2},{... | collective-permute-start | bytes 442376 | tf_op jit(solution)/shard_map/ppermute | solution.py:342
Sparse Core Ops, SparseCore 0:
  9.5 91.4 all-gather.1

commit v13 on v12

--- a/solution.py
+++ b/solution.py
@@ -260,7 +260,6 @@
     raw = lax.all_to_all(raw, "seq", 0, 0, tiled=True)
     out0, out1, out2, out3 = out_parts
     raw, out1, out2, out3 = lax.optimization_barrier((raw, out1, out2, out3))
-    out2 = lax.ppermute(out2, "seq", shift(2))
     hidden = pl.pallas_call(
         norm_kernel,
         in_specs=[in_smem, in_vmem, in_vmem],
@@ -303,7 +302,8 @@
 
     pairs = lax.all_to_all(pairs, "zl", 0, 0, tiled=True)
     queries = [queries] + [lax.ppermute(queries, "y", shift(k)) for k in (1, 2, 3)]
-    *queries, out1, out3 = lax.optimization_barrier((*queries, out1, out3))
+    *queries, out1, out2, out3 = lax.optimization_barrier((*queries, out1, out2, out3))
+    out2 = lax.ppermute(out2, "seq", shift(2))
     out1 = lax.ppermute(out1, "seq", shift(1))
     out3 = lax.ppermute(out3, "seq", shift(3))
 
@@ -320,7 +320,6 @@
         compiler_params=PARAMS,
         name="attend",
     )(place, *queries, pairs)
-    parts, out2 = lax.optimization_barrier((parts, out2))
     parts = lax.all_to_all(parts, ("y", "core"), 0, 0, tiled=True)
     around = pl.pallas_call(
         combine_kernel,

time: 212 us -> 220 us (1.038)
  waiting for transfers between devices: 57.3 us -> 67.7 us
    ppermute x1, waiting for transfers between devices: 0.01 us -> 8.71 us  [per_device(): out2 = lax.ppermute(out2, 'seq', shift(2))]
  transfers between devices with their start and end apart: 18 -> 18, of which waited for: 11 -> 12; matrix products, arithmetic and copies ran while one was open for 1% -> 0% of each run, Pallas kernels for 7% -> 7%
where the time goes in v13:
time: 220 us; the launch traced here: 217 us
  starting transfers between devices  90.7 us (41%)
  waiting for transfers between devices  67.7 us (31%)
  Pallas kernels  25.4 us (12%)
  between operations  15 us (7%)
  blocking collectives  13.4 us (6%)
  local copies, waits for them, and re-layouts  3.62 us (2%)
    ppermute x3, starting transfers between devices, per_device(): shares = [lax.ppermute(outs[k], 'head', shift(k)) for k in (2, 1, 3)]  17.8 us
    all_to_all x1, waiting for transfers between devices, per_device(): raw = lax.all_to_all(raw, 'seq', 0, 0, tiled=True)  17.7 us
    ppermute x3, waiting for transfers between devices, per_device(): shares = [lax.ppermute(outs[k], 'head', shift(k)) for k in (2, 1, 3)]  17 us
    ppermute x1, starting transfers between devices, per_device(): far_low = lax.ppermute(before[:half], 'head', shift(1))  15.1 us
    all_to_all x1, blocking collectives, per_device(): parts = lax.all_to_all(parts, ('y', 'core'), 0, 0, tiled=True)  13.4 us
    ppermute x3, starting transfers between devices, per_device(): lax.ppermute(queries, 'y', shift(k))  10.6 us
    ppermute x1, starting transfers between devices, per_device(): before = lax.ppermute(latents, 'head', shift(1))  9.65 us
    ppermute x1, waiting for transfers between devices, per_device(): out2 = lax.ppermute(out2, 'seq', shift(2))  8.71 us
  transfers between devices with their start and end apart: 18, of which 12 were waited for; matrix products, arithmetic and copies ran while one was open for 0% of the time, Pallas kernels for 7%

profile of v13, /device:TPU:1, one launch (start us, length us, event | category | flops | bytes accessed | tf_op | source)
XLA Modules:
  0.0 217.2 jit_solution(1563535744520279)
XLA Ops:
  6.5 0.0 copy-start
  6.5 0.0 all-gather.2.cloned.1.call-start
  7.3 1.9 average.1
  9.1 0.0 all-gather.2.cloned.1.call-update
  9.2 9.6 %collective-permute-start = (bf16[192,384]{1,0:T(8,128)(2,1)}, bf16[192,384]{1,0:T(8,128)(2,1)S(1)}, u32[]{:S(2)}, u32[]{:S(2)}) collective-permute-start(bf16[192,384]{1,0:T(8,128)(2,1)} %own_ref.1), channel_id=1, source_target_pairs={{0,4},{4,8},{8,12},{12,0},{1,5},{5,9},{9,13},{13,1},{2,6},{6,10},{... | collective-permute-start | bytes 442376 | tf_op jit(solution)/shard_map/ppermute | solution.py:246
  18.8 5.6 %collective-permute-start.2 = (bf16[192,384]{1,0:T(8,128)(2,1)}, bf16[192,384]{1,0:T(8,128)(2,1)S(1)}, u32[]{:S(2)}, u32[]{:S(2)}) collective-permute-start(bf16[192,384]{1,0:T(8,128)(2,1)} %own_ref.1), channel_id=1, source_target_pairs={{0,12},{4,0},{8,4},{12,8},{1,13},{5,1},{9,5},{13,9},{2,14},{6,2},{... | collective-permute-start | bytes 442376 | tf_op jit(solution)/shard_map/ppermute | solution.py:247
  24.4 1.5 collective-permute-done.before_ref
  25.9 15.1 %collective-permute-start.1 = (bf16[96,384]{1,0:T(8,128)(2,1)S(1)}, bf16[96,384]{1,0:T(8,128)(2,1)S(1)}, u32[]{:S(2)}, u32[]{:S(2)}) collective-permute-start(bf16[96,384]{1,0:T(8,128)(2,1)S(1)} %slice.13), channel_id=1, source_target_pairs={{0,4},{4,8},{8,12},{12,0},{1,5},{5,9},{9,13},{13,1},{2,6},{6,10},{... | collective-permute-start | bytes 221192 | tf_op jit(solution)/shard_map/ppermute | solution.py:248
  40.9 0.0 collective-permute-done.2.after_ref
  41.0 3.3 %collective-permute-start.3 = (bf16[96,384]{1,0:T(8,128)(2,1)S(1)}, bf16[96,384]{1,0:T(8,128)(2,1)S(1)}, u32[]{:S(2)}, u32[]{:S(2)}) collective-permute-start(bf16[96,384]{1,0:T(8,128)(2,1)S(1)} %slice.14), channel_id=1, source_target_pairs={{0,12},{4,0},{8,4},{12,8},{1,13},{5,1},{9,5},{13,9},{2,14},{6,2},{... | collective-permute-start | bytes 221192 | tf_op jit(solution)/shard_map/ppermute | solution.py:249
  44.3 2.2 %collective-permute-done.1.low_ref = bf16[96,384]{1,0:T(8,128)(2,1)S(1)} collective-permute-done((bf16[96,384]{1,0:T(8,128)(2,1)S(1)}, bf16[96,384]{1,0:T(8,128)(2,1)S(1)}, u32[]{:S(2)}, u32[]{:S(2)}) %collective-permute-start.1) | collective-permute-done | bytes 73760 | tf_op jit(solution)/shard_map/ppermute | solution.py:248
  46.5 4.8 %collective-permute-done.3.high_ref = bf16[96,384]{1,0:T(8,128)(2,1)S(1)} collective-permute-done((bf16[96,384]{1,0:T(8,128)(2,1)S(1)}, bf16[96,384]{1,0:T(8,128)(2,1)S(1)}, u32[]{:S(2)}, u32[]{:S(2)}) %collective-permute-start.3) | collective-permute-done | bytes 73760 | tf_op jit(solution)/shard_map/ppermute | solution.py:249
  51.2 0.0 copy-start.4
  51.2 0.9 copy-done.4
  52.1 1.6 spread.1
  53.7 4.0 %all-to-all-start = ((bf16[4,4,192,384]{3,2,1,0:T(8,128)(2,1)}), bf16[4,4,192,384]{3,2,1,0:T(8,128)(2,1)S(1)}, u32[]{:S(2)}, u32[]{:S(2)}) async-start(bf16[4,4,192,384]{3,2,1,0:T(8,128)(2,1)} %spread.1), calls=%async_computation | async-start | bytes 4718592 | tf_op jit(solution)/shard_map/all_to_all | solution.py:260
  58.4 0.0 copy-done
  58.4 0.2 dynamic-slice_reduce_fusion
  58.7 0.1 reshape.15.mod_ref
  58.7 0.7 pad_add_fusion.place_ref
  59.4 5.2 %pick.1 = (bf16[4,256,384]{2,1,0:T(8,128)(2,1)}, bf16[4,256,384]{2,1,0:T(8,128)(2,1)}, bf16[4,256,384]{2,1,0:T(8,128)(2,1)}, bf16[4,256,384]{2,1,0:T(8,128)(2,1)}) custom-call(s32[4]{0:T(128)} %pad_add_fusion.place_ref, bf16[256,6144]{1,0:T(8,128)(2,1)} %refs_3_.1, bf16[256,6144]{1,0:T(8,128)(2,1)} %refs_3_.1, bf16[256,6144]{1,0:T(8,128)(2,1)} %refs_3_.1, ...), custom_call_target="tpu_custom_call" | custom-call | tf_op jit(solution)/shard_map/pick/pallas_call | solution.py:232
  64.6 17.7 %all-to-all-done.raw_ref = bf16[4,4,192,384]{3,2,1,0:T(8,128)(2,1)S(1)} async-done(((bf16[4,4,192,384]{3,2,1,0:T(8,128)(2,1)}), bf16[4,4,192,384]{3,2,1,0:T(8,128)(2,1)S(1)}, u32[]{:S(2)}, u32[]{:S(2)}) %all-to-all-start) | async-done | bytes 2359328 | tf_op jit(solution)/shard_map/all_to_all | solution.py:260
  82.3 0.0 copy-done.6
  82.3 4.3 %norm.1.own_ref = bf16[192,6144]{1,0:T(8,128)(2,1)S(1)} custom-call(s32[4]{0:T(128)S(1)} %copy-done.6, bf16[4,4,192,384]{3,2,1,0:T(8,128)(2,1)S(1)} %all-to-all-done.raw_ref, f32[3,4,4,384]{3,2,1,0:T(4,128)S(1)} %reshape.15.mod_ref), custom_call_target="tpu_custom_call" | custom-call | tf_op jit(solution)/shard_map/norm/pallas_call | solution.py:263
  86.5 0.0 copy-start.1
  86.5 1.4 copy-done.1
  87.9 7.5 %collective-permute-start.4 = (bf16[192,6144]{1,0:T(8,128)(2,1)S(1)}, bf16[192,6144]{1,0:T(8,128)(2,1)S(1)}, u32[]{:S(2)}, u32[]{:S(2)}) collective-permute-start(bf16[192,6144]{1,0:T(8,128)(2,1)S(1)} %norm.1.own_ref), channel_id=1, source_target_pairs={{0,16},{16,0},{1,17},{17,1},{2,18},{18,2},{3,19},{19,3},{4,20},{20... | collective-permute-start | bytes 7077896 | tf_op jit(solution)/shard_map/ppermute | solution.py:275
  95.4 4.1 %collective-permute-done.4.other_ref = bf16[192,6144]{1,0:T(8,128)(2,1)S(1)} collective-permute-done((bf16[192,6144]{1,0:T(8,128)(2,1)S(1)}, bf16[192,6144]{1,0:T(8,128)(2,1)S(1)}, u32[]{:S(2)}, u32[]{:S(2)}) %collective-permute-start.4) | collective-permute-done | bytes 2359328 | tf_op jit(solution)/shard_map/ppermute | solution.py:275
  99.6 1.4 all-gather.2.cloned.1.call-done.weight_ref
  101.0 0.0 copy-done.7
  101.0 0.0 copy-done.8
  101.0 5.6 %project.1 = (bf16[2,192,128]{2,1,0:T(8,128)(2,1)S(1)}, bf16[4,2,2,192,128]{4,3,2,1,0:T(8,128)(2,1)S(1)}) custom-call(s32[4]{0:T(128)S(1)} %copy-done.6, bf16[192,6144]{1,0:T(8,128)(2,1)} %copy-done.1, bf16[192,6144]{1,0:T(8,128)(2,1)S(1)} %collective-permute-done.4.other_ref, bf16[2,6144,384]{2,1,0:T(8,128)(2,1)} %all-gather.2.cloned.1.call-done.weight_ref, ...), custom_call_target="tpu_custom_call" | custom-call | tf_op jit(solution)/shard_map/project/pallas_call | solution.py:279
  106.6 0.0 copy-start.2
  106.6 0.9 copy-done.2
  107.5 5.1 %all-to-all-start.1 = ((bf16[4,2,2,192,128]{4,3,2,1,0:T(8,128)(2,1)}), bf16[4,2,2,192,128]{4,3,2,1,0:T(8,128)(2,1)S(1)}, u32[]{:S(2)}, u32[]{:S(2)}) async-start(bf16[4,2,2,192,128]{4,3,2,1,0:T(8,128)(2,1)} %copy-done.2), calls=%async_computation.1 | async-start | bytes 1572864 | tf_op jit(solution)/shard_map/all_to_all | solution.py:303
  112.5 2.4 %collective-permute-start.5 = (bf16[2,192,128]{2,1,0:T(8,128)(2,1)S(1)}, bf16[2,192,128]{2,1,0:T(8,128)(2,1)S(1)}, u32[]{:S(2)}, u32[]{:S(2)}) collective-permute-start(bf16[2,192,128]{2,1,0:T(8,128)(2,1)S(1)} %get-tuple-element.34.q0), channel_id=1, source_target_pairs={{0,128},{128,256},{256,384},{384,0},{1,129},{129,257},{257,385},{3... | collective-permute-start | bytes 294920 | tf_op jit(solution)/shard_map/ppermute | solution.py:304
  114.9 6.3 %collective-permute-start.6 = (bf16[2,192,128]{2,1,0:T(8,128)(2,1)S(1)}, bf16[2,192,128]{2,1,0:T(8,128)(2,1)S(1)}, u32[]{:S(2)}, u32[]{:S(2)}) collective-permute-start(bf16[2,192,128]{2,1,0:T(8,128)(2,1)S(1)} %get-tuple-element.34.q0), channel_id=1, source_target_pairs={{0,256},{128,384},{256,0},{384,128},{1,257},{129,385},{257,1},{385... | collective-permute-start | bytes 294920 | tf_op jit(solution)/shard_map/ppermute | solution.py:304
  121.2 1.9 collective-permute-start.7
  123.2 0.0 collective-permute-done.5.q1
  123.2 0.7 collective-permute-done.6.q2
  123.9 2.7 %collective-permute-done.7.q3 = bf16[2,192,128]{2,1,0:T(8,128)(2,1)S(1)} collective-permute-done((bf16[2,192,128]{2,1,0:T(8,128)(2,1)S(1)}, bf16[2,192,128]{2,1,0:T(8,128)(2,1)S(1)}, u32[]{:S(2)}, u32[]{:S(2)}) %collective-permute-start.7) | collective-permute-done | bytes 98336 | tf_op jit(solution)/shard_map/ppermute | solution.py:304
  126.6 2.8 %collective-permute-start.10 = (bf16[4,256,384]{2,1,0:T(8,128)(2,1)}, bf16[4,256,384]{2,1,0:T(8,128)(2,1)S(1)}, u32[]{:S(2)}, u32[]{:S(2)}) collective-permute-start(bf16[4,256,384]{2,1,0:T(8,128)(2,1)} %get-tuple-element.42), channel_id=1, source_target_pairs={{0,3},{1,0},{2,1},{3,2},{4,7},{5,4},{6,5},{7,6},{8,11},{9,8},{10,9... | collective-permute-start | bytes 2359304 | tf_op jit(solution)/shard_map/ppermute | solution.py:308
  129.4 2.5 %collective-permute-start.8 = (bf16[4,256,384]{2,1,0:T(8,128)(2,1)}, bf16[4,256,384]{2,1,0:T(8,128)(2,1)}, u32[]{:S(2)}, u32[]{:S(2)}) collective-permute-start(bf16[4,256,384]{2,1,0:T(8,128)(2,1)} %get-tuple-element.40), channel_id=1, source_target_pairs={{0,1},{1,2},{2,3},{3,0},{4,5},{5,6},{6,7},{7,4},{8,9},{9,10},{10,1... | collective-permute-start | bytes 2359304 | tf_op jit(solution)/shard_map/ppermute | solution.py:307
  131.9 2.8 %collective-permute-start.9 = (bf16[4,256,384]{2,1,0:T(8,128)(2,1)}, bf16[4,256,384]{2,1,0:T(8,128)(2,1)}, u32[]{:S(2)}, u32[]{:S(2)}) collective-permute-start(bf16[4,256,384]{2,1,0:T(8,128)(2,1)} %get-tuple-element.41), channel_id=1, source_target_pairs={{0,2},{1,3},{2,0},{3,1},{4,6},{5,7},{6,4},{7,5},{8,10},{9,11},{10,... | collective-permute-start | bytes 2359304 | tf_op jit(solution)/shard_map/ppermute | solution.py:306
  134.7 0.0 all-to-all-done.1.kv_ref
  134.7 3.6 %attend.1 = bf16[8,208,128]{2,1,0:T(8,128)(2,1)S(1)} custom-call(s32[4]{0:T(128)S(1)} %copy-done.6, bf16[2,192,128]{2,1,0:T(8,128)(2,1)S(1)} %get-tuple-element.34.q0, bf16[2,192,128]{2,1,0:T(8,128)(2,1)S(1)} %collective-permute-done.5.q1, bf16[2,192,128]{2,1,0:T(8,128)(2,1)S(1)} %collective-permute-done.6.q2, ...), custom_call_target="tpu_custom_call" | custom-call | tf_op jit(solution)/shard_map/attend/pallas_call | solution.py:311
  138.3 13.4 %all_to_all.20.parts_ref = bf16[8,208,128]{2,1,0:T(8,128)(2,1)S(1)} all-to-all(bf16[8,208,128]{2,1,0:T(8,128)(2,1)S(1)} %attend.1), channel_id=1, replica_groups=mesh['y'=4,'zl'=4,'core'=2,'head'=4,'seq'=4] {'y','core'}, dimensions={0} | all-to-all | bytes 851968 | tf_op jit(solution)/shard_map/all_to_all | solution.py:323
  151.7 0.9 combine.1
  152.6 4.1 %all-to-all-start.3 = ((bf16[4,192,256]{2,1,0:T(8,128)(2,1)}), bf16[4,192,256]{2,1,0:T(8,128)(2,1)S(1)}, u32[]{:S(2)}, u32[]{:S(2)}) async-start(bf16[4,192,256]{2,1,0:T(8,128)(2,1)} %combine.1), calls=%async_computation.3 | async-start | bytes 786432 | tf_op jit(solution)/shard_map/all_to_all | solution.py:332
  156.8 0.0 collective-permute-done.10.w3
  156.8 0.0 collective-permute-done.8.w1
  156.8 8.7 %collective-permute-done.9.w2 = bf16[4,256,384]{2,1,0:T(8,128)(2,1)} collective-permute-done((bf16[4,256,384]{2,1,0:T(8,128)(2,1)}, bf16[4,256,384]{2,1,0:T(8,128)(2,1)}, u32[]{:S(2)}, u32[]{:S(2)}) %collective-permute-start.9) | collective-permute-done | bytes 786464 | tf_op jit(solution)/shard_map/ppermute | solution.py:306
  165.5 6.8 %all-to-all-done.3.a_ref = bf16[4,192,256]{2,1,0:T(8,128)(2,1)S(1)} async-done(((bf16[4,192,256]{2,1,0:T(8,128)(2,1)}), bf16[4,192,256]{2,1,0:T(8,128)(2,1)S(1)}, u32[]{:S(2)}, u32[]{:S(2)}) %all-to-all-start.3) | async-done | bytes 393248 | tf_op jit(solution)/shard_map/all_to_all | solution.py:332
  172.3 0.0 copy-done.3
  172.3 2.4 %branch.1 = (bf16[192,384]{1,0:T(8,128)(2,1)S(1)}, bf16[192,384]{1,0:T(8,128)(2,1)S(1)}, bf16[192,384]{1,0:T(8,128)(2,1)S(1)}, bf16[192,384]{1,0:T(8,128)(2,1)S(1)}) custom-call(s32[4]{0:T(128)S(1)} %copy-done.6, bf16[4,192,256]{2,1,0:T(8,128)(2,1)S(1)} %all-to-all-done.3.a_ref, bf16[4,256,384]{2,1,0:T(8,128)(2,1)S(1)} %copy-done.3, ...), custom_call_target="tpu_custom_call" | custom-call | tf_op jit(solution)/shard_map/branch/pallas_call | solution.py:333
  174.7 8.6 %collective-permute-start.11 = (bf16[192,384]{1,0:T(8,128)(2,1)S(1)}, bf16[192,384]{1,0:T(8,128)(2,1)S(1)}, u32[]{:S(2)}, u32[]{:S(2)}) collective-permute-start(bf16[192,384]{1,0:T(8,128)(2,1)S(1)} %get-tuple-element.44), channel_id=1, source_target_pairs={{0,8},{4,12},{8,0},{12,4},{1,9},{5,13},{9,1},{13,5},{2,10},{6,14},... | collective-permute-start | bytes 442376 | tf_op jit(solution)/shard_map/ppermute | solution.py:341
  183.3 4.3 %collective-permute-start.12 = (bf16[192,384]{1,0:T(8,128)(2,1)S(1)}, bf16[192,384]{1,0:T(8,128)(2,1)S(1)}, u32[]{:S(2)}, u32[]{:S(2)}) collective-permute-start(bf16[192,384]{1,0:T(8,128)(2,1)S(1)} %get-tuple-element.45), channel_id=1, source_target_pairs={{0,4},{4,8},{8,12},{12,0},{1,5},{5,9},{9,13},{13,1},{2,6},{6,10},{... | collective-permute-start | bytes 442376 | tf_op jit(solution)/shard_map/ppermute | solution.py:341
  187.6 4.9 %collective-permute-start.13 = (bf16[192,384]{1,0:T(8,128)(2,1)S(1)}, bf16[192,384]{1,0:T(8,128)(2,1)S(1)}, u32[]{:S(2)}, u32[]{:S(2)}) collective-permute-start(bf16[192,384]{1,0:T(8,128)(2,1)S(1)} %get-tuple-element.46), channel_id=1, source_target_pairs={{0,12},{4,0},{8,4},{12,8},{1,13},{5,1},{9,5},{13,9},{2,14},{6,2},{... | collective-permute-start | bytes 442376 | tf_op jit(solution)/shard_map/ppermute | solution.py:341
  192.5 0.1 dynamic-slice_reduce_fusion.1
  192.6 0.0 collective-permute-done.11
  192.6 5.6 %collective-permute-done.12 = bf16[192,384]{1,0:T(8,128)(2,1)S(1)} collective-permute-done((bf16[192,384]{1,0:T(8,128)(2,1)S(1)}, bf16[192,384]{1,0:T(8,128)(2,1)S(1)}, u32[]{:S(2)}, u32[]{:S(2)}) %collective-permute-start.12) | collective-permute-done | bytes 147488 | tf_op jit(solution)/shard_map/ppermute | solution.py:341
  198.2 11.4 %collective-permute-done.13 = bf16[192,384]{1,0:T(8,128)(2,1)S(1)} collective-permute-done((bf16[192,384]{1,0:T(8,128)(2,1)S(1)}, bf16[192,384]{1,0:T(8,128)(2,1)S(1)}, u32[]{:S(2)}, u32[]{:S(2)}) %collective-permute-start.13) | collective-permute-done | bytes 147488 | tf_op jit(solution)/shard_map/ppermute | solution.py:341
  209.6 0.0 copy-done.5
  209.6 0.8 add_convert_fusion
  (7 shorter events, 0.0 us)
Async XLA Ops:
  6.5 51.9 %copy-start = (f32[8,3,6144]{2,0,1:T(8,128)S(1)}, f32[8,3,6144]{2,0,1:T(8,128)}, u32[]{:S(2)}) copy-start(f32[8,3,6144]{2,0,1:T(8,128)} %param.15) | copy-start | bytes 1769476
  6.5 94.4 %all-gather.2.cloned.1.call-start = ((), (), s32[]{:S(2)}) async-start(), calls=%async_computation.4 | async-start | bytes 9732096 | tf_op jit(solution)/shard_map/all_gather | solution.py:223
  9.2 16.7 %collective-permute-start = (bf16[192,384]{1,0:T(8,128)(2,1)}, bf16[192,384]{1,0:T(8,128)(2,1)S(1)}, u32[]{:S(2)}, u32[]{:S(2)}) collective-permute-start(bf16[192,384]{1,0:T(8,128)(2,1)} %own_ref.1), channel_id=1, source_target_pairs={{0,4},{4,8},{8,12},{12,0},{1,5},{5,9},{9,13},{13,1},{2,6},{6,10},{... | collective-permute-start | bytes 442376 | tf_op jit(solution)/shard_map/ppermute | solution.py:246
  18.8 22.1 %collective-permute-start.2 = (bf16[192,384]{1,0:T(8,128)(2,1)}, bf16[192,384]{1,0:T(8,128)(2,1)S(1)}, u32[]{:S(2)}, u32[]{:S(2)}) collective-permute-start(bf16[192,384]{1,0:T(8,128)(2,1)} %own_ref.1), channel_id=1, source_target_pairs={{0,12},{4,0},{8,4},{12,8},{1,13},{5,1},{9,5},{13,9},{2,14},{6,2},{... | collective-permute-start | bytes 442376 | tf_op jit(solution)/shard_map/ppermute | solution.py:247
  25.9 20.6 %collective-permute-start.1 = (bf16[96,384]{1,0:T(8,128)(2,1)S(1)}, bf16[96,384]{1,0:T(8,128)(2,1)S(1)}, u32[]{:S(2)}, u32[]{:S(2)}) collective-permute-start(bf16[96,384]{1,0:T(8,128)(2,1)S(1)} %slice.13), channel_id=1, source_target_pairs={{0,4},{4,8},{8,12},{12,0},{1,5},{5,9},{9,13},{13,1},{2,6},{6,10},{... | collective-permute-start | bytes 221192 | tf_op jit(solution)/shard_map/ppermute | solution.py:248
  41.0 10.3 %collective-permute-start.3 = (bf16[96,384]{1,0:T(8,128)(2,1)S(1)}, bf16[96,384]{1,0:T(8,128)(2,1)S(1)}, u32[]{:S(2)}, u32[]{:S(2)}) collective-permute-start(bf16[96,384]{1,0:T(8,128)(2,1)S(1)} %slice.14), channel_id=1, source_target_pairs={{0,12},{4,0},{8,4},{12,8},{1,13},{5,1},{9,5},{13,9},{2,14},{6,2},{... | collective-permute-start | bytes 221192 | tf_op jit(solution)/shard_map/ppermute | solution.py:249
  51.2 0.9 copy-start.4
  53.7 28.5 %all-to-all-start = ((bf16[4,4,192,384]{3,2,1,0:T(8,128)(2,1)}), bf16[4,4,192,384]{3,2,1,0:T(8,128)(2,1)S(1)}, u32[]{:S(2)}, u32[]{:S(2)}) async-start(bf16[4,4,192,384]{3,2,1,0:T(8,128)(2,1)} %spread.1), calls=%async_computation | async-start | bytes 4718592 | tf_op jit(solution)/shard_map/all_to_all | solution.py:260
  59.4 22.9 %copy-start.6 = (s32[4]{0:T(128)S(1)}, s32[4]{0:T(128)}, u32[]{:S(2)}) copy-start(s32[4]{0:T(128)} %pad_add_fusion.place_ref) | copy-start | bytes 52
  82.3 18.7 %copy-start.7 = (f32[128]{0:T(128)S(1)}, f32[128]{0:T(128)}, u32[]{:S(2)}) copy-start(f32[128]{0:T(128)} %param.12) | copy-start | bytes 1540
  82.3 18.7 %copy-start.8 = (f32[128]{0:T(128)S(1)}, f32[128]{0:T(128)}, u32[]{:S(2)}) copy-start(f32[128]{0:T(128)} %param.13) | copy-start | bytes 1540
  86.5 1.4 copy-start.1
  87.9 11.6 %collective-permute-start.4 = (bf16[192,6144]{1,0:T(8,128)(2,1)S(1)}, bf16[192,6144]{1,0:T(8,128)(2,1)S(1)}, u32[]{:S(2)}, u32[]{:S(2)}) collective-permute-start(bf16[192,6144]{1,0:T(8,128)(2,1)S(1)} %norm.1.own_ref), channel_id=1, source_target_pairs={{0,16},{16,0},{1,17},{17,1},{2,18},{18,2},{3,19},{19,3},{4,20},{20... | collective-permute-start | bytes 7077896 | tf_op jit(solution)/shard_map/ppermute | solution.py:275
  106.6 0.9 copy-start.2
  107.5 27.2 %all-to-all-start.1 = ((bf16[4,2,2,192,128]{4,3,2,1,0:T(8,128)(2,1)}), bf16[4,2,2,192,128]{4,3,2,1,0:T(8,128)(2,1)S(1)}, u32[]{:S(2)}, u32[]{:S(2)}) async-start(bf16[4,2,2,192,128]{4,3,2,1,0:T(8,128)(2,1)} %copy-done.2), calls=%async_computation.1 | async-start | bytes 1572864 | tf_op jit(solution)/shard_map/all_to_all | solution.py:303
  112.5 59.8 %copy-start.3 = (bf16[4,256,384]{2,1,0:T(8,128)(2,1)S(1)}, bf16[4,256,384]{2,1,0:T(8,128)(2,1)}, u32[]{:S(2)}) copy-start(bf16[4,256,384]{2,1,0:T(8,128)(2,1)} %get-tuple-element.39.w0) | copy-start | bytes 2359300
  112.5 10.6 %collective-permute-start.5 = (bf16[2,192,128]{2,1,0:T(8,128)(2,1)S(1)}, bf16[2,192,128]{2,1,0:T(8,128)(2,1)S(1)}, u32[]{:S(2)}, u32[]{:S(2)}) collective-permute-start(bf16[2,192,128]{2,1,0:T(8,128)(2,1)S(1)} %get-tuple-element.34.q0), channel_id=1, source_target_pairs={{0,128},{128,256},{256,384},{384,0},{1,129},{129,257},{257,385},{3... | collective-permute-start | bytes 294920 | tf_op jit(solution)/shard_map/ppermute | solution.py:304
  114.9 9.0 %collective-permute-start.6 = (bf16[2,192,128]{2,1,0:T(8,128)(2,1)S(1)}, bf16[2,192,128]{2,1,0:T(8,128)(2,1)S(1)}, u32[]{:S(2)}, u32[]{:S(2)}) collective-permute-start(bf16[2,192,128]{2,1,0:T(8,128)(2,1)S(1)} %get-tuple-element.34.q0), channel_id=1, source_target_pairs={{0,256},{128,384},{256,0},{384,128},{1,257},{129,385},{257,1},{385... | collective-permute-start | bytes 294920 | tf_op jit(solution)/shard_map/ppermute | solution.py:304
  121.2 5.4 %collective-permute-start.7 = (bf16[2,192,128]{2,1,0:T(8,128)(2,1)S(1)}, bf16[2,192,128]{2,1,0:T(8,128)(2,1)S(1)}, u32[]{:S(2)}, u32[]{:S(2)}) collective-permute-start(bf16[2,192,128]{2,1,0:T(8,128)(2,1)S(1)} %get-tuple-element.34.q0), channel_id=1, source_target_pairs={{0,384},{128,0},{256,128},{384,256},{1,385},{129,1},{257,129},{385... | collective-permute-start | bytes 294920 | tf_op jit(solution)/shard_map/ppermute | solution.py:304
  126.6 30.2 %collective-permute-start.10 = (bf16[4,256,384]{2,1,0:T(8,128)(2,1)}, bf16[4,256,384]{2,1,0:T(8,128)(2,1)S(1)}, u32[]{:S(2)}, u32[]{:S(2)}) collective-permute-start(bf16[4,256,384]{2,1,0:T(8,128)(2,1)} %get-tuple-element.42), channel_id=1, source_target_pairs={{0,3},{1,0},{2,1},{3,2},{4,7},{5,4},{6,5},{7,6},{8,11},{9,8},{10,9... | collective-permute-start | bytes 2359304 | tf_op jit(solution)/shard_map/ppermute | solution.py:308
  129.4 27.4 %collective-permute-start.8 = (bf16[4,256,384]{2,1,0:T(8,128)(2,1)}, bf16[4,256,384]{2,1,0:T(8,128)(2,1)}, u32[]{:S(2)}, u32[]{:S(2)}) collective-permute-start(bf16[4,256,384]{2,1,0:T(8,128)(2,1)} %get-tuple-element.40), channel_id=1, source_target_pairs={{0,1},{1,2},{2,3},{3,0},{4,5},{5,6},{6,7},{7,4},{8,9},{9,10},{10,1... | collective-permute-start | bytes 2359304 | tf_op jit(solution)/shard_map/ppermute | solution.py:307
  131.9 33.6 %collective-permute-start.9 = (bf16[4,256,384]{2,1,0:T(8,128)(2,1)}, bf16[4,256,384]{2,1,0:T(8,128)(2,1)}, u32[]{:S(2)}, u32[]{:S(2)}) collective-permute-start(bf16[4,256,384]{2,1,0:T(8,128)(2,1)} %get-tuple-element.41), channel_id=1, source_target_pairs={{0,2},{1,3},{2,0},{3,1},{4,6},{5,7},{6,4},{7,5},{8,10},{9,11},{10,... | collective-permute-start | bytes 2359304 | tf_op jit(solution)/shard_map/ppermute | solution.py:306
  152.6 57.0 %copy-start.5 = (bf16[192,384]{1,0:T(8,128)(2,1)S(1)}, bf16[192,384]{1,0:T(8,128)(2,1)}, u32[]{:S(2)}) copy-start(bf16[192,384]{1,0:T(8,128)(2,1)} %own_ref.1) | copy-start | bytes 442372
  152.6 19.7 %all-to-all-start.3 = ((bf16[4,192,256]{2,1,0:T(8,128)(2,1)}), bf16[4,192,256]{2,1,0:T(8,128)(2,1)S(1)}, u32[]{:S(2)}, u32[]{:S(2)}) async-start(bf16[4,192,256]{2,1,0:T(8,128)(2,1)} %combine.1), calls=%async_computation.3 | async-start | bytes 786432 | tf_op jit(solution)/shard_map/all_to_all | solution.py:332
  174.7 17.9 %collective-permute-start.11 = (bf16[192,384]{1,0:T(8,128)(2,1)S(1)}, bf16[192,384]{1,0:T(8,128)(2,1)S(1)}, u32[]{:S(2)}, u32[]{:S(2)}) collective-permute-start(bf16[192,384]{1,0:T(8,128)(2,1)S(1)} %get-tuple-element.44), channel_id=1, source_target_pairs={{0,8},{4,12},{8,0},{12,4},{1,9},{5,13},{9,1},{13,5},{2,10},{6,14},... | collective-permute-start | bytes 442376 | tf_op jit(solution)/shard_map/ppermute | solution.py:341
  183.3 14.9 %collective-permute-start.12 = (bf16[192,384]{1,0:T(8,128)(2,1)S(1)}, bf16[192,384]{1,0:T(8,128)(2,1)S(1)}, u32[]{:S(2)}, u32[]{:S(2)}) collective-permute-start(bf16[192,384]{1,0:T(8,128)(2,1)S(1)} %get-tuple-element.45), channel_id=1, source_target_pairs={{0,4},{4,8},{8,12},{12,0},{1,5},{5,9},{9,13},{13,1},{2,6},{6,10},{... | collective-permute-start | bytes 442376 | tf_op jit(solution)/shard_map/ppermute | solution.py:341
  187.6 22.0 %collective-permute-start.13 = (bf16[192,384]{1,0:T(8,128)(2,1)S(1)}, bf16[192,384]{1,0:T(8,128)(2,1)S(1)}, u32[]{:S(2)}, u32[]{:S(2)}) collective-permute-start(bf16[192,384]{1,0:T(8,128)(2,1)S(1)} %get-tuple-element.46), channel_id=1, source_target_pairs={{0,12},{4,0},{8,4},{12,8},{1,13},{5,1},{9,5},{13,9},{2,14},{6,2},{... | collective-permute-start | bytes 442376 | tf_op jit(solution)/shard_map/ppermute | solution.py:341
Sparse Core Ops, SparseCore 0:
  9.5 91.4 all-gather.1
